TPU v7x, 32 devices: a whole 2x2x4 slice. The times are simulated.
32 devices in a mesh: fsdp: 4 (over y, x), context: 2 (over core), tensor: 4 (over z).
Axes of the slice: x: 2, y: 2, z: 4, core: 2. Of those that a mesh axis runs over, the one named last changes fastest.
Arguments:
- tokens: bfloat16 [2048, 640], P(('fsdp', 'context')), may hold values from -16 to 16
- lengths: int32 [4, 4], P('fsdp'), may hold values from 1 to 256, 512 in all within a row
- weight_query: bfloat16 [640, 1024], P('fsdp', 'tensor'), may hold values from -1 to 1
- weight_key: bfloat16 [640, 256], P('fsdp'), may hold values from -1 to 1
- weight_value: bfloat16 [640, 256], P('fsdp'), may hold values from -0.25 to 0.25
- weight_out: bfloat16 [1024, 640], P('tensor', 'fsdp'), may hold values from -0.1875 to 0.1875
- weight_gate: bfloat16 [640, 2048], P('fsdp', 'tensor'), may hold values from -0.25 to 0.25
- weight_up: bfloat16 [640, 2048], P('fsdp', 'tensor'), may hold values from -0.25 to 0.25
- weight_down: bfloat16 [2048, 640], P('tensor', 'fsdp'), may hold values from -0.125 to 0.125
- gain_attn_in: bfloat16 [640], P('fsdp'), may hold values from 0.099609375 to 1.8984375
- gain_attn_out: bfloat16 [640], P('fsdp'), may hold values from 0.099609375 to 1.8984375
- gain_ffn_in: bfloat16 [640], P('fsdp'), may hold values from 0.099609375 to 1.8984375
- gain_ffn_out: bfloat16 [640], P('fsdp'), may hold values from 0.099609375 to 1.8984375
- gain_query: bfloat16 [256], P('fsdp'), may hold values from 0.5 to 2
- gain_key: bfloat16 [256], P('fsdp'), may hold values from 0.5 to 2
- cotangent: bfloat16 [2048, 640], P(('fsdp', 'context')), may hold values from -6 to 6
Outputs:
- layer_output: float32 [2048, 640], P(('fsdp', 'context'))
- grad_input: float32 [2048, 640], P(('fsdp', 'context'))
- grad_weight_query: float32 [640, 1024], P('fsdp', 'tensor')
- grad_weight_key: float32 [640, 256], P('fsdp')
- grad_weight_value: float32 [640, 256], P('fsdp')
- grad_weight_out: float32 [1024, 640], P('tensor', 'fsdp')
- grad_weight_gate: float32 [640, 2048], P('fsdp', 'tensor')
- grad_weight_up: float32 [640, 2048], P('fsdp', 'tensor')
- grad_weight_down: float32 [2048, 640], P('tensor', 'fsdp')
- grad_gain_attn_in: float32 [640], P('fsdp')
- grad_gain_attn_out: float32 [640], P('fsdp')
- grad_gain_ffn_in: float32 [640], P('fsdp')
- grad_gain_ffn_out: float32 [640], P('fsdp')
- grad_gain_query: float32 [256], P('fsdp')
- grad_gain_key: float32 [256], P('fsdp')
Inputs may be any that keep to these rules, and one draw needn't show every extreme that they name: `lengths`: each row sums to 512; its largest entry is exactly 256.
All inputs are finite; a program needn't handle non-finite values.
Results may differ from a plain program's by a relative error of at most 0.015.
Values may be sent and summed in bfloat16 or wider, within the bound.
No kernel may reach another device: no remote copies, remote signals or barrier semaphores. Data moves between devices by JAX's collectives and lax.ppermute only.
A program may use at most 128 MiB of HBM per device.

v0:
```python
import math

import jax
import jax.numpy as jnp
from jax import lax
from jax.sharding import PartitionSpec as P

HD = 256


EPSILON = 1e-06
ROPE_BASE = 1000000.0
GELU_COEF = math.sqrt(2.0 / math.pi)
NEG_LARGE = -1e30


def rms_forward(values, gain_vec):
    inverse = lax.rsqrt(jnp.mean(values * values, axis=-1, keepdims=True) + EPSILON)
    normed = values * inverse
    return (normed * gain_vec, normed, inverse)


def rms_backward(grad_out, gain_vec, normed, inverse):
    gain_grad = jnp.sum(grad_out * normed, axis=tuple(range(grad_out.ndim - 1)))
    inner = grad_out * gain_vec
    grad_in = inverse * (inner - normed * jnp.mean(inner * normed, axis=-1, keepdims=True))
    return (grad_in, gain_grad)


def rope_tables(positions, width):
    half_width = width // 2
    freqs = ROPE_BASE ** (-jnp.arange(half_width, dtype=jnp.float32) * 2.0 / width)
    angles = positions.astype(jnp.float32)[:, None] * freqs[None, :]
    return (jnp.cos(angles)[:, None, :], jnp.sin(angles)[:, None, :])


def rotate(values, cosine, sine):
    half_width = values.shape[-1] // 2
    first_half = values[..., :half_width]
    second_half = values[..., half_width:]
    return jnp.concatenate(
        [first_half * cosine - second_half * sine, second_half * cosine + first_half * sine],
        axis=-1,
    )


def rotate_back(values, cosine, sine):
    half_width = values.shape[-1] // 2
    first_half = values[..., :half_width]
    second_half = values[..., half_width:]
    return jnp.concatenate(
        [first_half * cosine + second_half * sine, second_half * cosine - first_half * sine],
        axis=-1,
    )


def gelu_parts(pre_act):
    cubic = pre_act + 0.044715 * pre_act * pre_act * pre_act
    tangent = jnp.tanh(GELU_COEF * cubic)
    gelu_val = 0.5 * pre_act * (1.0 + tangent)
    slope = 0.5 * (1.0 + tangent) + 0.5 * pre_act * (1.0 - tangent * tangent) * GELU_COEF * (
        1.0 + 3.0 * 0.044715 * pre_act * pre_act
    )
    return (gelu_val, slope)


def doc_info(positions, doc_lengths):
    doc_ends = jnp.cumsum(doc_lengths)
    passed = positions[:, None] >= doc_ends[None, :]
    segment = jnp.sum(passed.astype(jnp.int32), axis=1)
    doc_start = jnp.sum(jnp.where(passed, doc_lengths[None, :], 0), axis=1)
    return (segment, positions - doc_start)


def dot32(mat_left, mat_right):
    return jnp.dot(mat_left, mat_right, preferred_element_type=jnp.float32)


def contract_last(mat_left, mat_right):
    return lax.dot_general(
        mat_left, mat_right, (((1,), (1,)), ((), ())), preferred_element_type=jnp.float32
    )


def contract_first(mat_left, mat_right):
    return lax.dot_general(
        mat_left, mat_right, (((0,), (0,)), ((), ())), preferred_element_type=jnp.float32
    )


def on_device(
    tokens,
    lengths,
    weight_query,
    weight_key,
    weight_value,
    weight_out,
    weight_gate,
    weight_up,
    weight_down,
    gain_attn_in,
    gain_attn_out,
    gain_ffn_in,
    gain_ffn_out,
    gain_query,
    gain_key,
    cotangent,
):
    gathered = (
        lax.all_gather(weight_query, "fsdp", axis=0, tiled=True),
        lax.all_gather(weight_key, "fsdp", axis=0, tiled=True),
        lax.all_gather(weight_value, "fsdp", axis=0, tiled=True),
        lax.all_gather(weight_out, "fsdp", axis=1, tiled=True),
        lax.all_gather(weight_gate, "fsdp", axis=0, tiled=True),
        lax.all_gather(weight_up, "fsdp", axis=0, tiled=True),
        lax.all_gather(weight_down, "fsdp", axis=1, tiled=True),
        lax.all_gather(gain_attn_in, "fsdp", axis=0, tiled=True),
        lax.all_gather(gain_attn_out, "fsdp", axis=0, tiled=True),
        lax.all_gather(gain_ffn_in, "fsdp", axis=0, tiled=True),
        lax.all_gather(gain_ffn_out, "fsdp", axis=0, tiled=True),
        lax.all_gather(gain_query, "fsdp", axis=0, tiled=True),
        lax.all_gather(gain_key, "fsdp", axis=0, tiled=True),
    )
    full_query, full_key, full_value, full_out, full_gate, full_up, full_down = gathered[:7]
    scale_ai, scale_ao, scale_fi, scale_fo, scale_q, scale_k = [
        gain_item.astype(jnp.float32) for gain_item in gathered[7:]
    ]
    group_rows = tokens.shape[0]
    n_context = lax.axis_size("context")
    stream_len = group_rows * n_context
    heads_here = full_query.shape[1] // HD
    query_count = heads_here * group_rows
    doc_lengths = lengths[0]
    own_index = lax.axis_index("context") * group_rows + jnp.arange(group_rows, dtype=jnp.int32)
    own_segment, own_position = doc_info(own_index, doc_lengths)
    cosine, sine = rope_tables(own_position, HD)
    row_segment = jnp.tile(own_segment, heads_here)
    row_index = jnp.tile(own_index, heads_here)
    att_scale = HD ** (-0.5)
    inputs_f = tokens.astype(jnp.float32)
    normed_one, hat_one, inv_one = rms_forward(inputs_f, scale_ai)
    act_one = normed_one.astype(jnp.bfloat16)
    query_pre = dot32(act_one, full_query).reshape(group_rows, heads_here, HD)
    query_norm, query_hat, query_inv = rms_forward(query_pre, scale_q)
    query_rot = (rotate(query_norm, cosine, sine) * att_scale).astype(jnp.bfloat16)
    query_rows = jnp.transpose(query_rot, (1, 0, 2)).reshape(query_count, HD)
    key_pre = dot32(act_one, full_key).reshape(group_rows, 1, HD)
    key_norm, key_hat, key_inv = rms_forward(key_pre, scale_k)
    key_rot = rotate(key_norm, cosine, sine).reshape(group_rows, HD).astype(jnp.bfloat16)
    value_own = dot32(act_one, full_value).astype(jnp.bfloat16)

    def key_mask(key_index):
        key_segment = doc_info(key_index, doc_lengths)[0]
        return (row_segment[:, None] == key_segment[None, :]) & (
            row_index[:, None] >= key_index[None, :]
        )

    key_piece = lax.all_gather(key_rot, "context", axis=0, tiled=True)
    value_piece = lax.all_gather(value_own, "context", axis=0, tiled=True)
    key_index = jnp.arange(key_piece.shape[0], dtype=jnp.int32)
    allowed = key_mask(key_index)
    scores = jnp.where(allowed, contract_last(query_rows, key_piece), NEG_LARGE)
    run_max = jnp.full((query_count,), NEG_LARGE, jnp.float32)
    new_max = jnp.maximum(run_max, jnp.max(scores, axis=1))
    weights = jnp.where(allowed, jnp.exp(scores - new_max[:, None]), 0.0)
    run_sum = jnp.sum(weights, axis=1)
    run_acc = dot32(weights.astype(jnp.bfloat16), value_piece)
    state = (new_max, run_sum, run_acc)
    run_max, run_sum, run_acc = state
    log_total = run_max + jnp.log(run_sum)
    out_rows = (run_acc / run_sum[:, None]).astype(jnp.bfloat16)
    attn_cat = jnp.transpose(out_rows.reshape(heads_here, group_rows, HD), (1, 0, 2)).reshape(
        group_rows, heads_here * HD
    )
    attn_total = lax.psum(dot32(attn_cat, full_out), "tensor")
    normed_two, hat_two, inv_two = rms_forward(attn_total, scale_ao)
    hidden_res = inputs_f + normed_two
    normed_three, hat_three, inv_three = rms_forward(hidden_res, scale_fi)
    act_three = normed_three.astype(jnp.bfloat16)
    gate_pre = dot32(act_three, full_gate)
    up_pre = dot32(act_three, full_up)
    gelu_val, gelu_slope = gelu_parts(gate_pre)
    inner_act = (gelu_val * up_pre).astype(jnp.bfloat16)
    ffn_total = lax.psum(dot32(inner_act, full_down), "tensor")
    normed_four, hat_four, inv_four = rms_forward(ffn_total, scale_fo)
    layer_out = hidden_res + normed_four
    grad_final = cotangent.astype(jnp.float32)
    grad_ffn, dscale_fo = rms_backward(grad_final, scale_fo, hat_four, inv_four)
    grad_ffn_b = grad_ffn.astype(jnp.bfloat16)
    dweight_down = contract_first(inner_act, grad_ffn_b)
    grad_inner = contract_last(grad_ffn_b, full_down)
    grad_gate_b = (grad_inner * up_pre * gelu_slope).astype(jnp.bfloat16)
    grad_up_b = (grad_inner * gelu_val).astype(jnp.bfloat16)
    dweight_gate = contract_first(act_three, grad_gate_b)
    dweight_up = contract_first(act_three, grad_up_b)
    grad_act_three = lax.psum(
        contract_last(grad_gate_b, full_gate) + contract_last(grad_up_b, full_up), "tensor"
    )
    grad_three, dscale_fi = rms_backward(grad_act_three, scale_fi, hat_three, inv_three)
    grad_hidden = grad_final + grad_three
    grad_attn, dscale_ao = rms_backward(grad_hidden, scale_ao, hat_two, inv_two)
    grad_attn_b = grad_attn.astype(jnp.bfloat16)
    dweight_out = contract_first(attn_cat, grad_attn_b)
    grad_cat = contract_last(grad_attn_b, full_out).astype(jnp.bfloat16)
    grad_rows = jnp.transpose(grad_cat.reshape(group_rows, heads_here, HD), (1, 0, 2)).reshape(
        query_count, HD
    )
    delta_rows = jnp.sum(grad_rows.astype(jnp.float32) * out_rows.astype(jnp.float32), axis=1)
    key_all, value_all = (
        lax.all_gather(key_rot, "context", axis=0, tiled=True),
        lax.all_gather(value_own, "context", axis=0, tiled=True),
    )

    def block_terms(block_num):
        row_begin = block_num * group_rows
        key_block = lax.dynamic_slice_in_dim(key_all, row_begin, group_rows, 0)
        value_block = lax.dynamic_slice_in_dim(value_all, row_begin, group_rows, 0)
        allowed = key_mask(row_begin + jnp.arange(group_rows, dtype=jnp.int32))
        scores = contract_last(query_rows, key_block)
        probs = jnp.where(allowed, jnp.exp(scores - log_total[:, None]), 0.0)
        grad_probs = contract_last(grad_rows, value_block)
        grad_scores_b = (probs * (grad_probs - delta_rows[:, None])).astype(jnp.bfloat16)
        return (key_block, probs, grad_scores_b)

    zero_query = jnp.zeros((query_count, HD), jnp.float32)

    def back_step(carry, block_num):
        key_block, probs, grad_scores_b = block_terms(block_num)
        carry = carry + dot32(grad_scores_b, key_block)
        key_grad = contract_first(grad_scores_b, query_rows)
        value_grad = contract_first(probs.astype(jnp.bfloat16), grad_rows)
        return (carry, jnp.concatenate([key_grad, value_grad], axis=1))

    grad_query_rows, kv_terms = lax.scan(
        back_step, zero_query, jnp.arange(n_context, dtype=jnp.int32)
    )
    kv_grads = lax.psum_scatter(
        kv_terms.reshape(stream_len, 2 * HD), "context", scatter_dimension=0, tiled=True
    )
    grad_query = jnp.transpose(grad_query_rows.reshape(heads_here, group_rows, HD), (1, 0, 2))
    grad_qnorm = rotate_back(grad_query * att_scale, cosine, sine)
    grad_qpre, dscale_q_part = rms_backward(grad_qnorm, scale_q, query_hat, query_inv)
    grad_qpre_b = grad_qpre.reshape(group_rows, heads_here * HD).astype(jnp.bfloat16)
    grad_act_part, kv_summed, dscale_q = lax.psum(
        (contract_last(grad_qpre_b, full_query), kv_grads, dscale_q_part), "tensor"
    )
    grad_knorm = rotate_back(kv_summed[:, :HD].reshape(group_rows, 1, HD), cosine, sine)
    grad_kpre, dscale_k = rms_backward(grad_knorm, scale_k, key_hat, key_inv)
    grad_kpre_b = grad_kpre.reshape(group_rows, HD).astype(jnp.bfloat16)
    grad_value_b = kv_summed[:, HD:].astype(jnp.bfloat16)
    dweight_query = contract_first(act_one, grad_qpre_b)
    dweight_key = contract_first(act_one, grad_kpre_b)
    dweight_value = contract_first(act_one, grad_value_b)
    grad_act_one = (
        grad_act_part
        + contract_last(grad_kpre_b, full_key)
        + contract_last(grad_value_b, full_value)
    )
    grad_one, dscale_ai = rms_backward(grad_act_one, scale_ai, hat_one, inv_one)
    grad_tokens = grad_hidden + grad_one
    grads = (
        dweight_query,
        dweight_key,
        dweight_value,
        dweight_out,
        dweight_gate,
        dweight_up,
        dweight_down,
        dscale_ai,
        dscale_ao,
        dscale_fi,
        dscale_fo,
        dscale_q,
        dscale_k,
    )
    shares = (
        lax.psum_scatter(grads[0], "fsdp", scatter_dimension=0, tiled=True),
        lax.psum_scatter(grads[1], "fsdp", scatter_dimension=0, tiled=True),
        lax.psum_scatter(grads[2], "fsdp", scatter_dimension=0, tiled=True),
        lax.psum_scatter(grads[3], "fsdp", scatter_dimension=1, tiled=True),
        lax.psum_scatter(grads[4], "fsdp", scatter_dimension=0, tiled=True),
        lax.psum_scatter(grads[5], "fsdp", scatter_dimension=0, tiled=True),
        lax.psum_scatter(grads[6], "fsdp", scatter_dimension=1, tiled=True),
        lax.psum_scatter(grads[7], "fsdp", scatter_dimension=0, tiled=True),
        lax.psum_scatter(grads[8], "fsdp", scatter_dimension=0, tiled=True),
        lax.psum_scatter(grads[9], "fsdp", scatter_dimension=0, tiled=True),
        lax.psum_scatter(grads[10], "fsdp", scatter_dimension=0, tiled=True),
        lax.psum_scatter(grads[11], "fsdp", scatter_dimension=0, tiled=True),
        lax.psum_scatter(grads[12], "fsdp", scatter_dimension=0, tiled=True),
    )
    owned = lax.psum(
        (
            shares[0],
            shares[1],
            shares[2],
            shares[3],
            shares[4],
            shares[5],
            shares[6],
            shares[7],
            shares[8],
            shares[9],
            shares[10],
            shares[11],
            shares[12],
        ),
        "context",
    )
    return (
        layer_out,
        grad_tokens,
        owned[0],
        owned[1],
        owned[2],
        owned[3],
        owned[4],
        owned[5],
        owned[6],
        owned[7],
        owned[8],
        owned[9],
        owned[10],
        owned[11],
        owned[12],
    )


def solution(mesh):
    in_specs = (
        P(("fsdp", "context"), None),
        P("fsdp", None),
        P("fsdp", "tensor"),
        P("fsdp", None),
        P("fsdp", None),
        P("tensor", "fsdp"),
        P("fsdp", "tensor"),
        P("fsdp", "tensor"),
        P("tensor", "fsdp"),
        P("fsdp"),
        P("fsdp"),
        P("fsdp"),
        P("fsdp"),
        P("fsdp"),
        P("fsdp"),
        P(("fsdp", "context"), None),
    )
    out_specs = (
        P(("fsdp", "context"), None),
        P(("fsdp", "context"), None),
        P("fsdp", "tensor"),
        P("fsdp", None),
        P("fsdp", None),
        P("tensor", "fsdp"),
        P("fsdp", "tensor"),
        P("fsdp", "tensor"),
        P("tensor", "fsdp"),
        P("fsdp"),
        P("fsdp"),
        P("fsdp"),
        P("fsdp"),
        P("fsdp"),
        P("fsdp"),
    )
    return jax.shard_map(
        on_device, mesh=mesh, in_specs=in_specs, out_specs=out_specs, check_vma=False
    )
```

profile of v0, /device:TPU:0, one launch (start us, length us, event | category | flops | bytes accessed | tf_op | source)
XLA Modules:
  0.0 581.4 jit_solution(9633353479863615204)
XLA Ops:
  7.3 1.3 fusion.98
  15.0 11.6 %all-reduce.16 = (bf16[640]{0:T(1024)(128)(2,1)S(1)}, bf16[256]{0:T(256)(128)(2,1)S(1)}, bf16[256]{0:T(256)(128)(2,1)S(1)}, bf16[640]{0:T(1024)(128)(2,1)S(1)}, ...) all-reduce(bf16[640]{0:T(1024)(128)(2,1)S(1)} %dynamic-update-slice, ...), channel_id=1, replica_groups=mesh['fsdp'=4,'context'=2,'tensor'=4] {'fsdp'}, use_global_device_ids=true, to_apply=%add | all-reduce | flops 3072 | bytes 12288
  27.8 8.6 %all_gather.50 = bf16[640,256]{1,0:T(8,128)(2,1)S(1)} all-gather(bf16[160,256]{1,0:T(8,128)(2,1)} %param.21), channel_id=1, replica_groups=mesh['fsdp'=4,'context'=2,'tensor'=4] {'fsdp'}, dimensions={0}, use_global_device_ids=true | all-gather | bytes 409600 | tf_op jit(solution)/shard_map/all_gather | solution.py:111
  36.4 1.5 multiply_reduce_fusion.12
  37.9 8.9 %all_gather.48 = bf16[640,256]{1,0:T(8,128)(2,1)S(1)} all-gather(bf16[160,256]{1,0:T(8,128)(2,1)S(1)} %copy-done.44), channel_id=1, replica_groups=mesh['fsdp'=4,'context'=2,'tensor'=4] {'fsdp'}, dimensions={0}, use_global_device_ids=true | all-gather | bytes 409600 | tf_op jit(solution)/shard_map/all_gather | solution.py:110
  49.9 2.0 all-gather
  53.0 8.6 %all_gather.53 = bf16[640,256]{1,0:T(8,128)(2,1)S(1)} all-gather(bf16[160,256]{1,0:T(8,128)(2,1)S(1)} %copy-done.45), channel_id=1, replica_groups=mesh['fsdp'=4,'context'=2,'tensor'=4] {'fsdp'}, dimensions={0}, use_global_device_ids=true | all-gather | bytes 409600 | tf_op jit(solution)/shard_map/all_gather | solution.py:112
  62.4 2.0 all_gather.54
  64.4 8.9 %all_gather.55 = bf16[256,640]{0,1:T(8,128)(2,1)S(1)} all-gather(bf16[256,160]{0,1:T(8,128)(2,1)S(1)} %copy-done.46), channel_id=1, replica_groups=mesh['fsdp'=4,'context'=2,'tensor'=4] {'fsdp'}, dimensions={1}, use_global_device_ids=true | all-gather | bytes 409600 | tf_op jit(solution)/shard_map/all_gather | solution.py:113
  76.7 10.8 %all_gather.58 = bf16[640,512]{1,0:T(8,128)(2,1)S(1)} all-gather(bf16[160,512]{1,0:T(8,128)(2,1)S(1)} %copy-done.41), channel_id=1, replica_groups=mesh['fsdp'=4,'context'=2,'tensor'=4] {'fsdp'}, dimensions={0}, use_global_device_ids=true | all-gather | bytes 819200 | tf_op jit(solution)/shard_map/all_gather | solution.py:114
  87.5 11.7 %all_gather.59 = bf16[640,512]{1,0:T(8,128)(2,1)} all-gather(bf16[160,512]{1,0:T(8,128)(2,1)S(1)} %copy-done.42), channel_id=1, replica_groups=mesh['fsdp'=4,'context'=2,'tensor'=4] {'fsdp'}, dimensions={0}, use_global_device_ids=true | all-gather | bytes 819200 | tf_op jit(solution)/shard_map/all_gather | solution.py:115
  99.2 10.1 %all_gather.60 = bf16[512,640]{0,1:T(8,128)(2,1)S(1)} all-gather(bf16[512,160]{0,1:T(8,128)(2,1)S(1)} %copy-done.43), channel_id=1, replica_groups=mesh['fsdp'=4,'context'=2,'tensor'=4] {'fsdp'}, dimensions={1}, use_global_device_ids=true | all-gather | bytes 819200 | tf_op jit(solution)/shard_map/all_gather | solution.py:116
  109.4 8.2 %all-reduce.23.cloned.1.call-done = f32[256,640]{1,0:T(8,128)} async-done(((f32[256,640]{1,0:T(8,128)}), f32[256,640]{1,0:T(8,128)}) %all-reduce.23.cloned.1.call-update) | async-done | bytes 655376 | tf_op jit(solution)/shard_map/psum | solution.py:175
  118.8 1.4 multiply_reduce_fusion.5
  123.1 1.2 fusion.103
  124.4 40.1 %all-reduce.25.cloned.1.call-done = f32[256,640]{1,0:T(8,128)} async-done(((f32[256,640]{1,0:T(8,128)}), f32[256,640]{1,0:T(8,128)}) %all-reduce.25.cloned.1.call-update) | async-done | bytes 655376 | tf_op jit(solution)/shard_map/psum | solution.py:184
  164.6 1.3 multiply_reduce_fusion.4
  165.9 2.0 fusion.33
  171.2 1.2 convolution_add_fusion.1
  174.1 38.5 %all-reduce.27.cloned.1.call-done = f32[256,640]{1,0:T(8,128)} async-done(((f32[256,640]{1,0:T(8,128)}), f32[256,640]{1,0:T(8,128)}) %all-reduce.27.cloned.1.call-update) | async-done | bytes 655376 | tf_op jit(solution)/shard_map/psum | solution.py:196
  212.6 2.0 multiply_reduce_fusion
  214.7 2.1 multiply_reduce_fusion.1
  218.4 31.8 %while.15 = (s32[]{:T(128)}, f32[256,256]{1,0:T(8,128)S(1)}, f32[2,256,512]{1,0,2:T(2,128)}, s32[256]{0:T(256)}, s32[2]{0:T(128)S(1)}, /*index=5*/s32[1,4]{1,0:T...) while((s32[]{:T(128)}, f32[256,256]{1,0:T(8,128)S(1)}, ...), condition=%wide.region_22.23_spmd.clone, body=%wide.region_20.22_spmd.clone.sunk | while | flops 168627456 | bytes 6301961 | solution.py:234
  222.7 11.4 %dynamic_update_slice.8 = f32[2,256,512]{1,0,2:T(2,128)} dynamic-update-slice(f32[2,256,512]{1,0,2:T(2,128)} %get-tuple-element.454, f32[1,256,512]{1,0,2:T(1,128)S(1)} %copy.71, s32[]{:T(128)} %get-tuple-element.452, s32[]{:T(128)} %constant.76.clone.1..sunk, s32[]{:T(128)} %constant.76.clone.1..sunk) | dynamic-update-slice | bytes 1048580 | tf_op jit(solution)/shard_map/while/body/jit(dynamic_update_index_in_dim)/dynamic_update_slice | solution.py:234
  238.6 11.4 %dynamic_update_slice.8 = f32[2,256,512]{1,0,2:T(2,128)} dynamic-update-slice(f32[2,256,512]{1,0,2:T(2,128)} %get-tuple-element.454, f32[1,256,512]{1,0,2:T(1,128)S(1)} %copy.71, s32[]{:T(128)} %get-tuple-element.452, s32[]{:T(128)} %constant.76.clone.1..sunk, s32[]{:T(128)} %constant.76.clone.1..sunk) | dynamic-update-slice | bytes 1048580 | tf_op jit(solution)/shard_map/while/body/jit(dynamic_update_index_in_dim)/dynamic_update_slice | solution.py:234
  250.3 2.3 copy.69
  255.2 5.5 reduce-scatter.9.cloned.1.call-done
  262.1 1.3 fusion.91
  263.4 1.5 fusion.109
  265.0 1.4 fusion.107
  266.5 1.4 fusion.108
  268.0 53.3 %all-reduce.29.cloned.1.call-done = (f32[256,640]{1,0:T(8,128)}, f32[256,512]{0,1:T(8,128)}) async-done(((f32[256,640]{1,0:T(8,128)}, f32[256,512]{0,1:T(8,128)}), (f32[256,640]{1,0:T(8,128)}, f32[256,512]{0,1:T(8,128)})) %all-reduce.29.cloned.1.call-update) | async-done | bytes 1179664 | tf_op jit(solution)/shard_map/psum | solution.py:244
  323.1 1.2 fusion.89
  324.4 1.2 fusion.83
  325.7 23.5 %reduce-scatter.17.cloned.1.call-done = f32[256,160]{0,1:T(8,128)} async-done(((f32[256,640]{0,1:T(8,128)}), f32[256,160]{0,1:T(8,128)}) %reduce-scatter.17.cloned.1.call-update) | async-done | bytes 163856 | tf_op jit(solution)/shard_map/reduce_scatter | solution.py:280
  349.2 28.3 %reduce-scatter.11.cloned.1.call-done = f32[160,256]{1,0:T(8,128)} async-done(((f32[640,256]{1,0:T(8,128)}), f32[160,256]{1,0:T(8,128)}) %reduce-scatter.11.cloned.1.call-update) | async-done | bytes 163856 | tf_op jit(solution)/shard_map/reduce_scatter | solution.py:277
  377.5 32.5 %reduce-scatter.23.cloned.1.call-done = f32[512,160]{0,1:T(8,128)} async-done(((f32[512,640]{0,1:T(8,128)}), f32[512,160]{0,1:T(8,128)}) %reduce-scatter.23.cloned.1.call-update) | async-done | bytes 327696 | tf_op jit(solution)/shard_map/reduce_scatter | solution.py:283
  410.0 32.6 %reduce-scatter.19.cloned.1.call-done = f32[160,512]{1,0:T(8,128)} async-done(((f32[640,512]{1,0:T(8,128)}), f32[160,512]{1,0:T(8,128)}) %reduce-scatter.19.cloned.1.call-update) | async-done | bytes 327696 | tf_op jit(solution)/shard_map/reduce_scatter | solution.py:281
  442.6 32.4 %reduce-scatter.21.cloned.1.call-done = f32[160,512]{1,0:T(8,128)} async-done(((f32[640,512]{1,0:T(8,128)}), f32[160,512]{1,0:T(8,128)}) %reduce-scatter.21.cloned.1.call-update) | async-done | bytes 327696 | tf_op jit(solution)/shard_map/reduce_scatter | solution.py:282
  475.0 29.1 %reduce-scatter.13.cloned.1.call-done = f32[160,256]{1,0:T(8,128)} async-done(((f32[640,256]{1,0:T(8,128)}), f32[160,256]{1,0:T(8,128)}) %reduce-scatter.13.cloned.1.call-update) | async-done | bytes 163856 | tf_op jit(solution)/shard_map/reduce_scatter | solution.py:278
  504.1 28.2 %reduce-scatter.15.cloned.1.call-done = f32[160,256]{1,0:T(8,128)} async-done(((f32[640,256]{1,0:T(8,128)}), f32[160,256]{1,0:T(8,128)}) %reduce-scatter.15.cloned.1.call-update) | async-done | bytes 163856 | tf_op jit(solution)/shard_map/reduce_scatter | solution.py:279
  534.7 15.3 %all-reduce.13 = (f32[640]{0:T(1024)S(1)}, f32[640]{0:T(1024)S(1)}, f32[640]{0:T(1024)S(1)}, f32[640]{0:T(1024)S(1)}, f32[256]{0:T(256)S(1)}, /*index=5*/f32[256]{0:T(256)S(1)}) all-reduce(f32[640]{0:T(1024)S(1)} %get-tuple-element.257, f32[640]{0:T(1024)S(1)} %copy-done.53, ...), channel_id=11, replica_groups=mesh['fsdp'=4,'context'=2,'tensor'=4] {'fsdp'}, use_global_device_ids=true, to_apply=%region_44.45.clone | all-reduce | flops 3072 | bytes 24576
  550.5 11.6 %psum.152 = f32[64]{0:T(128)S(1)} all-reduce(f32[64]{0:T(128)S(1)} %dynamic-slice.15), channel_id=1, replica_groups=mesh['fsdp'=4,'context'=2,'tensor'=4] {'tensor'}, use_global_device_ids=true, to_apply=%region_56.57 | all-reduce | flops 64 | bytes 512 | tf_op jit(solution)/shard_map/psum | solution.py:244
  562.1 3.0 all-reduce.14
  566.2 1.7 copy.100
  567.9 1.6 copy.101
  569.5 1.6 copy.102
  571.1 1.6 copy.103
  (280 shorter events, 43.5 us)
Async XLA Ops:
  7.2 40.4 %copy-start = (bf16[256,640]{1,0:T(8,128)(2,1)S(1)}, bf16[256,640]{1,0:T(8,128)(2,1)}, u32[]{:S(2)}) copy-start(bf16[256,640]{1,0:T(8,128)(2,1)} %param.18) | copy-start | bytes 983044
  7.2 30.7 %copy-start.44 = (bf16[160,256]{1,0:T(8,128)(2,1)S(1)}, bf16[160,256]{1,0:T(8,128)(2,1)}, u32[]{:S(2)}) copy-start(bf16[160,256]{1,0:T(8,128)(2,1)} %param.20) | copy-start | bytes 245764
  7.2 110.3 %all-reduce.23.cloned.1.call-start = ((), (), s32[]{:S(2)}) async-start(), calls=%async_computation.8 | async-start | bytes 1310720 | tf_op jit(solution)/shard_map/psum | solution.py:175
  7.3 41.9 %copy-start.64 = (f32[128]{0:T(128)}, f32[128]{0:T(128)S(1)}, u32[]{:S(2)}) copy-start(f32[128]{0:T(128)S(1)} %multiply_power_fusion) | copy-start | bytes 1540
  36.4 11.7 %copy-start.70 = (s32[1,4]{1,0:T(1,128)S(1)}, s32[1,4]{1,0:T(1,128)}, u32[]{:S(2)}) copy-start(s32[1,4]{1,0:T(1,128)} %param.19) | copy-start | bytes 52
  37.9 11.9 %copy-start.11 = (f32[256,256]{0,1:T(8,128)}, f32[256,256]{0,1:T(8,128)S(1)}, u32[]{:S(2)}) copy-start(f32[256,256]{0,1:T(8,128)S(1)} %get-tuple-element.340) | copy-start | bytes 786436
  37.9 11.9 %copy-start.54 = (f32[256]{0:T(256)}, f32[256]{0:T(256)S(1)}, u32[]{:S(2)}) copy-start(f32[256]{0:T(256)S(1)} %add_rsqrt_fusion.3) | copy-start | bytes 3076
  48.0 3.8 copy-start.13
  49.0 2.8 copy-start.56
  49.8 3.2 copy-start.45
  51.9 12.5 %copy-start.46 = (bf16[256,160]{0,1:T(8,128)(2,1)S(1)}, bf16[256,160]{0,1:T(8,128)(2,1)}, u32[]{:S(2)}) copy-start(bf16[256,160]{0,1:T(8,128)(2,1)} %param.23) | copy-start | bytes 245764
  53.0 20.3 %copy-start.68 = (f32[256]{0:T(256)}, f32[256]{0:T(256)S(1)}, u32[]{:S(2)}) copy-start(f32[256]{0:T(256)S(1)} %get-tuple-element.343) | copy-start | bytes 3076
  73.3 2.1 copy-start.3
  74.3 2.3 copy-start.66
  75.4 12.1 %copy-start.42 = (bf16[160,512]{1,0:T(8,128)(2,1)S(1)}, bf16[160,512]{1,0:T(8,128)(2,1)}, u32[]{:S(2)}) copy-start(bf16[160,512]{1,0:T(8,128)(2,1)} %param.25) | copy-start | bytes 491524
  76.6 22.6 %copy-start.43 = (bf16[512,160]{0,1:T(8,128)(2,1)S(1)}, bf16[512,160]{0,1:T(8,128)(2,1)}, u32[]{:S(2)}) copy-start(bf16[512,160]{0,1:T(8,128)(2,1)} %param.26) | copy-start | bytes 491524
  76.6 87.9 %all-reduce.25.cloned.1.call-start = ((), (), s32[]{:S(2)}) async-start(), calls=%async_computation.9 | async-start | bytes 1310720 | tf_op jit(solution)/shard_map/psum | solution.py:184
  120.2 2.2 copy-start.49
  123.1 42.8 %copy-start.5 = (bf16[256,640]{1,0:T(8,128)(2,1)S(1)}, bf16[256,640]{1,0:T(8,128)(2,1)}, u32[]{:S(2)}) copy-start(bf16[256,640]{1,0:T(8,128)(2,1)} %param.33) | copy-start | bytes 983044
  124.4 88.2 %all-reduce.27.cloned.1.call-start = ((), (), s32[]{:S(2)}) async-start(), calls=%async_computation.10 | async-start | bytes 1310720 | tf_op jit(solution)/shard_map/psum | solution.py:196
  164.6 3.3 copy-start.2
  169.8 2.6 copy-start.27
  171.1 2.4 copy-start.67
  171.1 2.4 copy-start.69
  171.1 41.5 %copy-start.50 = (f32[256]{0:T(256)S(1)}, f32[256]{0:T(256)}, u32[]{:S(2)}) copy-start(f32[256]{0:T(256)} %copy-done.49) | copy-start | bytes 3076
  172.4 42.2 %copy-start.1 = (f32[256,640]{1,0:T(8,128)S(1)}, f32[256,640]{1,0:T(8,128)}, u32[]{:S(2)}) copy-start(f32[256,640]{1,0:T(8,128)} %all-reduce.23.cloned.1.call-done) | copy-start | bytes 1966084
  172.4 88.3 %reduce-scatter.9.cloned.1.call-start = ((), (), s32[]{:S(2)}) async-start(), calls=%async_computation.11 | async-start | bytes 1572864 | tf_op jit(solution)/shard_map/reduce_scatter | solution.py:237
  212.6 2.0 copy-start.8
  214.6 2.1 copy-start.48
  252.6 68.7 %all-reduce.29.cloned.1.call-start = ((), (), s32[]{:S(2)}) async-start(), calls=%async_computation.19 | async-start | bytes 2359296 | tf_op jit(solution)/shard_map/psum | solution.py:244
  254.0 6.8 %copy-start.7 = (bf16[256,640]{1,0:T(8,128)(2,1)S(1)}, bf16[256,640]{1,0:T(8,128)(2,1)}, u32[]{:S(2)}) copy-start(bf16[256,640]{1,0:T(8,128)(2,1)} %copy-done.6) | copy-start | bytes 983044
  254.1 6.8 %copy-start.25 = (bf16[256,256]{0,1:T(8,128)(2,1)S(1)}, bf16[256,256]{0,1:T(8,128)(2,1)}, u32[]{:S(2)}) copy-start(bf16[256,256]{0,1:T(8,128)(2,1)} %copy-done.23) | copy-start | bytes 393220
  260.8 88.4 %reduce-scatter.17.cloned.1.call-start = ((), (), s32[]{:S(2)}) async-start(), calls=%async_computation.15 | async-start | bytes 819200 | tf_op jit(solution)/shard_map/reduce_scatter | solution.py:280
  262.0 115.5 %reduce-scatter.11.cloned.1.call-start = ((), (), s32[]{:S(2)}) async-start(), calls=%async_computation.12 | async-start | bytes 819200 | tf_op jit(solution)/shard_map/reduce_scatter | solution.py:277
  263.4 146.7 %reduce-scatter.23.cloned.1.call-start = ((), (), s32[]{:S(2)}) async-start(), calls=%async_computation.18 | async-start | bytes 1638400 | tf_op jit(solution)/shard_map/reduce_scatter | solution.py:283
  264.9 177.7 %reduce-scatter.19.cloned.1.call-start = ((), (), s32[]{:S(2)}) async-start(), calls=%async_computation.16 | async-start | bytes 1638400 | tf_op jit(solution)/shard_map/reduce_scatter | solution.py:281
  266.4 208.5 %reduce-scatter.21.cloned.1.call-start = ((), (), s32[]{:S(2)}) async-start(), calls=%async_computation.17 | async-start | bytes 1638400 | tf_op jit(solution)/shard_map/reduce_scatter | solution.py:282
  267.9 54.9 %copy-start.12 = (f32[256,256]{0,1:T(8,128)S(1)}, f32[256,256]{0,1:T(8,128)}, u32[]{:S(2)}) copy-start(f32[256,256]{0,1:T(8,128)} %copy-done.11) | copy-start | bytes 786436
  267.9 54.9 %copy-start.55 = (f32[256]{0:T(256)S(1)}, f32[256]{0:T(256)}, u32[]{:S(2)}) copy-start(f32[256]{0:T(256)} %copy-done.54) | copy-start | bytes 3076
  267.9 54.9 %copy-start.61 = (f32[256]{0:T(256)S(1)}, f32[256]{0:T(256)}, u32[]{:S(2)}) copy-start(f32[256]{0:T(256)} %copy-done.60) | copy-start | bytes 3076
  267.9 236.2 %reduce-scatter.13.cloned.1.call-start = ((), (), s32[]{:S(2)}) async-start(), calls=%async_computation.13 | async-start | bytes 819200 | tf_op jit(solution)/shard_map/reduce_scatter | solution.py:278
  324.3 207.9 %reduce-scatter.15.cloned.1.call-start = ((), (), s32[]{:S(2)}) async-start(), calls=%async_computation.14 | async-start | bytes 819200 | tf_op jit(solution)/shard_map/reduce_scatter | solution.py:279
  325.6 208.0 %copy-start.16 = (bf16[640,256]{1,0:T(8,128)(2,1)S(1)}, bf16[640,256]{1,0:T(8,128)(2,1)}, u32[]{:S(2)}) copy-start(bf16[640,256]{1,0:T(8,128)(2,1)} %copy-done.15) | copy-start | bytes 983044
  325.6 208.0 %copy-start.33 = (f32[256,640]{1,0:T(8,128)S(1)}, f32[256,640]{1,0:T(8,128)}, u32[]{:S(2)}) copy-start(f32[256,640]{1,0:T(8,128)} %get-tuple-element.291) | copy-start | bytes 1966084
  325.7 240.5 %all-reduce.31.cloned.1.call-start = ((), (), s32[]{:S(2)}) async-start(), calls=%async_computation.20 | async-start | bytes 3276800 | tf_op jit(solution)/shard_map/psum | solution.py:291
  566.2 6.5 %copy-start.40 = (f32[160,512]{1,0:T(8,128)S(1)}, f32[160,512]{1,0:T(8,128)}, u32[]{:S(2)}) copy-start(f32[160,512]{1,0:T(8,128)} %get-tuple-element.492) | copy-start | bytes 983044
  566.2 7.2 %copy-start.39 = (f32[160,512]{1,0:T(8,128)S(1)}, f32[160,512]{1,0:T(8,128)}, u32[]{:S(2)}) copy-start(f32[160,512]{1,0:T(8,128)} %get-tuple-element.493) | copy-start | bytes 983044
  566.2 7.9 %copy-start.38 = (f32[512,160]{0,1:T(8,128)S(1)}, f32[512,160]{0,1:T(8,128)}, u32[]{:S(2)}) copy-start(f32[512,160]{0,1:T(8,128)} %get-tuple-element.494) | copy-start | bytes 983044
  (38 other events, 45.2 us)
Sparse Core Ops, SparseCore 0:
  76.7 40.7 all-reduce.22
  124.5 40.0 all-reduce.24
  172.6 40.0 all-reduce.26
  252.7 8.0 reduce-scatter.8
  263.8 57.4 all-reduce.28
  324.2 24.9 reduce-scatter.16
  352.1 25.3 reduce-scatter.10
  380.7 29.2 reduce-scatter.22
  413.2 29.3 reduce-scatter.18
  445.6 29.2 reduce-scatter.20
  478.7 25.3 reduce-scatter.12
  506.8 25.3 reduce-scatter.14
  535.4 21.0 all-reduce.30
where the time goes:
time: 584 us; the launch traced here: 581 us
  waiting for transfers between devices  352 us (60%)
  blocking collectives  113 us (19%)
  local copies, waits for them, and re-layouts  49.4 us (8%)
  matrix products  25.8 us (4%)
  other arithmetic  20.8 us (4%)
  between operations  17.6 us (3%)
    psum x1, waiting for transfers between devices, on_device(): lax.psum((contract_last(grad_qpre_b, full_query), kv_grads, dscale_q_part...  53.3 us
    psum x1, waiting for transfers between devices, on_device(): ffn_total = lax.psum(dot32(inner_act, full_down), 'tensor')  40.1 us
    psum x1, waiting for transfers between devices, on_device(): lax.psum(contract_last(grad_gate_b, full_gate) + contract_last(grad_up_b,...  38.5 us
    reduce_scatter x1, waiting for transfers between devices, on_device(): lax.psum_scatter(grads[4], 'fsdp', scatter_dimension=0, tiled=True)  32.6 us
    reduce_scatter x1, waiting for transfers between devices, on_device(): lax.psum_scatter(grads[6], 'fsdp', scatter_dimension=1, tiled=True)  32.5 us
    reduce_scatter x1, waiting for transfers between devices, on_device(): lax.psum_scatter(grads[5], 'fsdp', scatter_dimension=0, tiled=True)  32.4 us
    reduce_scatter x1, waiting for transfers between devices, on_device(): lax.psum_scatter(grads[1], 'fsdp', scatter_dimension=0, tiled=True)  29.1 us
    reduce_scatter x1, waiting for transfers between devices, on_device(): lax.psum_scatter(grads[0], 'fsdp', scatter_dimension=0, tiled=True)  28.3 us
  transfers between devices with their start and end apart: 13, of which 12 were waited for; matrix products, arithmetic and copies ran while one was open for 3% of the time, Pallas kernels for 0%

commit v1 on v0

v1 whole, which is shorter than its diff:
```python
import math

import jax
import jax.numpy as jnp
from jax import lax
from jax.sharding import PartitionSpec as P

HD = 256

EPSILON = 1e-06
ROPE_BASE = 1000000.0
GELU_COEF = math.sqrt(2.0 / math.pi)
NEG_LARGE = -1e30
BF = jnp.bfloat16
F32 = jnp.float32


def rms_stats(values):
    inverse = lax.rsqrt(jnp.mean(values * values, axis=-1, keepdims=True) + EPSILON)
    return values * inverse, inverse


def rms_back(grad_out, gain_vec, normed, inverse):
    inner = grad_out * gain_vec
    return inverse * (inner - normed * jnp.mean(inner * normed, axis=-1, keepdims=True))


def rope_tables(positions):
    half_width = HD // 2
    freqs = ROPE_BASE ** (-jnp.arange(half_width, dtype=F32) * 2.0 / HD)
    angles = positions.astype(F32)[:, None] * freqs[None, :]
    return jnp.cos(angles), jnp.sin(angles)


def rotate(values, cosine, sine):
    half = values.shape[-1] // 2
    first, second = values[:, :half], values[:, half:]
    return jnp.concatenate(
        [first * cosine - second * sine, second * cosine + first * sine], axis=-1
    )


def gelu_parts(pre_act):
    cubic = pre_act + 0.044715 * pre_act * pre_act * pre_act
    tangent = jnp.tanh(GELU_COEF * cubic)
    gelu_val = 0.5 * pre_act * (1.0 + tangent)
    slope = 0.5 * (1.0 + tangent) + 0.5 * pre_act * (1.0 - tangent * tangent) * GELU_COEF * (
        1.0 + 3.0 * 0.044715 * pre_act * pre_act
    )
    return gelu_val, slope


def doc_info(index, lengths):
    ends = jnp.cumsum(lengths)
    passed = index[:, None] >= ends[None, :]
    segment = jnp.sum(passed.astype(jnp.int32), axis=1)
    start = jnp.sum(jnp.where(passed, lengths[None, :], 0), axis=1)
    return segment, index - start


def dot32(left, right):
    return jnp.dot(left, right, preferred_element_type=F32)


def dot_nt(left, right):
    return lax.dot_general(left, right, (((1,), (1,)), ((), ())), preferred_element_type=F32)


def dot_tn(left, right):
    return lax.dot_general(left, right, (((0,), (0,)), ((), ())), preferred_element_type=F32)


def make_program(n_fsdp, n_context, n_tensor):
    def core_swap(value):
        return lax.ppermute(value, "context", [(i, i ^ 1) for i in range(n_context)])

    def z_near(value):
        return lax.ppermute(value, "tensor", [(i, i ^ 1) for i in range(n_tensor)])

    def z_far(value):
        return lax.ppermute(value, "tensor", [(i, i ^ 2) for i in range(n_tensor)])

    def z_one_way(value, from_owner):
        pairs = []
        for ctx in range(n_context):
            for pos in range(n_tensor):
                owner = (pos // 2) == (ctx % 2)
                if owner == from_owner:
                    pairs.append((ctx * n_tensor + pos, ctx * n_tensor + (pos ^ 2)))
        return lax.ppermute(value, ("context", "tensor"), pairs)

    def fsdp_hop(value, step):
        return lax.ppermute(value, "fsdp", [(i, i ^ step) for i in range(n_fsdp)])

    def gather_blocks(value):
        return [value] + [fsdp_hop(value, step) for step in range(1, n_fsdp)]

    def across_pairs(value):
        step = 2
        while step < n_context:
            value = value.astype(F32) + lax.ppermute(
                value.astype(BF), "context", [(i, i ^ step) for i in range(n_context)]
            ).astype(F32)
            step *= 2
        return value

    def on_device(
        tokens, lengths, weight_query, weight_key, weight_value, weight_out, weight_gate,
        weight_up, weight_down, gain_attn_in, gain_attn_out, gain_ffn_in, gain_ffn_out,
        gain_query, gain_key, cotangent,
    ):
        own_f = lax.axis_index("fsdp")
        ctx = lax.axis_index("context")
        pos_z = lax.axis_index("tensor")
        group = pos_z // 2
        is_owner = group == (ctx % 2)
        rows, width = tokens.shape
        half = rows // 2
        stream = rows * n_context
        block = weight_query.shape[0]
        gain_block = gain_query.shape[0]
        att_scale = HD ** (-0.5)
        order = jnp.arange(n_fsdp) ^ own_f

        def in_order(blocks):
            stacked = jnp.take(jnp.stack(blocks), order, axis=0)
            return stacked.reshape((-1,) + stacked.shape[2:])

        gains = jnp.concatenate(
            [gain_attn_in, gain_attn_out, gain_ffn_in, gain_ffn_out, gain_query, gain_key]
        )
        gain_all = jnp.take(jnp.stack(gather_blocks(gains)), order, axis=0).astype(F32)
        scales = []
        for i in range(4):
            scales.append(gain_all[:, i * block : (i + 1) * block].reshape(-1))
        for i in range(2):
            first = 4 * block + i * gain_block
            scales.append(gain_all[:, first : first + gain_block].reshape(-1))
        scale_ai, scale_ao, scale_fi, scale_fo, scale_q, scale_k = scales

        tokens_other = core_swap(tokens)
        pack_kv = jnp.concatenate([weight_key, weight_value], axis=1)
        pack_qo = jnp.concatenate([weight_query, weight_out.T], axis=1)
        pack_ffn = jnp.concatenate([weight_gate, weight_up, weight_down.T], axis=1)
        full_kv = in_order(gather_blocks(pack_kv))
        pack_qo = jnp.where(is_owner, pack_qo, z_one_way(pack_qo, True))
        full_qo = in_order(gather_blocks(pack_qo))
        pack_ffn = jnp.where(is_owner, pack_ffn, z_one_way(pack_ffn, True))
        hidden = weight_gate.shape[1]
        full_gu = in_order(gather_blocks(pack_ffn[:, : 2 * hidden]))
        full_dt = in_order(gather_blocks(pack_ffn[:, 2 * hidden :]))
        full_q, full_ot = full_qo[:, :HD], full_qo[:, HD:]

        span = jnp.arange(rows, dtype=jnp.int32)
        if n_context == 2:
            tok_all = jnp.concatenate([tokens, tokens_other], axis=0)
            key_index = jnp.concatenate([ctx * rows + span, (ctx ^ 1) * rows + span])
            place = (group * half, rows + group * half)
        else:
            tok_all = lax.all_gather(tokens, "context", axis=0, tiled=True)
            key_index = jnp.arange(stream, dtype=jnp.int32)
            place = (ctx * rows + group * half, (ctx ^ 1) * rows + group * half)

        def pick(value):
            return jnp.concatenate(
                [lax.dynamic_slice_in_dim(value, start, half, 0) for start in place], axis=0
            )

        doc_lengths = lengths[0]
        key_segment, key_position = doc_info(key_index, doc_lengths)
        cos_k, sin_k = rope_tables(key_position)
        row_index, row_segment = pick(key_index), pick(key_segment)
        cos_q, sin_q = pick(cos_k), pick(sin_k)
        allowed = (row_segment[:, None] == key_segment[None, :]) & (
            row_index[:, None] >= key_index[None, :]
        )

        hat_one, inv_one = rms_stats(tok_all.astype(F32))
        act_all = (hat_one * scale_ai).astype(BF)
        act_q = pick(act_all)
        q_hat, q_inv = rms_stats(dot32(act_q, full_q))
        q_rot = (rotate(q_hat * scale_q, cos_q, sin_q) * att_scale).astype(BF)
        kv_pre = dot32(act_all, full_kv)
        k_hat, k_inv = rms_stats(kv_pre[:, :HD])
        k_rot = rotate(k_hat * scale_k, cos_k, sin_k).astype(BF)
        value_all = kv_pre[:, HD:].astype(BF)

        scores = jnp.where(allowed, dot_nt(q_rot, k_rot), NEG_LARGE)
        row_max = jnp.max(scores, axis=1, keepdims=True)
        weights = jnp.where(allowed, jnp.exp(scores - row_max), 0.0)
        total = jnp.sum(weights, axis=1, keepdims=True)
        log_total = row_max + jnp.log(total)
        attn = (dot32(weights.astype(BF), value_all) / total).astype(BF)

        def row_sum(partial):
            pair = partial[:half] + core_swap(partial[half:].astype(BF)).astype(F32)
            pair = pair.astype(BF)
            return pair.astype(F32) + z_near(pair).astype(F32)

        def both_halves(value):
            return jnp.concatenate([value, core_swap(value)], axis=0)

        own_tok = lax.dynamic_slice_in_dim(tokens, group * half, half, 0).astype(F32)
        own_cot = lax.dynamic_slice_in_dim(cotangent, group * half, half, 0).astype(F32)

        attn_total = row_sum(dot_nt(attn, full_ot))
        hat_two, inv_two = rms_stats(attn_total)
        hidden_res = own_tok + hat_two * scale_ao
        hat_three, inv_three = rms_stats(hidden_res)
        act_three = both_halves((hat_three * scale_fi).astype(BF))
        gate_up = dot32(act_three, full_gu)
        gate_pre, up_pre = gate_up[:, :hidden], gate_up[:, hidden:]
        gelu_val, gelu_slope = gelu_parts(gate_pre)
        inner_act = (gelu_val * up_pre).astype(BF)
        ffn_total = row_sum(dot_nt(inner_act, full_dt))
        hat_four, inv_four = rms_stats(ffn_total)
        layer_half = hidden_res + hat_four * scale_fo
        dscale_fo = jnp.sum(own_cot * hat_four, axis=0)
        grad_ffn = both_halves(rms_back(own_cot, scale_fo, hat_four, inv_four).astype(BF))
        grad_dt = dot_tn(grad_ffn, inner_act)
        grad_inner = dot32(grad_ffn, full_dt)
        grad_gu = jnp.concatenate(
            [(grad_inner * up_pre * gelu_slope).astype(BF), (grad_inner * gelu_val).astype(BF)],
            axis=1,
        )
        grad_wgu = dot_tn(act_three, grad_gu)
        grad_three = row_sum(dot_nt(grad_gu, full_gu))
        dscale_fi = jnp.sum(grad_three * hat_three, axis=0)
        grad_hidden = own_cot + rms_back(grad_three, scale_fi, hat_three, inv_three)
        dscale_ao = jnp.sum(grad_hidden * hat_two, axis=0)
        grad_attn = both_halves(rms_back(grad_hidden, scale_ao, hat_two, inv_two).astype(BF))
        grad_wot = dot_tn(grad_attn, attn)
        grad_heads = dot32(grad_attn, full_ot).astype(BF)
        delta = jnp.sum(grad_heads.astype(F32) * attn.astype(F32), axis=1, keepdims=True)
        probs = jnp.where(allowed, jnp.exp(dot_nt(q_rot, k_rot) - log_total), 0.0)
        grad_s = (probs * (dot_nt(grad_heads, value_all) - delta)).astype(BF)
        grad_qrot = dot32(grad_s, k_rot)
        grad_krot = dot_tn(grad_s, q_rot)
        grad_v = dot_tn(probs.astype(BF), grad_heads).astype(BF)
        grad_qn = rotate(grad_qrot * att_scale, cos_q, -sin_q)
        dscale_q = jnp.sum(grad_qn * q_hat, axis=0)
        grad_q = rms_back(grad_qn, scale_q, q_hat, q_inv).astype(BF)
        grad_kn = rotate(grad_krot, cos_k, -sin_k)
        dscale_k = jnp.sum(grad_kn * k_hat, axis=0)
        grad_k = rms_back(grad_kn, scale_k, k_hat, k_inv).astype(BF)
        grad_kv = jnp.concatenate([grad_k, grad_v], axis=1)
        grad_wq = dot_tn(act_q, grad_q)
        grad_wkv = dot_tn(act_all, grad_kv)
        part = dot_nt(grad_kv, full_kv)
        part_q = dot_nt(grad_q, full_q)
        for i, start in enumerate(place):
            piece = lax.dynamic_slice_in_dim(part, start, half, 0)
            piece = piece + part_q[i * half : (i + 1) * half]
            part = lax.dynamic_update_slice_in_dim(part, piece, start, 0)
        dscale_ai = jnp.sum(part * hat_one, axis=0)

        part = part.astype(BF)
        if n_context == 2:
            mine = part[:rows].astype(F32) + core_swap(part[rows:]).astype(F32)
        else:
            mine = lax.psum_scatter(
                part.astype(F32), "context", scatter_dimension=0, tiled=True
            )
        mine = mine.astype(BF)
        keep = lax.dynamic_slice_in_dim(mine, group * half, half, 0)
        give = lax.dynamic_slice_in_dim(mine, (1 - group) * half, half, 0)
        keep = (keep.astype(F32) + z_far(give).astype(F32)).astype(BF)
        grad_one = keep.astype(F32) + z_near(keep).astype(F32)
        own_hat, own_inv = rms_stats(own_tok)
        grad_half = grad_hidden + rms_back(grad_one, scale_ai, own_hat, own_inv)

        def both_groups(value):
            value = value.astype(BF)
            other = z_far(value)
            low = jnp.where(group == 0, value, other)
            high = jnp.where(group == 0, other, value)
            return jnp.concatenate([low, high], axis=0).astype(F32)

        def scatter_blocks(value):
            pieces = value.astype(BF).reshape((n_fsdp, -1) + value.shape[1:])
            total_piece = 0.0
            for step in range(n_fsdp):
                piece = lax.dynamic_index_in_dim(pieces, own_f ^ step, 0, keepdims=False)
                if step:
                    piece = fsdp_hop(piece, step)
                total_piece = total_piece + piece.astype(F32)
            return total_piece

        def to_owner(value):
            value = across_pairs(value).astype(BF)
            final = (value.astype(F32) + z_one_way(value, False).astype(F32)).astype(BF)
            return jnp.where(is_owner, final, core_swap(final)).astype(F32)

        def to_all(value):
            value = across_pairs(value).astype(BF)
            value = (value.astype(F32) + core_swap(value).astype(F32)).astype(BF)
            value = (value.astype(F32) + z_near(value).astype(F32)).astype(BF)
            return value.astype(F32) + z_far(value).astype(F32)

        ffn_sum = to_owner(scatter_blocks(jnp.concatenate([grad_wgu, grad_dt], axis=1)))
        qo_sum = to_owner(scatter_blocks(jnp.concatenate([grad_wq, grad_wot], axis=1)))
        wide = [x.reshape(n_fsdp, block) for x in (dscale_ai, dscale_ao * 0.5, dscale_fi * 0.5, dscale_fo * 0.5)]
        slim = [x.reshape(n_fsdp, gain_block) for x in (dscale_q, dscale_k)]
        small = jnp.concatenate(wide + slim, axis=1)
        extra_rows = 16
        small = jnp.pad(small, ((0, 0), (0, extra_rows * 2 * HD - small.shape[1])))
        small = small.reshape(n_fsdp, extra_rows, 2 * HD)
        kv_ext = jnp.concatenate([grad_wkv.reshape(n_fsdp, block, 2 * HD), small], axis=1)
        kv_sum = to_all(scatter_blocks(kv_ext.reshape(-1, 2 * HD)))
        small_sum = kv_sum[block:].reshape(-1)
        gain_outs = []
        for i in range(4):
            gain_outs.append(small_sum[i * block : (i + 1) * block])
        for i in range(2):
            first = 4 * block + i * gain_block
            gain_outs.append(small_sum[first : first + gain_block])
        return (
            both_groups(layer_half),
            both_groups(grad_half),
            qo_sum[:, :HD],
            kv_sum[:block, :HD],
            kv_sum[:block, HD:],
            qo_sum[:, HD:].T,
            ffn_sum[:, :hidden],
            ffn_sum[:, hidden : 2 * hidden],
            ffn_sum[:, 2 * hidden :].T,
            *gain_outs,
        )

    return on_device


def solution(mesh):
    in_specs = (
        P(("fsdp", "context"), None),
        P("fsdp", None),
        P("fsdp", "tensor"),
        P("fsdp", None),
        P("fsdp", None),
        P("tensor", "fsdp"),
        P("fsdp", "tensor"),
        P("fsdp", "tensor"),
        P("tensor", "fsdp"),
        P("fsdp"),
        P("fsdp"),
        P("fsdp"),
        P("fsdp"),
        P("fsdp"),
        P("fsdp"),
        P(("fsdp", "context"), None),
    )
    out_specs = (
        P(("fsdp", "context"), None),
        P(("fsdp", "context"), None),
        P("fsdp", "tensor"),
        P("fsdp", None),
        P("fsdp", None),
        P("tensor", "fsdp"),
        P("fsdp", "tensor"),
        P("fsdp", "tensor"),
        P("tensor", "fsdp"),
        P("fsdp"),
        P("fsdp"),
        P("fsdp"),
        P("fsdp"),
        P("fsdp"),
        P("fsdp"),
    )
    on_device = make_program(mesh.shape["fsdp"], mesh.shape["context"], mesh.shape["tensor"])
    return jax.shard_map(
        on_device, mesh=mesh, in_specs=in_specs, out_specs=out_specs, check_vma=False
    )
```

time: 584 us -> 205 us (0.35)
  waiting for transfers between devices: 352 us -> 69.3 us
  blocking collectives: 113 us -> 0 us
  starting transfers between devices: 0.72 us -> 64.8 us
  local copies, waits for them, and re-layouts: 49.4 us -> 23.1 us
  between operations: 17.6 us -> 2.25 us
  matrix products: 25.8 us -> 10.9 us
  other arithmetic: 20.8 us -> 33.8 us
    reduce_scatter x8 -> x0, waiting for transfers between devices: 212 us -> none  [the longest x1 32.6 us: on_device(): lax.psum_scatter(grads[4], 'fsdp', scatter_dimension=0, tiled=True)]
    psum x5 -> x0, waiting for transfers between devices: 140 us -> none  [the longest x1 53.3 us: on_device(): lax.psum((contract_last(grad_qpre_b, full_query), kv_grads, dscale_q_part...]
    all_gather x9 -> x0, blocking collectives: 71.6 us -> none  [the longest x1 11.7 us: on_device(): lax.all_gather(weight_up, 'fsdp', axis=0, tiled=True)]
    ppermute x0 -> x48, waiting for transfers between devices: none -> 69.3 us  [the longest x24 35.5 us: fsdp_hop(): return lax.ppermute(value, 'fsdp', [(i, i ^ step) for i in range(n_fsdp)])]
    ppermute x0 -> x48, starting transfers between devices: none -> 64.8 us  [the longest x24 30.5 us: fsdp_hop(): return lax.ppermute(value, 'fsdp', [(i, i ^ step) for i in range(n_fsdp)])]
    unnamed x2 -> x0, blocking collectives: 27 us -> none
    dynamic_update_slice x4 -> x0, local copies, waits for them, and re-layouts: 23.8 us -> none  [on_device(): lax.scan(back_step, zero_query, jnp.arange(n_context, dtype=jnp.int32))]
    unnamed x175 -> x168, local copies, waits for them, and re-layouts: 23.3 us -> 4.27 us
  transfers between devices with their start and end apart: 13 -> 48, of which waited for: 12 -> 23; matrix products, arithmetic and copies ran while one was open for 3% -> 22% of each run, Pallas kernels for 0% -> 0%
where the time goes in v1:
time: 205 us; the launch traced here: 204 us
  waiting for transfers between devices  69.3 us (34%)
  starting transfers between devices  64.8 us (32%)
  other arithmetic  33.8 us (16%)
  local copies, waits for them, and re-layouts  23.1 us (11%)
  matrix products  10.9 us (5%)
  between operations  2.25 us (1%)
    ppermute x24, waiting for transfers between devices, fsdp_hop(): return lax.ppermute(value, 'fsdp', [(i, i ^ step) for i in range(n_fsdp)])  35.5 us
    ppermute x24, starting transfers between devices, fsdp_hop(): return lax.ppermute(value, 'fsdp', [(i, i ^ step) for i in range(n_fsdp)])  30.5 us
    ppermute x4, waiting for transfers between devices, z_far(): return lax.ppermute(value, 'tensor', [(i, i ^ 2) for i in range(n_tensor)])  16 us
    ppermute x4, starting transfers between devices, z_one_way(): return lax.ppermute(value, ('context', 'tensor'), pairs)  13.8 us
    ppermute x5, waiting for transfers between devices, z_near(): return lax.ppermute(value, 'tensor', [(i, i ^ 1) for i in range(n_tensor)])  11.1 us
    ppermute x5, starting transfers between devices, z_near(): return lax.ppermute(value, 'tensor', [(i, i ^ 1) for i in range(n_tensor)])  9.38 us
    ppermute x4, starting transfers between devices, z_far(): return lax.ppermute(value, 'tensor', [(i, i ^ 2) for i in range(n_tensor)])  6.35 us
    ppermute x4, waiting for transfers between devices, z_one_way(): return lax.ppermute(value, ('context', 'tensor'), pairs)  4.98 us
  transfers between devices with their start and end apart: 48, of which 23 were waited for; matrix products, arithmetic and copies ran while one was open for 22% of the time, Pallas kernels for 0%

profile of v1, /device:TPU:0, one launch (start us, length us, event | category | flops | bytes accessed | tf_op | source)
XLA Modules:
  0.0 204.2 jit_solution(6892468709809896836)
XLA Ops:
  0.7 4.1 %concatenate.101 = bf16[768]{0:T(1024)(128)(2,1)S(1)} concatenate(bf16[160]{0:T(256)(128)(2,1)} %param.27, bf16[160]{0:T(256)(128)(2,1)} %param.28, bf16[160]{0:T(256)(128)(2,1)} %param.29, bf16[160]{0:T(256)(128)(2,1)} %param.30, bf16[64]{0:T(256)(128)(2,1)} %param.31, bf16[64]{0:T(256)(128)(2,1)} %param.32), dimensions={0} | concatenate | bytes 3072 | tf_op jit(solution)/shard_map/concatenate | solution.py:129
  4.8 3.9 %collective-permute-start.3 = (bf16[768]{0:T(1024)(128)(2,1)S(1)}, bf16[768]{0:T(1024)(128)(2,1)S(1)}, u32[]{:S(2)}, u32[]{:S(2)}) collective-permute-start(bf16[768]{0:T(1024)(128)(2,1)S(1)} %concatenate.101), channel_id=1, source_target_pairs={{0,24},{8,16},{16,8},{24,0},{1,25},{9,17},{17,9},{25,1},{2,26},{10... | collective-permute-start | bytes 4616 | tf_op jit(solution)/shard_map/ppermute | solution.py:93
  11.2 2.8 %collective-permute-start.10 = (bf16[160,512]{1,0:T(8,128)(2,1)S(1)}, bf16[160,512]{1,0:T(8,128)(2,1)S(1)}, u32[]{:S(2)}, u32[]{:S(2)}) collective-permute-start(bf16[160,512]{1,0:T(8,128)(2,1)S(1)} %constant_dynamic-update-slice_fusion), channel_id=1, source_target_pairs={{0,24},{8,16},{16,8},{24,0},{1,25},{9,17},{17,9},{25,1},{2,26},{10... | collective-permute-start | bytes 491528 | tf_op jit(solution)/shard_map/ppermute | solution.py:93
  19.8 4.9 %collective-permute-start.4 = (bf16[160,512]{1,0:T(8,128)(2,1)S(1)}, bf16[160,512]{1,0:T(8,128)(2,1)S(1)}, u32[]{:S(2)}, u32[]{:S(2)}) collective-permute-start(bf16[160,512]{1,0:T(8,128)(2,1)S(1)} %pad_maximum_fusion.29), channel_id=1, source_target_pairs={{0,2},{1,3},{6,4},{7,5},{8,10},{9,11},{14,12},{15,13},{16,18},{17,... | collective-permute-start | bytes 491528 | tf_op jit(solution)/shard_map/ppermute | solution.py:90
  25.9 1.6 collective-permute-done.4
  27.5 6.2 %collective-permute-start.14 = (bf16[160,1536]{1,0:T(8,128)(2,1)S(1)}, bf16[160,1536]{1,0:T(8,128)(2,1)}, u32[]{:S(2)}, u32[]{:S(2)}) collective-permute-start(bf16[160,1536]{1,0:T(8,128)(2,1)S(1)} %pad_maximum_fusion.8), channel_id=1, source_target_pairs={{0,2},{1,3},{6,4},{7,5},{8,10},{9,11},{14,12},{15,13},{16,18},{17,... | collective-permute-start | bytes 1474568 | tf_op jit(solution)/shard_map/ppermute | solution.py:90
  33.7 2.5 %collective-permute-start.7 = (bf16[160,512]{1,0:T(8,128)(2,1)S(1)}, bf16[160,512]{1,0:T(8,128)(2,1)S(1)}, u32[]{:S(2)}, u32[]{:S(2)}) collective-permute-start(bf16[160,512]{1,0:T(8,128)(2,1)S(1)} %broadcast_select_fusion.6), channel_id=1, source_target_pairs={{0,24},{8,16},{16,8},{24,0},{1,25},{9,17},{17,9},{25,1},{2,26},{10... | collective-permute-start | bytes 491528 | tf_op jit(solution)/shard_map/ppermute | solution.py:93
  40.1 1.5 collective-permute-start.19
  41.7 1.5 collective-permute-start.18
  45.8 1.5 collective-permute-done.18
  47.3 3.3 %collective-permute-done.20 = bf16[160,512]{1,0:T(8,128)(2,1)} collective-permute-done((bf16[160,512]{1,0:T(8,128)(2,1)}, bf16[160,512]{1,0:T(8,128)(2,1)}, u32[]{:S(2)}, u32[]{:S(2)}) %collective-permute-start.20) | collective-permute-done | bytes 163872 | tf_op jit(solution)/shard_map/ppermute | solution.py:93
  51.8 1.4 gather_fusion.4
  53.2 2.2 %broadcast_select_fusion = (bf16[4,160,512]{2,1,0:T(8,128)(2,1)}, bf16[4,160,512]{2,1,0:T(8,128)(2,1)S(1)}, bf16[4,160,512]{2,1,0:T(8,128)(2,1)S(1)}) fusion(bf16[4,160,512]{2,1,0:T(8,128)(2,1)} %gather_fusion.4, pred[4]{0:T(512)(128)(4,1)S(1)} %compare_and_fusion.1, bf16[4,160,512]{2,1,0:T(8,128)(2,1)S(1)} %gather_fusion.3, ...), kind=kLoop, calls=%fused_computation.59 | loop fusion | flops 983040 | bytes 3932164 | tf_op jit(solution)/shard_map/jit(_take)/select_n | solution.py:126
  60.2 2.5 %collective-permute-start.11 = (bf16[128,640]{1,0:T(8,128)(2,1)S(1)}, bf16[128,640]{1,0:T(8,128)(2,1)S(1)}, u32[]{:S(2)}, u32[]{:S(2)}) collective-permute-start(bf16[128,640]{1,0:T(8,128)(2,1)S(1)} %slice.320), channel_id=1, source_target_pairs={{0,4},{4,0},{1,5},{5,1},{2,6},{6,2},{3,7},{7,3},{8,12},{12,8},{9,1... | collective-permute-start | bytes 491528 | tf_op jit(solution)/shard_map/ppermute | solution.py:75
  64.4 1.5 collective-permute-start.15
  65.9 1.2 collective-permute-start.17
  67.2 4.0 %collective-permute-start.12 = (bf16[128,640]{1,0:T(8,128)(2,1)S(1)}, bf16[128,640]{1,0:T(8,128)(2,1)}, u32[]{:S(2)}, u32[]{:S(2)}) collective-permute-start(bf16[128,640]{1,0:T(8,128)(2,1)S(1)} %fusion.57), channel_id=1, source_target_pairs={{0,1},{1,0},{2,3},{3,2},{4,5},{5,4},{6,7},{7,6},{8,9},{9,8},{10,11... | collective-permute-start | bytes 491528 | tf_op jit(solution)/shard_map/ppermute | solution.py:78
  72.2 1.9 collective-permute-done.16
  75.2 7.2 %collective-permute-done.17 = bf16[160,1024]{1,0:T(8,128)(2,1)} collective-permute-done((bf16[160,1024]{1,0:T(8,128)(2,1)}, bf16[160,1024]{1,0:T(8,128)(2,1)}, u32[]{:S(2)}, u32[]{:S(2)}) %collective-permute-start.17) | collective-permute-done | bytes 327712 | tf_op jit(solution)/shard_map/ppermute | solution.py:93
  82.4 1.4 pad_maximum_fusion
  83.8 1.8 gather_fusion.1
  93.2 3.3 %collective-permute-start.22 = (bf16[128,640]{1,0:T(8,128)(2,1)S(1)}, bf16[128,640]{1,0:T(8,128)(2,1)S(1)}, u32[]{:S(2)}, u32[]{:S(2)}) collective-permute-start(bf16[128,640]{1,0:T(8,128)(2,1)S(1)} %fusion.56), channel_id=1, source_target_pairs={{0,1},{1,0},{2,3},{3,2},{4,5},{5,4},{6,7},{7,6},{8,9},{9,8},{10,11... | collective-permute-start | bytes 491528 | tf_op jit(solution)/shard_map/ppermute | solution.py:78
  97.0 4.0 %collective-permute-done.22 = bf16[128,640]{1,0:T(8,128)(2,1)S(1)} collective-permute-done((bf16[128,640]{1,0:T(8,128)(2,1)S(1)}, bf16[128,640]{1,0:T(8,128)(2,1)S(1)}, u32[]{:S(2)}, u32[]{:S(2)}) %collective-permute-start.22) | collective-permute-done | bytes 163872 | tf_op jit(solution)/shard_map/ppermute | solution.py:78
  103.0 4.5 %collective-permute-start.23 = (bf16[128,640]{1,0:T(8,128)(2,1)}, bf16[128,640]{1,0:T(8,128)(2,1)S(1)}, u32[]{:S(2)}, u32[]{:S(2)}) collective-permute-start(bf16[128,640]{1,0:T(8,128)(2,1)} %get-tuple-element.64), channel_id=1, source_target_pairs={{0,2},{1,3},{2,0},{3,1},{4,6},{5,7},{6,4},{7,5},{8,10},{9,11},{10,... | collective-permute-start | bytes 491528 | tf_op jit(solution)/shard_map/ppermute | solution.py:81
  107.6 1.9 fusion.17
  110.4 1.3 convolution_convert_fusion.1
  114.7 1.5 collective-permute-start.44
  117.4 1.8 collective-permute-start.26
  120.2 2.9 %collective-permute-done.26 = bf16[128,640]{1,0:T(8,128)(2,1)S(1)} collective-permute-done((bf16[128,640]{1,0:T(8,128)(2,1)S(1)}, bf16[128,640]{1,0:T(8,128)(2,1)S(1)}, u32[]{:S(2)}, u32[]{:S(2)}) %collective-permute-start.26) | collective-permute-done | bytes 163872 | tf_op jit(solution)/shard_map/ppermute | solution.py:78
  123.3 1.8 multiply_reduce_fusion.4
  128.2 10.4 %collective-permute-done.44 = bf16[160,1536]{1,0:T(8,128)(2,1)} collective-permute-done((bf16[160,1536]{1,0:T(8,128)(2,1)}, bf16[160,1536]{1,0:T(8,128)(2,1)}, u32[]{:S(2)}, u32[]{:S(2)}) %collective-permute-start.44) | collective-permute-done | bytes 491552 | tf_op jit(solution)/shard_map/ppermute | solution.py:93
  138.7 2.4 %fusion.10 = bf16[160,1536]{1,0:T(8,128)(2,1)} fusion(bf16[160,1536]{1,0:T(8,128)(2,1)} %collective-permute-done.45, bf16[160,1536]{1,0:T(8,128)(2,1)} %collective-permute-done.44, bf16[160,1536]{1,0:T(8,128)(2,1)} %collective-permute-done.43, s32[]{:T(128)S(6)} %select_n.174, bf16[4,160,1024]{2,1,0:T(8,128)(2,1)} %bitcast.100, ...), kind=kLoop, calls=%fused_computation.42 | loop fusion | flops 2949120 | bytes 3932164 | tf_op jit(solution)/shard_map/convert_element_type | solution.py:290
  141.1 1.5 collective-permute-start.46
  146.3 1.2 fusion.76
  149.6 1.2 collective-permute-start.32
  151.7 1.4 collective-permute-start.34
  155.0 1.6 collective-permute-done.32
  157.7 2.4 %collective-permute-done.33 = bf16[160,512]{1,0:T(8,128)(2,1)S(1)} collective-permute-done((bf16[160,512]{1,0:T(8,128)(2,1)}, bf16[160,512]{1,0:T(8,128)(2,1)S(1)}, u32[]{:S(2)}, u32[]{:S(2)}) %collective-permute-start.33) | collective-permute-done | bytes 163872 | tf_op jit(solution)/shard_map/ppermute | solution.py:93
  160.1 2.3 %collective-permute-start.38 = (bf16[176,512]{1,0:T(8,128)(2,1)S(1)}, bf16[176,512]{1,0:T(8,128)(2,1)S(1)}, u32[]{:S(2)}, u32[]{:S(2)}) collective-permute-start(bf16[176,512]{1,0:T(8,128)(2,1)S(1)} %get-tuple-element.42), channel_id=1, source_target_pairs={{0,16},{8,24},{16,0},{24,8},{1,17},{9,25},{17,1},{25,9},{2,18},{10... | collective-permute-start | bytes 540680 | tf_op jit(solution)/shard_map/ppermute | solution.py:93
  162.4 1.5 collective-permute-start.39
  164.9 1.3 collective-permute-start.35
  166.2 5.2 %collective-permute-done.38 = bf16[176,512]{1,0:T(8,128)(2,1)S(1)} collective-permute-done((bf16[176,512]{1,0:T(8,128)(2,1)S(1)}, bf16[176,512]{1,0:T(8,128)(2,1)S(1)}, u32[]{:S(2)}, u32[]{:S(2)}) %collective-permute-start.38) | collective-permute-done | bytes 180256 | tf_op jit(solution)/shard_map/ppermute | solution.py:93
  172.2 2.6 %collective-permute-done.35 = bf16[160,512]{1,0:T(8,128)(2,1)S(1)} collective-permute-done((bf16[160,512]{1,0:T(8,128)(2,1)S(1)}, bf16[160,512]{1,0:T(8,128)(2,1)S(1)}, u32[]{:S(2)}, u32[]{:S(2)}) %collective-permute-start.35) | collective-permute-done | bytes 163872 | tf_op jit(solution)/shard_map/ppermute | solution.py:90
  175.1 1.3 add_convert_fusion
  176.9 6.0 %collective-permute-done.29 = bf16[128,640]{1,0:T(8,128)(2,1)S(1)} collective-permute-done((bf16[128,640]{1,0:T(8,128)(2,1)S(1)}, bf16[128,640]{1,0:T(8,128)(2,1)S(1)}, u32[]{:S(2)}, u32[]{:S(2)}) %collective-permute-start.29) | collective-permute-done | bytes 163872 | tf_op jit(solution)/shard_map/ppermute | solution.py:81
  184.3 1.4 collective-permute-start.42
  185.6 3.8 %collective-permute-done.30 = bf16[128,640]{1,0:T(8,128)(2,1)S(1)} collective-permute-done((bf16[128,640]{1,0:T(8,128)(2,1)S(1)}, bf16[128,640]{1,0:T(8,128)(2,1)S(1)}, u32[]{:S(2)}, u32[]{:S(2)}) %collective-permute-start.30) | collective-permute-done | bytes 163872 | tf_op jit(solution)/shard_map/ppermute | solution.py:78
  190.2 9.4 %collective-permute-done.42 = bf16[176,512]{1,0:T(8,128)(2,1)S(1)} collective-permute-done((bf16[176,512]{1,0:T(8,128)(2,1)S(1)}, bf16[176,512]{1,0:T(8,128)(2,1)S(1)}, u32[]{:S(2)}, u32[]{:S(2)}) %collective-permute-start.42) | collective-permute-done | bytes 180256 | tf_op jit(solution)/shard_map/ppermute | solution.py:81
  (375 shorter events, 63.1 us)
Async XLA Ops:
  4.8 14.7 %collective-permute-start.3 = (bf16[768]{0:T(1024)(128)(2,1)S(1)}, bf16[768]{0:T(1024)(128)(2,1)S(1)}, u32[]{:S(2)}, u32[]{:S(2)}) collective-permute-start(bf16[768]{0:T(1024)(128)(2,1)S(1)} %concatenate.101), channel_id=1, source_target_pairs={{0,24},{8,16},{16,8},{24,0},{1,25},{9,17},{17,9},{25,1},{2,26},{10... | collective-permute-start | bytes 4616 | tf_op jit(solution)/shard_map/ppermute | solution.py:93
  8.7 11.0 %collective-permute-start.2 = (bf16[768]{0:T(1024)(128)(2,1)S(1)}, bf16[768]{0:T(1024)(128)(2,1)S(1)}, u32[]{:S(2)}, u32[]{:S(2)}) collective-permute-start(bf16[768]{0:T(1024)(128)(2,1)S(1)} %concatenate.101), channel_id=1, source_target_pairs={{0,16},{8,24},{16,0},{24,8},{1,17},{9,25},{17,1},{25,9},{2,18},{10... | collective-permute-start | bytes 4616 | tf_op jit(solution)/shard_map/ppermute | solution.py:93
  9.2 15.5 %collective-permute-start.1 = (bf16[768]{0:T(1024)(128)(2,1)S(1)}, bf16[768]{0:T(1024)(128)(2,1)S(1)}, u32[]{:S(2)}, u32[]{:S(2)}) collective-permute-start(bf16[768]{0:T(1024)(128)(2,1)S(1)} %concatenate.101), channel_id=1, source_target_pairs={{0,8},{8,0},{16,24},{24,16},{1,9},{9,1},{17,25},{25,17},{2,10},{10... | collective-permute-start | bytes 4616 | tf_op jit(solution)/shard_map/ppermute | solution.py:93
  11.2 22.6 %collective-permute-start.10 = (bf16[160,512]{1,0:T(8,128)(2,1)S(1)}, bf16[160,512]{1,0:T(8,128)(2,1)S(1)}, u32[]{:S(2)}, u32[]{:S(2)}) collective-permute-start(bf16[160,512]{1,0:T(8,128)(2,1)S(1)} %constant_dynamic-update-slice_fusion), channel_id=1, source_target_pairs={{0,24},{8,16},{16,8},{24,0},{1,25},{9,17},{17,9},{25,1},{2,26},{10... | collective-permute-start | bytes 491528 | tf_op jit(solution)/shard_map/ppermute | solution.py:93
  14.0 22.2 %collective-permute-start.9 = (bf16[160,512]{1,0:T(8,128)(2,1)S(1)}, bf16[160,512]{1,0:T(8,128)(2,1)S(1)}, u32[]{:S(2)}, u32[]{:S(2)}) collective-permute-start(bf16[160,512]{1,0:T(8,128)(2,1)S(1)} %constant_dynamic-update-slice_fusion), channel_id=1, source_target_pairs={{0,16},{8,24},{16,0},{24,8},{1,17},{9,25},{17,1},{25,9},{2,18},{10... | collective-permute-start | bytes 491528 | tf_op jit(solution)/shard_map/ppermute | solution.py:93
  19.6 17.2 %collective-permute-start.8 = (bf16[160,512]{1,0:T(8,128)(2,1)S(1)}, bf16[160,512]{1,0:T(8,128)(2,1)S(1)}, u32[]{:S(2)}, u32[]{:S(2)}) collective-permute-start(bf16[160,512]{1,0:T(8,128)(2,1)S(1)} %constant_dynamic-update-slice_fusion), channel_id=1, source_target_pairs={{0,8},{8,0},{16,24},{24,16},{1,9},{9,1},{17,25},{25,17},{2,10},{10... | collective-permute-start | bytes 491528 | tf_op jit(solution)/shard_map/ppermute | solution.py:93
  19.8 7.7 %collective-permute-start.4 = (bf16[160,512]{1,0:T(8,128)(2,1)S(1)}, bf16[160,512]{1,0:T(8,128)(2,1)S(1)}, u32[]{:S(2)}, u32[]{:S(2)}) collective-permute-start(bf16[160,512]{1,0:T(8,128)(2,1)S(1)} %pad_maximum_fusion.29), channel_id=1, source_target_pairs={{0,2},{1,3},{6,4},{7,5},{8,10},{9,11},{14,12},{15,13},{16,18},{17,... | collective-permute-start | bytes 491528 | tf_op jit(solution)/shard_map/ppermute | solution.py:90
  24.7 13.3 %collective-permute-start = (bf16[256,640]{1,0:T(8,128)(2,1)S(1)}, bf16[256,640]{1,0:T(8,128)(2,1)S(1)}, u32[]{:S(2)}, u32[]{:S(2)}) collective-permute-start(bf16[256,640]{1,0:T(8,128)(2,1)S(1)} %copy-done), channel_id=1, source_target_pairs={{0,4},{4,0},{1,5},{5,1},{2,6},{6,2},{3,7},{7,3},{8,12},{12,8},{9,1... | collective-permute-start | bytes 983048 | tf_op jit(solution)/shard_map/ppermute | solution.py:75
  27.5 11.7 %collective-permute-start.14 = (bf16[160,1536]{1,0:T(8,128)(2,1)S(1)}, bf16[160,1536]{1,0:T(8,128)(2,1)}, u32[]{:S(2)}, u32[]{:S(2)}) collective-permute-start(bf16[160,1536]{1,0:T(8,128)(2,1)S(1)} %pad_maximum_fusion.8), channel_id=1, source_target_pairs={{0,2},{1,3},{6,4},{7,5},{8,10},{9,11},{14,12},{15,13},{16,18},{17,... | collective-permute-start | bytes 1474568 | tf_op jit(solution)/shard_map/ppermute | solution.py:90
  33.7 9.4 %collective-permute-start.7 = (bf16[160,512]{1,0:T(8,128)(2,1)S(1)}, bf16[160,512]{1,0:T(8,128)(2,1)S(1)}, u32[]{:S(2)}, u32[]{:S(2)}) collective-permute-start(bf16[160,512]{1,0:T(8,128)(2,1)S(1)} %broadcast_select_fusion.6), channel_id=1, source_target_pairs={{0,24},{8,16},{16,8},{24,0},{1,25},{9,17},{17,9},{25,1},{2,26},{10... | collective-permute-start | bytes 491528 | tf_op jit(solution)/shard_map/ppermute | solution.py:93
  36.2 7.4 %collective-permute-start.6 = (bf16[160,512]{1,0:T(8,128)(2,1)S(1)}, bf16[160,512]{1,0:T(8,128)(2,1)}, u32[]{:S(2)}, u32[]{:S(2)}) collective-permute-start(bf16[160,512]{1,0:T(8,128)(2,1)S(1)} %broadcast_select_fusion.6), channel_id=1, source_target_pairs={{0,16},{8,24},{16,0},{24,8},{1,17},{9,25},{17,1},{25,9},{2,18},{10... | collective-permute-start | bytes 491528 | tf_op jit(solution)/shard_map/ppermute | solution.py:93
  36.7 6.9 %collective-permute-start.5 = (bf16[160,512]{1,0:T(8,128)(2,1)S(1)}, bf16[160,512]{1,0:T(8,128)(2,1)}, u32[]{:S(2)}, u32[]{:S(2)}) collective-permute-start(bf16[160,512]{1,0:T(8,128)(2,1)S(1)} %broadcast_select_fusion.6), channel_id=1, source_target_pairs={{0,8},{8,0},{16,24},{24,16},{1,9},{9,1},{17,25},{25,17},{2,10},{10... | collective-permute-start | bytes 491528 | tf_op jit(solution)/shard_map/ppermute | solution.py:93
  40.1 5.6 %collective-permute-start.19 = (bf16[160,512]{1,0:T(8,128)(2,1)}, bf16[160,512]{1,0:T(8,128)(2,1)}, u32[]{:S(2)}, u32[]{:S(2)}) collective-permute-start(bf16[160,512]{1,0:T(8,128)(2,1)} %get-tuple-element.58), channel_id=1, source_target_pairs={{0,16},{8,24},{16,0},{24,8},{1,17},{9,25},{17,1},{25,9},{2,18},{10... | collective-permute-start | bytes 491528 | tf_op jit(solution)/shard_map/ppermute | solution.py:93
  41.7 5.6 %collective-permute-start.18 = (bf16[160,512]{1,0:T(8,128)(2,1)}, bf16[160,512]{1,0:T(8,128)(2,1)}, u32[]{:S(2)}, u32[]{:S(2)}) collective-permute-start(bf16[160,512]{1,0:T(8,128)(2,1)} %get-tuple-element.58), channel_id=1, source_target_pairs={{0,8},{8,0},{16,24},{24,16},{1,9},{9,1},{17,25},{25,17},{2,10},{10... | collective-permute-start | bytes 491528 | tf_op jit(solution)/shard_map/ppermute | solution.py:93
  43.2 7.5 %collective-permute-start.20 = (bf16[160,512]{1,0:T(8,128)(2,1)}, bf16[160,512]{1,0:T(8,128)(2,1)}, u32[]{:S(2)}, u32[]{:S(2)}) collective-permute-start(bf16[160,512]{1,0:T(8,128)(2,1)} %get-tuple-element.58), channel_id=1, source_target_pairs={{0,24},{8,16},{16,8},{24,0},{1,25},{9,17},{17,9},{25,1},{2,26},{10... | collective-permute-start | bytes 491528 | tf_op jit(solution)/shard_map/ppermute | solution.py:93
  60.2 6.9 %collective-permute-start.11 = (bf16[128,640]{1,0:T(8,128)(2,1)S(1)}, bf16[128,640]{1,0:T(8,128)(2,1)S(1)}, u32[]{:S(2)}, u32[]{:S(2)}) collective-permute-start(bf16[128,640]{1,0:T(8,128)(2,1)S(1)} %slice.320), channel_id=1, source_target_pairs={{0,4},{4,0},{1,5},{5,1},{2,6},{6,2},{3,7},{7,3},{8,12},{12,8},{9,1... | collective-permute-start | bytes 491528 | tf_op jit(solution)/shard_map/ppermute | solution.py:75
  63.6 10.5 %collective-permute-start.16 = (bf16[160,1024]{1,0:T(8,128)(2,1)}, bf16[160,1024]{1,0:T(8,128)(2,1)S(1)}, u32[]{:S(2)}, u32[]{:S(2)}) collective-permute-start(bf16[160,1024]{1,0:T(8,128)(2,1)} %get-tuple-element.60), channel_id=1, source_target_pairs={{0,16},{8,24},{16,0},{24,8},{1,17},{9,25},{17,1},{25,9},{2,18},{10... | collective-permute-start | bytes 983048 | tf_op jit(solution)/shard_map/ppermute | solution.py:93
  64.4 10.8 %collective-permute-start.15 = (bf16[160,1024]{1,0:T(8,128)(2,1)}, bf16[160,1024]{1,0:T(8,128)(2,1)S(1)}, u32[]{:S(2)}, u32[]{:S(2)}) collective-permute-start(bf16[160,1024]{1,0:T(8,128)(2,1)} %get-tuple-element.60), channel_id=1, source_target_pairs={{0,8},{8,0},{16,24},{24,16},{1,9},{9,1},{17,25},{25,17},{2,10},{10... | collective-permute-start | bytes 983048 | tf_op jit(solution)/shard_map/ppermute | solution.py:93
  65.9 16.5 %collective-permute-start.17 = (bf16[160,1024]{1,0:T(8,128)(2,1)}, bf16[160,1024]{1,0:T(8,128)(2,1)}, u32[]{:S(2)}, u32[]{:S(2)}) collective-permute-start(bf16[160,1024]{1,0:T(8,128)(2,1)} %get-tuple-element.60), channel_id=1, source_target_pairs={{0,24},{8,16},{16,8},{24,0},{1,25},{9,17},{17,9},{25,1},{2,26},{10... | collective-permute-start | bytes 983048 | tf_op jit(solution)/shard_map/ppermute | solution.py:93
  67.2 18.5 %collective-permute-start.12 = (bf16[128,640]{1,0:T(8,128)(2,1)S(1)}, bf16[128,640]{1,0:T(8,128)(2,1)}, u32[]{:S(2)}, u32[]{:S(2)}) collective-permute-start(bf16[128,640]{1,0:T(8,128)(2,1)S(1)} %fusion.57), channel_id=1, source_target_pairs={{0,1},{1,0},{2,3},{3,2},{4,5},{5,4},{6,7},{7,6},{8,9},{9,8},{10,11... | collective-permute-start | bytes 491528 | tf_op jit(solution)/shard_map/ppermute | solution.py:78
  88.1 1.5 collective-permute-start.13
  91.7 1.5 collective-permute-start.21
  93.2 7.8 %collective-permute-start.22 = (bf16[128,640]{1,0:T(8,128)(2,1)S(1)}, bf16[128,640]{1,0:T(8,128)(2,1)S(1)}, u32[]{:S(2)}, u32[]{:S(2)}) collective-permute-start(bf16[128,640]{1,0:T(8,128)(2,1)S(1)} %fusion.56), channel_id=1, source_target_pairs={{0,1},{1,0},{2,3},{3,2},{4,5},{5,4},{6,7},{7,6},{8,9},{9,8},{10,11... | collective-permute-start | bytes 491528 | tf_op jit(solution)/shard_map/ppermute | solution.py:78
  102.4 5.2 %collective-permute-start.24 = (bf16[128,640]{1,0:T(8,128)(2,1)}, bf16[128,640]{1,0:T(8,128)(2,1)}, u32[]{:S(2)}, u32[]{:S(2)}) collective-permute-start(bf16[128,640]{1,0:T(8,128)(2,1)} %get-tuple-element.63), channel_id=1, source_target_pairs={{0,4},{4,0},{1,5},{5,1},{2,6},{6,2},{3,7},{7,3},{8,12},{12,8},{9,1... | collective-permute-start | bytes 491528 | tf_op jit(solution)/shard_map/ppermute | solution.py:75
  103.0 16.2 %collective-permute-start.23 = (bf16[128,640]{1,0:T(8,128)(2,1)}, bf16[128,640]{1,0:T(8,128)(2,1)S(1)}, u32[]{:S(2)}, u32[]{:S(2)}) collective-permute-start(bf16[128,640]{1,0:T(8,128)(2,1)} %get-tuple-element.64), channel_id=1, source_target_pairs={{0,2},{1,3},{2,0},{3,1},{4,6},{5,7},{6,4},{7,5},{8,10},{9,11},{10,... | collective-permute-start | bytes 491528 | tf_op jit(solution)/shard_map/ppermute | solution.py:81
  110.1 7.2 %collective-permute-start.25 = (bf16[128,640]{1,0:T(8,128)(2,1)S(1)}, bf16[128,640]{1,0:T(8,128)(2,1)S(1)}, u32[]{:S(2)}, u32[]{:S(2)}) collective-permute-start(bf16[128,640]{1,0:T(8,128)(2,1)S(1)} %slice.318), channel_id=1, source_target_pairs={{0,4},{4,0},{1,5},{5,1},{2,6},{6,2},{3,7},{7,3},{8,12},{12,8},{9,1... | collective-permute-start | bytes 491528 | tf_op jit(solution)/shard_map/ppermute | solution.py:75
  113.9 14.4 %collective-permute-start.43 = (bf16[160,1536]{1,0:T(8,128)(2,1)}, bf16[160,1536]{1,0:T(8,128)(2,1)}, u32[]{:S(2)}, u32[]{:S(2)}) collective-permute-start(bf16[160,1536]{1,0:T(8,128)(2,1)} %get-tuple-element.31), channel_id=1, source_target_pairs={{0,8},{8,0},{16,24},{24,16},{1,9},{9,1},{17,25},{25,17},{2,10},{10... | collective-permute-start | bytes 1474568 | tf_op jit(solution)/shard_map/ppermute | solution.py:93
  114.7 24.0 %collective-permute-start.44 = (bf16[160,1536]{1,0:T(8,128)(2,1)}, bf16[160,1536]{1,0:T(8,128)(2,1)}, u32[]{:S(2)}, u32[]{:S(2)}) collective-permute-start(bf16[160,1536]{1,0:T(8,128)(2,1)} %get-tuple-element.32), channel_id=1, source_target_pairs={{0,16},{8,24},{16,0},{24,8},{1,17},{9,25},{17,1},{25,9},{2,18},{10... | collective-permute-start | bytes 1474568 | tf_op jit(solution)/shard_map/ppermute | solution.py:93
  116.2 22.5 %collective-permute-start.45 = (bf16[160,1536]{1,0:T(8,128)(2,1)}, bf16[160,1536]{1,0:T(8,128)(2,1)}, u32[]{:S(2)}, u32[]{:S(2)}) collective-permute-start(bf16[160,1536]{1,0:T(8,128)(2,1)} %get-tuple-element.33), channel_id=1, source_target_pairs={{0,24},{8,16},{16,8},{24,0},{1,25},{9,17},{17,9},{25,1},{2,26},{10... | collective-permute-start | bytes 1474568 | tf_op jit(solution)/shard_map/ppermute | solution.py:93
  117.4 5.6 %collective-permute-start.26 = (bf16[128,640]{1,0:T(8,128)(2,1)S(1)}, bf16[128,640]{1,0:T(8,128)(2,1)S(1)}, u32[]{:S(2)}, u32[]{:S(2)}) collective-permute-start(bf16[128,640]{1,0:T(8,128)(2,1)S(1)} %fusion.55), channel_id=1, source_target_pairs={{0,1},{1,0},{2,3},{3,2},{4,5},{5,4},{6,7},{7,6},{8,9},{9,8},{10,11... | collective-permute-start | bytes 491528 | tf_op jit(solution)/shard_map/ppermute | solution.py:78
  127.7 14.9 %collective-permute-start.27 = (bf16[128,640]{1,0:T(8,128)(2,1)S(1)}, bf16[128,640]{1,0:T(8,128)(2,1)S(1)}, u32[]{:S(2)}, u32[]{:S(2)}) collective-permute-start(bf16[128,640]{1,0:T(8,128)(2,1)S(1)} %multiply_convert_fusion.3), channel_id=1, source_target_pairs={{0,4},{4,0},{1,5},{5,1},{2,6},{6,2},{3,7},{7,3},{8,12},{12,8},{9,1... | collective-permute-start | bytes 491528 | tf_op jit(solution)/shard_map/ppermute | solution.py:75
  141.1 34.0 %collective-permute-start.46 = (bf16[160,1536]{1,0:T(8,128)(2,1)}, bf16[160,1536]{1,0:T(8,128)(2,1)}, u32[]{:S(2)}, u32[]{:S(2)}) collective-permute-start(bf16[160,1536]{1,0:T(8,128)(2,1)} %fusion.10), channel_id=1, source_target_pairs={{2,0},{3,1},{4,6},{5,7},{10,8},{11,9},{12,14},{13,15},{18,16},{19,... | collective-permute-start | bytes 1474568 | tf_op jit(solution)/shard_map/ppermute | solution.py:90
  149.6 7.0 %collective-permute-start.32 = (bf16[160,512]{1,0:T(8,128)(2,1)}, bf16[160,512]{1,0:T(8,128)(2,1)S(1)}, u32[]{:S(2)}, u32[]{:S(2)}) collective-permute-start(bf16[160,512]{1,0:T(8,128)(2,1)} %get-tuple-element.44), channel_id=1, source_target_pairs={{0,8},{8,0},{16,24},{24,16},{1,9},{9,1},{17,25},{25,17},{2,10},{10... | collective-permute-start | bytes 491528 | tf_op jit(solution)/shard_map/ppermute | solution.py:93
  150.9 9.2 %collective-permute-start.33 = (bf16[160,512]{1,0:T(8,128)(2,1)}, bf16[160,512]{1,0:T(8,128)(2,1)S(1)}, u32[]{:S(2)}, u32[]{:S(2)}) collective-permute-start(bf16[160,512]{1,0:T(8,128)(2,1)} %get-tuple-element.45), channel_id=1, source_target_pairs={{0,16},{8,24},{16,0},{24,8},{1,17},{9,25},{17,1},{25,9},{2,18},{10... | collective-permute-start | bytes 491528 | tf_op jit(solution)/shard_map/ppermute | solution.py:93
  151.7 10.7 %collective-permute-start.34 = (bf16[160,512]{1,0:T(8,128)(2,1)}, bf16[160,512]{1,0:T(8,128)(2,1)}, u32[]{:S(2)}, u32[]{:S(2)}) collective-permute-start(bf16[160,512]{1,0:T(8,128)(2,1)} %get-tuple-element.46), channel_id=1, source_target_pairs={{0,24},{8,16},{16,8},{24,0},{1,25},{9,17},{17,9},{25,1},{2,26},{10... | collective-permute-start | bytes 491528 | tf_op jit(solution)/shard_map/ppermute | solution.py:93
  154.5 17.5 %collective-permute-start.28 = (bf16[256,640]{1,0:T(8,128)(2,1)S(1)}, bf16[256,640]{1,0:T(8,128)(2,1)S(1)}, u32[]{:S(2)}, u32[]{:S(2)}) collective-permute-start(bf16[256,640]{1,0:T(8,128)(2,1)S(1)} %slice.229), channel_id=1, source_target_pairs={{0,4},{4,0},{1,5},{5,1},{2,6},{6,2},{3,7},{7,3},{8,12},{12,8},{9,1... | collective-permute-start | bytes 983048 | tf_op jit(solution)/shard_map/ppermute | solution.py:75
  156.6 8.3 %collective-permute-start.37 = (bf16[176,512]{1,0:T(8,128)(2,1)S(1)}, bf16[176,512]{1,0:T(8,128)(2,1)S(1)}, u32[]{:S(2)}, u32[]{:S(2)}) collective-permute-start(bf16[176,512]{1,0:T(8,128)(2,1)S(1)} %get-tuple-element.41), channel_id=1, source_target_pairs={{0,8},{8,0},{16,24},{24,16},{1,9},{9,1},{17,25},{25,17},{2,10},{10... | collective-permute-start | bytes 540680 | tf_op jit(solution)/shard_map/ppermute | solution.py:93
  160.1 11.3 %collective-permute-start.38 = (bf16[176,512]{1,0:T(8,128)(2,1)S(1)}, bf16[176,512]{1,0:T(8,128)(2,1)S(1)}, u32[]{:S(2)}, u32[]{:S(2)}) collective-permute-start(bf16[176,512]{1,0:T(8,128)(2,1)S(1)} %get-tuple-element.42), channel_id=1, source_target_pairs={{0,16},{8,24},{16,0},{24,8},{1,17},{9,25},{17,1},{25,9},{2,18},{10... | collective-permute-start | bytes 540680 | tf_op jit(solution)/shard_map/ppermute | solution.py:93
  162.4 9.0 %collective-permute-start.39 = (bf16[176,512]{1,0:T(8,128)(2,1)S(1)}, bf16[176,512]{1,0:T(8,128)(2,1)S(1)}, u32[]{:S(2)}, u32[]{:S(2)}) collective-permute-start(bf16[176,512]{1,0:T(8,128)(2,1)S(1)} %get-tuple-element.43), channel_id=1, source_target_pairs={{0,24},{8,16},{16,8},{24,0},{1,25},{9,17},{17,9},{25,1},{2,26},{10... | collective-permute-start | bytes 540680 | tf_op jit(solution)/shard_map/ppermute | solution.py:93
  164.9 9.9 %collective-permute-start.35 = (bf16[160,512]{1,0:T(8,128)(2,1)S(1)}, bf16[160,512]{1,0:T(8,128)(2,1)S(1)}, u32[]{:S(2)}, u32[]{:S(2)}) collective-permute-start(bf16[160,512]{1,0:T(8,128)(2,1)S(1)} %fusion.60), channel_id=1, source_target_pairs={{2,0},{3,1},{4,6},{5,7},{10,8},{11,9},{12,14},{13,15},{18,16},{19,... | collective-permute-start | bytes 491528 | tf_op jit(solution)/shard_map/ppermute | solution.py:90
  171.5 3.4 %collective-permute-start.40 = (bf16[176,512]{1,0:T(8,128)(2,1)S(1)}, bf16[176,512]{1,0:T(8,128)(2,1)S(1)}, u32[]{:S(2)}, u32[]{:S(2)}) collective-permute-start(bf16[176,512]{1,0:T(8,128)(2,1)S(1)} %fusion.39), channel_id=1, source_target_pairs={{0,4},{4,0},{1,5},{5,1},{2,6},{6,2},{3,7},{7,3},{8,12},{12,8},{9,1... | collective-permute-start | bytes 540680 | tf_op jit(solution)/shard_map/ppermute | solution.py:75
  172.1 10.8 %collective-permute-start.29 = (bf16[128,640]{1,0:T(8,128)(2,1)S(1)}, bf16[128,640]{1,0:T(8,128)(2,1)S(1)}, u32[]{:S(2)}, u32[]{:S(2)}) collective-permute-start(bf16[128,640]{1,0:T(8,128)(2,1)S(1)} %constant_dynamic-slice_fusion), channel_id=1, source_target_pairs={{0,2},{1,3},{2,0},{3,1},{4,6},{5,7},{6,4},{7,5},{8,10},{9,11},{10,... | collective-permute-start | bytes 491528 | tf_op jit(solution)/shard_map/ppermute | solution.py:81
  174.8 8.2 %collective-permute-start.36 = (bf16[160,512]{1,0:T(8,128)(2,1)S(1)}, bf16[160,512]{1,0:T(8,128)(2,1)S(1)}, u32[]{:S(2)}, u32[]{:S(2)}) collective-permute-start(bf16[160,512]{1,0:T(8,128)(2,1)S(1)} %add_convert_fusion.4), channel_id=1, source_target_pairs={{0,4},{4,0},{1,5},{5,1},{2,6},{6,2},{3,7},{7,3},{8,12},{12,8},{9,1... | collective-permute-start | bytes 491528 | tf_op jit(solution)/shard_map/ppermute | solution.py:75
  175.0 9.2 %collective-permute-start.41 = (bf16[176,512]{1,0:T(8,128)(2,1)S(1)}, bf16[176,512]{1,0:T(8,128)(2,1)S(1)}, u32[]{:S(2)}, u32[]{:S(2)}) collective-permute-start(bf16[176,512]{1,0:T(8,128)(2,1)S(1)} %add_convert_fusion.3), channel_id=1, source_target_pairs={{0,1},{1,0},{2,3},{3,2},{4,5},{5,4},{6,7},{7,6},{8,9},{9,8},{10,11... | collective-permute-start | bytes 540680 | tf_op jit(solution)/shard_map/ppermute | solution.py:78
  176.4 26.8 %collective-permute-start.47 = (bf16[160,1536]{1,0:T(8,128)(2,1)S(1)}, bf16[160,1536]{1,0:T(8,128)(2,1)S(1)}, u32[]{:S(2)}, u32[]{:S(2)}) collective-permute-start(bf16[160,1536]{1,0:T(8,128)(2,1)S(1)} %add_convert_fusion), channel_id=1, source_target_pairs={{0,4},{4,0},{1,5},{5,1},{2,6},{6,2},{3,7},{7,3},{8,12},{12,8},{9,1... | collective-permute-start | bytes 1474568 | tf_op jit(solution)/shard_map/ppermute | solution.py:75
  182.9 6.5 %collective-permute-start.30 = (bf16[128,640]{1,0:T(8,128)(2,1)S(1)}, bf16[128,640]{1,0:T(8,128)(2,1)S(1)}, u32[]{:S(2)}, u32[]{:S(2)}) collective-permute-start(bf16[128,640]{1,0:T(8,128)(2,1)S(1)} %add_convert_fusion.5), channel_id=1, source_target_pairs={{0,1},{1,0},{2,3},{3,2},{4,5},{5,4},{6,7},{7,6},{8,9},{9,8},{10,11... | collective-permute-start | bytes 491528 | tf_op jit(solution)/shard_map/ppermute | solution.py:78
  184.3 15.3 %collective-permute-start.42 = (bf16[176,512]{1,0:T(8,128)(2,1)S(1)}, bf16[176,512]{1,0:T(8,128)(2,1)S(1)}, u32[]{:S(2)}, u32[]{:S(2)}) collective-permute-start(bf16[176,512]{1,0:T(8,128)(2,1)S(1)} %add_convert_fusion.2), channel_id=1, source_target_pairs={{0,2},{1,3},{2,0},{3,1},{4,6},{5,7},{6,4},{7,5},{8,10},{9,11},{10,... | collective-permute-start | bytes 540680 | tf_op jit(solution)/shard_map/ppermute | solution.py:81
  189.8 12.5 %collective-permute-start.31 = (bf16[128,640]{1,0:T(8,128)(2,1)S(1)}, bf16[128,640]{1,0:T(8,128)(2,1)S(1)}, u32[]{:S(2)}, u32[]{:S(2)}) collective-permute-start(bf16[128,640]{1,0:T(8,128)(2,1)S(1)} %fusion.50), channel_id=1, source_target_pairs={{0,2},{1,3},{2,0},{3,1},{4,6},{5,7},{6,4},{7,5},{8,10},{9,11},{10,... | collective-permute-start | bytes 491528 | tf_op jit(solution)/shard_map/ppermute | solution.py:81
  (82 other events, 526.6 us)

commit v2 on v1

v2 whole, which is shorter than its diff:
```python
import math

import jax
import jax.numpy as jnp
from jax import lax
from jax.experimental import pallas as pl
from jax.experimental.pallas import tpu as pltpu
from jax.sharding import PartitionSpec as P

HD = 256

EPSILON = 1e-06
ROPE_BASE = 1000000.0
GELU_COEF = math.sqrt(2.0 / math.pi)
NEG_LARGE = -1e30
BF = jnp.bfloat16
F32 = jnp.float32
EXTRA = 16
SMALL_VMEM = 16 * 2**20
LARGE_VMEM = 48 * 2**20


def rms_stats(values):
    inverse = lax.rsqrt(jnp.mean(values * values, axis=-1, keepdims=True) + EPSILON)
    return values * inverse, inverse


def rms_back(grad_out, gain_vec, normed, inverse):
    inner = grad_out * gain_vec
    return inverse * (inner - normed * jnp.mean(inner * normed, axis=-1, keepdims=True))


def rotate(values, cosine, sine):
    half = values.shape[-1] // 2
    first, second = values[:, :half], values[:, half:]
    return jnp.concatenate(
        [first * cosine - second * sine, second * cosine + first * sine], axis=-1
    )


def gelu_parts(pre_act):
    cubic = pre_act + 0.044715 * pre_act * pre_act * pre_act
    tangent = jnp.tanh(GELU_COEF * cubic)
    gelu_val = 0.5 * pre_act * (1.0 + tangent)
    slope = 0.5 * (1.0 + tangent) + 0.5 * pre_act * (1.0 - tangent * tangent) * GELU_COEF * (
        1.0 + 3.0 * 0.044715 * pre_act * pre_act
    )
    return gelu_val, slope


def dot32(left, right):
    return jnp.dot(left, right, preferred_element_type=F32)


def dot_nt(left, right):
    return lax.dot_general(left, right, (((1,), (1,)), ((), ())), preferred_element_type=F32)


def dot_tn(left, right):
    return lax.dot_general(left, right, (((0,), (0,)), ((), ())), preferred_element_type=F32)


def shape(dims, dtype):
    return jax.ShapeDtypeStruct(dims, dtype)


def call(
    body, name, outs, args, scalars=(), raw=(), hold=(), scratch=(), flops=0, limit=SMALL_VMEM
):
    vmem = pl.BlockSpec(memory_space=pltpu.VMEM)
    smem = pl.BlockSpec(memory_space=pltpu.SMEM)
    size = sum(x.size * x.dtype.itemsize for x in list(args) + list(outs))
    n_used = len(scalars) + len(raw) + len(args)
    n_hold = len(hold)

    def wrapped(*refs):
        body(*refs[:n_used], *refs[n_used + n_hold :])

    return pl.pallas_call(
        wrapped,
        name=name,
        out_shape=tuple(outs),
        in_specs=[smem] * len(scalars)
        + [pl.BlockSpec(memory_space=pltpu.HBM)] * len(raw)
        + [vmem] * len(args)
        + [pl.BlockSpec(memory_space=pl.ANY)] * n_hold,
        out_specs=tuple(vmem for _ in outs),
        scratch_shapes=list(scratch),
        compiler_params=pltpu.CompilerParams(vmem_limit_bytes=limit),
        cost_estimate=pl.CostEstimate(flops=flops, bytes_accessed=size, transcendentals=0),
    )(*scalars, *[pltpu.with_memory_space_constraint(x, pltpu.HBM) for x in raw], *args, *hold)


def tie(value, *others):
    return lax.optimization_barrier((value,) + others)[0]


def make_program(n_fsdp, n_context, n_tensor):
    def core_swap(value):
        return lax.ppermute(value, "context", [(i, i ^ 1) for i in range(n_context)])

    def z_near(value):
        return lax.ppermute(value, "tensor", [(i, i ^ 1) for i in range(n_tensor)])

    def z_far(value):
        return lax.ppermute(value, "tensor", [(i, i ^ 2) for i in range(n_tensor)])

    def cross(value):
        pairs = []
        for ctx in range(n_context):
            for pos in range(n_tensor):
                stay = (pos // 2) == (ctx % 2)
                to = ctx * n_tensor + pos if stay else (ctx ^ 1) * n_tensor + (pos ^ 2)
                pairs.append((ctx * n_tensor + pos, to))
        return lax.ppermute(value, ("context", "tensor"), pairs)

    def fsdp_hop(value, step):
        return lax.ppermute(value, "fsdp", [(i, i ^ step) for i in range(n_fsdp)])

    def gather_blocks(value, first):
        second = 3 - first
        near = fsdp_hop(value, first)
        far = fsdp_hop(value, second)
        both = fsdp_hop(near, second)
        return [value, near, far, both] if first == 1 else [value, far, near, both]

    def across_pairs(value):
        step = 2
        while step < n_context:
            value = value.astype(F32) + lax.ppermute(
                value.astype(BF), "context", [(i, i ^ step) for i in range(n_context)]
            ).astype(F32)
            step *= 2
        return value

    def on_device(
        tokens, lengths, weight_query, weight_key, weight_value, weight_out, weight_gate,
        weight_up, weight_down, gain_attn_in, gain_attn_out, gain_ffn_in, gain_ffn_out,
        gain_query, gain_key, cotangent,
    ):
        rows, width = tokens.shape
        half = rows // 2
        stream = rows * n_context
        block = weight_query.shape[0]
        gblock = gain_query.shape[0]
        hidden = weight_gate.shape[1]
        kvw = 2 * HD
        att_scale = HD ** (-0.5)
        n_doc = lengths.shape[1]
        two = n_context == 2
        limit = SMALL_VMEM if two else LARGE_VMEM
        blk_ext = block + EXTRA

        def own_f():
            return lax.axis_index("fsdp")

        def group_start():
            return pl.multiple_of((lax.axis_index("tensor") // 2) * half, half)

        def other_start():
            return pl.multiple_of((1 - lax.axis_index("tensor") // 2) * half, half)

        def bases():
            ctx = lax.axis_index("context")
            if two:
                return ctx * rows, (ctx ^ 1) * rows
            return 0, rows

        def places():
            ctx = lax.axis_index("context")
            if two:
                return group_start(), pl.multiple_of(rows + group_start(), half)
            return (
                pl.multiple_of(ctx * rows + group_start(), half),
                pl.multiple_of((ctx ^ 1) * rows + group_start(), half),
            )

        def key_index(dims, axis):
            base0, base1 = bases()
            at = lax.broadcasted_iota(jnp.int32, dims, axis)
            return at + jnp.where(at < rows, base0, base1 - rows)

        def query_index(dims):
            ctx = lax.axis_index("context")
            at = lax.broadcasted_iota(jnp.int32, dims, 0)
            first = ctx * rows + group_start()
            second = (ctx ^ 1) * rows + group_start()
            return at + jnp.where(at < half, first, second - half)

        def doc_of(index, lens):
            segment = jnp.zeros(index.shape, jnp.int32)
            start = jnp.zeros(index.shape, jnp.int32)
            end = jnp.int32(0)
            for i in range(n_doc):
                end = end + lens[0, i]
                passed = index >= end
                segment = segment + passed.astype(jnp.int32)
                start = jnp.where(passed, end, start)
            return segment, start

        def mask_of(lens):
            key_at = key_index((1, stream), 1)
            row_at = query_index((2 * half, 1))
            key_seg, _ = doc_of(key_at, lens)
            row_seg, _ = doc_of(row_at, lens)
            return (row_seg == key_seg) & (row_at >= key_at)

        def put_blocks(dest, blocks, columns=None):
            for step in range(n_fsdp):
                at = pl.multiple_of((own_f() ^ step) * block, EXTRA)
                dest[pl.ds(at, block), :] = blocks[step][:block, :]

        def take_block(source, step, size):
            at = pl.multiple_of((own_f() ^ step) * size, EXTRA)
            return source[pl.ds(at, size), :]

        ffn_cols = 3 * hidden // 2
        split = ffn_cols - hidden

        def pack(lens, k_in, v_in, q_in, o_in, g_in, u_in, d_in, *refs):
            gains = refs[:6]
            kv_out, qo_out, f1_out, f2_out, cos_out, sin_out = refs[6:12]
            held, sems = refs[12:18], refs[18]
            moves = [
                (k_in, kv_out.at[:block, :HD]),
                (v_in, kv_out.at[:block, HD:]),
                (q_in, qo_out.at[:, :HD]),
                (o_in, qo_out.at[:, HD:]),
                (g_in, f1_out.at[:, :hidden]),
                (u_in.at[:, :split], f1_out.at[:, hidden:]),
                (u_in.at[:, split:], f2_out.at[:, : hidden - split]),
                (d_in, f2_out.at[:, hidden - split :]),
            ] + list(zip(gains, held))
            copies = [
                pltpu.make_async_copy(src, dst, sems.at[i]) for i, (src, dst) in enumerate(moves)
            ]
            for copy in copies:
                copy.start()
            at = key_index((stream, 1), 0)
            _, start = doc_of(at, lens)
            lane = lax.broadcasted_iota(jnp.int32, (1, HD // 2), 1).astype(F32)
            freqs = jnp.exp(lane * (-2.0 * math.log(ROPE_BASE) / HD))
            angles = (at - start).astype(F32) * freqs
            cos_out[...] = jnp.cos(angles)
            sin_out[...] = jnp.sin(angles)
            for copy in copies:
                copy.wait()
            row = lax.broadcasted_iota(jnp.int32, (EXTRA, block), 0)
            tile = jnp.zeros((EXTRA, block), F32)
            for i in range(4):
                tile = jnp.where(row == i, held[i][...].astype(F32)[None, :], tile)
            kv_out[block:, :] = jnp.zeros((EXTRA, kvw), BF)
            kv_out[block:, :block] = tile.astype(BF)
            row = lax.broadcasted_iota(jnp.int32, (EXTRA, gblock), 0)
            tile = jnp.zeros((EXTRA, gblock), F32)
            for i in range(2):
                tile = jnp.where(row == i, held[4 + i][...].astype(F32)[None, :], tile)
            kv_out[block:, HD : HD + gblock] = tile.astype(BF)

        pack_kv, pack_qo, pack_f1, pack_f2, cos_t, sin_t = call(
            pack, "pack",
            [
                shape((blk_ext, kvw), BF), shape((block, kvw), BF), shape((block, ffn_cols), BF),
                shape((block, ffn_cols), BF), shape((stream, HD // 2), F32),
                shape((stream, HD // 2), F32),
            ],
            [], scalars=[lengths],
            raw=[
                weight_key, weight_value, weight_query, weight_out.T, weight_gate, weight_up,
                weight_down.T, gain_attn_in, gain_attn_out, gain_ffn_in, gain_ffn_out,
                gain_query, gain_key,
            ],
            scratch=[pltpu.VMEM((block,), BF)] * 4 + [pltpu.VMEM((gblock,), BF)] * 2
            + [pltpu.SemaphoreType.DMA((14,))],
        )
        tok_parts = [tokens, core_swap(tokens)] if two else [
            lax.all_gather(tokens, "context", axis=0, tiled=True)
        ]
        cross_qo = cross(pack_qo)
        cross_f1, cross_f2 = cross(pack_f1), cross(pack_f2)
        kv_blocks = gather_blocks(pack_kv, 1)
        qo_blocks = gather_blocks(cross_qo, 2)
        f1_blocks = gather_blocks(cross_f1, 1)
        f2_blocks = gather_blocks(cross_f2, 2)

        n_tok = len(tok_parts)

        def front(lens, *refs):
            toks = refs[:n_tok]
            kvb = refs[n_tok : n_tok + 4]
            qob = refs[n_tok + 4 : n_tok + 8]
            cos_ref, sin_ref = refs[n_tok + 8 : n_tok + 10]
            (act, q_rot, k_rot, val, q_pre, k_pre, attn, logt, keep, send, gw, gs, wkv, wqo) = (
                refs[n_tok + 10 :]
            )
            put_blocks(wkv, kvb)
            put_blocks(wqo, qob)
            f = own_f()
            tiles = [b[block:, :].astype(F32) for b in kvb]
            chunks = []
            for p in range(n_fsdp):
                tile = tiles[3]
                for step in range(3):
                    tile = jnp.where(f == (p ^ step), tiles[step], tile)
                chunks.append(tile)
            wide = jnp.concatenate([t[:8, :block] for t in chunks], axis=1)
            slim = jnp.concatenate([t[:8, HD : HD + gblock] for t in chunks], axis=1)
            gw[...] = wide
            gs[...] = slim
            scale_ai, scale_q, scale_k = wide[0:1], slim[0:1], slim[1:2]
            at = 0
            for tok in toks:
                hat, _ = rms_stats(tok[...].astype(F32))
                act[at : at + tok.shape[0], :] = (hat * scale_ai).astype(BF)
                at += tok.shape[0]
            kv = dot32(act[...], wkv[...])
            k_pre[...] = kv[:, :HD]
            val[...] = kv[:, HD:].astype(BF)
            k_hat, _ = rms_stats(kv[:, :HD])
            k_rot[...] = rotate(k_hat * scale_k, cos_ref[...], sin_ref[...]).astype(BF)
            for i, place in enumerate(places()):
                mine = slice(i * half, (i + 1) * half)
                pre = dot32(act[pl.ds(place, half), :], wqo[:, :HD])
                q_pre[mine, :] = pre
                hat, _ = rms_stats(pre)
                turned = rotate(
                    hat * scale_q, cos_ref[pl.ds(place, half), :], sin_ref[pl.ds(place, half), :]
                )
                q_rot[mine, :] = (turned * att_scale).astype(BF)
            allowed = mask_of(lens)
            scores = jnp.where(allowed, dot_nt(q_rot[...], k_rot[...]), NEG_LARGE)
            row_max = jnp.max(scores, axis=1, keepdims=True)
            weights = jnp.where(allowed, jnp.exp(scores - row_max), 0.0)
            total = jnp.sum(weights, axis=1, keepdims=True)
            logt[...] = row_max + jnp.log(total)
            heads = (dot32(weights.astype(BF), val[...]) / total).astype(BF)
            attn[...] = heads
            partial = dot_nt(heads, wqo[:, HD:])
            keep[...] = partial[:half]
            send[...] = partial[half:].astype(BF)

        n_q = 2 * half
        wide_f, wide_b = shape((half, width), F32), shape((half, width), BF)
        row_f = shape((1, width), F32)
        cos_t = tie(cos_t, cross_f1, cross_f2)
        (act, q_rot, k_rot, val, q_pre, k_pre, attn, logt, keep, send, gw, gs) = call(
            front, "front",
            [
                shape((stream, width), BF), shape((n_q, HD), BF), shape((stream, HD), BF),
                shape((stream, HD), BF), shape((n_q, HD), F32), shape((stream, HD), F32),
                shape((n_q, HD), BF), shape((n_q, 1), F32), wide_f, wide_b,
                shape((8, width), F32), shape((8, HD), F32),
            ],
            tok_parts + kv_blocks + qo_blocks + [cos_t, sin_t],
            scalars=[lengths],
            scratch=[pltpu.VMEM((width, kvw), BF), pltpu.VMEM((width, kvw), BF)],
            flops=2 * stream * width * kvw + 4 * n_q * stream * HD,
            limit=limit,
        )
        saved = [q_rot, k_rot, val, q_pre, k_pre, attn, logt, gs, cos_t, sin_t, act]
        saved = (saved + [gw] + kv_blocks + qo_blocks) if two else []

        def pair_sum(kept, sent):
            return (kept + core_swap(sent).astype(F32)).astype(BF)

        def mid_one(pair, near, tok, gains, total_out, res_out, act_out):
            total = pair[...].astype(F32) + near[...].astype(F32)
            total_out[...] = total
            hat, _ = rms_stats(total)
            res = tok[pl.ds(group_start(), half), :].astype(F32) + hat * gains[1:2, :]
            res_out[...] = res
            hat, _ = rms_stats(res)
            act_out[...] = (hat * gains[2:3, :]).astype(BF)

        pair = pair_sum(keep, send)
        attn_total, hidden_res, act_own = call(
            mid_one, "mid_one", [wide_f, wide_f, wide_b], [pair, z_near(pair), tokens, gw],
            hold=saved,
        )
        act_oth = core_swap(act_own)

        def put_ffn(wgu, wd, f1, f2):
            for step in range(n_fsdp):
                at = pl.ds(pl.multiple_of((own_f() ^ step) * block, EXTRA), block)
                wgu[at, :ffn_cols] = f1[step][...]
                wgu[at, ffn_cols:] = f2[step][:, : hidden - split]
                wd[at, :] = f2[step][:, hidden - split :]

        def ffn(a0, a1, *refs):
            gu_out, inner_out, keep, send, wgu, wd = refs[8:]
            put_ffn(wgu, wd, refs[:4], refs[4:8])
            for i, a in enumerate((a0, a1)):
                mine = slice(i * half, (i + 1) * half)
                gu = dot32(a[...], wgu[...])
                gu_out[mine, :] = gu
                gelu_val, _ = gelu_parts(gu[:, :hidden])
                inner = (gelu_val * gu[:, hidden:]).astype(BF)
                inner_out[mine, :] = inner
                partial = dot_nt(inner, wd[...])
                if i == 0:
                    keep[...] = partial
                else:
                    send[...] = partial.astype(BF)

        ffn_scratch = [pltpu.VMEM((width, 2 * hidden), BF), pltpu.VMEM((width, hidden), BF)]
        ffn_flops = 6 * n_q * width * hidden
        gate_up, inner_act, keep, send = call(
            ffn, "ffn",
            [shape((n_q, 2 * hidden), F32), shape((n_q, hidden), BF), wide_f, wide_b],
            [act_own, act_oth] + f1_blocks + f2_blocks, scratch=ffn_scratch, flops=ffn_flops,
            hold=saved + ([hidden_res, attn_total] if two else []),
        )

        def mid_two(pair, near, res, cot, gains, out_ref, grad_out, ds_out):
            hat, inv = rms_stats(pair[...].astype(F32) + near[...].astype(F32))
            out_ref[...] = (res[...] + hat * gains[3:4, :]).astype(BF)
            grad = cot[pl.ds(group_start(), half), :].astype(F32)
            ds_out[...] = jnp.sum(grad * hat, axis=0, keepdims=True)
            grad_out[...] = rms_back(grad, gains[3:4, :], hat, inv).astype(BF)

        pair = pair_sum(keep, send)
        layer_own, gf_own, ds_fo = call(
            mid_two, "mid_two", [wide_b, wide_b, row_f],
            [pair, z_near(pair), hidden_res, cotangent, gw],
            hold=saved + ([attn_total, act_own, act_oth] + f1_blocks + f2_blocks if two else []),
        )
        layer_oth = z_far(layer_own)
        gf_oth = core_swap(gf_own)

        def ffn_back(f0, f1, gu_ref, *refs):
            ggu_out, keep, send, wgu, wd = refs[8:]
            put_ffn(wgu, wd, refs[:4], refs[4:8])
            for i, g in enumerate((f0, f1)):
                mine = slice(i * half, (i + 1) * half)
                grad_inner = dot32(g[...], wd[...])
                gelu_val, slope = gelu_parts(gu_ref[mine, :hidden])
                up = gu_ref[mine, hidden:]
                ggu_out[mine, :hidden] = (grad_inner * up * slope).astype(BF)
                ggu_out[mine, hidden:] = (grad_inner * gelu_val).astype(BF)
                partial = dot_nt(ggu_out[mine, :], wgu[...])
                if i == 0:
                    keep[...] = partial
                else:
                    send[...] = partial.astype(BF)

        grad_gu, keep, send = call(
            ffn_back, "ffn_back", [shape((n_q, 2 * hidden), BF), wide_f, wide_b],
            [gf_own, gf_oth, gate_up] + f1_blocks + f2_blocks,
            scratch=ffn_scratch, flops=ffn_flops,
            hold=saved + ([hidden_res, attn_total, act_own, act_oth] if two else []),
        )
        pair = pair_sum(keep, send)

        def put_grads(full, first, mine_out, give_out, size, lanes=slice(None)):
            second = 3 - first
            for i, step in enumerate((0, second)):
                mine_out[i * size : (i + 1) * size, lanes] = take_block(full, step, size)
            for i, step in enumerate((first, 3)):
                give_out[i * size : (i + 1) * size, lanes] = take_block(full, step, size)

        def ffn_weights(a0, a1, f0, f1, ggu, inner, m1, s1, m2, s2, full1, full2):
            low, high = slice(0, half), slice(half, 2 * half)
            cut = ffn_cols
            full1[...] = (
                dot_tn(a0[...], ggu[low, :cut]) + dot_tn(a1[...], ggu[high, :cut])
            ).astype(BF)
            full2[:, : hidden - split] = (
                dot_tn(a0[...], ggu[low, cut:]) + dot_tn(a1[...], ggu[high, cut:])
            ).astype(BF)
            full2[:, hidden - split :] = (
                dot_tn(f0[...], inner[low, :]) + dot_tn(f1[...], inner[high, :])
            ).astype(BF)
            put_grads(full1, 1, m1, s1, block)
            put_grads(full2, 2, m2, s2, block)

        ffn_m1, ffn_s1, ffn_m2, ffn_s2 = call(
            ffn_weights, "ffn_weights", [shape((2 * block, ffn_cols), BF)] * 4,
            [act_own, act_oth, gf_own, gf_oth, tie(grad_gu, pair), inner_act],
            scratch=[pltpu.VMEM((width, ffn_cols), BF)] * 2, flops=ffn_flops,
        )

        def mid_three(pair, near, res, tot, cot, gains, hid_out, grad_out, fi_out, ao_out):
            total = pair[...].astype(F32) + near[...].astype(F32)
            hat, inv = rms_stats(res[...])
            fi_out[...] = jnp.sum(total * hat, axis=0, keepdims=True)
            grad = cot[pl.ds(group_start(), half), :].astype(F32)
            grad = grad + rms_back(total, gains[2:3, :], hat, inv)
            hid_out[...] = grad
            hat, inv = rms_stats(tot[...])
            ao_out[...] = jnp.sum(grad * hat, axis=0, keepdims=True)
            grad_out[...] = rms_back(grad, gains[1:2, :], hat, inv).astype(BF)

        grad_hidden, ga_own, ds_fi, ds_ao = call(
            mid_three, "mid_three", [wide_f, wide_b, row_f, row_f],
            [pair, z_near(pair), hidden_res, attn_total, cotangent, gw],
            hold=saved,
        )
        ga_oth = tie(core_swap(ga_own), layer_oth)

        def attn_back(lens, *refs):
            (a0, a1, attn_r, logt_r, q_r, k_r, v_r, qp, kp, cos_ref, sin_ref, gains) = refs[:12]
            kvb, qob = refs[12:16], refs[16:20]
            gq_out, gkv_out, part_keep, part_send, dsq, dsk, wkv, wqo, part = refs[20:]
            put_blocks(wkv, kvb)
            put_blocks(wqo, qob)
            scale_q, scale_k = gains[0:1, :], gains[1:2, :]
            grad_attn = jnp.concatenate([a0[...], a1[...]], axis=0)
            grad_heads = dot32(grad_attn, wqo[:, HD:]).astype(BF)
            delta = jnp.sum(
                grad_heads.astype(F32) * attn_r[...].astype(F32), axis=1, keepdims=True
            )
            allowed = mask_of(lens)
            scores = dot_nt(q_r[...], k_r[...])
            probs = jnp.where(allowed, jnp.exp(scores - logt_r[...]), 0.0)
            grad_s = (probs * (dot_nt(grad_heads, v_r[...]) - delta)).astype(BF)
            grad_kn = rotate(dot_tn(grad_s, q_r[...]), cos_ref[...], -sin_ref[...])
            hat, inv = rms_stats(kp[...])
            dsk[...] = jnp.sum(grad_kn * hat, axis=0, keepdims=True)
            gkv_out[:, :HD] = rms_back(grad_kn, scale_k, hat, inv).astype(BF)
            gkv_out[:, HD:] = dot_tn(probs.astype(BF), grad_heads).astype(BF)
            part[...] = dot_nt(gkv_out[...], wkv[...])
            grad_qr = dot32(grad_s, k_r[...]) * att_scale
            total_q = jnp.zeros((1, HD), F32)
            for i, place in enumerate(places()):
                mine = slice(i * half, (i + 1) * half)
                grad_qn = rotate(
                    grad_qr[mine], cos_ref[pl.ds(place, half), :], -sin_ref[pl.ds(place, half), :]
                )
                hat, inv = rms_stats(qp[mine, :])
                total_q = total_q + jnp.sum(grad_qn * hat, axis=0, keepdims=True)
                gq_out[mine, :] = rms_back(grad_qn, scale_q, hat, inv).astype(BF)
                part[pl.ds(place, half), :] += dot_nt(gq_out[mine, :], wqo[:, :HD])
            dsq[...] = total_q
            part_keep[...] = part[:rows, :]
            part_send[...] = part[rows:, :].astype(BF)

        n_rest = stream - rows
        grad_q, grad_kv, part_keep, part_send, ds_q, ds_k = call(
            attn_back, "attn_back",
            [
                shape((n_q, HD), BF), shape((stream, kvw), BF), shape((rows, width), F32),
                shape((n_rest, width), BF), shape((1, HD), F32), shape((1, HD), F32),
            ],
            [ga_own, ga_oth, attn, logt, q_rot, k_rot, val, q_pre, k_pre, cos_t, sin_t, gs]
            + kv_blocks + qo_blocks,
            scalars=[lengths],
            scratch=[
                pltpu.VMEM((width, kvw), BF), pltpu.VMEM((width, kvw), BF),
                pltpu.VMEM((stream, width), F32),
            ],
            flops=2 * stream * width * kvw + 10 * n_q * stream * HD, limit=limit,
        )

        def attn_weights(*refs):
            toks = refs[:n_tok]
            (act_r, gq, gkv, a0, a1, attn_r, pk, ps, dfo, dfi, dao, dq, dk) = (
                refs[n_tok : n_tok + 13]
            )
            kv_m, kv_s, qo_m, qo_s, full, ext = refs[n_tok + 13 :]
            low, high = slice(0, half), slice(half, 2 * half)
            dai = jnp.zeros((1, width), F32)
            at = 0
            for tok in toks:
                hat, _ = rms_stats(tok[...].astype(F32))
                size = tok.shape[0]
                if size > rows:
                    dai = dai + jnp.sum(hat[:rows] * pk[...], axis=0, keepdims=True)
                    dai = dai + jnp.sum(hat[rows:] * ps[...].astype(F32), axis=0, keepdims=True)
                else:
                    piece = (pk if at == 0 else ps)[...].astype(F32)
                    dai = dai + jnp.sum(hat * piece, axis=0, keepdims=True)
                at += size
            wide = [dai, dao[...] * 0.5, dfi[...] * 0.5, dfo[...] * 0.5]
            slim = [dq[...], dk[...]]
            ext[...] = jnp.zeros(ext.shape, BF)
            row_w = lax.broadcasted_iota(jnp.int32, (EXTRA, block), 0)
            row_s = lax.broadcasted_iota(jnp.int32, (EXTRA, gblock), 0)
            for p in range(n_fsdp):
                tile = jnp.zeros((EXTRA, block), F32)
                for i, vec in enumerate(wide):
                    tile = jnp.where(row_w == i, vec[:, p * block : (p + 1) * block], tile)
                ext[p * EXTRA : (p + 1) * EXTRA, :block] = tile.astype(BF)
                tile = jnp.zeros((EXTRA, gblock), F32)
                for i, vec in enumerate(slim):
                    tile = jnp.where(row_s == i, vec[:, p * gblock : (p + 1) * gblock], tile)
                ext[p * EXTRA : (p + 1) * EXTRA, HD : HD + gblock] = tile.astype(BF)
            full[...] = dot_tn(act_r[...], gkv[...]).astype(BF)
            for out, steps in ((kv_m, (0, 2)), (kv_s, (1, 3))):
                for i, step in enumerate(steps):
                    at = i * blk_ext
                    out[at : at + block, :] = take_block(full, step, block)
                    out[at + block : at + blk_ext, :] = take_block(ext, step, EXTRA)
            place0, place1 = places()
            full[:, :HD] = (
                dot_tn(act_r[pl.ds(place0, half), :], gq[low, :])
                + dot_tn(act_r[pl.ds(place1, half), :], gq[high, :])
            ).astype(BF)
            full[:, HD:] = (
                dot_tn(a0[...], attn_r[low, :]) + dot_tn(a1[...], attn_r[high, :])
            ).astype(BF)
            put_grads(full, 2, qo_m, qo_s, block)

        kv_m, kv_s, qo_m, qo_s = call(
            attn_weights, "attn_weights",
            [shape((2 * blk_ext, kvw), BF)] * 2 + [shape((2 * block, kvw), BF)] * 2,
            tok_parts
            + [act, grad_q, grad_kv, ga_own, ga_oth, attn, part_keep, part_send]
            + [ds_fo, ds_fi, ds_ao, ds_q, ds_k],
            scratch=[pltpu.VMEM((width, kvw), BF), pltpu.VMEM((n_fsdp * EXTRA, kvw), BF)],
            flops=2 * stream * width * kvw + 4 * n_q * width * HD, limit=limit,
        )

        if two:
            mine = part_keep + core_swap(part_send).astype(F32)
        else:
            mine = lax.psum_scatter(
                jnp.concatenate([part_keep, part_send.astype(F32)], axis=0),
                "context", scatter_dimension=0, tiled=True,
            )
        mine = mine.astype(BF)
        start = (lax.axis_index("tensor") // 2) * half
        kept = lax.dynamic_slice_in_dim(mine, start, half, 0)
        give = lax.dynamic_slice_in_dim(mine, half - start, half, 0)
        kept = (kept.astype(F32) + z_far(give).astype(F32)).astype(BF)

        def last_norm(kept, near, tok, hid, gains, out):
            grad = kept[...].astype(F32) + near[...].astype(F32)
            hat, inv = rms_stats(tok[pl.ds(group_start(), half), :].astype(F32))
            out[...] = (hid[...] + rms_back(grad, gains[0:1, :], hat, inv)).astype(BF)

        (input_own,) = call(
            last_norm, "last_norm", [wide_b], [kept, z_near(kept), tokens, grad_hidden, gw]
        )

        def join(own, oth, out):
            out[pl.ds(group_start(), half), :] = own[...].astype(F32)
            out[pl.ds(other_start(), half), :] = oth[...].astype(F32)

        def both_groups(own, other, name):
            return call(join, name, [shape((rows, width), F32)], [own, other])[0]

        layer_output = both_groups(layer_own, layer_oth, "join_output")
        grad_input = both_groups(input_own, z_far(input_own), "join_grad")

        def scatter(kept, sent, first):
            size = kept.shape[0] // 2
            both = (kept.astype(F32) + fsdp_hop(sent, first).astype(F32)).astype(BF)
            last = fsdp_hop(both[size:], 3 - first)
            return across_pairs(both[:size].astype(F32) + last.astype(F32)).astype(BF)

        def finish_ffn(x1, y1, x2, y2, g_out, u_out, d_out):
            both = x1[...].astype(F32) + y1[...].astype(F32)
            g_out[...] = both[:, :hidden]
            u_out[:, :split] = both[:, hidden:]
            both = x2[...].astype(F32) + y2[...].astype(F32)
            u_out[:, split:] = both[:, : hidden - split]
            d_out[...] = both[:, hidden - split :]

        ffn_c1 = cross(scatter(ffn_m1, ffn_s1, 1))
        ffn_c2 = cross(scatter(ffn_m2, ffn_s2, 2))
        grad_gate, grad_up, grad_down = call(
            finish_ffn, "finish_ffn",
            [shape((block, hidden), F32)] * 3,
            [ffn_c1, core_swap(ffn_c1), ffn_c2, core_swap(ffn_c2)],
        )

        kv_sum = scatter(kv_m, kv_s, 1)
        qo_mine = cross(scatter(qo_m, qo_s, 2))
        for move in (core_swap, z_near):
            kv_sum = (kv_sum.astype(F32) + move(kv_sum).astype(F32)).astype(BF)

        def finish_qo(x_ref, y_ref, q_out, o_out):
            both = x_ref[...].astype(F32) + y_ref[...].astype(F32)
            q_out[...] = both[:, :HD]
            o_out[...] = both[:, HD:]

        grad_wq, grad_wo = call(
            finish_qo, "finish_qo", [shape((block, HD), F32)] * 2,
            [qo_mine, core_swap(qo_mine)],
        )

        def finish_kv(x_ref, y_ref, k_out, v_out, *gain_outs):
            both = x_ref[...].astype(F32) + y_ref[...].astype(F32)
            k_out[...] = both[:block, :HD]
            v_out[...] = both[:block, HD:]
            for i in range(4):
                gain_outs[i][...] = both[block + i : block + i + 1, :block]
            for i in range(2):
                gain_outs[4 + i][...] = both[block + i : block + i + 1, HD : HD + gblock]

        grad_wk, grad_wv, *gain_grads = call(
            finish_kv, "finish_kv",
            [shape((block, HD), F32)] * 2 + [shape((1, block), F32)] * 4 + [shape((1, gblock), F32)] * 2,
            [kv_sum, z_far(kv_sum)],
        )
        return (
            layer_output, grad_input, grad_wq, grad_wk, grad_wv, grad_wo.T,
            grad_gate, grad_up, grad_down.T, *[g.reshape(-1) for g in gain_grads],
        )

    return on_device


def solution(mesh):
    in_specs = (
        P(("fsdp", "context"), None),
        P("fsdp", None),
        P("fsdp", "tensor"),
        P("fsdp", None),
        P("fsdp", None),
        P("tensor", "fsdp"),
        P("fsdp", "tensor"),
        P("fsdp", "tensor"),
        P("tensor", "fsdp"),
        P("fsdp"),
        P("fsdp"),
        P("fsdp"),
        P("fsdp"),
        P("fsdp"),
        P("fsdp"),
        P(("fsdp", "context"), None),
    )
    out_specs = (
        P(("fsdp", "context"), None),
        P(("fsdp", "context"), None),
        P("fsdp", "tensor"),
        P("fsdp", None),
        P("fsdp", None),
        P("tensor", "fsdp"),
        P("fsdp", "tensor"),
        P("fsdp", "tensor"),
        P("tensor", "fsdp"),
        P("fsdp"),
        P("fsdp"),
        P("fsdp"),
        P("fsdp"),
        P("fsdp"),
        P("fsdp"),
    )
    on_device = make_program(mesh.shape["fsdp"], mesh.shape["context"], mesh.shape["tensor"])
    return jax.shard_map(
        on_device, mesh=mesh, in_specs=in_specs, out_specs=out_specs, check_vma=False
    )
```

time: 205 us -> 154 us (0.75)
  other arithmetic: 33.8 us -> 3 us
  Pallas kernels: 0 us -> 21.9 us
  waiting for transfers between devices: 69.3 us -> 54 us
  local copies, waits for them, and re-layouts: 23.1 us -> 8.48 us
  matrix products: 10.9 us -> 0 us
    pallas_call x0 -> x16, Pallas kernels: none -> 21.9 us  [call(): pl.pallas_call(wrapped, name=name, out_shape=tuple(outs), in_specs=[smem]...]
    ppermute x11 -> x12, starting transfers between devices: 4.72 us -> 19.2 us  [core_swap(): lax.ppermute(value, 'context', [(i, i ^ 1) for i in range(n_context)])]
    dot_general x21 -> x0, matrix products: 10.9 us -> none  [the longest x7 4.4 us: dot32(): return jnp.dot(left, right, preferred_element_type=F32)]
    ppermute x4 -> x6, starting transfers between devices: 13.8 us -> 4.05 us  [cross(): return lax.ppermute(value, ('context', 'tensor'), pairs)]
    ppermute x24 -> x20, starting transfers between devices: 30.5 us -> 21.8 us  [fsdp_hop(): return lax.ppermute(value, 'fsdp', [(i, i ^ step) for i in range(n_fsdp)])]
    ppermute x4, starting transfers between devices: 6.35 us -> 14.7 us  [z_far(): return lax.ppermute(value, 'tensor', [(i, i ^ 2) for i in range(n_tensor)])]
    convert_element_type x25 -> x14, other arithmetic: 9.93 us -> 2.92 us  [the longest x4 2.47 us: scatter(): both = (kept.astype(F32) + fsdp_hop(sent, first).astype(F32)).astype(BF)]
    reduce_sum x14 -> x0, other arithmetic: 6.83 us -> none  [the longest x5 2.68 us: rms_stats(): jnp.mean(values * values, axis=-1, keepdims=True) + EPSILON]
  transfers between devices with their start and end apart: 48 -> 47, of which waited for: 23 -> 17; matrix products, arithmetic and copies ran while one was open for 22% -> 2% of each run, Pallas kernels for 0% -> 7%
where the time goes in v2:
time: 154 us; the launch traced here: 153 us
  starting transfers between devices  65 us (42%)
  waiting for transfers between devices  54 us (35%)
  Pallas kernels  21.9 us (14%)
  local copies, waits for them, and re-layouts  8.48 us (6%)
  other arithmetic  3 us (2%)
    ppermute x20, waiting for transfers between devices, fsdp_hop(): return lax.ppermute(value, 'fsdp', [(i, i ^ step) for i in range(n_fsdp)])  30.4 us
    pallas_call x16, Pallas kernels, call(): pl.pallas_call(wrapped, name=name, out_shape=tuple(outs), in_specs=[smem]...  21.9 us
    ppermute x20, starting transfers between devices, fsdp_hop(): return lax.ppermute(value, 'fsdp', [(i, i ^ step) for i in range(n_fsdp)])  21.8 us
    ppermute x12, starting transfers between devices, core_swap(): lax.ppermute(value, 'context', [(i, i ^ 1) for i in range(n_context)])  19.2 us
    ppermute x4, starting transfers between devices, z_far(): return lax.ppermute(value, 'tensor', [(i, i ^ 2) for i in range(n_tensor)])  14.7 us
    ppermute x4, waiting for transfers between devices, z_far(): return lax.ppermute(value, 'tensor', [(i, i ^ 2) for i in range(n_tensor)])  9.97 us
    ppermute x5, waiting for transfers between devices, z_near(): return lax.ppermute(value, 'tensor', [(i, i ^ 1) for i in range(n_tensor)])  9.3 us
    unnamed x58, local copies, waits for them, and re-layouts  8.39 us
  transfers between devices with their start and end apart: 47, of which 17 were waited for; matrix products, arithmetic and copies ran while one was open for 2% of the time, Pallas kernels for 7%

profile of v2, /device:TPU:0, one launch (start us, length us, event | category | flops | bytes accessed | tf_op | source)
XLA Modules:
  0.0 153.5 jit_solution(2905800518972150482)
XLA Ops:
  1.3 1.9 %pack.1 = (bf16[176,512]{1,0:T(8,128)(2,1)S(1)}, bf16[160,512]{1,0:T(8,128)(2,1)S(1)}, bf16[160,768]{1,0:T(8,128)(2,1)S(1)}, bf16[160,768]{1,0:T(8,128)(2,1)S(1)...) custom-call(s32[1,4]{1,0:T(1,128)S(1)} %copy-done.24, bf16[160,256]{1,0:T(8,128)(2,1)} %refs_1_.2, ...), custom_call_target="tpu_custom_call" | custom-call | bytes 1359872 | tf_op jit(solution)/shard_map/pack/pallas_call | solution.py:79
  5.3 3.0 %collective-permute-start.1 = (bf16[176,512]{1,0:T(8,128)(2,1)S(1)}, bf16[176,512]{1,0:T(8,128)(2,1)S(1)}, u32[]{:S(2)}, u32[]{:S(2)}) collective-permute-start(bf16[176,512]{1,0:T(8,128)(2,1)S(1)} %get-tuple-element.80.refs_3_.refs_16_.refs_22_.refs_17_.refs_23_.refs_18_.refs_13_), channel_id=1, source_target_pairs={{0,8},{8,0},{16,24},{24,16},{1,9},{9,1},{17,25},{25,17},{2,10},{10... | collective-permute-start | bytes 540680 | tf_op jit(solution)/shard_map/ppermute | solution.py:118
  8.3 8.8 %collective-permute-start = (bf16[256,640]{1,0:T(8,128)(2,1)S(1)}, bf16[256,640]{1,0:T(8,128)(2,1)S(1)}, u32[]{:S(2)}, u32[]{:S(2)}) collective-permute-start(bf16[256,640]{1,0:T(8,128)(2,1)S(1)} %copy-done.7), channel_id=1, source_target_pairs={{0,4},{4,0},{1,5},{5,1},{2,6},{6,2},{3,7},{7,3},{8,12},{12,8},{9,1... | collective-permute-start | bytes 983048 | tf_op jit(solution)/shard_map/ppermute | solution.py:100
  17.1 1.5 collective-permute-start.6
  19.1 1.5 collective-permute-start.3
  21.1 2.5 %collective-permute-done.6.refs_9_.refs_22_.refs_28_.refs_23_.refs_29_.refs_24_.refs_19_ = bf16[160,512]{1,0:T(8,128)(2,1)S(1)} collective-permute-done((bf16[160,512]{1,0:T(8,128)(2,1)S(1)}, bf16[160,512]{1,0:T(8,128)(2,1)S(1)}, u32[]{:S(2)}, u32[]{:S(2)}) %collective-permute-start.6) | collective-permute-done | bytes 163872 | tf_op jit(solution)/shard_map/ppermute | solution.py:118
  23.8 3.7 %collective-permute-done.2.refs_5_.refs_18_.refs_24_.refs_19_.refs_25_.refs_20_.refs_15_ = bf16[176,512]{1,0:T(8,128)(2,1)S(1)} collective-permute-done((bf16[176,512]{1,0:T(8,128)(2,1)S(1)}, bf16[176,512]{1,0:T(8,128)(2,1)S(1)}, u32[]{:S(2)}, u32[]{:S(2)}) %collective-permute-start.2) | collective-permute-done | bytes 180256 | tf_op jit(solution)/shard_map/ppermute | solution.py:118
  27.5 3.5 %collective-permute-done.3.refs_6_.refs_19_.refs_25_.refs_20_.refs_26_.refs_21_.refs_16_ = bf16[176,512]{1,0:T(8,128)(2,1)S(1)} collective-permute-done((bf16[176,512]{1,0:T(8,128)(2,1)S(1)}, bf16[176,512]{1,0:T(8,128)(2,1)S(1)}, u32[]{:S(2)}, u32[]{:S(2)}) %collective-permute-start.3) | collective-permute-done | bytes 180256 | tf_op jit(solution)/shard_map/ppermute | solution.py:118
  31.0 2.2 %front.1 = (bf16[512,640]{1,0:T(8,128)(2,1)S(1)}, bf16[256,256]{1,0:T(8,128)(2,1)S(1)}, bf16[512,256]{1,0:T(8,128)(2,1)S(1)}, bf16[512,256]{1,0:T(8,128)(2,1)S(1...) custom-call(s32[1,4]{1,0:T(1,128)S(1)} %copy-done.24, ...), custom_call_target="tpu_custom_call" | custom-call | flops 469762048 | bytes 5305344 | tf_op jit(solution)/shard_map/front/pallas_call | solution.py:79
  33.2 1.4 collective-permute-start.10
  35.4 1.5 collective-permute-start.17
  36.9 1.0 collective-permute-start.11
  38.5 1.0 collective-permute-start.16
  39.5 3.9 %collective-permute-done.13.refs_3_.refs_29_.refs_4_ = bf16[160,768]{1,0:T(8,128)(2,1)S(1)} collective-permute-done((bf16[160,768]{1,0:T(8,128)(2,1)S(1)}, bf16[160,768]{1,0:T(8,128)(2,1)S(1)}, u32[]{:S(2)}, u32[]{:S(2)}) %collective-permute-start.13) | collective-permute-done | bytes 245792 | tf_op jit(solution)/shard_map/ppermute | solution.py:118
  43.4 1.5 collective-permute-start.15
  46.1 3.4 %collective-permute-done.14.refs_4_.refs_30_.refs_5_ = bf16[160,768]{1,0:T(8,128)(2,1)S(1)} collective-permute-done((bf16[160,768]{1,0:T(8,128)(2,1)S(1)}, bf16[160,768]{1,0:T(8,128)(2,1)S(1)}, u32[]{:S(2)}, u32[]{:S(2)}) %collective-permute-start.14) | collective-permute-done | bytes 245792 | tf_op jit(solution)/shard_map/ppermute | solution.py:118
  49.5 4.1 %collective-permute-done.15.refs_5_.refs_31_.refs_6_ = bf16[160,768]{1,0:T(8,128)(2,1)S(1)} collective-permute-done((bf16[160,768]{1,0:T(8,128)(2,1)S(1)}, bf16[160,768]{1,0:T(8,128)(2,1)S(1)}, u32[]{:S(2)}, u32[]{:S(2)}) %collective-permute-start.15) | collective-permute-done | bytes 245792 | tf_op jit(solution)/shard_map/ppermute | solution.py:118
  53.6 1.2 ffn.1
  54.9 1.4 collective-permute-done.19
  56.3 1.0 collective-permute-start.20
  57.4 5.3 %collective-permute-done.20.refs_1_ = bf16[128,640]{1,0:T(8,128)(2,1)S(1)} collective-permute-done((bf16[128,640]{1,0:T(8,128)(2,1)S(1)}, bf16[128,640]{1,0:T(8,128)(2,1)S(1)}, u32[]{:S(2)}, u32[]{:S(2)}) %collective-permute-start.20) | collective-permute-done | bytes 163872 | tf_op jit(solution)/shard_map/ppermute | solution.py:103
  63.5 1.4 collective-permute-done.22.refs_1_.refs_3_
  64.9 1.5 ffn_back.1
  66.6 1.3 collective-permute-done.23
  67.9 2.1 %ffn_weights.1 = (bf16[320,768]{1,0:T(8,128)(2,1)S(1)}, bf16[320,768]{1,0:T(8,128)(2,1)}, bf16[320,768]{1,0:T(8,128)(2,1)S(1)}, bf16[320,768]{1,0:T(8,128)(2,1)}) custom-call(bf16[128,640]{1,0:T(8,128)(2,1)S(1)} %get-tuple-element.99.refs_0_.refs_26_.refs_33_, bf16[128,640]{1,0:T(8,128)(2,1)S(1)} %collective-permute-done.12.refs_1_.refs_27_.refs_34_, ...), custom_call_target="tpu_custom_call" | custom-call | flops 503316480 | bytes 3407872 | tf_op jit(solution)/shard_map/ffn_weights/pallas_call | solution.py:79
  70.0 1.5 collective-permute-start.43
  72.5 3.6 %collective-permute-start.21 = (bf16[128,640]{1,0:T(8,128)(2,1)}, bf16[128,640]{1,0:T(8,128)(2,1)}, u32[]{:S(2)}, u32[]{:S(2)}) collective-permute-start(bf16[128,640]{1,0:T(8,128)(2,1)} %get-tuple-element.104.refs_0_), channel_id=1, source_target_pairs={{0,2},{1,3},{2,0},{3,1},{4,6},{5,7},{6,4},{7,5},{8,10},{9,11},{10,... | collective-permute-start | bytes 491528 | tf_op jit(solution)/shard_map/ppermute | solution.py:106
  76.0 4.0 %collective-permute-done.24.refs_1_ = bf16[128,640]{1,0:T(8,128)(2,1)S(1)} collective-permute-done((bf16[128,640]{1,0:T(8,128)(2,1)S(1)}, bf16[128,640]{1,0:T(8,128)(2,1)S(1)}, u32[]{:S(2)}, u32[]{:S(2)}) %collective-permute-start.24) | collective-permute-done | bytes 163872 | tf_op jit(solution)/shard_map/ppermute | solution.py:103
  80.1 1.1 mid_three.1
  83.1 1.8 %collective-permute-start.39 = (bf16[320,768]{1,0:T(8,128)(2,1)}, bf16[320,768]{1,0:T(8,128)(2,1)}, u32[]{:S(2)}, u32[]{:S(2)}) collective-permute-start(bf16[320,768]{1,0:T(8,128)(2,1)} %get-tuple-element.133), channel_id=1, source_target_pairs={{0,8},{8,0},{16,24},{24,16},{1,9},{9,1},{17,25},{25,17},{2,10},{10... | collective-permute-start | bytes 1474568 | tf_op jit(solution)/shard_map/ppermute | solution.py:118
  89.4 3.0 %attn_back.1 = (bf16[256,256]{1,0:T(8,128)(2,1)S(1)}, bf16[512,512]{1,0:T(8,128)(2,1)S(1)}, f32[256,640]{1,0:T(8,128)S(1)}, bf16[256,640]{1,0:T(8,128)(2,1)S(1)}...) custom-call(s32[1,4]{1,0:T(1,128)S(1)} %copy-done.24, bf16[128,640]{1,0:T(8,128)(2,1)} %get-tuple-element.109.refs_1_.refs_5_, ...), custom_call_target="tpu_custom_call" | custom-call | flops 671088640 | bytes 5450752 | tf_op jit(solution)/shard_map/attn_back/pallas_call | solution.py:79
  93.4 2.2 %attn_weights.1 = (bf16[352,512]{1,0:T(8,128)(2,1)S(1)}, bf16[352,512]{1,0:T(8,128)(2,1)S(1)}, bf16[320,512]{1,0:T(8,128)(2,1)S(1)}, bf16[320,512]{1,0:T(8,128)(2,1)S(1)}) custom-call(bf16[256,640]{1,0:T(8,128)(2,1)S(1)} %copy-done.8, bf16[256,640]{1,0:T(8,128)(2,1)S(1)} %copy-done.17, ...), custom_call_target="tpu_custom_call" | custom-call | flops 503316480 | bytes 4793856 | tf_op jit(solution)/shard_map/attn_weights/pallas_call | solution.py:79
  95.6 1.7 %collective-permute-start.34 = (bf16[352,512]{1,0:T(8,128)(2,1)S(1)}, bf16[352,512]{1,0:T(8,128)(2,1)S(1)}, u32[]{:S(2)}, u32[]{:S(2)}) collective-permute-start(bf16[352,512]{1,0:T(8,128)(2,1)S(1)} %get-tuple-element.125), channel_id=1, source_target_pairs={{0,8},{8,0},{16,24},{24,16},{1,9},{9,1},{17,25},{25,17},{2,10},{10... | collective-permute-start | bytes 1081352 | tf_op jit(solution)/shard_map/ppermute | solution.py:118
  97.9 1.2 add_convert_fusion
  100.1 1.1 add_convert_fusion.1
  101.2 1.6 %collective-permute-start.40 = (bf16[160,768]{1,0:T(8,128)(2,1)S(1)}, bf16[160,768]{1,0:T(8,128)(2,1)S(1)}, u32[]{:S(2)}, u32[]{:S(2)}) collective-permute-start(bf16[160,768]{1,0:T(8,128)(2,1)S(1)} %slice.37), channel_id=1, source_target_pairs={{0,16},{8,24},{16,0},{24,8},{1,17},{9,25},{17,1},{25,9},{2,18},{10... | collective-permute-start | bytes 737288 | tf_op jit(solution)/shard_map/ppermute | solution.py:118
  102.8 5.1 %collective-permute-done.30 = bf16[320,512]{1,0:T(8,128)(2,1)S(1)} collective-permute-done((bf16[320,512]{1,0:T(8,128)(2,1)S(1)}, bf16[320,512]{1,0:T(8,128)(2,1)S(1)}, u32[]{:S(2)}, u32[]{:S(2)}) %collective-permute-start.30) | collective-permute-done | bytes 327712 | tf_op jit(solution)/shard_map/ppermute | solution.py:118
  108.6 1.3 collective-permute-start.27
  110.6 1.7 %collective-permute-done.44 = bf16[160,768]{1,0:T(8,128)(2,1)S(1)} collective-permute-done((bf16[160,768]{1,0:T(8,128)(2,1)S(1)}, bf16[160,768]{1,0:T(8,128)(2,1)S(1)}, u32[]{:S(2)}, u32[]{:S(2)}) %collective-permute-start.44) | collective-permute-done | bytes 245792 | tf_op jit(solution)/shard_map/ppermute | solution.py:118
  113.9 2.2 %collective-permute-done.35 = bf16[176,512]{1,0:T(8,128)(2,1)S(1)} collective-permute-done((bf16[176,512]{1,0:T(8,128)(2,1)S(1)}, bf16[176,512]{1,0:T(8,128)(2,1)S(1)}, u32[]{:S(2)}, u32[]{:S(2)}) %collective-permute-start.35) | collective-permute-done | bytes 180256 | tf_op jit(solution)/shard_map/ppermute | solution.py:118
  116.2 1.5 %collective-permute-start.36 = (bf16[176,512]{1,0:T(8,128)(2,1)S(1)}, bf16[176,512]{1,0:T(8,128)(2,1)S(1)}, u32[]{:S(2)}, u32[]{:S(2)}) collective-permute-start(bf16[176,512]{1,0:T(8,128)(2,1)S(1)} %add_convert_fusion.9), channel_id=1, source_target_pairs={{0,4},{4,0},{1,5},{5,1},{2,6},{6,2},{3,7},{7,3},{8,12},{12,8},{9,1... | collective-permute-start | bytes 540680 | tf_op jit(solution)/shard_map/ppermute | solution.py:100
  118.9 1.8 %collective-permute-start.37 = (bf16[176,512]{1,0:T(8,128)(2,1)S(1)}, bf16[176,512]{1,0:T(8,128)(2,1)S(1)}, u32[]{:S(2)}, u32[]{:S(2)}) collective-permute-start(bf16[176,512]{1,0:T(8,128)(2,1)S(1)} %add_convert_fusion.8), channel_id=1, source_target_pairs={{0,1},{1,0},{2,3},{3,2},{4,5},{5,4},{6,7},{7,6},{8,9},{9,8},{10,11... | collective-permute-start | bytes 540680 | tf_op jit(solution)/shard_map/ppermute | solution.py:103
  121.1 3.1 %collective-permute-start.46 = (bf16[160,768]{1,0:T(8,128)(2,1)S(1)}, bf16[160,768]{1,0:T(8,128)(2,1)S(1)}, u32[]{:S(2)}, u32[]{:S(2)}) collective-permute-start(bf16[160,768]{1,0:T(8,128)(2,1)S(1)} %collective-permute-done.45.refs_2_), channel_id=1, source_target_pairs={{0,4},{4,0},{1,5},{5,1},{2,6},{6,2},{3,7},{7,3},{8,12},{12,8},{9,1... | collective-permute-start | bytes 737288 | tf_op jit(solution)/shard_map/ppermute | solution.py:100
  124.2 3.8 %collective-permute-start.42 = (bf16[160,768]{1,0:T(8,128)(2,1)S(1)}, bf16[160,768]{1,0:T(8,128)(2,1)S(1)}, u32[]{:S(2)}, u32[]{:S(2)}) collective-permute-start(bf16[160,768]{1,0:T(8,128)(2,1)S(1)} %collective-permute-done.41.refs_0_), channel_id=1, source_target_pairs={{0,4},{4,0},{1,5},{5,1},{2,6},{6,2},{3,7},{7,3},{8,12},{12,8},{9,1... | collective-permute-start | bytes 737288 | tf_op jit(solution)/shard_map/ppermute | solution.py:100
  128.1 6.6 %collective-permute-start.38 = (bf16[176,512]{1,0:T(8,128)(2,1)S(1)}, bf16[176,512]{1,0:T(8,128)(2,1)S(1)}, u32[]{:S(2)}, u32[]{:S(2)}) collective-permute-start(bf16[176,512]{1,0:T(8,128)(2,1)S(1)} %add_convert_fusion.7.refs_0_), channel_id=1, source_target_pairs={{0,2},{1,3},{2,0},{3,1},{4,6},{5,7},{6,4},{7,5},{8,10},{9,11},{10,... | collective-permute-start | bytes 540680 | tf_op jit(solution)/shard_map/ppermute | solution.py:106
  134.9 3.3 %collective-permute-start.29 = (bf16[128,640]{1,0:T(8,128)(2,1)S(1)}, bf16[128,640]{1,0:T(8,128)(2,1)S(1)}, u32[]{:S(2)}, u32[]{:S(2)}) collective-permute-start(bf16[128,640]{1,0:T(8,128)(2,1)S(1)} %last_norm.1.refs_0_), channel_id=1, source_target_pairs={{0,2},{1,3},{2,0},{3,1},{4,6},{5,7},{6,4},{7,5},{8,10},{9,11},{10,... | collective-permute-start | bytes 491528 | tf_op jit(solution)/shard_map/ppermute | solution.py:106
  138.2 1.9 %join_output.1 = f32[256,640]{1,0:T(8,128)} custom-call(bf16[128,640]{1,0:T(8,128)(2,1)} %get-tuple-element.104.refs_0_, bf16[128,640]{1,0:T(8,128)(2,1)} %collective-permute-done.21.refs_1_), custom_call_target="tpu_custom_call" | custom-call | bytes 983040 | tf_op jit(solution)/shard_map/join_output/pallas_call | solution.py:79
  140.9 10.0 %collective-permute-done.29.refs_1_ = bf16[128,640]{1,0:T(8,128)(2,1)S(1)} collective-permute-done((bf16[128,640]{1,0:T(8,128)(2,1)S(1)}, bf16[128,640]{1,0:T(8,128)(2,1)S(1)}, u32[]{:S(2)}, u32[]{:S(2)}) %collective-permute-start.29) | collective-permute-done | bytes 163872 | tf_op jit(solution)/shard_map/ppermute | solution.py:106
  (140 shorter events, 25.7 us)
Async XLA Ops:
  3.2 13.8 %collective-permute-start.4 = (bf16[160,512]{1,0:T(8,128)(2,1)S(1)}, bf16[160,512]{1,0:T(8,128)(2,1)S(1)}, u32[]{:S(2)}, u32[]{:S(2)}) collective-permute-start(bf16[160,512]{1,0:T(8,128)(2,1)S(1)} %get-tuple-element.81), channel_id=1, source_target_pairs={{0,0},{1,1},{2,4},{3,5},{4,2},{5,3},{6,6},{7,7},{8,8},{9,9},{10,12... | collective-permute-start | bytes 491528 | tf_op jit(solution)/shard_map/ppermute | solution.py:115
  3.9 15.2 %collective-permute-start.8 = (bf16[160,768]{1,0:T(8,128)(2,1)S(1)}, bf16[160,768]{1,0:T(8,128)(2,1)S(1)}, u32[]{:S(2)}, u32[]{:S(2)}) collective-permute-start(bf16[160,768]{1,0:T(8,128)(2,1)S(1)} %get-tuple-element.83), channel_id=1, source_target_pairs={{0,0},{1,1},{2,4},{3,5},{4,2},{5,3},{6,6},{7,7},{8,8},{9,9},{10,12... | collective-permute-start | bytes 737288 | tf_op jit(solution)/shard_map/ppermute | solution.py:115
  4.6 16.0 %collective-permute-start.9 = (bf16[160,768]{1,0:T(8,128)(2,1)S(1)}, bf16[160,768]{1,0:T(8,128)(2,1)S(1)}, u32[]{:S(2)}, u32[]{:S(2)}) collective-permute-start(bf16[160,768]{1,0:T(8,128)(2,1)S(1)} %get-tuple-element.84), channel_id=1, source_target_pairs={{0,0},{1,1},{2,4},{3,5},{4,2},{5,3},{6,6},{7,7},{8,8},{9,9},{10,12... | collective-permute-start | bytes 737288 | tf_op jit(solution)/shard_map/ppermute | solution.py:115
  5.3 13.3 %collective-permute-start.1 = (bf16[176,512]{1,0:T(8,128)(2,1)S(1)}, bf16[176,512]{1,0:T(8,128)(2,1)S(1)}, u32[]{:S(2)}, u32[]{:S(2)}) collective-permute-start(bf16[176,512]{1,0:T(8,128)(2,1)S(1)} %get-tuple-element.80.refs_3_.refs_16_.refs_22_.refs_17_.refs_23_.refs_18_.refs_13_), channel_id=1, source_target_pairs={{0,8},{8,0},{16,24},{24,16},{1,9},{9,1},{17,25},{25,17},{2,10},{10... | collective-permute-start | bytes 540680 | tf_op jit(solution)/shard_map/ppermute | solution.py:118
  8.3 19.2 %collective-permute-start = (bf16[256,640]{1,0:T(8,128)(2,1)S(1)}, bf16[256,640]{1,0:T(8,128)(2,1)S(1)}, u32[]{:S(2)}, u32[]{:S(2)}) collective-permute-start(bf16[256,640]{1,0:T(8,128)(2,1)S(1)} %copy-done.7), channel_id=1, source_target_pairs={{0,4},{4,0},{1,5},{5,1},{2,6},{6,2},{3,7},{7,3},{8,12},{12,8},{9,1... | collective-permute-start | bytes 983048 | tf_op jit(solution)/shard_map/ppermute | solution.py:100
  17.1 6.6 %collective-permute-start.6 = (bf16[160,512]{1,0:T(8,128)(2,1)S(1)}, bf16[160,512]{1,0:T(8,128)(2,1)S(1)}, u32[]{:S(2)}, u32[]{:S(2)}) collective-permute-start(bf16[160,512]{1,0:T(8,128)(2,1)S(1)} %collective-permute-done.4.refs_7_.refs_20_.refs_26_.refs_21_.refs_27_.refs_22_.refs_17_), channel_id=1, source_target_pairs={{0,16},{8,24},{16,0},{24,8},{1,17},{9,25},{17,1},{25,9},{2,18},{10... | collective-permute-start | bytes 491528 | tf_op jit(solution)/shard_map/ppermute | solution.py:118
  18.6 8.9 %collective-permute-start.2 = (bf16[176,512]{1,0:T(8,128)(2,1)S(1)}, bf16[176,512]{1,0:T(8,128)(2,1)S(1)}, u32[]{:S(2)}, u32[]{:S(2)}) collective-permute-start(bf16[176,512]{1,0:T(8,128)(2,1)S(1)} %get-tuple-element.80.refs_3_.refs_16_.refs_22_.refs_17_.refs_23_.refs_18_.refs_13_), channel_id=1, source_target_pairs={{0,16},{8,24},{16,0},{24,8},{1,17},{9,25},{17,1},{25,9},{2,18},{10... | collective-permute-start | bytes 540680 | tf_op jit(solution)/shard_map/ppermute | solution.py:118
  19.1 11.9 %collective-permute-start.3 = (bf16[176,512]{1,0:T(8,128)(2,1)S(1)}, bf16[176,512]{1,0:T(8,128)(2,1)S(1)}, u32[]{:S(2)}, u32[]{:S(2)}) collective-permute-start(bf16[176,512]{1,0:T(8,128)(2,1)S(1)} %collective-permute-done.1.refs_4_.refs_17_.refs_23_.refs_18_.refs_24_.refs_19_.refs_14_), channel_id=1, source_target_pairs={{0,16},{8,24},{16,0},{24,8},{1,17},{9,25},{17,1},{25,9},{2,18},{10... | collective-permute-start | bytes 540680 | tf_op jit(solution)/shard_map/ppermute | solution.py:118
  20.6 6.9 %collective-permute-start.5 = (bf16[160,512]{1,0:T(8,128)(2,1)S(1)}, bf16[160,512]{1,0:T(8,128)(2,1)S(1)}, u32[]{:S(2)}, u32[]{:S(2)}) collective-permute-start(bf16[160,512]{1,0:T(8,128)(2,1)S(1)} %collective-permute-done.4.refs_7_.refs_20_.refs_26_.refs_21_.refs_27_.refs_22_.refs_17_), channel_id=1, source_target_pairs={{0,8},{8,0},{16,24},{24,16},{1,9},{9,1},{17,25},{25,17},{2,10},{10... | collective-permute-start | bytes 491528 | tf_op jit(solution)/shard_map/ppermute | solution.py:118
  23.6 7.3 %collective-permute-start.7 = (bf16[160,512]{1,0:T(8,128)(2,1)S(1)}, bf16[160,512]{1,0:T(8,128)(2,1)S(1)}, u32[]{:S(2)}, u32[]{:S(2)}) collective-permute-start(bf16[160,512]{1,0:T(8,128)(2,1)S(1)} %collective-permute-done.6.refs_9_.refs_22_.refs_28_.refs_23_.refs_29_.refs_24_.refs_19_), channel_id=1, source_target_pairs={{0,8},{8,0},{16,24},{24,16},{1,9},{9,1},{17,25},{25,17},{2,10},{10... | collective-permute-start | bytes 491528 | tf_op jit(solution)/shard_map/ppermute | solution.py:118
  27.5 52.6 %copy-start = (bf16[160,512]{1,0:T(8,128)(2,1)}, bf16[160,512]{1,0:T(8,128)(2,1)S(1)}, u32[]{:S(2)}) copy-start(bf16[160,512]{1,0:T(8,128)(2,1)S(1)} %collective-permute-done.5.refs_8_.refs_21_.refs_27_.refs_22_.refs_28_.refs_23_.refs_18_) | copy-start | bytes 491524
  33.2 3.7 %collective-permute-start.10 = (bf16[128,640]{1,0:T(8,128)(2,1)S(1)}, bf16[128,640]{1,0:T(8,128)(2,1)S(1)}, u32[]{:S(2)}, u32[]{:S(2)}) collective-permute-start(bf16[128,640]{1,0:T(8,128)(2,1)S(1)} %get-tuple-element.88), channel_id=1, source_target_pairs={{0,4},{4,0},{1,5},{5,1},{2,6},{6,2},{3,7},{7,3},{8,12},{12,8},{9,1... | collective-permute-start | bytes 491528 | tf_op jit(solution)/shard_map/ppermute | solution.py:100
  34.6 8.8 %collective-permute-start.13 = (bf16[160,768]{1,0:T(8,128)(2,1)S(1)}, bf16[160,768]{1,0:T(8,128)(2,1)S(1)}, u32[]{:S(2)}, u32[]{:S(2)}) collective-permute-start(bf16[160,768]{1,0:T(8,128)(2,1)S(1)} %collective-permute-done.8.refs_2_.refs_28_.refs_3_), channel_id=1, source_target_pairs={{0,8},{8,0},{16,24},{24,16},{1,9},{9,1},{17,25},{25,17},{2,10},{10... | collective-permute-start | bytes 737288 | tf_op jit(solution)/shard_map/ppermute | solution.py:118
  35.4 9.6 %collective-permute-start.17 = (bf16[160,768]{1,0:T(8,128)(2,1)S(1)}, bf16[160,768]{1,0:T(8,128)(2,1)S(1)}, u32[]{:S(2)}, u32[]{:S(2)}) collective-permute-start(bf16[160,768]{1,0:T(8,128)(2,1)S(1)} %collective-permute-done.9.refs_6_.refs_32_.refs_7_), channel_id=1, source_target_pairs={{0,16},{8,24},{16,0},{24,8},{1,17},{9,25},{17,1},{25,9},{2,18},{10... | collective-permute-start | bytes 737288 | tf_op jit(solution)/shard_map/ppermute | solution.py:118
  36.9 8.8 %collective-permute-start.11 = (bf16[128,640]{1,0:T(8,128)(2,1)S(1)}, bf16[128,640]{1,0:T(8,128)(2,1)S(1)}, u32[]{:S(2)}, u32[]{:S(2)}) collective-permute-start(bf16[128,640]{1,0:T(8,128)(2,1)S(1)} %add_convert_fusion.14.refs_0_), channel_id=1, source_target_pairs={{0,1},{1,0},{2,3},{3,2},{4,5},{5,4},{6,7},{7,6},{8,9},{9,8},{10,11... | collective-permute-start | bytes 491528 | tf_op jit(solution)/shard_map/ppermute | solution.py:103
  38.0 11.5 %collective-permute-start.14 = (bf16[160,768]{1,0:T(8,128)(2,1)S(1)}, bf16[160,768]{1,0:T(8,128)(2,1)S(1)}, u32[]{:S(2)}, u32[]{:S(2)}) collective-permute-start(bf16[160,768]{1,0:T(8,128)(2,1)S(1)} %collective-permute-done.8.refs_2_.refs_28_.refs_3_), channel_id=1, source_target_pairs={{0,16},{8,24},{16,0},{24,8},{1,17},{9,25},{17,1},{25,9},{2,18},{10... | collective-permute-start | bytes 737288 | tf_op jit(solution)/shard_map/ppermute | solution.py:118
  38.5 11.0 %collective-permute-start.16 = (bf16[160,768]{1,0:T(8,128)(2,1)S(1)}, bf16[160,768]{1,0:T(8,128)(2,1)S(1)}, u32[]{:S(2)}, u32[]{:S(2)}) collective-permute-start(bf16[160,768]{1,0:T(8,128)(2,1)S(1)} %collective-permute-done.9.refs_6_.refs_32_.refs_7_), channel_id=1, source_target_pairs={{0,8},{8,0},{16,24},{24,16},{1,9},{9,1},{17,25},{25,17},{2,10},{10... | collective-permute-start | bytes 737288 | tf_op jit(solution)/shard_map/ppermute | solution.py:118
  43.4 10.1 %collective-permute-start.15 = (bf16[160,768]{1,0:T(8,128)(2,1)S(1)}, bf16[160,768]{1,0:T(8,128)(2,1)S(1)}, u32[]{:S(2)}, u32[]{:S(2)}) collective-permute-start(bf16[160,768]{1,0:T(8,128)(2,1)S(1)} %collective-permute-done.13.refs_3_.refs_29_.refs_4_), channel_id=1, source_target_pairs={{0,16},{8,24},{16,0},{24,8},{1,17},{9,25},{17,1},{25,9},{2,18},{10... | collective-permute-start | bytes 737288 | tf_op jit(solution)/shard_map/ppermute | solution.py:118
  45.0 8.6 %collective-permute-start.18 = (bf16[160,768]{1,0:T(8,128)(2,1)S(1)}, bf16[160,768]{1,0:T(8,128)(2,1)S(1)}, u32[]{:S(2)}, u32[]{:S(2)}) collective-permute-start(bf16[160,768]{1,0:T(8,128)(2,1)S(1)} %collective-permute-done.17.refs_8_.refs_34_.refs_9_), channel_id=1, source_target_pairs={{0,8},{8,0},{16,24},{24,16},{1,9},{9,1},{17,25},{25,17},{2,10},{10... | collective-permute-start | bytes 737288 | tf_op jit(solution)/shard_map/ppermute | solution.py:118
  46.0 7.6 %collective-permute-start.12 = (bf16[128,640]{1,0:T(8,128)(2,1)S(1)}, bf16[128,640]{1,0:T(8,128)(2,1)S(1)}, u32[]{:S(2)}, u32[]{:S(2)}) collective-permute-start(bf16[128,640]{1,0:T(8,128)(2,1)S(1)} %get-tuple-element.99.refs_0_.refs_26_.refs_33_), channel_id=1, source_target_pairs={{0,4},{4,0},{1,5},{5,1},{2,6},{6,2},{3,7},{7,3},{8,12},{12,8},{9,1... | collective-permute-start | bytes 491528 | tf_op jit(solution)/shard_map/ppermute | solution.py:100
  54.8 1.5 collective-permute-start.19
  56.3 6.3 %collective-permute-start.20 = (bf16[128,640]{1,0:T(8,128)(2,1)S(1)}, bf16[128,640]{1,0:T(8,128)(2,1)S(1)}, u32[]{:S(2)}, u32[]{:S(2)}) collective-permute-start(bf16[128,640]{1,0:T(8,128)(2,1)S(1)} %add_convert_fusion.13.refs_0_), channel_id=1, source_target_pairs={{0,1},{1,0},{2,3},{3,2},{4,5},{5,4},{6,7},{7,6},{8,9},{9,8},{10,11... | collective-permute-start | bytes 491528 | tf_op jit(solution)/shard_map/ppermute | solution.py:103
  63.5 1.4 collective-permute-start.22
  66.4 1.5 collective-permute-start.23
  70.0 27.9 %collective-permute-start.43 = (bf16[320,768]{1,0:T(8,128)(2,1)}, bf16[320,768]{1,0:T(8,128)(2,1)}, u32[]{:S(2)}, u32[]{:S(2)}) collective-permute-start(bf16[320,768]{1,0:T(8,128)(2,1)} %get-tuple-element.135), channel_id=1, source_target_pairs={{0,16},{8,24},{16,0},{24,8},{1,17},{9,25},{17,1},{25,9},{2,18},{10... | collective-permute-start | bytes 1474568 | tf_op jit(solution)/shard_map/ppermute | solution.py:118
  71.5 8.6 %collective-permute-start.24 = (bf16[128,640]{1,0:T(8,128)(2,1)S(1)}, bf16[128,640]{1,0:T(8,128)(2,1)S(1)}, u32[]{:S(2)}, u32[]{:S(2)}) collective-permute-start(bf16[128,640]{1,0:T(8,128)(2,1)S(1)} %add_convert_fusion.12.refs_0_), channel_id=1, source_target_pairs={{0,1},{1,0},{2,3},{3,2},{4,5},{5,4},{6,7},{7,6},{8,9},{9,8},{10,11... | collective-permute-start | bytes 491528 | tf_op jit(solution)/shard_map/ppermute | solution.py:103
  72.5 12.4 %collective-permute-start.21 = (bf16[128,640]{1,0:T(8,128)(2,1)}, bf16[128,640]{1,0:T(8,128)(2,1)}, u32[]{:S(2)}, u32[]{:S(2)}) collective-permute-start(bf16[128,640]{1,0:T(8,128)(2,1)} %get-tuple-element.104.refs_0_), channel_id=1, source_target_pairs={{0,2},{1,3},{2,0},{3,1},{4,6},{5,7},{6,4},{7,5},{8,10},{9,11},{10,... | collective-permute-start | bytes 491528 | tf_op jit(solution)/shard_map/ppermute | solution.py:106
  83.1 1.8 %collective-permute-start.25 = (bf16[128,640]{1,0:T(8,128)(2,1)}, bf16[128,640]{1,0:T(8,128)(2,1)}, u32[]{:S(2)}, u32[]{:S(2)}) collective-permute-start(bf16[128,640]{1,0:T(8,128)(2,1)} %get-tuple-element.109.refs_1_.refs_5_), channel_id=1, source_target_pairs={{0,4},{4,0},{1,5},{5,1},{2,6},{6,2},{3,7},{7,3},{8,12},{12,8},{9,1... | collective-permute-start | bytes 491528 | tf_op jit(solution)/shard_map/ppermute | solution.py:100
  83.1 16.4 %collective-permute-start.39 = (bf16[320,768]{1,0:T(8,128)(2,1)}, bf16[320,768]{1,0:T(8,128)(2,1)}, u32[]{:S(2)}, u32[]{:S(2)}) collective-permute-start(bf16[320,768]{1,0:T(8,128)(2,1)} %get-tuple-element.133), channel_id=1, source_target_pairs={{0,8},{8,0},{16,24},{24,16},{1,9},{9,1},{17,25},{25,17},{2,10},{10... | collective-permute-start | bytes 1474568 | tf_op jit(solution)/shard_map/ppermute | solution.py:118
  92.5 16.0 %collective-permute-start.26 = (bf16[256,640]{1,0:T(8,128)(2,1)S(1)}, bf16[256,640]{1,0:T(8,128)(2,1)S(1)}, u32[]{:S(2)}, u32[]{:S(2)}) collective-permute-start(bf16[256,640]{1,0:T(8,128)(2,1)S(1)} %get-tuple-element.112.refs_9_), channel_id=1, source_target_pairs={{0,4},{4,0},{1,5},{5,1},{2,6},{6,2},{3,7},{7,3},{8,12},{12,8},{9,1... | collective-permute-start | bytes 983048 | tf_op jit(solution)/shard_map/ppermute | solution.py:100
  95.6 14.2 %collective-permute-start.34 = (bf16[352,512]{1,0:T(8,128)(2,1)S(1)}, bf16[352,512]{1,0:T(8,128)(2,1)S(1)}, u32[]{:S(2)}, u32[]{:S(2)}) collective-permute-start(bf16[352,512]{1,0:T(8,128)(2,1)S(1)} %get-tuple-element.125), channel_id=1, source_target_pairs={{0,8},{8,0},{16,24},{24,16},{1,9},{9,1},{17,25},{25,17},{2,10},{10... | collective-permute-start | bytes 1081352 | tf_op jit(solution)/shard_map/ppermute | solution.py:118
  97.4 10.6 %collective-permute-start.30 = (bf16[320,512]{1,0:T(8,128)(2,1)S(1)}, bf16[320,512]{1,0:T(8,128)(2,1)S(1)}, u32[]{:S(2)}, u32[]{:S(2)}) collective-permute-start(bf16[320,512]{1,0:T(8,128)(2,1)S(1)} %get-tuple-element.122), channel_id=1, source_target_pairs={{0,16},{8,24},{16,0},{24,8},{1,17},{9,25},{17,1},{25,9},{2,18},{10... | collective-permute-start | bytes 983048 | tf_op jit(solution)/shard_map/ppermute | solution.py:118
  99.1 13.2 %collective-permute-start.44 = (bf16[160,768]{1,0:T(8,128)(2,1)S(1)}, bf16[160,768]{1,0:T(8,128)(2,1)S(1)}, u32[]{:S(2)}, u32[]{:S(2)}) collective-permute-start(bf16[160,768]{1,0:T(8,128)(2,1)S(1)} %slice.39), channel_id=1, source_target_pairs={{0,8},{8,0},{16,24},{24,16},{1,9},{9,1},{17,25},{25,17},{2,10},{10... | collective-permute-start | bytes 737288 | tf_op jit(solution)/shard_map/ppermute | solution.py:118
  101.2 12.0 %collective-permute-start.40 = (bf16[160,768]{1,0:T(8,128)(2,1)S(1)}, bf16[160,768]{1,0:T(8,128)(2,1)S(1)}, u32[]{:S(2)}, u32[]{:S(2)}) collective-permute-start(bf16[160,768]{1,0:T(8,128)(2,1)S(1)} %slice.37), channel_id=1, source_target_pairs={{0,16},{8,24},{16,0},{24,8},{1,17},{9,25},{17,1},{25,9},{2,18},{10... | collective-permute-start | bytes 737288 | tf_op jit(solution)/shard_map/ppermute | solution.py:118
  108.0 9.7 %collective-permute-start.31 = (bf16[160,512]{1,0:T(8,128)(2,1)S(1)}, bf16[160,512]{1,0:T(8,128)(2,1)S(1)}, u32[]{:S(2)}, u32[]{:S(2)}) collective-permute-start(bf16[160,512]{1,0:T(8,128)(2,1)S(1)} %slice.33), channel_id=1, source_target_pairs={{0,8},{8,0},{16,24},{24,16},{1,9},{9,1},{17,25},{25,17},{2,10},{10... | collective-permute-start | bytes 491528 | tf_op jit(solution)/shard_map/ppermute | solution.py:118
  108.6 12.1 %collective-permute-start.27 = (bf16[128,640]{1,0:T(8,128)(2,1)S(1)}, bf16[128,640]{1,0:T(8,128)(2,1)S(1)}, u32[]{:S(2)}, u32[]{:S(2)}) collective-permute-start(bf16[128,640]{1,0:T(8,128)(2,1)S(1)} %constant_dynamic-slice_fusion), channel_id=1, source_target_pairs={{0,2},{1,3},{2,0},{3,1},{4,6},{5,7},{6,4},{7,5},{8,10},{9,11},{10,... | collective-permute-start | bytes 491528 | tf_op jit(solution)/shard_map/ppermute | solution.py:106
  110.0 6.2 %collective-permute-start.35 = (bf16[176,512]{1,0:T(8,128)(2,1)S(1)}, bf16[176,512]{1,0:T(8,128)(2,1)S(1)}, u32[]{:S(2)}, u32[]{:S(2)}) collective-permute-start(bf16[176,512]{1,0:T(8,128)(2,1)S(1)} %slice.35), channel_id=1, source_target_pairs={{0,16},{8,24},{16,0},{24,8},{1,17},{9,25},{17,1},{25,9},{2,18},{10... | collective-permute-start | bytes 540680 | tf_op jit(solution)/shard_map/ppermute | solution.py:118
  112.3 8.8 %collective-permute-start.45 = (bf16[160,768]{1,0:T(8,128)(2,1)S(1)}, bf16[160,768]{1,0:T(8,128)(2,1)S(1)}, u32[]{:S(2)}, u32[]{:S(2)}) collective-permute-start(bf16[160,768]{1,0:T(8,128)(2,1)S(1)} %add_convert_fusion.5), channel_id=1, source_target_pairs={{0,0},{1,1},{2,4},{3,5},{4,2},{5,3},{6,6},{7,7},{8,8},{9,9},{10,12... | collective-permute-start | bytes 737288 | tf_op jit(solution)/shard_map/ppermute | solution.py:115
  113.3 11.0 %collective-permute-start.41 = (bf16[160,768]{1,0:T(8,128)(2,1)S(1)}, bf16[160,768]{1,0:T(8,128)(2,1)S(1)}, u32[]{:S(2)}, u32[]{:S(2)}) collective-permute-start(bf16[160,768]{1,0:T(8,128)(2,1)S(1)} %add_convert_fusion.6), channel_id=1, source_target_pairs={{0,0},{1,1},{2,4},{3,5},{4,2},{5,3},{6,6},{7,7},{8,8},{9,9},{10,12... | collective-permute-start | bytes 737288 | tf_op jit(solution)/shard_map/ppermute | solution.py:115
  116.2 2.6 %collective-permute-start.36 = (bf16[176,512]{1,0:T(8,128)(2,1)S(1)}, bf16[176,512]{1,0:T(8,128)(2,1)S(1)}, u32[]{:S(2)}, u32[]{:S(2)}) collective-permute-start(bf16[176,512]{1,0:T(8,128)(2,1)S(1)} %add_convert_fusion.9), channel_id=1, source_target_pairs={{0,4},{4,0},{1,5},{5,1},{2,6},{6,2},{3,7},{7,3},{8,12},{12,8},{9,1... | collective-permute-start | bytes 540680 | tf_op jit(solution)/shard_map/ppermute | solution.py:100
  117.8 16.8 %collective-permute-start.32 = (bf16[160,512]{1,0:T(8,128)(2,1)S(1)}, bf16[160,512]{1,0:T(8,128)(2,1)S(1)}, u32[]{:S(2)}, u32[]{:S(2)}) collective-permute-start(bf16[160,512]{1,0:T(8,128)(2,1)S(1)} %add_convert_fusion.10), channel_id=1, source_target_pairs={{0,0},{1,1},{2,4},{3,5},{4,2},{5,3},{6,6},{7,7},{8,8},{9,9},{10,12... | collective-permute-start | bytes 491528 | tf_op jit(solution)/shard_map/ppermute | solution.py:115
  118.9 9.2 %collective-permute-start.37 = (bf16[176,512]{1,0:T(8,128)(2,1)S(1)}, bf16[176,512]{1,0:T(8,128)(2,1)S(1)}, u32[]{:S(2)}, u32[]{:S(2)}) collective-permute-start(bf16[176,512]{1,0:T(8,128)(2,1)S(1)} %add_convert_fusion.8), channel_id=1, source_target_pairs={{0,1},{1,0},{2,3},{3,2},{4,5},{5,4},{6,7},{7,6},{8,9},{9,8},{10,11... | collective-permute-start | bytes 540680 | tf_op jit(solution)/shard_map/ppermute | solution.py:103
  120.8 13.9 %collective-permute-start.28 = (bf16[128,640]{1,0:T(8,128)(2,1)S(1)}, bf16[128,640]{1,0:T(8,128)(2,1)S(1)}, u32[]{:S(2)}, u32[]{:S(2)}) collective-permute-start(bf16[128,640]{1,0:T(8,128)(2,1)S(1)} %add_convert_fusion.11.refs_0_), channel_id=1, source_target_pairs={{0,1},{1,0},{2,3},{3,2},{4,5},{5,4},{6,7},{7,6},{8,9},{9,8},{10,11... | collective-permute-start | bytes 491528 | tf_op jit(solution)/shard_map/ppermute | solution.py:103
  121.1 30.6 %collective-permute-start.46 = (bf16[160,768]{1,0:T(8,128)(2,1)S(1)}, bf16[160,768]{1,0:T(8,128)(2,1)S(1)}, u32[]{:S(2)}, u32[]{:S(2)}) collective-permute-start(bf16[160,768]{1,0:T(8,128)(2,1)S(1)} %collective-permute-done.45.refs_2_), channel_id=1, source_target_pairs={{0,4},{4,0},{1,5},{5,1},{2,6},{6,2},{3,7},{7,3},{8,12},{12,8},{9,1... | collective-permute-start | bytes 737288 | tf_op jit(solution)/shard_map/ppermute | solution.py:100
  124.2 27.5 %collective-permute-start.42 = (bf16[160,768]{1,0:T(8,128)(2,1)S(1)}, bf16[160,768]{1,0:T(8,128)(2,1)S(1)}, u32[]{:S(2)}, u32[]{:S(2)}) collective-permute-start(bf16[160,768]{1,0:T(8,128)(2,1)S(1)} %collective-permute-done.41.refs_0_), channel_id=1, source_target_pairs={{0,4},{4,0},{1,5},{5,1},{2,6},{6,2},{3,7},{7,3},{8,12},{12,8},{9,1... | collective-permute-start | bytes 737288 | tf_op jit(solution)/shard_map/ppermute | solution.py:100
  128.1 24.6 %collective-permute-start.38 = (bf16[176,512]{1,0:T(8,128)(2,1)S(1)}, bf16[176,512]{1,0:T(8,128)(2,1)S(1)}, u32[]{:S(2)}, u32[]{:S(2)}) collective-permute-start(bf16[176,512]{1,0:T(8,128)(2,1)S(1)} %add_convert_fusion.7.refs_0_), channel_id=1, source_target_pairs={{0,2},{1,3},{2,0},{3,1},{4,6},{5,7},{6,4},{7,5},{8,10},{9,11},{10,... | collective-permute-start | bytes 540680 | tf_op jit(solution)/shard_map/ppermute | solution.py:106
  134.7 5.5 %collective-permute-start.33 = (bf16[160,512]{1,0:T(8,128)(2,1)S(1)}, bf16[160,512]{1,0:T(8,128)(2,1)S(1)}, u32[]{:S(2)}, u32[]{:S(2)}) collective-permute-start(bf16[160,512]{1,0:T(8,128)(2,1)S(1)} %collective-permute-done.32.refs_0_), channel_id=1, source_target_pairs={{0,4},{4,0},{1,5},{5,1},{2,6},{6,2},{3,7},{7,3},{8,12},{12,8},{9,1... | collective-permute-start | bytes 491528 | tf_op jit(solution)/shard_map/ppermute | solution.py:100
  134.9 15.9 %collective-permute-start.29 = (bf16[128,640]{1,0:T(8,128)(2,1)S(1)}, bf16[128,640]{1,0:T(8,128)(2,1)S(1)}, u32[]{:S(2)}, u32[]{:S(2)}) collective-permute-start(bf16[128,640]{1,0:T(8,128)(2,1)S(1)} %last_norm.1.refs_0_), channel_id=1, source_target_pairs={{0,2},{1,3},{2,0},{3,1},{4,6},{5,7},{6,4},{7,5},{8,10},{9,11},{10,... | collective-permute-start | bytes 491528 | tf_op jit(solution)/shard_map/ppermute | solution.py:106
  (28 other events, 329.7 us)

commit v3 on v2

--- a/solution.py
+++ b/solution.py
@@ -93,6 +93,10 @@
 
 def tie(value, *others):
     return lax.optimization_barrier((value,) + others)[0]
+
+
+def together(*values):
+    return lax.optimization_barrier(values)
 
 
 def make_program(n_fsdp, n_context, n_tensor):
@@ -257,6 +261,9 @@
                 tile = jnp.where(row == i, held[4 + i][...].astype(F32)[None, :], tile)
             kv_out[block:, HD : HD + gblock] = tile.astype(BF)
 
+        tok_parts = [tokens, core_swap(tokens)] if two else [
+            lax.all_gather(tokens, "context", axis=0, tiled=True)
+        ]
         pack_kv, pack_qo, pack_f1, pack_f2, cos_t, sin_t = call(
             pack, "pack",
             [
@@ -273,9 +280,10 @@
             scratch=[pltpu.VMEM((block,), BF)] * 4 + [pltpu.VMEM((gblock,), BF)] * 2
             + [pltpu.SemaphoreType.DMA((14,))],
         )
-        tok_parts = [tokens, core_swap(tokens)] if two else [
-            lax.all_gather(tokens, "context", axis=0, tiled=True)
-        ]
+        pack_kv, pack_qo, pack_f1, pack_f2, tok_other = together(
+            pack_kv, pack_qo, pack_f1, pack_f2, tok_parts[-1]
+        )
+        tok_parts = tok_parts[:-1] + [tok_other]
         cross_qo = cross(pack_qo)
         cross_f1, cross_f2 = cross(pack_f1), cross(pack_f2)
         kv_blocks = gather_blocks(pack_kv, 1)
@@ -285,17 +293,23 @@
 
         n_tok = len(tok_parts)
 
+        n_q = 2 * half
+        at_q, at_o = slice(0, n_q), slice(n_q, 2 * n_q)
+        at_k = slice(2 * n_q, 2 * n_q + stream)
+        at_v = slice(2 * n_q + stream, 2 * n_q + 2 * stream)
+        at_g = 2 * n_q + stream
+
         def front(lens, *refs):
             toks = refs[:n_tok]
             kvb = refs[n_tok : n_tok + 4]
             qob = refs[n_tok + 4 : n_tok + 8]
             cos_ref, sin_ref = refs[n_tok + 8 : n_tok + 10]
-            (act, q_rot, k_rot, val, q_pre, k_pre, attn, logt, keep, send, gw, gs, wkv, wqo) = (
-                refs[n_tok + 10 :]
-            )
-            put_blocks(wkv, kvb)
-            put_blocks(wqo, qob)
+            act, att_b, att_f, w_att, keep, send, gw = refs[n_tok + 10 :]
             f = own_f()
+            for step in range(n_fsdp):
+                at = pl.ds(pl.multiple_of((f ^ step) * block, EXTRA), block)
+                w_att[at, :kvw] = kvb[step][:block, :]
+                w_att[at, kvw:] = qob[step][...]
             tiles = [b[block:, :].astype(F32) for b in kvb]
             chunks = []
             for p in range(n_fsdp):
@@ -306,59 +320,55 @@
             wide = jnp.concatenate([t[:8, :block] for t in chunks], axis=1)
             slim = jnp.concatenate([t[:8, HD : HD + gblock] for t in chunks], axis=1)
             gw[...] = wide
-            gs[...] = slim
+            att_f[at_g:, :] = slim
             scale_ai, scale_q, scale_k = wide[0:1], slim[0:1], slim[1:2]
             at = 0
             for tok in toks:
                 hat, _ = rms_stats(tok[...].astype(F32))
                 act[at : at + tok.shape[0], :] = (hat * scale_ai).astype(BF)
                 at += tok.shape[0]
-            kv = dot32(act[...], wkv[...])
-            k_pre[...] = kv[:, :HD]
-            val[...] = kv[:, HD:].astype(BF)
+            kv = dot32(act[...], w_att[:, :kvw])
+            att_f[at_k, :] = kv[:, :HD]
+            att_b[at_v, :] = kv[:, HD:].astype(BF)
             k_hat, _ = rms_stats(kv[:, :HD])
-            k_rot[...] = rotate(k_hat * scale_k, cos_ref[...], sin_ref[...]).astype(BF)
+            att_b[at_k, :] = rotate(k_hat * scale_k, cos_ref[...], sin_ref[...]).astype(BF)
             for i, place in enumerate(places()):
                 mine = slice(i * half, (i + 1) * half)
-                pre = dot32(act[pl.ds(place, half), :], wqo[:, :HD])
-                q_pre[mine, :] = pre
+                pre = dot32(act[pl.ds(place, half), :], w_att[:, kvw : kvw + HD])
+                att_f[mine, :] = pre
                 hat, _ = rms_stats(pre)
                 turned = rotate(
                     hat * scale_q, cos_ref[pl.ds(place, half), :], sin_ref[pl.ds(place, half), :]
                 )
-                q_rot[mine, :] = (turned * att_scale).astype(BF)
+                att_b[mine, :] = (turned * att_scale).astype(BF)
             allowed = mask_of(lens)
-            scores = jnp.where(allowed, dot_nt(q_rot[...], k_rot[...]), NEG_LARGE)
+            scores = jnp.where(allowed, dot_nt(att_b[at_q, :], att_b[at_k, :]), NEG_LARGE)
             row_max = jnp.max(scores, axis=1, keepdims=True)
             weights = jnp.where(allowed, jnp.exp(scores - row_max), 0.0)
             total = jnp.sum(weights, axis=1, keepdims=True)
-            logt[...] = row_max + jnp.log(total)
-            heads = (dot32(weights.astype(BF), val[...]) / total).astype(BF)
-            attn[...] = heads
-            partial = dot_nt(heads, wqo[:, HD:])
+            att_f[at_o, :] = jnp.broadcast_to(row_max + jnp.log(total), (n_q, HD))
+            heads = (dot32(weights.astype(BF), att_b[at_v, :]) / total).astype(BF)
+            att_b[at_o, :] = heads
+            partial = dot_nt(heads, w_att[:, kvw + HD :])
             keep[...] = partial[:half]
             send[...] = partial[half:].astype(BF)
 
-        n_q = 2 * half
         wide_f, wide_b = shape((half, width), F32), shape((half, width), BF)
         row_f = shape((1, width), F32)
         cos_t = tie(cos_t, cross_f1, cross_f2)
-        (act, q_rot, k_rot, val, q_pre, k_pre, attn, logt, keep, send, gw, gs) = call(
+        act, att_b, att_f, w_att, keep, send, gw = call(
             front, "front",
             [
-                shape((stream, width), BF), shape((n_q, HD), BF), shape((stream, HD), BF),
-                shape((stream, HD), BF), shape((n_q, HD), F32), shape((stream, HD), F32),
-                shape((n_q, HD), BF), shape((n_q, 1), F32), wide_f, wide_b,
-                shape((8, width), F32), shape((8, HD), F32),
+                shape((stream, width), BF), shape((2 * n_q + 2 * stream, HD), BF),
+                shape((at_g + 8, HD), F32), shape((width, 2 * kvw), BF), wide_f, wide_b,
+                shape((8, width), F32),
             ],
             tok_parts + kv_blocks + qo_blocks + [cos_t, sin_t],
             scalars=[lengths],
-            scratch=[pltpu.VMEM((width, kvw), BF), pltpu.VMEM((width, kvw), BF)],
             flops=2 * stream * width * kvw + 4 * n_q * stream * HD,
             limit=limit,
         )
-        saved = [q_rot, k_rot, val, q_pre, k_pre, attn, logt, gs, cos_t, sin_t, act]
-        saved = (saved + [gw] + kv_blocks + qo_blocks) if two else []
+        saved = [att_b, att_f, cos_t, sin_t, act, gw, w_att] + tok_parts if two else []
 
         def pair_sum(kept, sent):
             return (kept + core_swap(sent).astype(F32)).astype(BF)
@@ -402,14 +412,17 @@
                 else:
                     send[...] = partial.astype(BF)
 
-        ffn_scratch = [pltpu.VMEM((width, 2 * hidden), BF), pltpu.VMEM((width, hidden), BF)]
         ffn_flops = 6 * n_q * width * hidden
-        gate_up, inner_act, keep, send = call(
+        gate_up, inner_act, keep, send, w_gu, w_d = call(
             ffn, "ffn",
-            [shape((n_q, 2 * hidden), F32), shape((n_q, hidden), BF), wide_f, wide_b],
-            [act_own, act_oth] + f1_blocks + f2_blocks, scratch=ffn_scratch, flops=ffn_flops,
+            [
+                shape((n_q, 2 * hidden), F32), shape((n_q, hidden), BF), wide_f, wide_b,
+                shape((width, 2 * hidden), BF), shape((width, hidden), BF),
+            ],
+            [act_own, act_oth] + f1_blocks + f2_blocks, flops=ffn_flops,
             hold=saved + ([hidden_res, attn_total] if two else []),
         )
+        kept_ffn = [attn_total, act_own, act_oth, inner_act] if two else []
 
         def mid_two(pair, near, res, cot, gains, out_ref, grad_out, ds_out):
             hat, inv = rms_stats(pair[...].astype(F32) + near[...].astype(F32))
@@ -422,14 +435,12 @@
         layer_own, gf_own, ds_fo = call(
             mid_two, "mid_two", [wide_b, wide_b, row_f],
             [pair, z_near(pair), hidden_res, cotangent, gw],
-            hold=saved + ([attn_total, act_own, act_oth] + f1_blocks + f2_blocks if two else []),
+            hold=saved + kept_ffn + ([gate_up, w_gu, w_d] if two else []),
         )
         layer_oth = z_far(layer_own)
         gf_oth = core_swap(gf_own)
 
-        def ffn_back(f0, f1, gu_ref, *refs):
-            ggu_out, keep, send, wgu, wd = refs[8:]
-            put_ffn(wgu, wd, refs[:4], refs[4:8])
+        def ffn_back(f0, f1, gu_ref, wgu, wd, ggu_out, keep, send):
             for i, g in enumerate((f0, f1)):
                 mine = slice(i * half, (i + 1) * half)
                 grad_inner = dot32(g[...], wd[...])
@@ -445,80 +456,77 @@
 
         grad_gu, keep, send = call(
             ffn_back, "ffn_back", [shape((n_q, 2 * hidden), BF), wide_f, wide_b],
-            [gf_own, gf_oth, gate_up] + f1_blocks + f2_blocks,
-            scratch=ffn_scratch, flops=ffn_flops,
-            hold=saved + ([hidden_res, attn_total, act_own, act_oth] if two else []),
+            [gf_own, gf_oth, gate_up, w_gu, w_d], flops=ffn_flops,
+            hold=saved + kept_ffn + ([hidden_res] if two else []),
         )
         pair = pair_sum(keep, send)
 
-        def put_grads(full, first, mine_out, give_out, size, lanes=slice(None)):
-            second = 3 - first
-            for i, step in enumerate((0, second)):
-                mine_out[i * size : (i + 1) * size, lanes] = take_block(full, step, size)
-            for i, step in enumerate((first, 3)):
-                give_out[i * size : (i + 1) * size, lanes] = take_block(full, step, size)
-
-        def ffn_weights(a0, a1, f0, f1, ggu, inner, m1, s1, m2, s2, full1, full2):
+        all_cols = 3 * hidden
+
+        def ffn_weights(a0, a1, f0, f1, ggu, inner, o0, o1, o2, o3, full):
             low, high = slice(0, half), slice(half, 2 * half)
-            cut = ffn_cols
-            full1[...] = (
-                dot_tn(a0[...], ggu[low, :cut]) + dot_tn(a1[...], ggu[high, :cut])
-            ).astype(BF)
-            full2[:, : hidden - split] = (
-                dot_tn(a0[...], ggu[low, cut:]) + dot_tn(a1[...], ggu[high, cut:])
-            ).astype(BF)
-            full2[:, hidden - split :] = (
+            cut = 2 * hidden
+            full[:, :cut] = (dot_tn(a0[...], ggu[low, :]) + dot_tn(a1[...], ggu[high, :])).astype(BF)
+            full[:, cut:] = (
                 dot_tn(f0[...], inner[low, :]) + dot_tn(f1[...], inner[high, :])
             ).astype(BF)
-            put_grads(full1, 1, m1, s1, block)
-            put_grads(full2, 2, m2, s2, block)
-
-        ffn_m1, ffn_s1, ffn_m2, ffn_s2 = call(
-            ffn_weights, "ffn_weights", [shape((2 * block, ffn_cols), BF)] * 4,
+            for step, out in enumerate((o0, o1, o2, o3)):
+                out[...] = take_block(full, step, block)
+
+        def sum_blocks(blocks):
+            total = blocks[0].astype(F32)
+            for piece in blocks[1:]:
+                total = total + piece.astype(F32)
+            return across_pairs(total).astype(BF)
+
+        ffn_parts = call(
+            ffn_weights, "ffn_weights", [shape((block, all_cols), BF)] * 4,
             [act_own, act_oth, gf_own, gf_oth, tie(grad_gu, pair), inner_act],
-            scratch=[pltpu.VMEM((width, ffn_cols), BF)] * 2, flops=ffn_flops,
-        )
-
-        def mid_three(pair, near, res, tot, cot, gains, hid_out, grad_out, fi_out, ao_out):
+            scratch=[pltpu.VMEM((width, all_cols), BF)], flops=ffn_flops,
+        )
+        ffn_hops = [fsdp_hop(ffn_parts[step], step) for step in (1, 2, 3)]
+
+        def mid_three(pair, near, res, tot, cot, gains, fo, hid_out, grad_out):
             total = pair[...].astype(F32) + near[...].astype(F32)
             hat, inv = rms_stats(res[...])
-            fi_out[...] = jnp.sum(total * hat, axis=0, keepdims=True)
+            hid_out[half : half + 1, :] = fo[...]
+            hid_out[half + 1 : half + 2, :] = jnp.sum(total * hat, axis=0, keepdims=True)
             grad = cot[pl.ds(group_start(), half), :].astype(F32)
             grad = grad + rms_back(total, gains[2:3, :], hat, inv)
-            hid_out[...] = grad
+            hid_out[:half, :] = grad
             hat, inv = rms_stats(tot[...])
-            ao_out[...] = jnp.sum(grad * hat, axis=0, keepdims=True)
+            hid_out[half + 2 : half + 3, :] = jnp.sum(grad * hat, axis=0, keepdims=True)
+            hid_out[half + 3 : half + 8, :] = gains[0:5, :]
             grad_out[...] = rms_back(grad, gains[1:2, :], hat, inv).astype(BF)
 
-        grad_hidden, ga_own, ds_fi, ds_ao = call(
-            mid_three, "mid_three", [wide_f, wide_b, row_f, row_f],
-            [pair, z_near(pair), hidden_res, attn_total, cotangent, gw],
+        grad_hidden, ga_own = call(
+            mid_three, "mid_three", [shape((half + 8, width), F32), wide_b],
+            [pair, z_near(pair), hidden_res, attn_total, cotangent, gw, ds_fo],
             hold=saved,
         )
-        ga_oth = tie(core_swap(ga_own), layer_oth)
+        ga_oth = tie(core_swap(ga_own), ffn_parts[1])
 
         def attn_back(lens, *refs):
-            (a0, a1, attn_r, logt_r, q_r, k_r, v_r, qp, kp, cos_ref, sin_ref, gains) = refs[:12]
-            kvb, qob = refs[12:16], refs[16:20]
-            gq_out, gkv_out, part_keep, part_send, dsq, dsk, wkv, wqo, part = refs[20:]
-            put_blocks(wkv, kvb)
-            put_blocks(wqo, qob)
-            scale_q, scale_k = gains[0:1, :], gains[1:2, :]
+            a0, a1, att_r, pre_r, cos_ref, sin_ref, w_r = refs[:7]
+            gq_out, gkv_out, part_keep, part_send, dsq, dsk, part = refs[7:]
+            attn_r, q_r, k_r, v_r = (att_r.at[x, :] for x in (at_o, at_q, at_k, at_v))
+            qp, kp, logt_r = (pre_r.at[x, :] for x in (at_q, at_k, at_o))
+            scale_q, scale_k = pre_r[at_g : at_g + 1, :], pre_r[at_g + 1 : at_g + 2, :]
             grad_attn = jnp.concatenate([a0[...], a1[...]], axis=0)
-            grad_heads = dot32(grad_attn, wqo[:, HD:]).astype(BF)
+            grad_heads = dot32(grad_attn, w_r[:, kvw + HD :]).astype(BF)
             delta = jnp.sum(
                 grad_heads.astype(F32) * attn_r[...].astype(F32), axis=1, keepdims=True
             )
             allowed = mask_of(lens)
             scores = dot_nt(q_r[...], k_r[...])
-            probs = jnp.where(allowed, jnp.exp(scores - logt_r[...]), 0.0)
+            probs = jnp.where(allowed, jnp.exp(scores - logt_r[:, :1]), 0.0)
             grad_s = (probs * (dot_nt(grad_heads, v_r[...]) - delta)).astype(BF)
             grad_kn = rotate(dot_tn(grad_s, q_r[...]), cos_ref[...], -sin_ref[...])
             hat, inv = rms_stats(kp[...])
             dsk[...] = jnp.sum(grad_kn * hat, axis=0, keepdims=True)
             gkv_out[:, :HD] = rms_back(grad_kn, scale_k, hat, inv).astype(BF)
             gkv_out[:, HD:] = dot_tn(probs.astype(BF), grad_heads).astype(BF)
-            part[...] = dot_nt(gkv_out[...], wkv[...])
+            part[...] = dot_nt(gkv_out[...], w_r[:, :kvw])
             grad_qr = dot32(grad_s, k_r[...]) * att_scale
             total_q = jnp.zeros((1, HD), F32)
             for i, place in enumerate(places()):
@@ -529,7 +537,7 @@
                 hat, inv = rms_stats(qp[mine, :])
                 total_q = total_q + jnp.sum(grad_qn * hat, axis=0, keepdims=True)
                 gq_out[mine, :] = rms_back(grad_qn, scale_q, hat, inv).astype(BF)
-                part[pl.ds(place, half), :] += dot_nt(gq_out[mine, :], wqo[:, :HD])
+                part[pl.ds(place, half), :] += dot_nt(gq_out[mine, :], w_r[:, kvw : kvw + HD])
             dsq[...] = total_q
             part_keep[...] = part[:rows, :]
             part_send[...] = part[rows:, :].astype(BF)
@@ -541,22 +549,41 @@
                 shape((n_q, HD), BF), shape((stream, kvw), BF), shape((rows, width), F32),
                 shape((n_rest, width), BF), shape((1, HD), F32), shape((1, HD), F32),
             ],
-            [ga_own, ga_oth, attn, logt, q_rot, k_rot, val, q_pre, k_pre, cos_t, sin_t, gs]
-            + kv_blocks + qo_blocks,
+            [ga_own, ga_oth, att_b, att_f, cos_t, sin_t, w_att],
             scalars=[lengths],
-            scratch=[
-                pltpu.VMEM((width, kvw), BF), pltpu.VMEM((width, kvw), BF),
-                pltpu.VMEM((stream, width), F32),
-            ],
+            scratch=[pltpu.VMEM((stream, width), F32)],
+            hold=[act, grad_hidden] + tok_parts if two else [],
             flops=2 * stream * width * kvw + 10 * n_q * stream * HD, limit=limit,
         )
+
+        quarter = half // 2
+
+        def near_at():
+            return lax.axis_index("tensor") % 2
+
+        def share(kept, recv, keep_out, give_out):
+            for g in range(2):
+                to = slice(g * quarter, (g + 1) * quarter)
+                for out, which in ((keep_out, near_at()), (give_out, 1 - near_at())):
+                    at = pl.ds(pl.multiple_of(g * half + which * quarter, quarter), quarter)
+                    out[to, :] = (kept[at, :] + recv[at, :].astype(F32)).astype(BF)
+
+        if two:
+            part_recv = core_swap(part_send)
+            part_mine = part_keep
+        else:
+            part_mine = lax.psum_scatter(
+                jnp.concatenate([part_keep, part_send.astype(F32)], axis=0),
+                "context", scatter_dimension=0, tiled=True,
+            )
+            part_recv = jnp.zeros((rows, width), BF)
+        row_keep, row_give = call(share, "share_rows", [wide_b, wide_b], [part_mine, part_recv])
 
         def attn_weights(*refs):
             toks = refs[:n_tok]
-            (act_r, gq, gkv, a0, a1, attn_r, pk, ps, dfo, dfi, dao, dq, dk) = (
-                refs[n_tok : n_tok + 13]
-            )
-            kv_m, kv_s, qo_m, qo_s, full, ext = refs[n_tok + 13 :]
+            act_r, gq, gkv, a0, a1, att_r, pk, ps, hid, dq, dk = refs[n_tok : n_tok + 11]
+            kv_k, kv_s, qo_m, qo_s, full, ext = refs[n_tok + 11 :]
+            attn_r = att_r.at[at_o, :]
             low, high = slice(0, half), slice(half, 2 * half)
             dai = jnp.zeros((1, width), F32)
             at = 0
@@ -570,7 +597,7 @@
                     piece = (pk if at == 0 else ps)[...].astype(F32)
                     dai = dai + jnp.sum(hat * piece, axis=0, keepdims=True)
                 at += size
-            wide = [dai, dao[...] * 0.5, dfi[...] * 0.5, dfo[...] * 0.5]
+            wide = [dai] + [hid[half + i : half + i + 1, :] * 0.5 for i in (2, 1, 0)]
             slim = [dq[...], dk[...]]
             ext[...] = jnp.zeros(ext.shape, BF)
             row_w = lax.broadcasted_iota(jnp.int32, (EXTRA, block), 0)
@@ -585,11 +612,15 @@
                     tile = jnp.where(row_s == i, vec[:, p * gblock : (p + 1) * gblock], tile)
                 ext[p * EXTRA : (p + 1) * EXTRA, HD : HD + gblock] = tile.astype(BF)
             full[...] = dot_tn(act_r[...], gkv[...]).astype(BF)
-            for out, steps in ((kv_m, (0, 2)), (kv_s, (1, 3))):
-                for i, step in enumerate(steps):
+            core = lax.axis_index("context") % 2
+            for out, side in ((kv_k, core), (kv_s, 1 - core)):
+                lanes = pl.ds(pl.multiple_of(side * HD, HD), HD)
+                for i, step in enumerate((0, 2, 1, 3)):
                     at = i * blk_ext
-                    out[at : at + block, :] = take_block(full, step, block)
-                    out[at + block : at + blk_ext, :] = take_block(ext, step, EXTRA)
+                    from_row = pl.multiple_of((own_f() ^ step) * block, EXTRA)
+                    out[at : at + block, :] = full[pl.ds(from_row, block), lanes]
+                    from_row = pl.multiple_of((own_f() ^ step) * EXTRA, EXTRA)
+                    out[at + block : at + blk_ext, :] = ext[pl.ds(from_row, EXTRA), lanes]
             place0, place1 = places()
             full[:, :HD] = (
                 dot_tn(act_r[pl.ds(place0, half), :], gq[low, :])
@@ -598,100 +629,118 @@
             full[:, HD:] = (
                 dot_tn(a0[...], attn_r[low, :]) + dot_tn(a1[...], attn_r[high, :])
             ).astype(BF)
-            put_grads(full, 2, qo_m, qo_s, block)
-
-        kv_m, kv_s, qo_m, qo_s = call(
+            for out, steps in ((qo_m, (0, 1)), (qo_s, (2, 3))):
+                for i, step in enumerate(steps):
+                    out[i * block : (i + 1) * block, :] = take_block(full, step, block)
+
+        kv_k, kv_s, qo_m, qo_s = call(
             attn_weights, "attn_weights",
-            [shape((2 * blk_ext, kvw), BF)] * 2 + [shape((2 * block, kvw), BF)] * 2,
+            [shape((4 * blk_ext, HD), BF)] * 2 + [shape((2 * block, kvw), BF)] * 2,
             tok_parts
-            + [act, grad_q, grad_kv, ga_own, ga_oth, attn, part_keep, part_send]
-            + [ds_fo, ds_fi, ds_ao, ds_q, ds_k],
+            + [act, tie(grad_q, row_keep), grad_kv, ga_own, ga_oth, att_b]
+            + [part_keep, part_send, grad_hidden, ds_q, ds_k],
             scratch=[pltpu.VMEM((width, kvw), BF), pltpu.VMEM((n_fsdp * EXTRA, kvw), BF)],
             flops=2 * stream * width * kvw + 4 * n_q * width * HD, limit=limit,
         )
 
-        if two:
-            mine = part_keep + core_swap(part_send).astype(F32)
-        else:
-            mine = lax.psum_scatter(
-                jnp.concatenate([part_keep, part_send.astype(F32)], axis=0),
-                "context", scatter_dimension=0, tiled=True,
-            )
-        mine = mine.astype(BF)
-        start = (lax.axis_index("tensor") // 2) * half
-        kept = lax.dynamic_slice_in_dim(mine, start, half, 0)
-        give = lax.dynamic_slice_in_dim(mine, half - start, half, 0)
-        kept = (kept.astype(F32) + z_far(give).astype(F32)).astype(BF)
-
-        def last_norm(kept, near, tok, hid, gains, out):
-            grad = kept[...].astype(F32) + near[...].astype(F32)
-            hat, inv = rms_stats(tok[pl.ds(group_start(), half), :].astype(F32))
-            out[...] = (hid[...] + rms_back(grad, gains[0:1, :], hat, inv)).astype(BF)
-
-        (input_own,) = call(
-            last_norm, "last_norm", [wide_b], [kept, z_near(kept), tokens, grad_hidden, gw]
-        )
-
-        def join(own, oth, out):
-            out[pl.ds(group_start(), half), :] = own[...].astype(F32)
-            out[pl.ds(other_start(), half), :] = oth[...].astype(F32)
-
-        def both_groups(own, other, name):
-            return call(join, name, [shape((rows, width), F32)], [own, other])[0]
-
-        layer_output = both_groups(layer_own, layer_oth, "join_output")
-        grad_input = both_groups(input_own, z_far(input_own), "join_grad")
-
-        def scatter(kept, sent, first):
-            size = kept.shape[0] // 2
-            both = (kept.astype(F32) + fsdp_hop(sent, first).astype(F32)).astype(BF)
-            last = fsdp_hop(both[size:], 3 - first)
-            return across_pairs(both[:size].astype(F32) + last.astype(F32)).astype(BF)
-
-        def finish_ffn(x1, y1, x2, y2, g_out, u_out, d_out):
-            both = x1[...].astype(F32) + y1[...].astype(F32)
-            g_out[...] = both[:, :hidden]
-            u_out[:, :split] = both[:, hidden:]
-            both = x2[...].astype(F32) + y2[...].astype(F32)
-            u_out[:, split:] = both[:, : hidden - split]
-            d_out[...] = both[:, hidden - split :]
-
-        ffn_c1 = cross(scatter(ffn_m1, ffn_s1, 1))
-        ffn_c2 = cross(scatter(ffn_m2, ffn_s2, 2))
-        grad_gate, grad_up, grad_down = call(
-            finish_ffn, "finish_ffn",
-            [shape((block, hidden), F32)] * 3,
-            [ffn_c1, core_swap(ffn_c1), ffn_c2, core_swap(ffn_c2)],
-        )
-
-        kv_sum = scatter(kv_m, kv_s, 1)
-        qo_mine = cross(scatter(qo_m, qo_s, 2))
-        for move in (core_swap, z_near):
-            kv_sum = (kv_sum.astype(F32) + move(kv_sum).astype(F32)).astype(BF)
-
-        def finish_qo(x_ref, y_ref, q_out, o_out):
-            both = x_ref[...].astype(F32) + y_ref[...].astype(F32)
-            q_out[...] = both[:, :HD]
-            o_out[...] = both[:, HD:]
-
-        grad_wq, grad_wo = call(
-            finish_qo, "finish_qo", [shape((block, HD), F32)] * 2,
-            [qo_mine, core_swap(qo_mine)],
-        )
-
-        def finish_kv(x_ref, y_ref, k_out, v_out, *gain_outs):
-            both = x_ref[...].astype(F32) + y_ref[...].astype(F32)
-            k_out[...] = both[:block, :HD]
-            v_out[...] = both[:block, HD:]
+        def add(x, y):
+            return (x.astype(F32) + y.astype(F32)).astype(BF)
+
+        def last_add(both, hop):
+            size = both.shape[0] // 2
+            return across_pairs(both[:size].astype(F32) + hop.astype(F32)).astype(BF)
+
+        row_near = z_near(row_give)
+        kv_recv = core_swap(kv_s)
+        row_near, kv_recv = together(row_near, kv_recv)
+        kv_both = add(kv_k[: 2 * blk_ext], kv_recv[: 2 * blk_ext])
+        kv_h1 = fsdp_hop(add(kv_k[2 * blk_ext :], kv_recv[2 * blk_ext :]), 1)
+        qo_h1 = fsdp_hop(qo_s, 2)
+
+        def halve(kept, recv, keep_out, give_out):
+            group = lax.axis_index("tensor") // 2
+            for out, which in ((keep_out, group), (give_out, 1 - group)):
+                at = pl.ds(pl.multiple_of(which * quarter, quarter), quarter)
+                out[...] = (kept[at, :].astype(F32) + recv[at, :].astype(F32)).astype(BF)
+
+        small_b = shape((quarter, width), BF)
+        row_mine, row_far = call(halve, "halve_rows", [small_b, small_b], [row_keep, row_near])
+        row_far = z_far(row_far)
+        row_far, kv_h1, qo_h1, layer_oth, *ffn_hops = together(
+            row_far, kv_h1, qo_h1, layer_oth, *ffn_hops
+        )
+        ffn_mine = cross(sum_blocks([ffn_parts[0]] + ffn_hops))
+        kv_both = add(kv_both, kv_h1)
+        kv_h2 = fsdp_hop(kv_both[blk_ext:], 2)
+        qo_both = add(qo_m, qo_h1)
+        qo_h2 = fsdp_hop(qo_both[block:], 1)
+
+        def last_norm(kept, recv, tok, hid, out):
+            grad = kept[...].astype(F32) + recv[...].astype(F32)
+            inner = pl.multiple_of(near_at() * quarter, quarter)
+            at = pl.multiple_of(group_start() + inner, quarter)
+            hat, inv = rms_stats(tok[pl.ds(at, quarter), :].astype(F32))
+            hidden_part = hid[pl.ds(inner, quarter), :]
+            gain = hid[half + 3 : half + 4, :]
+            out[...] = (hidden_part + rms_back(grad, gain, hat, inv)).astype(BF)
+
+        (row_done,) = call(
+            last_norm, "last_norm", [small_b], [row_mine, row_far, tokens, grad_hidden]
+        )
+        row_fars, row_nears = z_far(row_done), z_near(row_done)
+        row_fars, row_nears, kv_h2, qo_h2 = together(row_fars, row_nears, kv_h2, qo_h2)
+        row_both = z_near(row_fars)
+        kv_sum = last_add(kv_both, kv_h2)
+        kv_n = z_near(kv_sum)
+        qo_c = cross(last_add(qo_both, qo_h2))
+        row_both, kv_n, ffn_mine = together(row_both, kv_n, ffn_mine)
+        kv_sum = add(kv_sum, kv_n)
+        kv_sum = add(kv_sum, z_far(kv_sum))
+        kv_other = core_swap(kv_sum)
+
+        qo_x, ffn_x = core_swap(qo_c), core_swap(ffn_mine)
+
+        def finish(
+            l0, l1, r0, r1, r2, r3, qx, qy, fx, fy, kx, ky,
+            layer_out, in_out, q_out, k_out, v_out, o_out, g_out, u_out, d_out, *gain_outs,
+        ):
+            layer_out[pl.ds(group_start(), half), :] = l0[...].astype(F32)
+            layer_out[pl.ds(other_start(), half), :] = l1[...].astype(F32)
+            group, near = lax.axis_index("tensor") // 2, near_at()
+            for ref, g, n in (
+                (r0, group, near), (r1, group, 1 - near),
+                (r2, 1 - group, near), (r3, 1 - group, 1 - near),
+            ):
+                at = pl.multiple_of(g * half + n * quarter, quarter)
+                in_out[pl.ds(at, quarter), :] = ref[...].astype(F32)
+            q_out[...] = qx[:, :HD].astype(F32) + qy[:, :HD].astype(F32)
+            o_out[...] = qx[:, HD:].astype(F32) + qy[:, HD:].astype(F32)
+            for i, out in enumerate((g_out, u_out, d_out)):
+                cols = slice(i * hidden, (i + 1) * hidden)
+                out[...] = fx[:, cols].astype(F32) + fy[:, cols].astype(F32)
+            first = lax.axis_index("context") % 2 == 0
+            mine, other = kx[...].astype(F32), ky[...].astype(F32)
+            left = jnp.where(first, mine, other)
+            right = jnp.where(first, other, mine)
+            k_out[...] = left[:block]
+            v_out[...] = right[:block]
             for i in range(4):
-                gain_outs[i][...] = both[block + i : block + i + 1, :block]
+                gain_outs[i][...] = left[block + i : block + i + 1, :block]
             for i in range(2):
-                gain_outs[4 + i][...] = both[block + i : block + i + 1, HD : HD + gblock]
-
-        grad_wk, grad_wv, *gain_grads = call(
-            finish_kv, "finish_kv",
-            [shape((block, HD), F32)] * 2 + [shape((1, block), F32)] * 4 + [shape((1, gblock), F32)] * 2,
-            [kv_sum, z_far(kv_sum)],
+                gain_outs[4 + i][...] = right[block + i : block + i + 1, :gblock]
+
+        (
+            layer_output, grad_input, grad_wq, grad_wk, grad_wv, grad_wo,
+            grad_gate, grad_up, grad_down, *gain_grads,
+        ) = call(
+            finish, "finish",
+            [shape((rows, width), F32)] * 2 + [shape((block, HD), F32)] * 4
+            + [shape((block, hidden), F32)] * 3 + [shape((1, block), F32)] * 4
+            + [shape((1, gblock), F32)] * 2,
+            [
+                layer_own, layer_oth, row_done, row_nears, row_fars, row_both,
+                qo_c, qo_x, ffn_mine, ffn_x, kv_sum, kv_other,
+            ],
         )
         return (
             layer_output, grad_input, grad_wq, grad_wk, grad_wv, grad_wo.T,

time: 154 us -> 145 us (0.942)
  waiting for transfers between devices: 54 us -> 64.8 us
  Pallas kernels: 21.9 us -> 14.7 us
  local copies, waits for them, and re-layouts: 8.48 us -> 1.66 us
  starting transfers between devices: 65 us -> 61.9 us
  other arithmetic: 3 us -> 0.67 us
    ppermute x5 -> x7, starting transfers between devices: 5.19 us -> 14.4 us  [z_near(): return lax.ppermute(value, 'tensor', [(i, i ^ 1) for i in range(n_tensor)])]
    ppermute x4, starting transfers between devices: 14.7 us -> 6.25 us  [z_far(): return lax.ppermute(value, 'tensor', [(i, i ^ 2) for i in range(n_tensor)])]
    pallas_call x16 -> x14, Pallas kernels: 21.9 us -> 14.7 us  [call(): pl.pallas_call(wrapped, name=name, out_shape=tuple(outs), in_specs=[smem]...]
    unnamed x58 -> x10, local copies, waits for them, and re-layouts: 8.39 us -> 1.64 us
    ppermute x5 -> x7, waiting for transfers between devices: 9.3 us -> 13.7 us  [z_near(): return lax.ppermute(value, 'tensor', [(i, i ^ 1) for i in range(n_tensor)])]
    ppermute x12, starting transfers between devices: 19.2 us -> 14.8 us  [core_swap(): lax.ppermute(value, 'context', [(i, i ^ 1) for i in range(n_context)])]
    ppermute x4, waiting for transfers between devices: 9.97 us -> 12.4 us  [z_far(): return lax.ppermute(value, 'tensor', [(i, i ^ 2) for i in range(n_tensor)])]
    convert_element_type x12 -> x8, other arithmetic: 2.89 us -> 0.57 us  [the longest x5 0.25 us: add(): return (x.astype(F32) + y.astype(F32)).astype(BF)]
  transfers between devices with their start and end apart: 47 -> 47, of which waited for: 17 -> 25; matrix products, arithmetic and copies ran while one was open for 2% -> 0% of each run, Pallas kernels for 7% -> 2%
where the time goes in v3:
time: 145 us
  waiting for transfers between devices  64.8 us (45%)
  starting transfers between devices  61.9 us (43%)
  Pallas kernels  14.7 us (10%)
  local copies, waits for them, and re-layouts  1.66 us (1%)
    ppermute x19, waiting for transfers between devices, fsdp_hop(): return lax.ppermute(value, 'fsdp', [(i, i ^ step) for i in range(n_fsdp)])  32.1 us
    ppermute x19, starting transfers between devices, fsdp_hop(): return lax.ppermute(value, 'fsdp', [(i, i ^ step) for i in range(n_fsdp)])  23 us
    ppermute x12, starting transfers between devices, core_swap(): lax.ppermute(value, 'context', [(i, i ^ 1) for i in range(n_context)])  14.8 us
    pallas_call x14, Pallas kernels, call(): pl.pallas_call(wrapped, name=name, out_shape=tuple(outs), in_specs=[smem]...  14.7 us
    ppermute x7, starting transfers between devices, z_near(): return lax.ppermute(value, 'tensor', [(i, i ^ 1) for i in range(n_tensor)])  14.4 us
    ppermute x7, waiting for transfers between devices, z_near(): return lax.ppermute(value, 'tensor', [(i, i ^ 1) for i in range(n_tensor)])  13.7 us
    ppermute x4, waiting for transfers between devices, z_far(): return lax.ppermute(value, 'tensor', [(i, i ^ 2) for i in range(n_tensor)])  12.4 us
    ppermute x12, waiting for transfers between devices, core_swap(): lax.ppermute(value, 'context', [(i, i ^ 1) for i in range(n_context)])  6.55 us
  transfers between devices with their start and end apart: 47, of which 25 were waited for; matrix products, arithmetic and copies ran while one was open for 0% of the time, Pallas kernels for 2%

profile of v3, /device:TPU:0, one launch (start us, length us, event | category | flops | bytes accessed | tf_op | source)
XLA Modules:
  0.0 144.8 jit_solution(1827881700828638766)
XLA Ops:
  1.8 1.9 %pack.1 = (bf16[176,512]{1,0:T(8,128)(2,1)S(1)}, bf16[160,512]{1,0:T(8,128)(2,1)S(1)}, bf16[160,768]{1,0:T(8,128)(2,1)S(1)}, bf16[160,768]{1,0:T(8,128)(2,1)S(1)...) custom-call(s32[1,4]{1,0:T(1,128)S(1)} %copy-done.3, bf16[160,256]{1,0:T(8,128)(2,1)} %refs_1_.2, ...), custom_call_target="tpu_custom_call" | custom-call | bytes 1359872 | tf_op jit(solution)/shard_map/pack/pallas_call | solution.py:79
  5.1 2.6 %collective-permute-start.1 = (bf16[176,512]{1,0:T(8,128)(2,1)S(1)}, bf16[176,512]{1,0:T(8,128)(2,1)S(1)}, u32[]{:S(2)}, u32[]{:S(2)}) collective-permute-start(bf16[176,512]{1,0:T(8,128)(2,1)S(1)} %get-tuple-element.108.refs_3_), channel_id=1, source_target_pairs={{0,8},{8,0},{16,24},{24,16},{1,9},{9,1},{17,25},{25,17},{2,10},{10... | collective-permute-start | bytes 540680 | tf_op jit(solution)/shard_map/ppermute | solution.py:122
  7.7 1.5 %collective-permute-start.6 = (bf16[160,512]{1,0:T(8,128)(2,1)S(1)}, bf16[160,512]{1,0:T(8,128)(2,1)S(1)}, u32[]{:S(2)}, u32[]{:S(2)}) collective-permute-start(bf16[160,512]{1,0:T(8,128)(2,1)S(1)} %collective-permute-done.4.refs_7_), channel_id=1, source_target_pairs={{0,16},{8,24},{16,0},{24,8},{1,17},{9,25},{17,1},{25,9},{2,18},{10... | collective-permute-start | bytes 491528 | tf_op jit(solution)/shard_map/ppermute | solution.py:122
  11.2 2.0 %collective-permute-start.3 = (bf16[176,512]{1,0:T(8,128)(2,1)S(1)}, bf16[176,512]{1,0:T(8,128)(2,1)S(1)}, u32[]{:S(2)}, u32[]{:S(2)}) collective-permute-start(bf16[176,512]{1,0:T(8,128)(2,1)S(1)} %collective-permute-done.1.refs_4_), channel_id=1, source_target_pairs={{0,16},{8,24},{16,0},{24,8},{1,17},{9,25},{17,1},{25,9},{2,18},{10... | collective-permute-start | bytes 540680 | tf_op jit(solution)/shard_map/ppermute | solution.py:122
  13.2 1.5 %collective-permute-start.5 = (bf16[160,512]{1,0:T(8,128)(2,1)S(1)}, bf16[160,512]{1,0:T(8,128)(2,1)S(1)}, u32[]{:S(2)}, u32[]{:S(2)}) collective-permute-start(bf16[160,512]{1,0:T(8,128)(2,1)S(1)} %collective-permute-done.4.refs_7_), channel_id=1, source_target_pairs={{0,8},{8,0},{16,24},{24,16},{1,9},{9,1},{17,25},{25,17},{2,10},{10... | collective-permute-start | bytes 491528 | tf_op jit(solution)/shard_map/ppermute | solution.py:122
  15.4 3.1 %collective-permute-done.5.refs_8_ = bf16[160,512]{1,0:T(8,128)(2,1)S(1)} collective-permute-done((bf16[160,512]{1,0:T(8,128)(2,1)S(1)}, bf16[160,512]{1,0:T(8,128)(2,1)S(1)}, u32[]{:S(2)}, u32[]{:S(2)}) %collective-permute-start.5) | collective-permute-done | bytes 163872 | tf_op jit(solution)/shard_map/ppermute | solution.py:122
  18.5 1.8 %collective-permute-done.7.refs_10_ = bf16[160,512]{1,0:T(8,128)(2,1)S(1)} collective-permute-done((bf16[160,512]{1,0:T(8,128)(2,1)S(1)}, bf16[160,512]{1,0:T(8,128)(2,1)S(1)}, u32[]{:S(2)}, u32[]{:S(2)}) %collective-permute-start.7) | collective-permute-done | bytes 163872 | tf_op jit(solution)/shard_map/ppermute | solution.py:122
  21.3 2.3 %front.1 = (bf16[512,640]{1,0:T(8,128)(2,1)S(1)}, bf16[1536,256]{1,0:T(8,128)(2,1)S(1)}, f32[1032,256]{1,0:T(8,128)S(1)}, bf16[640,1024]{1,0:T(8,128)(2,1)S(1)},...) custom-call(s32[1,4]{1,0:T(1,128)S(1)} %copy-done.3, bf16[256,640]{1,0:T(8,128)(2,1)S(1)} %copy-done, ...), custom_call_target="tpu_custom_call" | custom-call | flops 469762048 | bytes 6877184 | tf_op jit(solution)/shard_map/front/pallas_call | solution.py:79
  23.6 6.2 %collective-permute-start.10 = (bf16[128,640]{1,0:T(8,128)(2,1)S(1)}, bf16[128,640]{1,0:T(8,128)(2,1)S(1)}, u32[]{:S(2)}, u32[]{:S(2)}) collective-permute-start(bf16[128,640]{1,0:T(8,128)(2,1)S(1)} %get-tuple-element.116), channel_id=1, source_target_pairs={{0,4},{4,0},{1,5},{5,1},{2,6},{6,2},{3,7},{7,3},{8,12},{12,8},{9,1... | collective-permute-start | bytes 491528 | tf_op jit(solution)/shard_map/ppermute | solution.py:104
  29.7 1.5 %collective-permute-start.13 = (bf16[160,768]{1,0:T(8,128)(2,1)S(1)}, bf16[160,768]{1,0:T(8,128)(2,1)S(1)}, u32[]{:S(2)}, u32[]{:S(2)}) collective-permute-start(bf16[160,768]{1,0:T(8,128)(2,1)S(1)} %collective-permute-done.8.refs_2_), channel_id=1, source_target_pairs={{0,8},{8,0},{16,24},{24,16},{1,9},{9,1},{17,25},{25,17},{2,10},{10... | collective-permute-start | bytes 737288 | tf_op jit(solution)/shard_map/ppermute | solution.py:122
  31.2 1.5 %collective-permute-start.17 = (bf16[160,768]{1,0:T(8,128)(2,1)S(1)}, bf16[160,768]{1,0:T(8,128)(2,1)S(1)}, u32[]{:S(2)}, u32[]{:S(2)}) collective-permute-start(bf16[160,768]{1,0:T(8,128)(2,1)S(1)} %collective-permute-done.9.refs_6_), channel_id=1, source_target_pairs={{0,16},{8,24},{16,0},{24,8},{1,17},{9,25},{17,1},{25,9},{2,18},{10... | collective-permute-start | bytes 737288 | tf_op jit(solution)/shard_map/ppermute | solution.py:122
  32.8 4.4 %collective-permute-start.11 = (bf16[128,640]{1,0:T(8,128)(2,1)S(1)}, bf16[128,640]{1,0:T(8,128)(2,1)S(1)}, u32[]{:S(2)}, u32[]{:S(2)}) collective-permute-start(bf16[128,640]{1,0:T(8,128)(2,1)S(1)} %add_convert_fusion.8.refs_0_), channel_id=1, source_target_pairs={{0,1},{1,0},{2,3},{3,2},{4,5},{5,4},{6,7},{7,6},{8,9},{9,8},{10,11... | collective-permute-start | bytes 491528 | tf_op jit(solution)/shard_map/ppermute | solution.py:107
  37.2 1.5 %collective-permute-start.14 = (bf16[160,768]{1,0:T(8,128)(2,1)S(1)}, bf16[160,768]{1,0:T(8,128)(2,1)S(1)}, u32[]{:S(2)}, u32[]{:S(2)}) collective-permute-start(bf16[160,768]{1,0:T(8,128)(2,1)S(1)} %collective-permute-done.8.refs_2_), channel_id=1, source_target_pairs={{0,16},{8,24},{16,0},{24,8},{1,17},{9,25},{17,1},{25,9},{2,18},{10... | collective-permute-start | bytes 737288 | tf_op jit(solution)/shard_map/ppermute | solution.py:122
  39.8 1.5 %collective-permute-start.18 = (bf16[160,768]{1,0:T(8,128)(2,1)S(1)}, bf16[160,768]{1,0:T(8,128)(2,1)S(1)}, u32[]{:S(2)}, u32[]{:S(2)}) collective-permute-start(bf16[160,768]{1,0:T(8,128)(2,1)S(1)} %collective-permute-done.17.refs_8_), channel_id=1, source_target_pairs={{0,8},{8,0},{16,24},{24,16},{1,9},{9,1},{17,25},{25,17},{2,10},{10... | collective-permute-start | bytes 737288 | tf_op jit(solution)/shard_map/ppermute | solution.py:122
  41.6 4.5 %collective-permute-done.14.refs_4_ = bf16[160,768]{1,0:T(8,128)(2,1)S(1)} collective-permute-done((bf16[160,768]{1,0:T(8,128)(2,1)S(1)}, bf16[160,768]{1,0:T(8,128)(2,1)S(1)}, u32[]{:S(2)}, u32[]{:S(2)}) %collective-permute-start.14) | collective-permute-done | bytes 245792 | tf_op jit(solution)/shard_map/ppermute | solution.py:122
  46.1 1.5 %collective-permute-done.16.refs_7_ = bf16[160,768]{1,0:T(8,128)(2,1)S(1)} collective-permute-done((bf16[160,768]{1,0:T(8,128)(2,1)S(1)}, bf16[160,768]{1,0:T(8,128)(2,1)S(1)}, u32[]{:S(2)}, u32[]{:S(2)}) %collective-permute-start.16) | collective-permute-done | bytes 245792 | tf_op jit(solution)/shard_map/ppermute | solution.py:122
  47.6 2.0 %collective-permute-done.15.refs_5_ = bf16[160,768]{1,0:T(8,128)(2,1)S(1)} collective-permute-done((bf16[160,768]{1,0:T(8,128)(2,1)S(1)}, bf16[160,768]{1,0:T(8,128)(2,1)S(1)}, u32[]{:S(2)}, u32[]{:S(2)}) %collective-permute-start.15) | collective-permute-done | bytes 245792 | tf_op jit(solution)/shard_map/ppermute | solution.py:122
  52.1 1.4 collective-permute-done.19
  53.5 4.1 %collective-permute-start.20 = (bf16[128,640]{1,0:T(8,128)(2,1)S(1)}, bf16[128,640]{1,0:T(8,128)(2,1)S(1)}, u32[]{:S(2)}, u32[]{:S(2)}) collective-permute-start(bf16[128,640]{1,0:T(8,128)(2,1)S(1)} %add_convert_fusion.7.refs_0_), channel_id=1, source_target_pairs={{0,1},{1,0},{2,3},{3,2},{4,5},{5,4},{6,7},{7,6},{8,9},{9,8},{10,11... | collective-permute-start | bytes 491528 | tf_op jit(solution)/shard_map/ppermute | solution.py:107
  57.6 4.5 %collective-permute-done.20.refs_1_ = bf16[128,640]{1,0:T(8,128)(2,1)S(1)} collective-permute-done((bf16[128,640]{1,0:T(8,128)(2,1)S(1)}, bf16[128,640]{1,0:T(8,128)(2,1)S(1)}, u32[]{:S(2)}, u32[]{:S(2)}) %collective-permute-start.20) | collective-permute-done | bytes 163872 | tf_op jit(solution)/shard_map/ppermute | solution.py:107
  62.4 1.4 collective-permute-done.21.refs_1_.refs_3_
  63.8 1.3 ffn_back.1
  66.7 1.8 %collective-permute-start.23 = (bf16[128,640]{1,0:T(8,128)(2,1)S(1)}, bf16[128,640]{1,0:T(8,128)(2,1)S(1)}, u32[]{:S(2)}, u32[]{:S(2)}) collective-permute-start(bf16[128,640]{1,0:T(8,128)(2,1)S(1)} %add_convert_fusion.6.refs_0_), channel_id=1, source_target_pairs={{0,1},{1,0},{2,3},{3,2},{4,5},{5,4},{6,7},{7,6},{8,9},{9,8},{10,11... | collective-permute-start | bytes 491528 | tf_op jit(solution)/shard_map/ppermute | solution.py:107
  68.5 4.5 %collective-permute-done.23.refs_1_ = bf16[128,640]{1,0:T(8,128)(2,1)S(1)} collective-permute-done((bf16[128,640]{1,0:T(8,128)(2,1)S(1)}, bf16[128,640]{1,0:T(8,128)(2,1)S(1)}, u32[]{:S(2)}, u32[]{:S(2)}) %collective-permute-start.23) | collective-permute-done | bytes 163872 | tf_op jit(solution)/shard_map/ppermute | solution.py:107
  73.5 1.4 ffn_weights.1
  74.9 2.5 %attn_back.1 = (bf16[256,256]{1,0:T(8,128)(2,1)S(1)}, bf16[512,512]{1,0:T(8,128)(2,1)S(1)}, f32[256,640]{1,0:T(8,128)S(1)}, bf16[256,640]{1,0:T(8,128)(2,1)S(1)}...) custom-call(s32[1,4]{1,0:T(1,128)S(1)} %copy-done.4, bf16[128,640]{1,0:T(8,128)(2,1)S(1)} %get-tuple-element.136.refs_1_.refs_5_, ...), custom_call_target="tpu_custom_call" | custom-call | flops 671088640 | bytes 5646336 | tf_op jit(solution)/shard_map/attn_back/pallas_call | solution.py:79
  77.9 1.3 collective-permute-done.25.refs_1_
  80.8 1.7 %collective-permute-start.26 = (bf16[128,640]{1,0:T(8,128)(2,1)S(1)}, bf16[128,640]{1,0:T(8,128)(2,1)S(1)}, u32[]{:S(2)}, u32[]{:S(2)}) collective-permute-start(bf16[128,640]{1,0:T(8,128)(2,1)S(1)} %get-tuple-element.145), channel_id=1, source_target_pairs={{0,1},{1,0},{2,3},{3,2},{4,5},{5,4},{6,7},{7,6},{8,9},{9,8},{10,11... | collective-permute-start | bytes 491528 | tf_op jit(solution)/shard_map/ppermute | solution.py:107
  83.1 1.5 %collective-permute-start.34 = (bf16[160,1536]{1,0:T(8,128)(2,1)S(1)}, bf16[160,1536]{1,0:T(8,128)(2,1)S(1)}, u32[]{:S(2)}, u32[]{:S(2)}) collective-permute-start(bf16[160,1536]{1,0:T(8,128)(2,1)S(1)} %get-tuple-element.158), channel_id=1, source_target_pairs={{0,24},{8,16},{16,8},{24,0},{1,25},{9,17},{17,9},{25,1},{2,26},{10... | collective-permute-start | bytes 1474568 | tf_op jit(solution)/shard_map/ppermute | solution.py:122
  84.5 1.5 %collective-permute-start.32 = (bf16[160,1536]{1,0:T(8,128)(2,1)S(1)}, bf16[160,1536]{1,0:T(8,128)(2,1)S(1)}, u32[]{:S(2)}, u32[]{:S(2)}) collective-permute-start(bf16[160,1536]{1,0:T(8,128)(2,1)S(1)} %get-tuple-element.139), channel_id=1, source_target_pairs={{0,8},{8,0},{16,24},{24,16},{1,9},{9,1},{17,25},{25,17},{2,10},{10... | collective-permute-start | bytes 1474568 | tf_op jit(solution)/shard_map/ppermute | solution.py:122
  87.0 2.1 %collective-permute-start.31 = (bf16[128,640]{1,0:T(8,128)(2,1)S(1)}, bf16[128,640]{1,0:T(8,128)(2,1)S(1)}, u32[]{:S(2)}, u32[]{:S(2)}) collective-permute-start(bf16[128,640]{1,0:T(8,128)(2,1)S(1)} %get-tuple-element.131.refs_0_), channel_id=1, source_target_pairs={{0,2},{1,3},{2,0},{3,1},{4,6},{5,7},{6,4},{7,5},{8,10},{9,11},{10,... | collective-permute-start | bytes 491528 | tf_op jit(solution)/shard_map/ppermute | solution.py:110
  89.1 1.2 collective-permute-start.30
  90.4 6.5 %collective-permute-done.31.refs_1_ = bf16[128,640]{1,0:T(8,128)(2,1)S(1)} collective-permute-done((bf16[128,640]{1,0:T(8,128)(2,1)S(1)}, bf16[128,640]{1,0:T(8,128)(2,1)S(1)}, u32[]{:S(2)}, u32[]{:S(2)}) %collective-permute-start.31) | collective-permute-done | bytes 163872 | tf_op jit(solution)/shard_map/ppermute | solution.py:110
  97.5 9.7 %collective-permute-done.33 = bf16[160,1536]{1,0:T(8,128)(2,1)S(1)} collective-permute-done((bf16[160,1536]{1,0:T(8,128)(2,1)S(1)}, bf16[160,1536]{1,0:T(8,128)(2,1)S(1)}, u32[]{:S(2)}, u32[]{:S(2)}) %collective-permute-start.33) | collective-permute-done | bytes 491552 | tf_op jit(solution)/shard_map/ppermute | solution.py:122
  107.2 2.1 %collective-permute-start.28 = (bf16[64,640]{1,0:T(8,128)(2,1)S(1)}, bf16[64,640]{1,0:T(8,128)(2,1)S(1)}, u32[]{:S(2)}, u32[]{:S(2)}) collective-permute-start(bf16[64,640]{1,0:T(8,128)(2,1)S(1)} %get-tuple-element.153), channel_id=1, source_target_pairs={{0,2},{1,3},{2,0},{3,1},{4,6},{5,7},{6,4},{7,5},{8,10},{9,11},{10,... | collective-permute-start | bytes 245768 | tf_op jit(solution)/shard_map/ppermute | solution.py:110
  109.3 3.8 %collective-permute-done.30 = bf16[320,512]{1,0:T(8,128)(2,1)S(1)} collective-permute-done((bf16[320,512]{1,0:T(8,128)(2,1)S(1)}, bf16[320,512]{1,0:T(8,128)(2,1)S(1)}, u32[]{:S(2)}, u32[]{:S(2)}) %collective-permute-start.30) | collective-permute-done | bytes 327712 | tf_op jit(solution)/shard_map/ppermute | solution.py:122
  113.7 2.1 %collective-permute-start.35 = (bf16[64,640]{1,0:T(8,128)(2,1)S(1)}, bf16[64,640]{1,0:T(8,128)(2,1)S(1)}, u32[]{:S(2)}, u32[]{:S(2)}) collective-permute-start(bf16[64,640]{1,0:T(8,128)(2,1)S(1)} %last_norm.1.refs_2_), channel_id=1, source_target_pairs={{0,2},{1,3},{2,0},{3,1},{4,6},{5,7},{6,4},{7,5},{8,10},{9,11},{10,... | collective-permute-start | bytes 245768 | tf_op jit(solution)/shard_map/ppermute | solution.py:110
  115.8 1.3 collective-permute-start.37
  119.1 1.3 collective-permute-done.37
  120.4 2.2 %collective-permute-done.38 = bf16[160,512]{1,0:T(8,128)(2,1)S(1)} collective-permute-done((bf16[160,512]{1,0:T(8,128)(2,1)S(1)}, bf16[160,512]{1,0:T(8,128)(2,1)S(1)}, u32[]{:S(2)}, u32[]{:S(2)}) %collective-permute-start.38) | collective-permute-done | bytes 163872 | tf_op jit(solution)/shard_map/ppermute | solution.py:122
  122.6 1.7 %collective-permute-start.39 = (bf16[64,640]{1,0:T(8,128)(2,1)S(1)}, bf16[64,640]{1,0:T(8,128)(2,1)S(1)}, u32[]{:S(2)}, u32[]{:S(2)}) collective-permute-start(bf16[64,640]{1,0:T(8,128)(2,1)S(1)} %collective-permute-done.35.refs_4_), channel_id=1, source_target_pairs={{0,1},{1,0},{2,3},{3,2},{4,5},{5,4},{6,7},{7,6},{8,9},{9,8},{10,11... | collective-permute-start | bytes 245768 | tf_op jit(solution)/shard_map/ppermute | solution.py:107
  125.5 1.8 %collective-permute-done.39.refs_5_ = bf16[64,640]{1,0:T(8,128)(2,1)S(1)} collective-permute-done((bf16[64,640]{1,0:T(8,128)(2,1)S(1)}, bf16[64,640]{1,0:T(8,128)(2,1)S(1)}, u32[]{:S(2)}, u32[]{:S(2)}) %collective-permute-start.39) | collective-permute-done | bytes 81952 | tf_op jit(solution)/shard_map/ppermute | solution.py:107
  127.3 1.9 %collective-permute-done.40 = bf16[176,256]{1,0:T(8,128)(2,1)S(1)} collective-permute-done((bf16[176,256]{1,0:T(8,128)(2,1)S(1)}, bf16[176,256]{1,0:T(8,128)(2,1)S(1)}, u32[]{:S(2)}, u32[]{:S(2)}) %collective-permute-start.40) | collective-permute-done | bytes 90144 | tf_op jit(solution)/shard_map/ppermute | solution.py:107
  129.2 4.9 %collective-permute-start.44 = (bf16[160,1536]{1,0:T(8,128)(2,1)S(1)}, bf16[160,1536]{1,0:T(8,128)(2,1)S(1)}, u32[]{:S(2)}, u32[]{:S(2)}) collective-permute-start(bf16[160,1536]{1,0:T(8,128)(2,1)S(1)} %collective-permute-done.41.refs_8_), channel_id=1, source_target_pairs={{0,4},{4,0},{1,5},{5,1},{2,6},{6,2},{3,7},{7,3},{8,12},{12,8},{9,1... | collective-permute-start | bytes 1474568 | tf_op jit(solution)/shard_map/ppermute | solution.py:104
  134.3 1.6 %collective-permute-start.43 = (bf16[160,512]{1,0:T(8,128)(2,1)S(1)}, bf16[160,512]{1,0:T(8,128)(2,1)S(1)}, u32[]{:S(2)}, u32[]{:S(2)}) collective-permute-start(bf16[160,512]{1,0:T(8,128)(2,1)S(1)} %collective-permute-done.42.refs_6_), channel_id=1, source_target_pairs={{0,4},{4,0},{1,5},{5,1},{2,6},{6,2},{3,7},{7,3},{8,12},{12,8},{9,1... | collective-permute-start | bytes 491528 | tf_op jit(solution)/shard_map/ppermute | solution.py:104
  135.9 5.7 %collective-permute-done.45 = bf16[176,256]{1,0:T(8,128)(2,1)S(1)} collective-permute-done((bf16[176,256]{1,0:T(8,128)(2,1)S(1)}, bf16[176,256]{1,0:T(8,128)(2,1)S(1)}, u32[]{:S(2)}, u32[]{:S(2)}) %collective-permute-start.45) | collective-permute-done | bytes 90144 | tf_op jit(solution)/shard_map/ppermute | solution.py:110
  141.7 1.3 collective-permute-done.46.refs_11_
  143.0 1.8 %finish.1 = (f32[256,640]{1,0:T(8,128)}, f32[256,640]{1,0:T(8,128)}, f32[160,256]{1,0:T(8,128)}, f32[160,256]{1,0:T(8,128)}, f32[160,256]{1,0:T(8,128)}, /*index...) custom-call(bf16[128,640]{1,0:T(8,128)(2,1)S(1)} %get-tuple-element., ...), custom_call_target="tpu_custom_call" | custom-call | bytes 5098496 | tf_op jit(solution)/shard_map/finish/pallas_call | solution.py:79
  (83 shorter events, 20.7 us)
Async XLA Ops:
  0.6 3.1 %collective-permute-start = (bf16[256,640]{1,0:T(8,128)(2,1)}, bf16[256,640]{1,0:T(8,128)(2,1)S(1)}, u32[]{:S(2)}, u32[]{:S(2)}) collective-permute-start(bf16[256,640]{1,0:T(8,128)(2,1)} %refs_2_.5), channel_id=1, source_target_pairs={{0,4},{4,0},{1,5},{5,1},{2,6},{6,2},{3,7},{7,3},{8,12},{12,8},{9,1... | collective-permute-start | bytes 983048 | tf_op jit(solution)/shard_map/ppermute | solution.py:104
  3.7 3.9 %collective-permute-start.4 = (bf16[160,512]{1,0:T(8,128)(2,1)S(1)}, bf16[160,512]{1,0:T(8,128)(2,1)S(1)}, u32[]{:S(2)}, u32[]{:S(2)}) collective-permute-start(bf16[160,512]{1,0:T(8,128)(2,1)S(1)} %get-tuple-element.109), channel_id=1, source_target_pairs={{0,0},{1,1},{2,4},{3,5},{4,2},{5,3},{6,6},{7,7},{8,8},{9,9},{10,12... | collective-permute-start | bytes 491528 | tf_op jit(solution)/shard_map/ppermute | solution.py:119
  4.4 8.8 %collective-permute-start.8 = (bf16[160,768]{1,0:T(8,128)(2,1)S(1)}, bf16[160,768]{1,0:T(8,128)(2,1)S(1)}, u32[]{:S(2)}, u32[]{:S(2)}) collective-permute-start(bf16[160,768]{1,0:T(8,128)(2,1)S(1)} %get-tuple-element.111), channel_id=1, source_target_pairs={{0,0},{1,1},{2,4},{3,5},{4,2},{5,3},{6,6},{7,7},{8,8},{9,9},{10,12... | collective-permute-start | bytes 737288 | tf_op jit(solution)/shard_map/ppermute | solution.py:119
  5.1 6.0 %collective-permute-start.1 = (bf16[176,512]{1,0:T(8,128)(2,1)S(1)}, bf16[176,512]{1,0:T(8,128)(2,1)S(1)}, u32[]{:S(2)}, u32[]{:S(2)}) collective-permute-start(bf16[176,512]{1,0:T(8,128)(2,1)S(1)} %get-tuple-element.108.refs_3_), channel_id=1, source_target_pairs={{0,8},{8,0},{16,24},{24,16},{1,9},{9,1},{17,25},{25,17},{2,10},{10... | collective-permute-start | bytes 540680 | tf_op jit(solution)/shard_map/ppermute | solution.py:122
  7.7 7.0 %collective-permute-start.6 = (bf16[160,512]{1,0:T(8,128)(2,1)S(1)}, bf16[160,512]{1,0:T(8,128)(2,1)S(1)}, u32[]{:S(2)}, u32[]{:S(2)}) collective-permute-start(bf16[160,512]{1,0:T(8,128)(2,1)S(1)} %collective-permute-done.4.refs_7_), channel_id=1, source_target_pairs={{0,16},{8,24},{16,0},{24,8},{1,17},{9,25},{17,1},{25,9},{2,18},{10... | collective-permute-start | bytes 491528 | tf_op jit(solution)/shard_map/ppermute | solution.py:122
  9.2 6.0 %collective-permute-start.9 = (bf16[160,768]{1,0:T(8,128)(2,1)S(1)}, bf16[160,768]{1,0:T(8,128)(2,1)S(1)}, u32[]{:S(2)}, u32[]{:S(2)}) collective-permute-start(bf16[160,768]{1,0:T(8,128)(2,1)S(1)} %get-tuple-element.112), channel_id=1, source_target_pairs={{0,0},{1,1},{2,4},{3,5},{4,2},{5,3},{6,6},{7,7},{8,8},{9,9},{10,12... | collective-permute-start | bytes 737288 | tf_op jit(solution)/shard_map/ppermute | solution.py:119
  9.9 5.6 %collective-permute-start.2 = (bf16[176,512]{1,0:T(8,128)(2,1)S(1)}, bf16[176,512]{1,0:T(8,128)(2,1)S(1)}, u32[]{:S(2)}, u32[]{:S(2)}) collective-permute-start(bf16[176,512]{1,0:T(8,128)(2,1)S(1)} %get-tuple-element.108.refs_3_), channel_id=1, source_target_pairs={{0,16},{8,24},{16,0},{24,8},{1,17},{9,25},{17,1},{25,9},{2,18},{10... | collective-permute-start | bytes 540680 | tf_op jit(solution)/shard_map/ppermute | solution.py:122
  11.2 7.4 %collective-permute-start.3 = (bf16[176,512]{1,0:T(8,128)(2,1)S(1)}, bf16[176,512]{1,0:T(8,128)(2,1)S(1)}, u32[]{:S(2)}, u32[]{:S(2)}) collective-permute-start(bf16[176,512]{1,0:T(8,128)(2,1)S(1)} %collective-permute-done.1.refs_4_), channel_id=1, source_target_pairs={{0,16},{8,24},{16,0},{24,8},{1,17},{9,25},{17,1},{25,9},{2,18},{10... | collective-permute-start | bytes 540680 | tf_op jit(solution)/shard_map/ppermute | solution.py:122
  13.2 5.3 %collective-permute-start.5 = (bf16[160,512]{1,0:T(8,128)(2,1)S(1)}, bf16[160,512]{1,0:T(8,128)(2,1)S(1)}, u32[]{:S(2)}, u32[]{:S(2)}) collective-permute-start(bf16[160,512]{1,0:T(8,128)(2,1)S(1)} %collective-permute-done.4.refs_7_), channel_id=1, source_target_pairs={{0,8},{8,0},{16,24},{24,16},{1,9},{9,1},{17,25},{25,17},{2,10},{10... | collective-permute-start | bytes 491528 | tf_op jit(solution)/shard_map/ppermute | solution.py:122
  14.7 5.6 %collective-permute-start.7 = (bf16[160,512]{1,0:T(8,128)(2,1)S(1)}, bf16[160,512]{1,0:T(8,128)(2,1)S(1)}, u32[]{:S(2)}, u32[]{:S(2)}) collective-permute-start(bf16[160,512]{1,0:T(8,128)(2,1)S(1)} %collective-permute-done.6.refs_9_), channel_id=1, source_target_pairs={{0,8},{8,0},{16,24},{24,16},{1,9},{9,1},{17,25},{25,17},{2,10},{10... | collective-permute-start | bytes 491528 | tf_op jit(solution)/shard_map/ppermute | solution.py:122
  21.3 20.0 %copy-start.1 = (bf16[256,640]{1,0:T(8,128)(2,1)S(1)}, bf16[256,640]{1,0:T(8,128)(2,1)}, u32[]{:S(2)}) copy-start(bf16[256,640]{1,0:T(8,128)(2,1)} %refs_2_.5) | copy-start | bytes 983044
  23.6 9.2 %collective-permute-start.10 = (bf16[128,640]{1,0:T(8,128)(2,1)S(1)}, bf16[128,640]{1,0:T(8,128)(2,1)S(1)}, u32[]{:S(2)}, u32[]{:S(2)}) collective-permute-start(bf16[128,640]{1,0:T(8,128)(2,1)S(1)} %get-tuple-element.116), channel_id=1, source_target_pairs={{0,4},{4,0},{1,5},{5,1},{2,6},{6,2},{3,7},{7,3},{8,12},{12,8},{9,1... | collective-permute-start | bytes 491528 | tf_op jit(solution)/shard_map/ppermute | solution.py:104
  29.7 9.5 %collective-permute-start.13 = (bf16[160,768]{1,0:T(8,128)(2,1)S(1)}, bf16[160,768]{1,0:T(8,128)(2,1)S(1)}, u32[]{:S(2)}, u32[]{:S(2)}) collective-permute-start(bf16[160,768]{1,0:T(8,128)(2,1)S(1)} %collective-permute-done.8.refs_2_), channel_id=1, source_target_pairs={{0,8},{8,0},{16,24},{24,16},{1,9},{9,1},{17,25},{25,17},{2,10},{10... | collective-permute-start | bytes 737288 | tf_op jit(solution)/shard_map/ppermute | solution.py:122
  31.2 8.6 %collective-permute-start.17 = (bf16[160,768]{1,0:T(8,128)(2,1)S(1)}, bf16[160,768]{1,0:T(8,128)(2,1)S(1)}, u32[]{:S(2)}, u32[]{:S(2)}) collective-permute-start(bf16[160,768]{1,0:T(8,128)(2,1)S(1)} %collective-permute-done.9.refs_6_), channel_id=1, source_target_pairs={{0,16},{8,24},{16,0},{24,8},{1,17},{9,25},{17,1},{25,9},{2,18},{10... | collective-permute-start | bytes 737288 | tf_op jit(solution)/shard_map/ppermute | solution.py:122
  32.8 8.5 %collective-permute-start.11 = (bf16[128,640]{1,0:T(8,128)(2,1)S(1)}, bf16[128,640]{1,0:T(8,128)(2,1)S(1)}, u32[]{:S(2)}, u32[]{:S(2)}) collective-permute-start(bf16[128,640]{1,0:T(8,128)(2,1)S(1)} %add_convert_fusion.8.refs_0_), channel_id=1, source_target_pairs={{0,1},{1,0},{2,3},{3,2},{4,5},{5,4},{6,7},{7,6},{8,9},{9,8},{10,11... | collective-permute-start | bytes 491528 | tf_op jit(solution)/shard_map/ppermute | solution.py:107
  37.2 8.9 %collective-permute-start.14 = (bf16[160,768]{1,0:T(8,128)(2,1)S(1)}, bf16[160,768]{1,0:T(8,128)(2,1)S(1)}, u32[]{:S(2)}, u32[]{:S(2)}) collective-permute-start(bf16[160,768]{1,0:T(8,128)(2,1)S(1)} %collective-permute-done.8.refs_2_), channel_id=1, source_target_pairs={{0,16},{8,24},{16,0},{24,8},{1,17},{9,25},{17,1},{25,9},{2,18},{10... | collective-permute-start | bytes 737288 | tf_op jit(solution)/shard_map/ppermute | solution.py:122
  38.7 8.9 %collective-permute-start.16 = (bf16[160,768]{1,0:T(8,128)(2,1)S(1)}, bf16[160,768]{1,0:T(8,128)(2,1)S(1)}, u32[]{:S(2)}, u32[]{:S(2)}) collective-permute-start(bf16[160,768]{1,0:T(8,128)(2,1)S(1)} %collective-permute-done.9.refs_6_), channel_id=1, source_target_pairs={{0,8},{8,0},{16,24},{24,16},{1,9},{9,1},{17,25},{25,17},{2,10},{10... | collective-permute-start | bytes 737288 | tf_op jit(solution)/shard_map/ppermute | solution.py:122
  39.3 10.3 %collective-permute-start.15 = (bf16[160,768]{1,0:T(8,128)(2,1)S(1)}, bf16[160,768]{1,0:T(8,128)(2,1)S(1)}, u32[]{:S(2)}, u32[]{:S(2)}) collective-permute-start(bf16[160,768]{1,0:T(8,128)(2,1)S(1)} %collective-permute-done.13.refs_3_), channel_id=1, source_target_pairs={{0,16},{8,24},{16,0},{24,8},{1,17},{9,25},{17,1},{25,9},{2,18},{10... | collective-permute-start | bytes 737288 | tf_op jit(solution)/shard_map/ppermute | solution.py:122
  39.8 11.0 %collective-permute-start.18 = (bf16[160,768]{1,0:T(8,128)(2,1)S(1)}, bf16[160,768]{1,0:T(8,128)(2,1)S(1)}, u32[]{:S(2)}, u32[]{:S(2)}) collective-permute-start(bf16[160,768]{1,0:T(8,128)(2,1)S(1)} %collective-permute-done.17.refs_8_), channel_id=1, source_target_pairs={{0,8},{8,0},{16,24},{24,16},{1,9},{9,1},{17,25},{25,17},{2,10},{10... | collective-permute-start | bytes 737288 | tf_op jit(solution)/shard_map/ppermute | solution.py:122
  41.5 9.3 %collective-permute-start.12 = (bf16[128,640]{1,0:T(8,128)(2,1)S(1)}, bf16[128,640]{1,0:T(8,128)(2,1)S(1)}, u32[]{:S(2)}, u32[]{:S(2)}) collective-permute-start(bf16[128,640]{1,0:T(8,128)(2,1)S(1)} %get-tuple-element.122.refs_0_.refs_15_), channel_id=1, source_target_pairs={{0,4},{4,0},{1,5},{5,1},{2,6},{6,2},{3,7},{7,3},{8,12},{12,8},{9,1... | collective-permute-start | bytes 491528 | tf_op jit(solution)/shard_map/ppermute | solution.py:104
  52.0 1.5 %collective-permute-start.19 = (bf16[128,640]{1,0:T(8,128)(2,1)S(1)}, bf16[128,640]{1,0:T(8,128)(2,1)S(1)}, u32[]{:S(2)}, u32[]{:S(2)}) collective-permute-start(bf16[128,640]{1,0:T(8,128)(2,1)S(1)} %get-tuple-element.126), channel_id=1, source_target_pairs={{0,4},{4,0},{1,5},{5,1},{2,6},{6,2},{3,7},{7,3},{8,12},{12,8},{9,1... | collective-permute-start | bytes 491528 | tf_op jit(solution)/shard_map/ppermute | solution.py:104
  53.5 8.6 %collective-permute-start.20 = (bf16[128,640]{1,0:T(8,128)(2,1)S(1)}, bf16[128,640]{1,0:T(8,128)(2,1)S(1)}, u32[]{:S(2)}, u32[]{:S(2)}) collective-permute-start(bf16[128,640]{1,0:T(8,128)(2,1)S(1)} %add_convert_fusion.7.refs_0_), channel_id=1, source_target_pairs={{0,1},{1,0},{2,3},{3,2},{4,5},{5,4},{6,7},{7,6},{8,9},{9,8},{10,11... | collective-permute-start | bytes 491528 | tf_op jit(solution)/shard_map/ppermute | solution.py:107
  62.4 1.5 %collective-permute-start.21 = (bf16[128,640]{1,0:T(8,128)(2,1)S(1)}, bf16[128,640]{1,0:T(8,128)(2,1)S(1)}, u32[]{:S(2)}, u32[]{:S(2)}) collective-permute-start(bf16[128,640]{1,0:T(8,128)(2,1)S(1)} %get-tuple-element.132.refs_0_.refs_2_), channel_id=1, source_target_pairs={{0,4},{4,0},{1,5},{5,1},{2,6},{6,2},{3,7},{7,3},{8,12},{12,8},{9,1... | collective-permute-start | bytes 491528 | tf_op jit(solution)/shard_map/ppermute | solution.py:104
  65.2 1.5 %collective-permute-start.22 = (bf16[128,640]{1,0:T(8,128)(2,1)S(1)}, bf16[128,640]{1,0:T(8,128)(2,1)S(1)}, u32[]{:S(2)}, u32[]{:S(2)}) collective-permute-start(bf16[128,640]{1,0:T(8,128)(2,1)S(1)} %get-tuple-element.134), channel_id=1, source_target_pairs={{0,4},{4,0},{1,5},{5,1},{2,6},{6,2},{3,7},{7,3},{8,12},{12,8},{9,1... | collective-permute-start | bytes 491528 | tf_op jit(solution)/shard_map/ppermute | solution.py:104
  66.7 6.3 %collective-permute-start.23 = (bf16[128,640]{1,0:T(8,128)(2,1)S(1)}, bf16[128,640]{1,0:T(8,128)(2,1)S(1)}, u32[]{:S(2)}, u32[]{:S(2)}) collective-permute-start(bf16[128,640]{1,0:T(8,128)(2,1)S(1)} %add_convert_fusion.6.refs_0_), channel_id=1, source_target_pairs={{0,1},{1,0},{2,3},{3,2},{4,5},{5,4},{6,7},{7,6},{8,9},{9,8},{10,11... | collective-permute-start | bytes 491528 | tf_op jit(solution)/shard_map/ppermute | solution.py:107
  73.4 1.5 %collective-permute-start.24 = (bf16[128,640]{1,0:T(8,128)(2,1)S(1)}, bf16[128,640]{1,0:T(8,128)(2,1)S(1)}, u32[]{:S(2)}, u32[]{:S(2)}) collective-permute-start(bf16[128,640]{1,0:T(8,128)(2,1)S(1)} %get-tuple-element.136.refs_1_.refs_5_), channel_id=1, source_target_pairs={{0,4},{4,0},{1,5},{5,1},{2,6},{6,2},{3,7},{7,3},{8,12},{12,8},{9,1... | collective-permute-start | bytes 491528 | tf_op jit(solution)/shard_map/ppermute | solution.py:104
  77.3 1.8 %collective-permute-start.25 = (bf16[256,640]{1,0:T(8,128)(2,1)S(1)}, bf16[256,640]{1,0:T(8,128)(2,1)S(1)}, u32[]{:S(2)}, u32[]{:S(2)}) collective-permute-start(bf16[256,640]{1,0:T(8,128)(2,1)S(1)} %get-tuple-element.143.refs_9_), channel_id=1, source_target_pairs={{0,4},{4,0},{1,5},{5,1},{2,6},{6,2},{3,7},{7,3},{8,12},{12,8},{9,1... | collective-permute-start | bytes 983048 | tf_op jit(solution)/shard_map/ppermute | solution.py:104
  80.4 8.7 %collective-permute-start.27 = (bf16[704,256]{1,0:T(8,128)(2,1)S(1)}, bf16[704,256]{1,0:T(8,128)(2,1)S(1)}, u32[]{:S(2)}, u32[]{:S(2)}) collective-permute-start(bf16[704,256]{1,0:T(8,128)(2,1)S(1)} %get-tuple-element.151), channel_id=1, source_target_pairs={{0,4},{4,0},{1,5},{5,1},{2,6},{6,2},{3,7},{7,3},{8,12},{12,8},{9,1... | collective-permute-start | bytes 1081352 | tf_op jit(solution)/shard_map/ppermute | solution.py:104
  80.8 6.2 %collective-permute-start.26 = (bf16[128,640]{1,0:T(8,128)(2,1)S(1)}, bf16[128,640]{1,0:T(8,128)(2,1)S(1)}, u32[]{:S(2)}, u32[]{:S(2)}) collective-permute-start(bf16[128,640]{1,0:T(8,128)(2,1)S(1)} %get-tuple-element.145), channel_id=1, source_target_pairs={{0,1},{1,0},{2,3},{3,2},{4,5},{5,4},{6,7},{7,6},{8,9},{9,8},{10,11... | collective-permute-start | bytes 491528 | tf_op jit(solution)/shard_map/ppermute | solution.py:107
  82.5 24.6 %collective-permute-start.33 = (bf16[160,1536]{1,0:T(8,128)(2,1)S(1)}, bf16[160,1536]{1,0:T(8,128)(2,1)S(1)}, u32[]{:S(2)}, u32[]{:S(2)}) collective-permute-start(bf16[160,1536]{1,0:T(8,128)(2,1)S(1)} %get-tuple-element.157), channel_id=1, source_target_pairs={{0,16},{8,24},{16,0},{24,8},{1,17},{9,25},{17,1},{25,9},{2,18},{10... | collective-permute-start | bytes 1474568 | tf_op jit(solution)/shard_map/ppermute | solution.py:122
  83.1 26.2 %collective-permute-start.34 = (bf16[160,1536]{1,0:T(8,128)(2,1)S(1)}, bf16[160,1536]{1,0:T(8,128)(2,1)S(1)}, u32[]{:S(2)}, u32[]{:S(2)}) collective-permute-start(bf16[160,1536]{1,0:T(8,128)(2,1)S(1)} %get-tuple-element.158), channel_id=1, source_target_pairs={{0,24},{8,16},{16,8},{24,0},{1,25},{9,17},{17,9},{25,1},{2,26},{10... | collective-permute-start | bytes 1474568 | tf_op jit(solution)/shard_map/ppermute | solution.py:122
  84.5 24.7 %collective-permute-start.32 = (bf16[160,1536]{1,0:T(8,128)(2,1)S(1)}, bf16[160,1536]{1,0:T(8,128)(2,1)S(1)}, u32[]{:S(2)}, u32[]{:S(2)}) collective-permute-start(bf16[160,1536]{1,0:T(8,128)(2,1)S(1)} %get-tuple-element.139), channel_id=1, source_target_pairs={{0,8},{8,0},{16,24},{24,16},{1,9},{9,1},{17,25},{25,17},{2,10},{10... | collective-permute-start | bytes 1474568 | tf_op jit(solution)/shard_map/ppermute | solution.py:122
  87.0 9.8 %collective-permute-start.31 = (bf16[128,640]{1,0:T(8,128)(2,1)S(1)}, bf16[128,640]{1,0:T(8,128)(2,1)S(1)}, u32[]{:S(2)}, u32[]{:S(2)}) collective-permute-start(bf16[128,640]{1,0:T(8,128)(2,1)S(1)} %get-tuple-element.131.refs_0_), channel_id=1, source_target_pairs={{0,2},{1,3},{2,0},{3,1},{4,6},{5,7},{6,4},{7,5},{8,10},{9,11},{10,... | collective-permute-start | bytes 491528 | tf_op jit(solution)/shard_map/ppermute | solution.py:110
  89.1 24.0 %collective-permute-start.30 = (bf16[320,512]{1,0:T(8,128)(2,1)S(1)}, bf16[320,512]{1,0:T(8,128)(2,1)S(1)}, u32[]{:S(2)}, u32[]{:S(2)}) collective-permute-start(bf16[320,512]{1,0:T(8,128)(2,1)S(1)} %get-tuple-element.156), channel_id=1, source_target_pairs={{0,16},{8,24},{16,0},{24,8},{1,17},{9,25},{17,1},{25,9},{2,18},{10... | collective-permute-start | bytes 983048 | tf_op jit(solution)/shard_map/ppermute | solution.py:122
  96.9 16.3 %collective-permute-start.29 = (bf16[352,256]{1,0:T(8,128)(2,1)S(1)}, bf16[352,256]{1,0:T(8,128)(2,1)S(1)}, u32[]{:S(2)}, u32[]{:S(2)}) collective-permute-start(bf16[352,256]{1,0:T(8,128)(2,1)S(1)} %add_convert_fusion.4), channel_id=1, source_target_pairs={{0,8},{8,0},{16,24},{24,16},{1,9},{9,1},{17,25},{25,17},{2,10},{10... | collective-permute-start | bytes 540680 | tf_op jit(solution)/shard_map/ppermute | solution.py:122
  107.2 5.9 %collective-permute-start.28 = (bf16[64,640]{1,0:T(8,128)(2,1)S(1)}, bf16[64,640]{1,0:T(8,128)(2,1)S(1)}, u32[]{:S(2)}, u32[]{:S(2)}) collective-permute-start(bf16[64,640]{1,0:T(8,128)(2,1)S(1)} %get-tuple-element.153), channel_id=1, source_target_pairs={{0,2},{1,3},{2,0},{3,1},{4,6},{5,7},{6,4},{7,5},{8,10},{9,11},{10,... | collective-permute-start | bytes 245768 | tf_op jit(solution)/shard_map/ppermute | solution.py:110
  113.3 5.5 %collective-permute-start.36 = (bf16[64,640]{1,0:T(8,128)(2,1)S(1)}, bf16[64,640]{1,0:T(8,128)(2,1)S(1)}, u32[]{:S(2)}, u32[]{:S(2)}) collective-permute-start(bf16[64,640]{1,0:T(8,128)(2,1)S(1)} %last_norm.1.refs_2_), channel_id=1, source_target_pairs={{0,1},{1,0},{2,3},{3,2},{4,5},{5,4},{6,7},{7,6},{8,9},{9,8},{10,11... | collective-permute-start | bytes 245768 | tf_op jit(solution)/shard_map/ppermute | solution.py:107
  113.7 5.4 %collective-permute-start.35 = (bf16[64,640]{1,0:T(8,128)(2,1)S(1)}, bf16[64,640]{1,0:T(8,128)(2,1)S(1)}, u32[]{:S(2)}, u32[]{:S(2)}) collective-permute-start(bf16[64,640]{1,0:T(8,128)(2,1)S(1)} %last_norm.1.refs_2_), channel_id=1, source_target_pairs={{0,2},{1,3},{2,0},{3,1},{4,6},{5,7},{6,4},{7,5},{8,10},{9,11},{10,... | collective-permute-start | bytes 245768 | tf_op jit(solution)/shard_map/ppermute | solution.py:110
  115.8 4.6 %collective-permute-start.37 = (bf16[176,256]{1,0:T(8,128)(2,1)S(1)}, bf16[176,256]{1,0:T(8,128)(2,1)S(1)}, u32[]{:S(2)}, u32[]{:S(2)}) collective-permute-start(bf16[176,256]{1,0:T(8,128)(2,1)S(1)} %slice.32), channel_id=1, source_target_pairs={{0,16},{8,24},{16,0},{24,8},{1,17},{9,25},{17,1},{25,9},{2,18},{10... | collective-permute-start | bytes 270344 | tf_op jit(solution)/shard_map/ppermute | solution.py:122
  117.2 5.4 %collective-permute-start.38 = (bf16[160,512]{1,0:T(8,128)(2,1)S(1)}, bf16[160,512]{1,0:T(8,128)(2,1)S(1)}, u32[]{:S(2)}, u32[]{:S(2)}) collective-permute-start(bf16[160,512]{1,0:T(8,128)(2,1)S(1)} %slice.33), channel_id=1, source_target_pairs={{0,8},{8,0},{16,24},{24,16},{1,9},{9,1},{17,25},{25,17},{2,10},{10... | collective-permute-start | bytes 491528 | tf_op jit(solution)/shard_map/ppermute | solution.py:122
  118.1 11.1 %collective-permute-start.41 = (bf16[160,1536]{1,0:T(8,128)(2,1)S(1)}, bf16[160,1536]{1,0:T(8,128)(2,1)S(1)}, u32[]{:S(2)}, u32[]{:S(2)}) collective-permute-start(bf16[160,1536]{1,0:T(8,128)(2,1)S(1)} %add_convert_fusion), channel_id=1, source_target_pairs={{0,0},{1,1},{2,4},{3,5},{4,2},{5,3},{6,6},{7,7},{8,8},{9,9},{10,12... | collective-permute-start | bytes 1474568 | tf_op jit(solution)/shard_map/ppermute | solution.py:119
  122.6 4.6 %collective-permute-start.39 = (bf16[64,640]{1,0:T(8,128)(2,1)S(1)}, bf16[64,640]{1,0:T(8,128)(2,1)S(1)}, u32[]{:S(2)}, u32[]{:S(2)}) collective-permute-start(bf16[64,640]{1,0:T(8,128)(2,1)S(1)} %collective-permute-done.35.refs_4_), channel_id=1, source_target_pairs={{0,1},{1,0},{2,3},{3,2},{4,5},{5,4},{6,7},{7,6},{8,9},{9,8},{10,11... | collective-permute-start | bytes 245768 | tf_op jit(solution)/shard_map/ppermute | solution.py:107
  124.4 4.8 %collective-permute-start.40 = (bf16[176,256]{1,0:T(8,128)(2,1)S(1)}, bf16[176,256]{1,0:T(8,128)(2,1)S(1)}, u32[]{:S(2)}, u32[]{:S(2)}) collective-permute-start(bf16[176,256]{1,0:T(8,128)(2,1)S(1)} %add_convert_fusion.11), channel_id=1, source_target_pairs={{0,1},{1,0},{2,3},{3,2},{4,5},{5,4},{6,7},{7,6},{8,9},{9,8},{10,11... | collective-permute-start | bytes 270344 | tf_op jit(solution)/shard_map/ppermute | solution.py:107
  124.8 9.4 %collective-permute-start.42 = (bf16[160,512]{1,0:T(8,128)(2,1)S(1)}, bf16[160,512]{1,0:T(8,128)(2,1)S(1)}, u32[]{:S(2)}, u32[]{:S(2)}) collective-permute-start(bf16[160,512]{1,0:T(8,128)(2,1)S(1)} %add_convert_fusion.5), channel_id=1, source_target_pairs={{0,0},{1,1},{2,4},{3,5},{4,2},{5,3},{6,6},{7,7},{8,8},{9,9},{10,12... | collective-permute-start | bytes 491528 | tf_op jit(solution)/shard_map/ppermute | solution.py:119
  129.2 13.8 %collective-permute-start.44 = (bf16[160,1536]{1,0:T(8,128)(2,1)S(1)}, bf16[160,1536]{1,0:T(8,128)(2,1)S(1)}, u32[]{:S(2)}, u32[]{:S(2)}) collective-permute-start(bf16[160,1536]{1,0:T(8,128)(2,1)S(1)} %collective-permute-done.41.refs_8_), channel_id=1, source_target_pairs={{0,4},{4,0},{1,5},{5,1},{2,6},{6,2},{3,7},{7,3},{8,12},{12,8},{9,1... | collective-permute-start | bytes 1474568 | tf_op jit(solution)/shard_map/ppermute | solution.py:104
  134.2 7.4 %collective-permute-start.45 = (bf16[176,256]{1,0:T(8,128)(2,1)S(1)}, bf16[176,256]{1,0:T(8,128)(2,1)S(1)}, u32[]{:S(2)}, u32[]{:S(2)}) collective-permute-start(bf16[176,256]{1,0:T(8,128)(2,1)S(1)} %add_convert_fusion.10), channel_id=1, source_target_pairs={{0,2},{1,3},{2,0},{3,1},{4,6},{5,7},{6,4},{7,5},{8,10},{9,11},{10,... | collective-permute-start | bytes 270344 | tf_op jit(solution)/shard_map/ppermute | solution.py:110
  134.3 7.4 %collective-permute-start.43 = (bf16[160,512]{1,0:T(8,128)(2,1)S(1)}, bf16[160,512]{1,0:T(8,128)(2,1)S(1)}, u32[]{:S(2)}, u32[]{:S(2)}) collective-permute-start(bf16[160,512]{1,0:T(8,128)(2,1)S(1)} %collective-permute-done.42.refs_6_), channel_id=1, source_target_pairs={{0,4},{4,0},{1,5},{5,1},{2,6},{6,2},{3,7},{7,3},{8,12},{12,8},{9,1... | collective-permute-start | bytes 491528 | tf_op jit(solution)/shard_map/ppermute | solution.py:104
  141.6 1.4 collective-permute-start.46
  (4 other events, 14.4 us)

commit v4 on v3

--- a/solution.py
+++ b/solution.py
@@ -355,7 +355,6 @@
 
         wide_f, wide_b = shape((half, width), F32), shape((half, width), BF)
         row_f = shape((1, width), F32)
-        cos_t = tie(cos_t, cross_f1, cross_f2)
         act, att_b, att_f, w_att, keep, send, gw = call(
             front, "front",
             [
@@ -461,30 +460,39 @@
         )
         pair = pair_sum(keep, send)
 
-        all_cols = 3 * hidden
-
-        def ffn_weights(a0, a1, f0, f1, ggu, inner, o0, o1, o2, o3, full):
+        def put_grads(full, first, mine_out, give_out, size, lanes=slice(None)):
+            second = 3 - first
+            for i, step in enumerate((0, second)):
+                mine_out[i * size : (i + 1) * size, lanes] = take_block(full, step, size)
+            for i, step in enumerate((first, 3)):
+                give_out[i * size : (i + 1) * size, lanes] = take_block(full, step, size)
+
+        def ffn_weights(a0, a1, f0, f1, ggu, inner, m1, s1, m2, s2, full1, full2):
             low, high = slice(0, half), slice(half, 2 * half)
-            cut = 2 * hidden
-            full[:, :cut] = (dot_tn(a0[...], ggu[low, :]) + dot_tn(a1[...], ggu[high, :])).astype(BF)
-            full[:, cut:] = (
+            cut = ffn_cols
+            full1[...] = (
+                dot_tn(a0[...], ggu[low, :cut]) + dot_tn(a1[...], ggu[high, :cut])
+            ).astype(BF)
+            full2[:, : hidden - split] = (
+                dot_tn(a0[...], ggu[low, cut:]) + dot_tn(a1[...], ggu[high, cut:])
+            ).astype(BF)
+            full2[:, hidden - split :] = (
                 dot_tn(f0[...], inner[low, :]) + dot_tn(f1[...], inner[high, :])
             ).astype(BF)
-            for step, out in enumerate((o0, o1, o2, o3)):
-                out[...] = take_block(full, step, block)
-
-        def sum_blocks(blocks):
-            total = blocks[0].astype(F32)
-            for piece in blocks[1:]:
-                total = total + piece.astype(F32)
-            return across_pairs(total).astype(BF)
-
-        ffn_parts = call(
-            ffn_weights, "ffn_weights", [shape((block, all_cols), BF)] * 4,
+            put_grads(full1, 1, m1, s1, block)
+            put_grads(full2, 2, m2, s2, block)
+
+        ffn_m1, ffn_s1, ffn_m2, ffn_s2 = call(
+            ffn_weights, "ffn_weights", [shape((2 * block, ffn_cols), BF)] * 4,
             [act_own, act_oth, gf_own, gf_oth, tie(grad_gu, pair), inner_act],
-            scratch=[pltpu.VMEM((width, all_cols), BF)], flops=ffn_flops,
-        )
-        ffn_hops = [fsdp_hop(ffn_parts[step], step) for step in (1, 2, 3)]
+            scratch=[pltpu.VMEM((width, ffn_cols), BF)] * 2, flops=ffn_flops,
+        )
+
+        def hop_add(kept, sent, first):
+            return (kept.astype(F32) + fsdp_hop(sent, first).astype(F32)).astype(BF)
+
+        ffn_b1 = hop_add(ffn_m1, ffn_s1, 1)
+        ffn_b2 = hop_add(ffn_m2, ffn_s2, 2)
 
         def mid_three(pair, near, res, tot, cot, gains, fo, hid_out, grad_out):
             total = pair[...].astype(F32) + near[...].astype(F32)
@@ -504,7 +512,7 @@
             [pair, z_near(pair), hidden_res, attn_total, cotangent, gw, ds_fo],
             hold=saved,
         )
-        ga_oth = tie(core_swap(ga_own), ffn_parts[1])
+        ga_oth = core_swap(ga_own)
 
         def attn_back(lens, *refs):
             a0, a1, att_r, pre_r, cos_ref, sin_ref, w_r = refs[:7]
@@ -629,15 +637,13 @@
             full[:, HD:] = (
                 dot_tn(a0[...], attn_r[low, :]) + dot_tn(a1[...], attn_r[high, :])
             ).astype(BF)
-            for out, steps in ((qo_m, (0, 1)), (qo_s, (2, 3))):
-                for i, step in enumerate(steps):
-                    out[i * block : (i + 1) * block, :] = take_block(full, step, block)
+            put_grads(full, 2, qo_m, qo_s, block)
 
         kv_k, kv_s, qo_m, qo_s = call(
             attn_weights, "attn_weights",
             [shape((4 * blk_ext, HD), BF)] * 2 + [shape((2 * block, kvw), BF)] * 2,
             tok_parts
-            + [act, tie(grad_q, row_keep), grad_kv, ga_own, ga_oth, att_b]
+            + [act, tie(grad_q, row_keep, ffn_b1, ffn_b2), grad_kv, ga_own, ga_oth, att_b]
             + [part_keep, part_send, grad_hidden, ds_q, ds_k],
             scratch=[pltpu.VMEM((width, kvw), BF), pltpu.VMEM((n_fsdp * EXTRA, kvw), BF)],
             flops=2 * stream * width * kvw + 4 * n_q * width * HD, limit=limit,
@@ -652,7 +658,11 @@
 
         row_near = z_near(row_give)
         kv_recv = core_swap(kv_s)
-        row_near, kv_recv = together(row_near, kv_recv)
+        ffn_l1 = fsdp_hop(ffn_b1[block:], 2)
+        ffn_l2 = fsdp_hop(ffn_b2[block:], 1)
+        row_near, kv_recv, ffn_l1, ffn_l2 = together(row_near, kv_recv, ffn_l1, ffn_l2)
+        ffn_c1 = cross(last_add(ffn_b1, ffn_l1))
+        ffn_c2 = cross(last_add(ffn_b2, ffn_l2))
         kv_both = add(kv_k[: 2 * blk_ext], kv_recv[: 2 * blk_ext])
         kv_h1 = fsdp_hop(add(kv_k[2 * blk_ext :], kv_recv[2 * blk_ext :]), 1)
         qo_h1 = fsdp_hop(qo_s, 2)
@@ -666,10 +676,7 @@
         small_b = shape((quarter, width), BF)
         row_mine, row_far = call(halve, "halve_rows", [small_b, small_b], [row_keep, row_near])
         row_far = z_far(row_far)
-        row_far, kv_h1, qo_h1, layer_oth, *ffn_hops = together(
-            row_far, kv_h1, qo_h1, layer_oth, *ffn_hops
-        )
-        ffn_mine = cross(sum_blocks([ffn_parts[0]] + ffn_hops))
+        row_far, kv_h1, qo_h1, layer_oth = together(row_far, kv_h1, qo_h1, layer_oth)
         kv_both = add(kv_both, kv_h1)
         kv_h2 = fsdp_hop(kv_both[blk_ext:], 2)
         qo_both = add(qo_m, qo_h1)
@@ -693,15 +700,15 @@
         kv_sum = last_add(kv_both, kv_h2)
         kv_n = z_near(kv_sum)
         qo_c = cross(last_add(qo_both, qo_h2))
-        row_both, kv_n, ffn_mine = together(row_both, kv_n, ffn_mine)
+        row_both, kv_n, ffn_c1, ffn_c2 = together(row_both, kv_n, ffn_c1, ffn_c2)
         kv_sum = add(kv_sum, kv_n)
         kv_sum = add(kv_sum, z_far(kv_sum))
         kv_other = core_swap(kv_sum)
 
-        qo_x, ffn_x = core_swap(qo_c), core_swap(ffn_mine)
+        qo_x, ffn_x1, ffn_x2 = core_swap(qo_c), core_swap(ffn_c1), core_swap(ffn_c2)
 
         def finish(
-            l0, l1, r0, r1, r2, r3, qx, qy, fx, fy, kx, ky,
+            l0, l1, r0, r1, r2, r3, qx, qy, fx1, fy1, fx2, fy2, kx, ky,
             layer_out, in_out, q_out, k_out, v_out, o_out, g_out, u_out, d_out, *gain_outs,
         ):
             layer_out[pl.ds(group_start(), half), :] = l0[...].astype(F32)
@@ -715,9 +722,12 @@
                 in_out[pl.ds(at, quarter), :] = ref[...].astype(F32)
             q_out[...] = qx[:, :HD].astype(F32) + qy[:, :HD].astype(F32)
             o_out[...] = qx[:, HD:].astype(F32) + qy[:, HD:].astype(F32)
-            for i, out in enumerate((g_out, u_out, d_out)):
-                cols = slice(i * hidden, (i + 1) * hidden)
-                out[...] = fx[:, cols].astype(F32) + fy[:, cols].astype(F32)
+            both = fx1[...].astype(F32) + fy1[...].astype(F32)
+            g_out[...] = both[:, :hidden]
+            u_out[:, :split] = both[:, hidden:]
+            both = fx2[...].astype(F32) + fy2[...].astype(F32)
+            u_out[:, split:] = both[:, : hidden - split]
+            d_out[...] = both[:, hidden - split :]
             first = lax.axis_index("context") % 2 == 0
             mine, other = kx[...].astype(F32), ky[...].astype(F32)
             left = jnp.where(first, mine, other)
@@ -739,7 +749,7 @@
             + [shape((1, gblock), F32)] * 2,
             [
                 layer_own, layer_oth, row_done, row_nears, row_fars, row_both,
-                qo_c, qo_x, ffn_mine, ffn_x, kv_sum, kv_other,
+                qo_c, qo_x, ffn_c1, ffn_x1, ffn_c2, ffn_x2, kv_sum, kv_other,
             ],
         )
         return (

time: 145 us -> 132 us (0.910)
  waiting for transfers between devices: 64.8 us -> 45.9 us
  starting transfers between devices: 61.9 us -> 67.3 us
    ppermute x4, waiting for transfers between devices: 12.4 us -> 1.15 us  [z_far(): return lax.ppermute(value, 'tensor', [(i, i ^ 2) for i in range(n_tensor)])]
    ppermute x19 -> x20, waiting for transfers between devices: 32.1 us -> 23.2 us  [fsdp_hop(): return lax.ppermute(value, 'fsdp', [(i, i ^ step) for i in range(n_fsdp)])]
    ppermute x7, starting transfers between devices: 14.4 us -> 7.92 us  [z_near(): return lax.ppermute(value, 'tensor', [(i, i ^ 1) for i in range(n_tensor)])]
    ppermute x12 -> x13, starting transfers between devices: 14.8 us -> 21.2 us  [core_swap(): lax.ppermute(value, 'context', [(i, i ^ 1) for i in range(n_context)])]
    ppermute x4, starting transfers between devices: 6.25 us -> 9.38 us  [z_far(): return lax.ppermute(value, 'tensor', [(i, i ^ 2) for i in range(n_tensor)])]
    ppermute x19 -> x20, starting transfers between devices: 23 us -> 24.7 us  [fsdp_hop(): return lax.ppermute(value, 'fsdp', [(i, i ^ step) for i in range(n_fsdp)])]
    ppermute x7, waiting for transfers between devices: 13.7 us -> 15.5 us  [z_near(): return lax.ppermute(value, 'tensor', [(i, i ^ 1) for i in range(n_tensor)])]
    ppermute x5 -> x6, starting transfers between devices: 3.37 us -> 4.04 us  [cross(): return lax.ppermute(value, ('context', 'tensor'), pairs)]
  transfers between devices with their start and end apart: 47 -> 50, of which waited for: 25 -> 23; matrix products, arithmetic and copies ran while one was open for 0% -> 1% of each run, Pallas kernels for 2% -> 6%
where the time goes in v4:
time: 132 us; the launch traced here: 131 us
  starting transfers between devices  67.3 us (51%)
  waiting for transfers between devices  45.9 us (35%)
  Pallas kernels  14.7 us (11%)
  local copies, waits for them, and re-layouts  1.69 us (1%)
    ppermute x20, starting transfers between devices, fsdp_hop(): return lax.ppermute(value, 'fsdp', [(i, i ^ step) for i in range(n_fsdp)])  24.7 us
    ppermute x20, waiting for transfers between devices, fsdp_hop(): return lax.ppermute(value, 'fsdp', [(i, i ^ step) for i in range(n_fsdp)])  23.2 us
    ppermute x13, starting transfers between devices, core_swap(): lax.ppermute(value, 'context', [(i, i ^ 1) for i in range(n_context)])  21.2 us
    ppermute x7, waiting for transfers between devices, z_near(): return lax.ppermute(value, 'tensor', [(i, i ^ 1) for i in range(n_tensor)])  15.5 us
    pallas_call x14, Pallas kernels, call(): pl.pallas_call(wrapped, name=name, out_shape=tuple(outs), in_specs=[smem]...  14.7 us
    ppermute x4, starting transfers between devices, z_far(): return lax.ppermute(value, 'tensor', [(i, i ^ 2) for i in range(n_tensor)])  9.38 us
    ppermute x7, starting transfers between devices, z_near(): return lax.ppermute(value, 'tensor', [(i, i ^ 1) for i in range(n_tensor)])  7.92 us
    ppermute x13, waiting for transfers between devices, core_swap(): lax.ppermute(value, 'context', [(i, i ^ 1) for i in range(n_context)])  5.99 us
  transfers between devices with their start and end apart: 50, of which 23 were waited for; matrix products, arithmetic and copies ran while one was open for 1% of the time, Pallas kernels for 6%

profile of v4, /device:TPU:0, one launch (start us, length us, event | category | flops | bytes accessed | tf_op | source)
XLA Modules:
  0.0 131.4 jit_solution(17419737855203862206)
XLA Ops:
  1.8 1.9 %pack.1 = (bf16[176,512]{1,0:T(8,128)(2,1)S(1)}, bf16[160,512]{1,0:T(8,128)(2,1)S(1)}, bf16[160,768]{1,0:T(8,128)(2,1)S(1)}, bf16[160,768]{1,0:T(8,128)(2,1)S(1)...) custom-call(s32[1,4]{1,0:T(1,128)S(1)} %copy-done.3, bf16[160,256]{1,0:T(8,128)(2,1)} %refs_1_.2, ...), custom_call_target="tpu_custom_call" | custom-call | bytes 1359872 | tf_op jit(solution)/shard_map/pack/pallas_call | solution.py:79
  4.4 2.6 %collective-permute-start.1 = (bf16[176,512]{1,0:T(8,128)(2,1)S(1)}, bf16[176,512]{1,0:T(8,128)(2,1)S(1)}, u32[]{:S(2)}, u32[]{:S(2)}) collective-permute-start(bf16[176,512]{1,0:T(8,128)(2,1)S(1)} %get-tuple-element.106.refs_3_), channel_id=1, source_target_pairs={{0,8},{8,0},{16,24},{24,16},{1,9},{9,1},{17,25},{25,17},{2,10},{10... | collective-permute-start | bytes 540680 | tf_op jit(solution)/shard_map/ppermute | solution.py:122
  7.0 1.5 %collective-permute-start.6 = (bf16[160,512]{1,0:T(8,128)(2,1)S(1)}, bf16[160,512]{1,0:T(8,128)(2,1)S(1)}, u32[]{:S(2)}, u32[]{:S(2)}) collective-permute-start(bf16[160,512]{1,0:T(8,128)(2,1)S(1)} %collective-permute-done.4.refs_7_), channel_id=1, source_target_pairs={{0,16},{8,24},{16,0},{24,8},{1,17},{9,25},{17,1},{25,9},{2,18},{10... | collective-permute-start | bytes 491528 | tf_op jit(solution)/shard_map/ppermute | solution.py:122
  9.0 1.4 %collective-permute-done.1.refs_4_ = bf16[176,512]{1,0:T(8,128)(2,1)S(1)} collective-permute-done((bf16[176,512]{1,0:T(8,128)(2,1)S(1)}, bf16[176,512]{1,0:T(8,128)(2,1)S(1)}, u32[]{:S(2)}, u32[]{:S(2)}) %collective-permute-start.1) | collective-permute-done | bytes 180256 | tf_op jit(solution)/shard_map/ppermute | solution.py:122
  10.5 2.0 %collective-permute-start.3 = (bf16[176,512]{1,0:T(8,128)(2,1)S(1)}, bf16[176,512]{1,0:T(8,128)(2,1)S(1)}, u32[]{:S(2)}, u32[]{:S(2)}) collective-permute-start(bf16[176,512]{1,0:T(8,128)(2,1)S(1)} %collective-permute-done.1.refs_4_), channel_id=1, source_target_pairs={{0,16},{8,24},{16,0},{24,8},{1,17},{9,25},{17,1},{25,9},{2,18},{10... | collective-permute-start | bytes 540680 | tf_op jit(solution)/shard_map/ppermute | solution.py:122
  12.5 1.5 %collective-permute-start.5 = (bf16[160,512]{1,0:T(8,128)(2,1)S(1)}, bf16[160,512]{1,0:T(8,128)(2,1)S(1)}, u32[]{:S(2)}, u32[]{:S(2)}) collective-permute-start(bf16[160,512]{1,0:T(8,128)(2,1)S(1)} %collective-permute-done.4.refs_7_), channel_id=1, source_target_pairs={{0,8},{8,0},{16,24},{24,16},{1,9},{9,1},{17,25},{25,17},{2,10},{10... | collective-permute-start | bytes 491528 | tf_op jit(solution)/shard_map/ppermute | solution.py:122
  15.9 1.9 %collective-permute-done.5.refs_8_ = bf16[160,512]{1,0:T(8,128)(2,1)S(1)} collective-permute-done((bf16[160,512]{1,0:T(8,128)(2,1)S(1)}, bf16[160,512]{1,0:T(8,128)(2,1)S(1)}, u32[]{:S(2)}, u32[]{:S(2)}) %collective-permute-start.5) | collective-permute-done | bytes 163872 | tf_op jit(solution)/shard_map/ppermute | solution.py:122
  17.8 1.8 %collective-permute-done.7.refs_10_ = bf16[160,512]{1,0:T(8,128)(2,1)S(1)} collective-permute-done((bf16[160,512]{1,0:T(8,128)(2,1)S(1)}, bf16[160,512]{1,0:T(8,128)(2,1)S(1)}, u32[]{:S(2)}, u32[]{:S(2)}) %collective-permute-start.7) | collective-permute-done | bytes 163872 | tf_op jit(solution)/shard_map/ppermute | solution.py:122
  20.6 2.3 %front.1 = (bf16[512,640]{1,0:T(8,128)(2,1)S(1)}, bf16[1536,256]{1,0:T(8,128)(2,1)S(1)}, f32[1032,256]{1,0:T(8,128)S(1)}, bf16[640,1024]{1,0:T(8,128)(2,1)S(1)},...) custom-call(s32[1,4]{1,0:T(1,128)S(1)} %copy-done.3, bf16[256,640]{1,0:T(8,128)(2,1)S(1)} %copy-done, ...), custom_call_target="tpu_custom_call" | custom-call | flops 469762048 | bytes 6877184 | tf_op jit(solution)/shard_map/front/pallas_call | solution.py:79
  22.9 7.2 %collective-permute-start.8 = (bf16[128,640]{1,0:T(8,128)(2,1)S(1)}, bf16[128,640]{1,0:T(8,128)(2,1)S(1)}, u32[]{:S(2)}, u32[]{:S(2)}) collective-permute-start(bf16[128,640]{1,0:T(8,128)(2,1)S(1)} %get-tuple-element.111), channel_id=1, source_target_pairs={{0,4},{4,0},{1,5},{5,1},{2,6},{6,2},{3,7},{7,3},{8,12},{12,8},{9,1... | collective-permute-start | bytes 491528 | tf_op jit(solution)/shard_map/ppermute | solution.py:104
  30.4 1.4 %collective-permute-start.17 = (bf16[160,768]{1,0:T(8,128)(2,1)S(1)}, bf16[160,768]{1,0:T(8,128)(2,1)S(1)}, u32[]{:S(2)}, u32[]{:S(2)}) collective-permute-start(bf16[160,768]{1,0:T(8,128)(2,1)S(1)} %collective-permute-done.15.refs_6_), channel_id=1, source_target_pairs={{0,16},{8,24},{16,0},{24,8},{1,17},{9,25},{17,1},{25,9},{2,18},{10... | collective-permute-start | bytes 737288 | tf_op jit(solution)/shard_map/ppermute | solution.py:122
  31.9 2.5 %collective-permute-start.9 = (bf16[128,640]{1,0:T(8,128)(2,1)S(1)}, bf16[128,640]{1,0:T(8,128)(2,1)S(1)}, u32[]{:S(2)}, u32[]{:S(2)}) collective-permute-start(bf16[128,640]{1,0:T(8,128)(2,1)S(1)} %add_convert_fusion.11.refs_0_), channel_id=1, source_target_pairs={{0,1},{1,0},{2,3},{3,2},{4,5},{5,4},{6,7},{7,6},{8,9},{9,8},{10,11... | collective-permute-start | bytes 491528 | tf_op jit(solution)/shard_map/ppermute | solution.py:107
  34.9 1.5 %collective-permute-start.16 = (bf16[160,768]{1,0:T(8,128)(2,1)S(1)}, bf16[160,768]{1,0:T(8,128)(2,1)S(1)}, u32[]{:S(2)}, u32[]{:S(2)}) collective-permute-start(bf16[160,768]{1,0:T(8,128)(2,1)S(1)} %collective-permute-done.15.refs_6_), channel_id=1, source_target_pairs={{0,8},{8,0},{16,24},{24,16},{1,9},{9,1},{17,25},{25,17},{2,10},{10... | collective-permute-start | bytes 737288 | tf_op jit(solution)/shard_map/ppermute | solution.py:122
  36.4 2.3 %collective-permute-done.12.refs_3_ = bf16[160,768]{1,0:T(8,128)(2,1)S(1)} collective-permute-done((bf16[160,768]{1,0:T(8,128)(2,1)S(1)}, bf16[160,768]{1,0:T(8,128)(2,1)S(1)}, u32[]{:S(2)}, u32[]{:S(2)}) %collective-permute-start.12) | collective-permute-done | bytes 245792 | tf_op jit(solution)/shard_map/ppermute | solution.py:122
  38.7 1.2 collective-permute-start.14
  40.7 4.1 %collective-permute-start.10 = (bf16[128,640]{1,0:T(8,128)(2,1)S(1)}, bf16[128,640]{1,0:T(8,128)(2,1)S(1)}, u32[]{:S(2)}, u32[]{:S(2)}) collective-permute-start(bf16[128,640]{1,0:T(8,128)(2,1)S(1)} %get-tuple-element.117.refs_0_.refs_15_), channel_id=1, source_target_pairs={{0,4},{4,0},{1,5},{5,1},{2,6},{6,2},{3,7},{7,3},{8,12},{12,8},{9,1... | collective-permute-start | bytes 491528 | tf_op jit(solution)/shard_map/ppermute | solution.py:104
  44.8 2.8 %collective-permute-done.14.refs_5_ = bf16[160,768]{1,0:T(8,128)(2,1)S(1)} collective-permute-done((bf16[160,768]{1,0:T(8,128)(2,1)S(1)}, bf16[160,768]{1,0:T(8,128)(2,1)S(1)}, u32[]{:S(2)}, u32[]{:S(2)}) %collective-permute-start.14) | collective-permute-done | bytes 245792 | tf_op jit(solution)/shard_map/ppermute | solution.py:122
  47.6 1.2 ffn.1
  48.8 3.4 %collective-permute-start.19 = (bf16[128,640]{1,0:T(8,128)(2,1)S(1)}, bf16[128,640]{1,0:T(8,128)(2,1)S(1)}, u32[]{:S(2)}, u32[]{:S(2)}) collective-permute-start(bf16[128,640]{1,0:T(8,128)(2,1)S(1)} %get-tuple-element.123), channel_id=1, source_target_pairs={{0,4},{4,0},{1,5},{5,1},{2,6},{6,2},{3,7},{7,3},{8,12},{12,8},{9,1... | collective-permute-start | bytes 491528 | tf_op jit(solution)/shard_map/ppermute | solution.py:104
  54.4 5.4 %collective-permute-done.20.refs_1_ = bf16[128,640]{1,0:T(8,128)(2,1)S(1)} collective-permute-done((bf16[128,640]{1,0:T(8,128)(2,1)S(1)}, bf16[128,640]{1,0:T(8,128)(2,1)S(1)}, u32[]{:S(2)}, u32[]{:S(2)}) %collective-permute-start.20) | collective-permute-done | bytes 163872 | tf_op jit(solution)/shard_map/ppermute | solution.py:107
  60.2 1.4 %collective-permute-done.21.refs_1_.refs_3_ = bf16[128,640]{1,0:T(8,128)(2,1)S(1)} collective-permute-done((bf16[128,640]{1,0:T(8,128)(2,1)S(1)}, bf16[128,640]{1,0:T(8,128)(2,1)S(1)}, u32[]{:S(2)}, u32[]{:S(2)}) %collective-permute-start.21) | collective-permute-done | bytes 163872 | tf_op jit(solution)/shard_map/ppermute | solution.py:104
  61.6 1.3 %ffn_back.1 = (bf16[256,1024]{1,0:T(8,128)(2,1)S(1)}, f32[128,640]{1,0:T(8,128)S(1)}, bf16[128,640]{1,0:T(8,128)(2,1)S(1)}) custom-call(bf16[128,640]{1,0:T(8,128)(2,1)S(1)} %get-tuple-element.129.refs_0_.refs_2_, bf16[128,640]{1,0:T(8,128)(2,1)S(1)} %collective-permute-done.21.refs_1_.refs_3_, f32[256,1024]{1,0:T(8,128)S(1)} %get-tuple-element.125.refs_18_.refs_2_, ...), custom_call_target="tpu_custom_call" | custom-call | flops 503316480 | bytes 4358144 | tf_op jit(solution)/shard_map/ffn_back/pallas_call | solution.py:79
  63.2 1.2 collective-permute-done.22
  64.5 1.3 %ffn_weights.1 = (bf16[320,768]{1,0:T(8,128)(2,1)S(1)}, bf16[320,768]{1,0:T(8,128)(2,1)S(1)}, bf16[320,768]{1,0:T(8,128)(2,1)S(1)}, bf16[320,768]{1,0:T(8,128)(2,1)S(1)}) custom-call(bf16[128,640]{1,0:T(8,128)(2,1)S(1)} %get-tuple-element.117.refs_0_.refs_15_, bf16[128,640]{1,0:T(8,128)(2,1)S(1)} %collective-permute-done.10.refs_1_.refs_16_, ...), custom_call_target="tpu_custom_call" | custom-call | flops 503316480 | bytes 3407872 | tf_op jit(solution)/shard_map/ffn_weights/pallas_call | solution.py:79
  65.8 1.5 %collective-permute-start.27 = (bf16[320,768]{1,0:T(8,128)(2,1)S(1)}, bf16[320,768]{1,0:T(8,128)(2,1)S(1)}, u32[]{:S(2)}, u32[]{:S(2)}) collective-permute-start(bf16[320,768]{1,0:T(8,128)(2,1)S(1)} %get-tuple-element.143), channel_id=1, source_target_pairs={{0,8},{8,0},{16,24},{24,16},{1,9},{9,1},{17,25},{25,17},{2,10},{10... | collective-permute-start | bytes 1474568 | tf_op jit(solution)/shard_map/ppermute | solution.py:122
  68.4 1.6 %collective-permute-start.28 = (bf16[320,768]{1,0:T(8,128)(2,1)S(1)}, bf16[320,768]{1,0:T(8,128)(2,1)S(1)}, u32[]{:S(2)}, u32[]{:S(2)}) collective-permute-start(bf16[320,768]{1,0:T(8,128)(2,1)S(1)} %get-tuple-element.145), channel_id=1, source_target_pairs={{0,16},{8,24},{16,0},{24,8},{1,17},{9,25},{17,1},{25,9},{2,18},{10... | collective-permute-start | bytes 1474568 | tf_op jit(solution)/shard_map/ppermute | solution.py:122
  69.9 3.4 %collective-permute-done.23.refs_1_ = bf16[128,640]{1,0:T(8,128)(2,1)S(1)} collective-permute-done((bf16[128,640]{1,0:T(8,128)(2,1)S(1)}, bf16[128,640]{1,0:T(8,128)(2,1)S(1)}, u32[]{:S(2)}, u32[]{:S(2)}) %collective-permute-start.23) | collective-permute-done | bytes 163872 | tf_op jit(solution)/shard_map/ppermute | solution.py:107
  73.8 1.4 %collective-permute-done.24.refs_2_.refs_6_ = bf16[128,640]{1,0:T(8,128)(2,1)S(1)} collective-permute-done((bf16[128,640]{1,0:T(8,128)(2,1)S(1)}, bf16[128,640]{1,0:T(8,128)(2,1)S(1)}, u32[]{:S(2)}, u32[]{:S(2)}) %collective-permute-start.24) | collective-permute-done | bytes 163872 | tf_op jit(solution)/shard_map/ppermute | solution.py:104
  75.1 2.5 %attn_back.1 = (bf16[256,256]{1,0:T(8,128)(2,1)S(1)}, bf16[512,512]{1,0:T(8,128)(2,1)S(1)}, f32[256,640]{1,0:T(8,128)S(1)}, bf16[256,640]{1,0:T(8,128)(2,1)S(1)}...) custom-call(s32[1,4]{1,0:T(1,128)S(1)} %copy-done.4, bf16[128,640]{1,0:T(8,128)(2,1)S(1)} %get-tuple-element.133.refs_1_.refs_5_, ...), custom_call_target="tpu_custom_call" | custom-call | flops 671088640 | bytes 5646336 | tf_op jit(solution)/shard_map/attn_back/pallas_call | solution.py:79
  77.8 1.3 collective-permute-done.27
  79.3 1.8 %collective-permute-done.28 = bf16[320,768]{1,0:T(8,128)(2,1)S(1)} collective-permute-done((bf16[320,768]{1,0:T(8,128)(2,1)S(1)}, bf16[320,768]{1,0:T(8,128)(2,1)S(1)}, u32[]{:S(2)}, u32[]{:S(2)}) %collective-permute-start.28) | collective-permute-done | bytes 491552 | tf_op jit(solution)/shard_map/ppermute | solution.py:122
  82.5 1.6 %collective-permute-start.30 = (bf16[160,768]{1,0:T(8,128)(2,1)S(1)}, bf16[160,768]{1,0:T(8,128)(2,1)S(1)}, u32[]{:S(2)}, u32[]{:S(2)}) collective-permute-start(bf16[160,768]{1,0:T(8,128)(2,1)S(1)} %slice.48), channel_id=1, source_target_pairs={{0,16},{8,24},{16,0},{24,8},{1,17},{9,25},{17,1},{25,9},{2,18},{10... | collective-permute-start | bytes 737288 | tf_op jit(solution)/shard_map/ppermute | solution.py:122
  85.0 2.9 %collective-permute-start.35 = (bf16[128,640]{1,0:T(8,128)(2,1)S(1)}, bf16[128,640]{1,0:T(8,128)(2,1)S(1)}, u32[]{:S(2)}, u32[]{:S(2)}) collective-permute-start(bf16[128,640]{1,0:T(8,128)(2,1)S(1)} %get-tuple-element.128.refs_0_), channel_id=1, source_target_pairs={{0,2},{1,3},{2,0},{3,1},{4,6},{5,7},{6,4},{7,5},{8,10},{9,11},{10,... | collective-permute-start | bytes 491528 | tf_op jit(solution)/shard_map/ppermute | solution.py:110
  87.9 3.1 %collective-permute-done.30 = bf16[160,768]{1,0:T(8,128)(2,1)S(1)} collective-permute-done((bf16[160,768]{1,0:T(8,128)(2,1)S(1)}, bf16[160,768]{1,0:T(8,128)(2,1)S(1)}, u32[]{:S(2)}, u32[]{:S(2)}) %collective-permute-start.30) | collective-permute-done | bytes 245792 | tf_op jit(solution)/shard_map/ppermute | solution.py:122
  91.0 1.6 %collective-permute-start.34 = (bf16[320,512]{1,0:T(8,128)(2,1)S(1)}, bf16[320,512]{1,0:T(8,128)(2,1)S(1)}, u32[]{:S(2)}, u32[]{:S(2)}) collective-permute-start(bf16[320,512]{1,0:T(8,128)(2,1)S(1)} %get-tuple-element.155), channel_id=1, source_target_pairs={{0,16},{8,24},{16,0},{24,8},{1,17},{9,25},{17,1},{25,9},{2,18},{10... | collective-permute-start | bytes 983048 | tf_op jit(solution)/shard_map/ppermute | solution.py:122
  92.5 1.8 %collective-permute-done.26.refs_1_ = bf16[128,640]{1,0:T(8,128)(2,1)S(1)} collective-permute-done((bf16[128,640]{1,0:T(8,128)(2,1)S(1)}, bf16[128,640]{1,0:T(8,128)(2,1)S(1)}, u32[]{:S(2)}, u32[]{:S(2)}) %collective-permute-start.26) | collective-permute-done | bytes 163872 | tf_op jit(solution)/shard_map/ppermute | solution.py:107
  94.9 1.3 collective-permute-start.33
  96.2 4.1 %collective-permute-done.34 = bf16[320,512]{1,0:T(8,128)(2,1)S(1)} collective-permute-done((bf16[320,512]{1,0:T(8,128)(2,1)S(1)}, bf16[320,512]{1,0:T(8,128)(2,1)S(1)}, u32[]{:S(2)}, u32[]{:S(2)}) %collective-permute-start.34) | collective-permute-done | bytes 327712 | tf_op jit(solution)/shard_map/ppermute | solution.py:122
  101.5 1.9 %collective-permute-start.36 = (bf16[64,640]{1,0:T(8,128)(2,1)S(1)}, bf16[64,640]{1,0:T(8,128)(2,1)S(1)}, u32[]{:S(2)}, u32[]{:S(2)}) collective-permute-start(bf16[64,640]{1,0:T(8,128)(2,1)S(1)} %last_norm.1.refs_2_), channel_id=1, source_target_pairs={{0,2},{1,3},{2,0},{3,1},{4,6},{5,7},{6,4},{7,5},{8,10},{9,11},{10,... | collective-permute-start | bytes 245768 | tf_op jit(solution)/shard_map/ppermute | solution.py:110
  104.8 1.3 %collective-permute-start.39 = (bf16[160,512]{1,0:T(8,128)(2,1)S(1)}, bf16[160,512]{1,0:T(8,128)(2,1)S(1)}, u32[]{:S(2)}, u32[]{:S(2)}) collective-permute-start(bf16[160,512]{1,0:T(8,128)(2,1)S(1)} %slice.51), channel_id=1, source_target_pairs={{0,8},{8,0},{16,24},{24,16},{1,9},{9,1},{17,25},{25,17},{2,10},{10... | collective-permute-start | bytes 491528 | tf_op jit(solution)/shard_map/ppermute | solution.py:122
  108.2 2.0 %collective-permute-done.39 = bf16[160,512]{1,0:T(8,128)(2,1)S(1)} collective-permute-done((bf16[160,512]{1,0:T(8,128)(2,1)S(1)}, bf16[160,512]{1,0:T(8,128)(2,1)S(1)}, u32[]{:S(2)}, u32[]{:S(2)}) %collective-permute-start.39) | collective-permute-done | bytes 163872 | tf_op jit(solution)/shard_map/ppermute | solution.py:122
  110.2 1.8 %collective-permute-start.40 = (bf16[64,640]{1,0:T(8,128)(2,1)S(1)}, bf16[64,640]{1,0:T(8,128)(2,1)S(1)}, u32[]{:S(2)}, u32[]{:S(2)}) collective-permute-start(bf16[64,640]{1,0:T(8,128)(2,1)S(1)} %collective-permute-done.36.refs_4_), channel_id=1, source_target_pairs={{0,1},{1,0},{2,3},{3,2},{4,5},{5,4},{6,7},{7,6},{8,9},{9,8},{10,11... | collective-permute-start | bytes 245768 | tf_op jit(solution)/shard_map/ppermute | solution.py:107
  113.0 3.2 %collective-permute-done.40.refs_5_ = bf16[64,640]{1,0:T(8,128)(2,1)S(1)} collective-permute-done((bf16[64,640]{1,0:T(8,128)(2,1)S(1)}, bf16[64,640]{1,0:T(8,128)(2,1)S(1)}, u32[]{:S(2)}, u32[]{:S(2)}) %collective-permute-start.40) | collective-permute-done | bytes 81952 | tf_op jit(solution)/shard_map/ppermute | solution.py:107
  116.2 1.7 %collective-permute-done.41 = bf16[176,256]{1,0:T(8,128)(2,1)S(1)} collective-permute-done((bf16[176,256]{1,0:T(8,128)(2,1)S(1)}, bf16[176,256]{1,0:T(8,128)(2,1)S(1)}, u32[]{:S(2)}, u32[]{:S(2)}) %collective-permute-start.41) | collective-permute-done | bytes 90144 | tf_op jit(solution)/shard_map/ppermute | solution.py:107
  117.9 4.1 %collective-permute-start.48 = (bf16[176,256]{1,0:T(8,128)(2,1)S(1)}, bf16[176,256]{1,0:T(8,128)(2,1)S(1)}, u32[]{:S(2)}, u32[]{:S(2)}) collective-permute-start(bf16[176,256]{1,0:T(8,128)(2,1)S(1)} %add_convert_fusion.13), channel_id=1, source_target_pairs={{0,2},{1,3},{2,0},{3,1},{4,6},{5,7},{6,4},{7,5},{8,10},{9,11},{10,... | collective-permute-start | bytes 270344 | tf_op jit(solution)/shard_map/ppermute | solution.py:110
  122.6 1.4 %collective-permute-start.45 = (bf16[160,512]{1,0:T(8,128)(2,1)S(1)}, bf16[160,512]{1,0:T(8,128)(2,1)S(1)}, u32[]{:S(2)}, u32[]{:S(2)}) collective-permute-start(bf16[160,512]{1,0:T(8,128)(2,1)S(1)} %collective-permute-done.44.refs_6_), channel_id=1, source_target_pairs={{0,4},{4,0},{1,5},{5,1},{2,6},{6,2},{3,7},{7,3},{8,12},{12,8},{9,1... | collective-permute-start | bytes 491528 | tf_op jit(solution)/shard_map/ppermute | solution.py:104
  125.1 3.5 %collective-permute-start.49 = (bf16[176,256]{1,0:T(8,128)(2,1)S(1)}, bf16[176,256]{1,0:T(8,128)(2,1)S(1)}, u32[]{:S(2)}, u32[]{:S(2)}) collective-permute-start(bf16[176,256]{1,0:T(8,128)(2,1)S(1)} %add_convert_fusion.12.refs_12_), channel_id=1, source_target_pairs={{0,4},{4,0},{1,5},{5,1},{2,6},{6,2},{3,7},{7,3},{8,12},{12,8},{9,1... | collective-permute-start | bytes 270344 | tf_op jit(solution)/shard_map/ppermute | solution.py:104
  129.6 1.8 %finish.1 = (f32[256,640]{1,0:T(8,128)}, f32[256,640]{1,0:T(8,128)}, f32[160,256]{1,0:T(8,128)}, f32[160,256]{1,0:T(8,128)}, f32[160,256]{1,0:T(8,128)}, /*index...) custom-call(bf16[128,640]{1,0:T(8,128)(2,1)S(1)} %get-tuple-element., ...), custom_call_target="tpu_custom_call" | custom-call | bytes 5098496 | tf_op jit(solution)/shard_map/finish/pallas_call | solution.py:79
  (94 shorter events, 22.6 us)
Async XLA Ops:
  0.7 3.1 %collective-permute-start = (bf16[256,640]{1,0:T(8,128)(2,1)}, bf16[256,640]{1,0:T(8,128)(2,1)S(1)}, u32[]{:S(2)}, u32[]{:S(2)}) collective-permute-start(bf16[256,640]{1,0:T(8,128)(2,1)} %refs_2_.5), channel_id=1, source_target_pairs={{0,4},{4,0},{1,5},{5,1},{2,6},{6,2},{3,7},{7,3},{8,12},{12,8},{9,1... | collective-permute-start | bytes 983048 | tf_op jit(solution)/shard_map/ppermute | solution.py:104
  3.7 3.3 %collective-permute-start.4 = (bf16[160,512]{1,0:T(8,128)(2,1)S(1)}, bf16[160,512]{1,0:T(8,128)(2,1)S(1)}, u32[]{:S(2)}, u32[]{:S(2)}) collective-permute-start(bf16[160,512]{1,0:T(8,128)(2,1)S(1)} %get-tuple-element.107), channel_id=1, source_target_pairs={{0,0},{1,1},{2,4},{3,5},{4,2},{5,3},{6,6},{7,7},{8,8},{9,9},{10,12... | collective-permute-start | bytes 491528 | tf_op jit(solution)/shard_map/ppermute | solution.py:119
  4.4 6.0 %collective-permute-start.1 = (bf16[176,512]{1,0:T(8,128)(2,1)S(1)}, bf16[176,512]{1,0:T(8,128)(2,1)S(1)}, u32[]{:S(2)}, u32[]{:S(2)}) collective-permute-start(bf16[176,512]{1,0:T(8,128)(2,1)S(1)} %get-tuple-element.106.refs_3_), channel_id=1, source_target_pairs={{0,8},{8,0},{16,24},{24,16},{1,9},{9,1},{17,25},{25,17},{2,10},{10... | collective-permute-start | bytes 540680 | tf_op jit(solution)/shard_map/ppermute | solution.py:122
  7.0 7.0 %collective-permute-start.6 = (bf16[160,512]{1,0:T(8,128)(2,1)S(1)}, bf16[160,512]{1,0:T(8,128)(2,1)S(1)}, u32[]{:S(2)}, u32[]{:S(2)}) collective-permute-start(bf16[160,512]{1,0:T(8,128)(2,1)S(1)} %collective-permute-done.4.refs_7_), channel_id=1, source_target_pairs={{0,16},{8,24},{16,0},{24,8},{1,17},{9,25},{17,1},{25,9},{2,18},{10... | collective-permute-start | bytes 491528 | tf_op jit(solution)/shard_map/ppermute | solution.py:122
  8.5 6.7 %collective-permute-start.2 = (bf16[176,512]{1,0:T(8,128)(2,1)S(1)}, bf16[176,512]{1,0:T(8,128)(2,1)S(1)}, u32[]{:S(2)}, u32[]{:S(2)}) collective-permute-start(bf16[176,512]{1,0:T(8,128)(2,1)S(1)} %get-tuple-element.106.refs_3_), channel_id=1, source_target_pairs={{0,16},{8,24},{16,0},{24,8},{1,17},{9,25},{17,1},{25,9},{2,18},{10... | collective-permute-start | bytes 540680 | tf_op jit(solution)/shard_map/ppermute | solution.py:122
  10.5 7.4 %collective-permute-start.3 = (bf16[176,512]{1,0:T(8,128)(2,1)S(1)}, bf16[176,512]{1,0:T(8,128)(2,1)S(1)}, u32[]{:S(2)}, u32[]{:S(2)}) collective-permute-start(bf16[176,512]{1,0:T(8,128)(2,1)S(1)} %collective-permute-done.1.refs_4_), channel_id=1, source_target_pairs={{0,16},{8,24},{16,0},{24,8},{1,17},{9,25},{17,1},{25,9},{2,18},{10... | collective-permute-start | bytes 540680 | tf_op jit(solution)/shard_map/ppermute | solution.py:122
  12.5 5.3 %collective-permute-start.5 = (bf16[160,512]{1,0:T(8,128)(2,1)S(1)}, bf16[160,512]{1,0:T(8,128)(2,1)S(1)}, u32[]{:S(2)}, u32[]{:S(2)}) collective-permute-start(bf16[160,512]{1,0:T(8,128)(2,1)S(1)} %collective-permute-done.4.refs_7_), channel_id=1, source_target_pairs={{0,8},{8,0},{16,24},{24,16},{1,9},{9,1},{17,25},{25,17},{2,10},{10... | collective-permute-start | bytes 491528 | tf_op jit(solution)/shard_map/ppermute | solution.py:122
  14.0 5.6 %collective-permute-start.7 = (bf16[160,512]{1,0:T(8,128)(2,1)S(1)}, bf16[160,512]{1,0:T(8,128)(2,1)S(1)}, u32[]{:S(2)}, u32[]{:S(2)}) collective-permute-start(bf16[160,512]{1,0:T(8,128)(2,1)S(1)} %collective-permute-done.6.refs_9_), channel_id=1, source_target_pairs={{0,8},{8,0},{16,24},{24,16},{1,9},{9,1},{17,25},{25,17},{2,10},{10... | collective-permute-start | bytes 491528 | tf_op jit(solution)/shard_map/ppermute | solution.py:122
  14.6 15.5 %collective-permute-start.11 = (bf16[160,768]{1,0:T(8,128)(2,1)S(1)}, bf16[160,768]{1,0:T(8,128)(2,1)S(1)}, u32[]{:S(2)}, u32[]{:S(2)}) collective-permute-start(bf16[160,768]{1,0:T(8,128)(2,1)S(1)} %get-tuple-element.118), channel_id=1, source_target_pairs={{0,0},{1,1},{2,4},{3,5},{4,2},{5,3},{6,6},{7,7},{8,8},{9,9},{10,12... | collective-permute-start | bytes 737288 | tf_op jit(solution)/shard_map/ppermute | solution.py:119
  15.2 15.2 %collective-permute-start.15 = (bf16[160,768]{1,0:T(8,128)(2,1)S(1)}, bf16[160,768]{1,0:T(8,128)(2,1)S(1)}, u32[]{:S(2)}, u32[]{:S(2)}) collective-permute-start(bf16[160,768]{1,0:T(8,128)(2,1)S(1)} %get-tuple-element.119), channel_id=1, source_target_pairs={{0,0},{1,1},{2,4},{3,5},{4,2},{5,3},{6,6},{7,7},{8,8},{9,9},{10,12... | collective-permute-start | bytes 737288 | tf_op jit(solution)/shard_map/ppermute | solution.py:119
  22.9 9.0 %collective-permute-start.8 = (bf16[128,640]{1,0:T(8,128)(2,1)S(1)}, bf16[128,640]{1,0:T(8,128)(2,1)S(1)}, u32[]{:S(2)}, u32[]{:S(2)}) collective-permute-start(bf16[128,640]{1,0:T(8,128)(2,1)S(1)} %get-tuple-element.111), channel_id=1, source_target_pairs={{0,4},{4,0},{1,5},{5,1},{2,6},{6,2},{3,7},{7,3},{8,12},{12,8},{9,1... | collective-permute-start | bytes 491528 | tf_op jit(solution)/shard_map/ppermute | solution.py:104
  30.1 8.6 %collective-permute-start.12 = (bf16[160,768]{1,0:T(8,128)(2,1)S(1)}, bf16[160,768]{1,0:T(8,128)(2,1)S(1)}, u32[]{:S(2)}, u32[]{:S(2)}) collective-permute-start(bf16[160,768]{1,0:T(8,128)(2,1)S(1)} %collective-permute-done.11.refs_2_), channel_id=1, source_target_pairs={{0,8},{8,0},{16,24},{24,16},{1,9},{9,1},{17,25},{25,17},{2,10},{10... | collective-permute-start | bytes 737288 | tf_op jit(solution)/shard_map/ppermute | solution.py:122
  30.4 9.5 %collective-permute-start.17 = (bf16[160,768]{1,0:T(8,128)(2,1)S(1)}, bf16[160,768]{1,0:T(8,128)(2,1)S(1)}, u32[]{:S(2)}, u32[]{:S(2)}) collective-permute-start(bf16[160,768]{1,0:T(8,128)(2,1)S(1)} %collective-permute-done.15.refs_6_), channel_id=1, source_target_pairs={{0,16},{8,24},{16,0},{24,8},{1,17},{9,25},{17,1},{25,9},{2,18},{10... | collective-permute-start | bytes 737288 | tf_op jit(solution)/shard_map/ppermute | solution.py:122
  31.9 8.6 %collective-permute-start.9 = (bf16[128,640]{1,0:T(8,128)(2,1)S(1)}, bf16[128,640]{1,0:T(8,128)(2,1)S(1)}, u32[]{:S(2)}, u32[]{:S(2)}) collective-permute-start(bf16[128,640]{1,0:T(8,128)(2,1)S(1)} %add_convert_fusion.11.refs_0_), channel_id=1, source_target_pairs={{0,1},{1,0},{2,3},{3,2},{4,5},{5,4},{6,7},{7,6},{8,9},{9,8},{10,11... | collective-permute-start | bytes 491528 | tf_op jit(solution)/shard_map/ppermute | solution.py:107
  34.4 10.4 %collective-permute-start.13 = (bf16[160,768]{1,0:T(8,128)(2,1)S(1)}, bf16[160,768]{1,0:T(8,128)(2,1)S(1)}, u32[]{:S(2)}, u32[]{:S(2)}) collective-permute-start(bf16[160,768]{1,0:T(8,128)(2,1)S(1)} %collective-permute-done.11.refs_2_), channel_id=1, source_target_pairs={{0,16},{8,24},{16,0},{24,8},{1,17},{9,25},{17,1},{25,9},{2,18},{10... | collective-permute-start | bytes 737288 | tf_op jit(solution)/shard_map/ppermute | solution.py:122
  34.9 9.9 %collective-permute-start.16 = (bf16[160,768]{1,0:T(8,128)(2,1)S(1)}, bf16[160,768]{1,0:T(8,128)(2,1)S(1)}, u32[]{:S(2)}, u32[]{:S(2)}) collective-permute-start(bf16[160,768]{1,0:T(8,128)(2,1)S(1)} %collective-permute-done.15.refs_6_), channel_id=1, source_target_pairs={{0,8},{8,0},{16,24},{24,16},{1,9},{9,1},{17,25},{25,17},{2,10},{10... | collective-permute-start | bytes 737288 | tf_op jit(solution)/shard_map/ppermute | solution.py:122
  38.7 8.9 %collective-permute-start.14 = (bf16[160,768]{1,0:T(8,128)(2,1)S(1)}, bf16[160,768]{1,0:T(8,128)(2,1)S(1)}, u32[]{:S(2)}, u32[]{:S(2)}) collective-permute-start(bf16[160,768]{1,0:T(8,128)(2,1)S(1)} %collective-permute-done.12.refs_3_), channel_id=1, source_target_pairs={{0,16},{8,24},{16,0},{24,8},{1,17},{9,25},{17,1},{25,9},{2,18},{10... | collective-permute-start | bytes 737288 | tf_op jit(solution)/shard_map/ppermute | solution.py:122
  40.0 7.7 %collective-permute-start.18 = (bf16[160,768]{1,0:T(8,128)(2,1)S(1)}, bf16[160,768]{1,0:T(8,128)(2,1)S(1)}, u32[]{:S(2)}, u32[]{:S(2)}) collective-permute-start(bf16[160,768]{1,0:T(8,128)(2,1)S(1)} %collective-permute-done.17.refs_8_), channel_id=1, source_target_pairs={{0,8},{8,0},{16,24},{24,16},{1,9},{9,1},{17,25},{25,17},{2,10},{10... | collective-permute-start | bytes 737288 | tf_op jit(solution)/shard_map/ppermute | solution.py:122
  40.7 6.9 %collective-permute-start.10 = (bf16[128,640]{1,0:T(8,128)(2,1)S(1)}, bf16[128,640]{1,0:T(8,128)(2,1)S(1)}, u32[]{:S(2)}, u32[]{:S(2)}) collective-permute-start(bf16[128,640]{1,0:T(8,128)(2,1)S(1)} %get-tuple-element.117.refs_0_.refs_15_), channel_id=1, source_target_pairs={{0,4},{4,0},{1,5},{5,1},{2,6},{6,2},{3,7},{7,3},{8,12},{12,8},{9,1... | collective-permute-start | bytes 491528 | tf_op jit(solution)/shard_map/ppermute | solution.py:104
  48.8 4.5 %collective-permute-start.19 = (bf16[128,640]{1,0:T(8,128)(2,1)S(1)}, bf16[128,640]{1,0:T(8,128)(2,1)S(1)}, u32[]{:S(2)}, u32[]{:S(2)}) collective-permute-start(bf16[128,640]{1,0:T(8,128)(2,1)S(1)} %get-tuple-element.123), channel_id=1, source_target_pairs={{0,4},{4,0},{1,5},{5,1},{2,6},{6,2},{3,7},{7,3},{8,12},{12,8},{9,1... | collective-permute-start | bytes 491528 | tf_op jit(solution)/shard_map/ppermute | solution.py:104
  53.3 6.5 %collective-permute-start.20 = (bf16[128,640]{1,0:T(8,128)(2,1)S(1)}, bf16[128,640]{1,0:T(8,128)(2,1)S(1)}, u32[]{:S(2)}, u32[]{:S(2)}) collective-permute-start(bf16[128,640]{1,0:T(8,128)(2,1)S(1)} %add_convert_fusion.10.refs_0_), channel_id=1, source_target_pairs={{0,1},{1,0},{2,3},{3,2},{4,5},{5,4},{6,7},{7,6},{8,9},{9,8},{10,11... | collective-permute-start | bytes 491528 | tf_op jit(solution)/shard_map/ppermute | solution.py:107
  65.8 13.3 %collective-permute-start.27 = (bf16[320,768]{1,0:T(8,128)(2,1)S(1)}, bf16[320,768]{1,0:T(8,128)(2,1)S(1)}, u32[]{:S(2)}, u32[]{:S(2)}) collective-permute-start(bf16[320,768]{1,0:T(8,128)(2,1)S(1)} %get-tuple-element.143), channel_id=1, source_target_pairs={{0,8},{8,0},{16,24},{24,16},{1,9},{9,1},{17,25},{25,17},{2,10},{10... | collective-permute-start | bytes 1474568 | tf_op jit(solution)/shard_map/ppermute | solution.py:122
  67.3 6.0 %collective-permute-start.23 = (bf16[128,640]{1,0:T(8,128)(2,1)S(1)}, bf16[128,640]{1,0:T(8,128)(2,1)S(1)}, u32[]{:S(2)}, u32[]{:S(2)}) collective-permute-start(bf16[128,640]{1,0:T(8,128)(2,1)S(1)} %add_convert_fusion.9.refs_0_), channel_id=1, source_target_pairs={{0,1},{1,0},{2,3},{3,2},{4,5},{5,4},{6,7},{7,6},{8,9},{9,8},{10,11... | collective-permute-start | bytes 491528 | tf_op jit(solution)/shard_map/ppermute | solution.py:107
  68.4 12.7 %collective-permute-start.28 = (bf16[320,768]{1,0:T(8,128)(2,1)S(1)}, bf16[320,768]{1,0:T(8,128)(2,1)S(1)}, u32[]{:S(2)}, u32[]{:S(2)}) collective-permute-start(bf16[320,768]{1,0:T(8,128)(2,1)S(1)} %get-tuple-element.145), channel_id=1, source_target_pairs={{0,16},{8,24},{16,0},{24,8},{1,17},{9,25},{17,1},{25,9},{2,18},{10... | collective-permute-start | bytes 1474568 | tf_op jit(solution)/shard_map/ppermute | solution.py:122
  73.7 1.5 %collective-permute-start.24 = (bf16[128,640]{1,0:T(8,128)(2,1)S(1)}, bf16[128,640]{1,0:T(8,128)(2,1)S(1)}, u32[]{:S(2)}, u32[]{:S(2)}) collective-permute-start(bf16[128,640]{1,0:T(8,128)(2,1)S(1)} %get-tuple-element.133.refs_1_.refs_5_), channel_id=1, source_target_pairs={{0,4},{4,0},{1,5},{5,1},{2,6},{6,2},{3,7},{7,3},{8,12},{12,8},{9,1... | collective-permute-start | bytes 491528 | tf_op jit(solution)/shard_map/ppermute | solution.py:104
  77.6 3.6 %collective-permute-start.25 = (bf16[256,640]{1,0:T(8,128)(2,1)S(1)}, bf16[256,640]{1,0:T(8,128)(2,1)S(1)}, u32[]{:S(2)}, u32[]{:S(2)}) collective-permute-start(bf16[256,640]{1,0:T(8,128)(2,1)S(1)} %get-tuple-element.136.refs_9_), channel_id=1, source_target_pairs={{0,4},{4,0},{1,5},{5,1},{2,6},{6,2},{3,7},{7,3},{8,12},{12,8},{9,1... | collective-permute-start | bytes 983048 | tf_op jit(solution)/shard_map/ppermute | solution.py:104
  82.4 11.9 %collective-permute-start.29 = (bf16[704,256]{1,0:T(8,128)(2,1)S(1)}, bf16[704,256]{1,0:T(8,128)(2,1)S(1)}, u32[]{:S(2)}, u32[]{:S(2)}) collective-permute-start(bf16[704,256]{1,0:T(8,128)(2,1)S(1)} %get-tuple-element.150), channel_id=1, source_target_pairs={{0,4},{4,0},{1,5},{5,1},{2,6},{6,2},{3,7},{7,3},{8,12},{12,8},{9,1... | collective-permute-start | bytes 1081352 | tf_op jit(solution)/shard_map/ppermute | solution.py:104
  82.5 8.4 %collective-permute-start.30 = (bf16[160,768]{1,0:T(8,128)(2,1)S(1)}, bf16[160,768]{1,0:T(8,128)(2,1)S(1)}, u32[]{:S(2)}, u32[]{:S(2)}) collective-permute-start(bf16[160,768]{1,0:T(8,128)(2,1)S(1)} %slice.48), channel_id=1, source_target_pairs={{0,16},{8,24},{16,0},{24,8},{1,17},{9,25},{17,1},{25,9},{2,18},{10... | collective-permute-start | bytes 737288 | tf_op jit(solution)/shard_map/ppermute | solution.py:122
  84.2 8.3 %collective-permute-start.31 = (bf16[160,768]{1,0:T(8,128)(2,1)S(1)}, bf16[160,768]{1,0:T(8,128)(2,1)S(1)}, u32[]{:S(2)}, u32[]{:S(2)}) collective-permute-start(bf16[160,768]{1,0:T(8,128)(2,1)S(1)} %slice.49), channel_id=1, source_target_pairs={{0,8},{8,0},{16,24},{24,16},{1,9},{9,1},{17,25},{25,17},{2,10},{10... | collective-permute-start | bytes 737288 | tf_op jit(solution)/shard_map/ppermute | solution.py:122
  84.8 9.5 %collective-permute-start.26 = (bf16[128,640]{1,0:T(8,128)(2,1)S(1)}, bf16[128,640]{1,0:T(8,128)(2,1)S(1)}, u32[]{:S(2)}, u32[]{:S(2)}) collective-permute-start(bf16[128,640]{1,0:T(8,128)(2,1)S(1)} %get-tuple-element.138), channel_id=1, source_target_pairs={{0,1},{1,0},{2,3},{3,2},{4,5},{5,4},{6,7},{7,6},{8,9},{9,8},{10,11... | collective-permute-start | bytes 491528 | tf_op jit(solution)/shard_map/ppermute | solution.py:107
  85.0 11.2 %collective-permute-start.35 = (bf16[128,640]{1,0:T(8,128)(2,1)S(1)}, bf16[128,640]{1,0:T(8,128)(2,1)S(1)}, u32[]{:S(2)}, u32[]{:S(2)}) collective-permute-start(bf16[128,640]{1,0:T(8,128)(2,1)S(1)} %get-tuple-element.128.refs_0_), channel_id=1, source_target_pairs={{0,2},{1,3},{2,0},{3,1},{4,6},{5,7},{6,4},{7,5},{8,10},{9,11},{10,... | collective-permute-start | bytes 491528 | tf_op jit(solution)/shard_map/ppermute | solution.py:110
  91.0 9.3 %collective-permute-start.34 = (bf16[320,512]{1,0:T(8,128)(2,1)S(1)}, bf16[320,512]{1,0:T(8,128)(2,1)S(1)}, u32[]{:S(2)}, u32[]{:S(2)}) collective-permute-start(bf16[320,512]{1,0:T(8,128)(2,1)S(1)} %get-tuple-element.155), channel_id=1, source_target_pairs={{0,16},{8,24},{16,0},{24,8},{1,17},{9,25},{17,1},{25,9},{2,18},{10... | collective-permute-start | bytes 983048 | tf_op jit(solution)/shard_map/ppermute | solution.py:122
  94.4 5.9 %collective-permute-start.32 = (bf16[64,640]{1,0:T(8,128)(2,1)S(1)}, bf16[64,640]{1,0:T(8,128)(2,1)S(1)}, u32[]{:S(2)}, u32[]{:S(2)}) collective-permute-start(bf16[64,640]{1,0:T(8,128)(2,1)S(1)} %get-tuple-element.152), channel_id=1, source_target_pairs={{0,2},{1,3},{2,0},{3,1},{4,6},{5,7},{6,4},{7,5},{8,10},{9,11},{10,... | collective-permute-start | bytes 245768 | tf_op jit(solution)/shard_map/ppermute | solution.py:110
  94.9 5.6 %collective-permute-start.33 = (bf16[352,256]{1,0:T(8,128)(2,1)S(1)}, bf16[352,256]{1,0:T(8,128)(2,1)S(1)}, u32[]{:S(2)}, u32[]{:S(2)}) collective-permute-start(bf16[352,256]{1,0:T(8,128)(2,1)S(1)} %add_convert_fusion.7), channel_id=1, source_target_pairs={{0,8},{8,0},{16,24},{24,16},{1,9},{9,1},{17,25},{25,17},{2,10},{10... | collective-permute-start | bytes 540680 | tf_op jit(solution)/shard_map/ppermute | solution.py:122
  100.7 6.2 %collective-permute-start.37 = (bf16[64,640]{1,0:T(8,128)(2,1)S(1)}, bf16[64,640]{1,0:T(8,128)(2,1)S(1)}, u32[]{:S(2)}, u32[]{:S(2)}) collective-permute-start(bf16[64,640]{1,0:T(8,128)(2,1)S(1)} %last_norm.1.refs_2_), channel_id=1, source_target_pairs={{0,1},{1,0},{2,3},{3,2},{4,5},{5,4},{6,7},{7,6},{8,9},{9,8},{10,11... | collective-permute-start | bytes 245768 | tf_op jit(solution)/shard_map/ppermute | solution.py:107
  101.5 6.0 %collective-permute-start.36 = (bf16[64,640]{1,0:T(8,128)(2,1)S(1)}, bf16[64,640]{1,0:T(8,128)(2,1)S(1)}, u32[]{:S(2)}, u32[]{:S(2)}) collective-permute-start(bf16[64,640]{1,0:T(8,128)(2,1)S(1)} %last_norm.1.refs_2_), channel_id=1, source_target_pairs={{0,2},{1,3},{2,0},{3,1},{4,6},{5,7},{6,4},{7,5},{8,10},{9,11},{10,... | collective-permute-start | bytes 245768 | tf_op jit(solution)/shard_map/ppermute | solution.py:110
  103.6 4.6 %collective-permute-start.38 = (bf16[176,256]{1,0:T(8,128)(2,1)S(1)}, bf16[176,256]{1,0:T(8,128)(2,1)S(1)}, u32[]{:S(2)}, u32[]{:S(2)}) collective-permute-start(bf16[176,256]{1,0:T(8,128)(2,1)S(1)} %slice.50), channel_id=1, source_target_pairs={{0,16},{8,24},{16,0},{24,8},{1,17},{9,25},{17,1},{25,9},{2,18},{10... | collective-permute-start | bytes 270344 | tf_op jit(solution)/shard_map/ppermute | solution.py:122
  104.8 5.4 %collective-permute-start.39 = (bf16[160,512]{1,0:T(8,128)(2,1)S(1)}, bf16[160,512]{1,0:T(8,128)(2,1)S(1)}, u32[]{:S(2)}, u32[]{:S(2)}) collective-permute-start(bf16[160,512]{1,0:T(8,128)(2,1)S(1)} %slice.51), channel_id=1, source_target_pairs={{0,8},{8,0},{16,24},{24,16},{1,9},{9,1},{17,25},{25,17},{2,10},{10... | collective-permute-start | bytes 491528 | tf_op jit(solution)/shard_map/ppermute | solution.py:122
  106.2 6.8 %collective-permute-start.42 = (bf16[160,768]{1,0:T(8,128)(2,1)S(1)}, bf16[160,768]{1,0:T(8,128)(2,1)S(1)}, u32[]{:S(2)}, u32[]{:S(2)}) collective-permute-start(bf16[160,768]{1,0:T(8,128)(2,1)S(1)} %add_convert_fusion.4), channel_id=1, source_target_pairs={{0,0},{1,1},{2,4},{3,5},{4,2},{5,3},{6,6},{7,7},{8,8},{9,9},{10,12... | collective-permute-start | bytes 737288 | tf_op jit(solution)/shard_map/ppermute | solution.py:119
  106.9 6.2 %collective-permute-start.43 = (bf16[160,768]{1,0:T(8,128)(2,1)S(1)}, bf16[160,768]{1,0:T(8,128)(2,1)S(1)}, u32[]{:S(2)}, u32[]{:S(2)}) collective-permute-start(bf16[160,768]{1,0:T(8,128)(2,1)S(1)} %add_convert_fusion.3), channel_id=1, source_target_pairs={{0,0},{1,1},{2,4},{3,5},{4,2},{5,3},{6,6},{7,7},{8,8},{9,9},{10,12... | collective-permute-start | bytes 737288 | tf_op jit(solution)/shard_map/ppermute | solution.py:119
  110.2 6.1 %collective-permute-start.40 = (bf16[64,640]{1,0:T(8,128)(2,1)S(1)}, bf16[64,640]{1,0:T(8,128)(2,1)S(1)}, u32[]{:S(2)}, u32[]{:S(2)}) collective-permute-start(bf16[64,640]{1,0:T(8,128)(2,1)S(1)} %collective-permute-done.36.refs_4_), channel_id=1, source_target_pairs={{0,1},{1,0},{2,3},{3,2},{4,5},{5,4},{6,7},{7,6},{8,9},{9,8},{10,11... | collective-permute-start | bytes 245768 | tf_op jit(solution)/shard_map/ppermute | solution.py:107
  112.0 5.9 %collective-permute-start.41 = (bf16[176,256]{1,0:T(8,128)(2,1)S(1)}, bf16[176,256]{1,0:T(8,128)(2,1)S(1)}, u32[]{:S(2)}, u32[]{:S(2)}) collective-permute-start(bf16[176,256]{1,0:T(8,128)(2,1)S(1)} %add_convert_fusion.14), channel_id=1, source_target_pairs={{0,1},{1,0},{2,3},{3,2},{4,5},{5,4},{6,7},{7,6},{8,9},{9,8},{10,11... | collective-permute-start | bytes 270344 | tf_op jit(solution)/shard_map/ppermute | solution.py:107
  112.3 10.3 %collective-permute-start.44 = (bf16[160,512]{1,0:T(8,128)(2,1)S(1)}, bf16[160,512]{1,0:T(8,128)(2,1)S(1)}, u32[]{:S(2)}, u32[]{:S(2)}) collective-permute-start(bf16[160,512]{1,0:T(8,128)(2,1)S(1)} %add_convert_fusion.8), channel_id=1, source_target_pairs={{0,0},{1,1},{2,4},{3,5},{4,2},{5,3},{6,6},{7,7},{8,8},{9,9},{10,12... | collective-permute-start | bytes 491528 | tf_op jit(solution)/shard_map/ppermute | solution.py:119
  117.9 7.2 %collective-permute-start.48 = (bf16[176,256]{1,0:T(8,128)(2,1)S(1)}, bf16[176,256]{1,0:T(8,128)(2,1)S(1)}, u32[]{:S(2)}, u32[]{:S(2)}) collective-permute-start(bf16[176,256]{1,0:T(8,128)(2,1)S(1)} %add_convert_fusion.13), channel_id=1, source_target_pairs={{0,2},{1,3},{2,0},{3,1},{4,6},{5,7},{6,4},{7,5},{8,10},{9,11},{10,... | collective-permute-start | bytes 270344 | tf_op jit(solution)/shard_map/ppermute | solution.py:110
  122.1 7.5 %collective-permute-start.46 = (bf16[160,768]{1,0:T(8,128)(2,1)S(1)}, bf16[160,768]{1,0:T(8,128)(2,1)S(1)}, u32[]{:S(2)}, u32[]{:S(2)}) collective-permute-start(bf16[160,768]{1,0:T(8,128)(2,1)S(1)} %collective-permute-done.42.refs_8_), channel_id=1, source_target_pairs={{0,4},{4,0},{1,5},{5,1},{2,6},{6,2},{3,7},{7,3},{8,12},{12,8},{9,1... | collective-permute-start | bytes 737288 | tf_op jit(solution)/shard_map/ppermute | solution.py:104
  122.4 7.2 %collective-permute-start.47 = (bf16[160,768]{1,0:T(8,128)(2,1)S(1)}, bf16[160,768]{1,0:T(8,128)(2,1)S(1)}, u32[]{:S(2)}, u32[]{:S(2)}) collective-permute-start(bf16[160,768]{1,0:T(8,128)(2,1)S(1)} %collective-permute-done.43.refs_10_), channel_id=1, source_target_pairs={{0,4},{4,0},{1,5},{5,1},{2,6},{6,2},{3,7},{7,3},{8,12},{12,8},{9,1... | collective-permute-start | bytes 737288 | tf_op jit(solution)/shard_map/ppermute | solution.py:104
  122.6 7.0 %collective-permute-start.45 = (bf16[160,512]{1,0:T(8,128)(2,1)S(1)}, bf16[160,512]{1,0:T(8,128)(2,1)S(1)}, u32[]{:S(2)}, u32[]{:S(2)}) collective-permute-start(bf16[160,512]{1,0:T(8,128)(2,1)S(1)} %collective-permute-done.44.refs_6_), channel_id=1, source_target_pairs={{0,4},{4,0},{1,5},{5,1},{2,6},{6,2},{3,7},{7,3},{8,12},{12,8},{9,1... | collective-permute-start | bytes 491528 | tf_op jit(solution)/shard_map/ppermute | solution.py:104
  125.1 4.4 %collective-permute-start.49 = (bf16[176,256]{1,0:T(8,128)(2,1)S(1)}, bf16[176,256]{1,0:T(8,128)(2,1)S(1)}, u32[]{:S(2)}, u32[]{:S(2)}) collective-permute-start(bf16[176,256]{1,0:T(8,128)(2,1)S(1)} %add_convert_fusion.12.refs_12_), channel_id=1, source_target_pairs={{0,4},{4,0},{1,5},{5,1},{2,6},{6,2},{3,7},{7,3},{8,12},{12,8},{9,1... | collective-permute-start | bytes 270344 | tf_op jit(solution)/shard_map/ppermute | solution.py:104
  (7 other events, 38.6 us)

commit v5 on v4

--- a/solution.py
+++ b/solution.py
@@ -127,6 +127,9 @@
         far = fsdp_hop(value, second)
         both = fsdp_hop(near, second)
         return [value, near, far, both] if first == 1 else [value, far, near, both]
+
+    def gather_direct(value):
+        return [value] + [fsdp_hop(value, step) for step in range(1, n_fsdp)]
 
     def across_pairs(value):
         step = 2
@@ -287,7 +290,7 @@
         cross_qo = cross(pack_qo)
         cross_f1, cross_f2 = cross(pack_f1), cross(pack_f2)
         kv_blocks = gather_blocks(pack_kv, 1)
-        qo_blocks = gather_blocks(cross_qo, 2)
+        qo_blocks = gather_direct(cross_qo)
         f1_blocks = gather_blocks(cross_f1, 1)
         f2_blocks = gather_blocks(cross_f2, 2)
 
@@ -700,7 +703,7 @@
         kv_sum = last_add(kv_both, kv_h2)
         kv_n = z_near(kv_sum)
         qo_c = cross(last_add(qo_both, qo_h2))
-        row_both, kv_n, ffn_c1, ffn_c2 = together(row_both, kv_n, ffn_c1, ffn_c2)
+        row_both, kv_n = together(row_both, kv_n)
         kv_sum = add(kv_sum, kv_n)
         kv_sum = add(kv_sum, z_far(kv_sum))
         kv_other = core_swap(kv_sum)

time: 132 us -> 130 us (0.985)
  starting transfers between devices: 67.3 us -> 57.1 us
  waiting for transfers between devices: 45.9 us -> 54.4 us
    ppermute x20, waiting for transfers between devices: 23.2 us -> 30.8 us  [fsdp_hop(): return lax.ppermute(value, 'fsdp', [(i, i ^ step) for i in range(n_fsdp)])]
    ppermute x13, starting transfers between devices: 21.2 us -> 15.7 us  [core_swap(): lax.ppermute(value, 'context', [(i, i ^ 1) for i in range(n_context)])]
    ppermute x20, starting transfers between devices: 24.7 us -> 20.3 us  [fsdp_hop(): return lax.ppermute(value, 'fsdp', [(i, i ^ step) for i in range(n_fsdp)])]
    ppermute x4, starting transfers between devices: 9.38 us -> 8.03 us  [z_far(): return lax.ppermute(value, 'tensor', [(i, i ^ 2) for i in range(n_tensor)])]
  transfers between devices with their start and end apart: 50 -> 50, of which waited for: 23 -> 22; matrix products, arithmetic and copies ran while one was open for 1% -> 1% of each run, Pallas kernels for 6% -> 6%
where the time goes in v5:
time: 130 us
  starting transfers between devices  57.1 us (44%)
  waiting for transfers between devices  54.4 us (42%)
  Pallas kernels  14.7 us (11%)
  local copies, waits for them, and re-layouts  1.69 us (1%)
    ppermute x20, waiting for transfers between devices, fsdp_hop(): return lax.ppermute(value, 'fsdp', [(i, i ^ step) for i in range(n_fsdp)])  30.8 us
    ppermute x20, starting transfers between devices, fsdp_hop(): return lax.ppermute(value, 'fsdp', [(i, i ^ step) for i in range(n_fsdp)])  20.3 us
    ppermute x7, waiting for transfers between devices, z_near(): return lax.ppermute(value, 'tensor', [(i, i ^ 1) for i in range(n_tensor)])  16.1 us
    ppermute x13, starting transfers between devices, core_swap(): lax.ppermute(value, 'context', [(i, i ^ 1) for i in range(n_context)])  15.7 us
    pallas_call x14, Pallas kernels, call(): pl.pallas_call(wrapped, name=name, out_shape=tuple(outs), in_specs=[smem]...  14.7 us
    ppermute x7, starting transfers between devices, z_near(): return lax.ppermute(value, 'tensor', [(i, i ^ 1) for i in range(n_tensor)])  8.92 us
    ppermute x4, starting transfers between devices, z_far(): return lax.ppermute(value, 'tensor', [(i, i ^ 2) for i in range(n_tensor)])  8.03 us
    ppermute x13, waiting for transfers between devices, core_swap(): lax.ppermute(value, 'context', [(i, i ^ 1) for i in range(n_context)])  6.32 us
  transfers between devices with their start and end apart: 50, of which 22 were waited for; matrix products, arithmetic and copies ran while one was open for 1% of the time, Pallas kernels for 6%

profile of v5, /device:TPU:0, one launch (start us, length us, event | category | flops | bytes accessed | tf_op | source)
XLA Modules:
  0.0 129.6 jit_solution(12360121157566655798)
XLA Ops:
  1.8 1.9 %pack.1 = (bf16[176,512]{1,0:T(8,128)(2,1)S(1)}, bf16[160,512]{1,0:T(8,128)(2,1)S(1)}, bf16[160,768]{1,0:T(8,128)(2,1)S(1)}, bf16[160,768]{1,0:T(8,128)(2,1)S(1)...) custom-call(s32[1,4]{1,0:T(1,128)S(1)} %copy-done.3, bf16[160,256]{1,0:T(8,128)(2,1)} %refs_1_.2, ...), custom_call_target="tpu_custom_call" | custom-call | bytes 1359872 | tf_op jit(solution)/shard_map/pack/pallas_call | solution.py:79
  4.4 2.6 %collective-permute-start.1 = (bf16[176,512]{1,0:T(8,128)(2,1)S(1)}, bf16[176,512]{1,0:T(8,128)(2,1)S(1)}, u32[]{:S(2)}, u32[]{:S(2)}) collective-permute-start(bf16[176,512]{1,0:T(8,128)(2,1)S(1)} %get-tuple-element.104.refs_3_), channel_id=1, source_target_pairs={{0,8},{8,0},{16,24},{24,16},{1,9},{9,1},{17,25},{25,17},{2,10},{10... | collective-permute-start | bytes 540680 | tf_op jit(solution)/shard_map/ppermute | solution.py:122
  7.0 1.5 %collective-permute-start.2 = (bf16[176,512]{1,0:T(8,128)(2,1)S(1)}, bf16[176,512]{1,0:T(8,128)(2,1)S(1)}, u32[]{:S(2)}, u32[]{:S(2)}) collective-permute-start(bf16[176,512]{1,0:T(8,128)(2,1)S(1)} %get-tuple-element.104.refs_3_), channel_id=1, source_target_pairs={{0,16},{8,24},{16,0},{24,8},{1,17},{9,25},{17,1},{25,9},{2,18},{10... | collective-permute-start | bytes 540680 | tf_op jit(solution)/shard_map/ppermute | solution.py:122
  8.5 1.9 %collective-permute-done.1.refs_4_ = bf16[176,512]{1,0:T(8,128)(2,1)S(1)} collective-permute-done((bf16[176,512]{1,0:T(8,128)(2,1)S(1)}, bf16[176,512]{1,0:T(8,128)(2,1)S(1)}, u32[]{:S(2)}, u32[]{:S(2)}) %collective-permute-start.1) | collective-permute-done | bytes 180256 | tf_op jit(solution)/shard_map/ppermute | solution.py:122
  10.5 2.0 %collective-permute-start.3 = (bf16[176,512]{1,0:T(8,128)(2,1)S(1)}, bf16[176,512]{1,0:T(8,128)(2,1)S(1)}, u32[]{:S(2)}, u32[]{:S(2)}) collective-permute-start(bf16[176,512]{1,0:T(8,128)(2,1)S(1)} %collective-permute-done.1.refs_4_), channel_id=1, source_target_pairs={{0,16},{8,24},{16,0},{24,8},{1,17},{9,25},{17,1},{25,9},{2,18},{10... | collective-permute-start | bytes 540680 | tf_op jit(solution)/shard_map/ppermute | solution.py:122
  12.6 2.0 %collective-permute-start.5 = (bf16[160,512]{1,0:T(8,128)(2,1)S(1)}, bf16[160,512]{1,0:T(8,128)(2,1)S(1)}, u32[]{:S(2)}, u32[]{:S(2)}) collective-permute-start(bf16[160,512]{1,0:T(8,128)(2,1)S(1)} %collective-permute-done.4.refs_7_), channel_id=1, source_target_pairs={{0,8},{8,0},{16,24},{24,16},{1,9},{9,1},{17,25},{25,17},{2,10},{10... | collective-permute-start | bytes 491528 | tf_op jit(solution)/shard_map/ppermute | solution.py:122
  15.2 1.3 collective-permute-done.7.refs_10_
  17.2 6.9 %collective-permute-done.6.refs_9_ = bf16[160,512]{1,0:T(8,128)(2,1)S(1)} collective-permute-done((bf16[160,512]{1,0:T(8,128)(2,1)S(1)}, bf16[160,512]{1,0:T(8,128)(2,1)S(1)}, u32[]{:S(2)}, u32[]{:S(2)}) %collective-permute-start.6) | collective-permute-done | bytes 163872 | tf_op jit(solution)/shard_map/ppermute | solution.py:122
  25.1 2.3 %front.1 = (bf16[512,640]{1,0:T(8,128)(2,1)S(1)}, bf16[1536,256]{1,0:T(8,128)(2,1)S(1)}, f32[1032,256]{1,0:T(8,128)S(1)}, bf16[640,1024]{1,0:T(8,128)(2,1)S(1)},...) custom-call(s32[1,4]{1,0:T(1,128)S(1)} %copy-done.3, bf16[256,640]{1,0:T(8,128)(2,1)S(1)} %copy-done, ...), custom_call_target="tpu_custom_call" | custom-call | flops 469762048 | bytes 6877184 | tf_op jit(solution)/shard_map/front/pallas_call | solution.py:79
  27.4 1.7 %collective-permute-start.8 = (bf16[128,640]{1,0:T(8,128)(2,1)S(1)}, bf16[128,640]{1,0:T(8,128)(2,1)S(1)}, u32[]{:S(2)}, u32[]{:S(2)}) collective-permute-start(bf16[128,640]{1,0:T(8,128)(2,1)S(1)} %get-tuple-element.109), channel_id=1, source_target_pairs={{0,4},{4,0},{1,5},{5,1},{2,6},{6,2},{3,7},{7,3},{8,12},{12,8},{9,1... | collective-permute-start | bytes 491528 | tf_op jit(solution)/shard_map/ppermute | solution.py:104
  30.6 2.4 %collective-permute-start.9 = (bf16[128,640]{1,0:T(8,128)(2,1)S(1)}, bf16[128,640]{1,0:T(8,128)(2,1)S(1)}, u32[]{:S(2)}, u32[]{:S(2)}) collective-permute-start(bf16[128,640]{1,0:T(8,128)(2,1)S(1)} %add_convert_fusion.11.refs_0_), channel_id=1, source_target_pairs={{0,1},{1,0},{2,3},{3,2},{4,5},{5,4},{6,7},{7,6},{8,9},{9,8},{10,11... | collective-permute-start | bytes 491528 | tf_op jit(solution)/shard_map/ppermute | solution.py:107
  33.0 1.1 collective-permute-start.13
  34.1 1.4 %collective-permute-start.16 = (bf16[160,768]{1,0:T(8,128)(2,1)S(1)}, bf16[160,768]{1,0:T(8,128)(2,1)S(1)}, u32[]{:S(2)}, u32[]{:S(2)}) collective-permute-start(bf16[160,768]{1,0:T(8,128)(2,1)S(1)} %collective-permute-done.15.refs_6_), channel_id=1, source_target_pairs={{0,8},{8,0},{16,24},{24,16},{1,9},{9,1},{17,25},{25,17},{2,10},{10... | collective-permute-start | bytes 737288 | tf_op jit(solution)/shard_map/ppermute | solution.py:122
  35.5 2.4 %collective-permute-done.12.refs_3_ = bf16[160,768]{1,0:T(8,128)(2,1)S(1)} collective-permute-done((bf16[160,768]{1,0:T(8,128)(2,1)S(1)}, bf16[160,768]{1,0:T(8,128)(2,1)S(1)}, u32[]{:S(2)}, u32[]{:S(2)}) %collective-permute-start.12) | collective-permute-done | bytes 245792 | tf_op jit(solution)/shard_map/ppermute | solution.py:122
  38.7 4.7 %collective-permute-start.10 = (bf16[128,640]{1,0:T(8,128)(2,1)S(1)}, bf16[128,640]{1,0:T(8,128)(2,1)S(1)}, u32[]{:S(2)}, u32[]{:S(2)}) collective-permute-start(bf16[128,640]{1,0:T(8,128)(2,1)S(1)} %get-tuple-element.115.refs_0_.refs_15_), channel_id=1, source_target_pairs={{0,4},{4,0},{1,5},{5,1},{2,6},{6,2},{3,7},{7,3},{8,12},{12,8},{9,1... | collective-permute-start | bytes 491528 | tf_op jit(solution)/shard_map/ppermute | solution.py:104
  43.4 3.4 %collective-permute-done.14.refs_5_ = bf16[160,768]{1,0:T(8,128)(2,1)S(1)} collective-permute-done((bf16[160,768]{1,0:T(8,128)(2,1)S(1)}, bf16[160,768]{1,0:T(8,128)(2,1)S(1)}, u32[]{:S(2)}, u32[]{:S(2)}) %collective-permute-start.14) | collective-permute-done | bytes 245792 | tf_op jit(solution)/shard_map/ppermute | solution.py:122
  46.8 1.2 ffn.1
  48.0 2.8 %collective-permute-start.19 = (bf16[128,640]{1,0:T(8,128)(2,1)S(1)}, bf16[128,640]{1,0:T(8,128)(2,1)S(1)}, u32[]{:S(2)}, u32[]{:S(2)}) collective-permute-start(bf16[128,640]{1,0:T(8,128)(2,1)S(1)} %get-tuple-element.121), channel_id=1, source_target_pairs={{0,4},{4,0},{1,5},{5,1},{2,6},{6,2},{3,7},{7,3},{8,12},{12,8},{9,1... | collective-permute-start | bytes 491528 | tf_op jit(solution)/shard_map/ppermute | solution.py:104
  51.9 1.7 %collective-permute-start.20 = (bf16[128,640]{1,0:T(8,128)(2,1)S(1)}, bf16[128,640]{1,0:T(8,128)(2,1)S(1)}, u32[]{:S(2)}, u32[]{:S(2)}) collective-permute-start(bf16[128,640]{1,0:T(8,128)(2,1)S(1)} %add_convert_fusion.10.refs_0_), channel_id=1, source_target_pairs={{0,1},{1,0},{2,3},{3,2},{4,5},{5,4},{6,7},{7,6},{8,9},{9,8},{10,11... | collective-permute-start | bytes 491528 | tf_op jit(solution)/shard_map/ppermute | solution.py:107
  53.6 4.8 %collective-permute-done.20.refs_1_ = bf16[128,640]{1,0:T(8,128)(2,1)S(1)} collective-permute-done((bf16[128,640]{1,0:T(8,128)(2,1)S(1)}, bf16[128,640]{1,0:T(8,128)(2,1)S(1)}, u32[]{:S(2)}, u32[]{:S(2)}) %collective-permute-start.20) | collective-permute-done | bytes 163872 | tf_op jit(solution)/shard_map/ppermute | solution.py:107
  58.8 1.4 %collective-permute-done.21.refs_1_.refs_3_ = bf16[128,640]{1,0:T(8,128)(2,1)S(1)} collective-permute-done((bf16[128,640]{1,0:T(8,128)(2,1)S(1)}, bf16[128,640]{1,0:T(8,128)(2,1)S(1)}, u32[]{:S(2)}, u32[]{:S(2)}) %collective-permute-start.21) | collective-permute-done | bytes 163872 | tf_op jit(solution)/shard_map/ppermute | solution.py:104
  60.2 1.3 %ffn_back.1 = (bf16[256,1024]{1,0:T(8,128)(2,1)S(1)}, f32[128,640]{1,0:T(8,128)S(1)}, bf16[128,640]{1,0:T(8,128)(2,1)S(1)}) custom-call(bf16[128,640]{1,0:T(8,128)(2,1)S(1)} %get-tuple-element.127.refs_0_.refs_2_, bf16[128,640]{1,0:T(8,128)(2,1)S(1)} %collective-permute-done.21.refs_1_.refs_3_, f32[256,1024]{1,0:T(8,128)S(1)} %get-tuple-element.123.refs_18_.refs_2_, ...), custom_call_target="tpu_custom_call" | custom-call | flops 503316480 | bytes 4358144 | tf_op jit(solution)/shard_map/ffn_back/pallas_call | solution.py:79
  61.7 1.2 collective-permute-done.22
  63.0 1.3 %ffn_weights.1 = (bf16[320,768]{1,0:T(8,128)(2,1)S(1)}, bf16[320,768]{1,0:T(8,128)(2,1)S(1)}, bf16[320,768]{1,0:T(8,128)(2,1)S(1)}, bf16[320,768]{1,0:T(8,128)(2,1)S(1)}) custom-call(bf16[128,640]{1,0:T(8,128)(2,1)S(1)} %get-tuple-element.115.refs_0_.refs_15_, bf16[128,640]{1,0:T(8,128)(2,1)S(1)} %collective-permute-done.10.refs_1_.refs_16_, ...), custom_call_target="tpu_custom_call" | custom-call | flops 503316480 | bytes 3407872 | tf_op jit(solution)/shard_map/ffn_weights/pallas_call | solution.py:79
  64.3 1.4 %collective-permute-start.27 = (bf16[320,768]{1,0:T(8,128)(2,1)S(1)}, bf16[320,768]{1,0:T(8,128)(2,1)S(1)}, u32[]{:S(2)}, u32[]{:S(2)}) collective-permute-start(bf16[320,768]{1,0:T(8,128)(2,1)S(1)} %get-tuple-element.141), channel_id=1, source_target_pairs={{0,8},{8,0},{16,24},{24,16},{1,9},{9,1},{17,25},{25,17},{2,10},{10... | collective-permute-start | bytes 1474568 | tf_op jit(solution)/shard_map/ppermute | solution.py:122
  65.7 1.7 %collective-permute-start.23 = (bf16[128,640]{1,0:T(8,128)(2,1)S(1)}, bf16[128,640]{1,0:T(8,128)(2,1)S(1)}, u32[]{:S(2)}, u32[]{:S(2)}) collective-permute-start(bf16[128,640]{1,0:T(8,128)(2,1)S(1)} %add_convert_fusion.9.refs_0_), channel_id=1, source_target_pairs={{0,1},{1,0},{2,3},{3,2},{4,5},{5,4},{6,7},{7,6},{8,9},{9,8},{10,11... | collective-permute-start | bytes 491528 | tf_op jit(solution)/shard_map/ppermute | solution.py:107
  67.8 3.8 %collective-permute-done.23.refs_1_ = bf16[128,640]{1,0:T(8,128)(2,1)S(1)} collective-permute-done((bf16[128,640]{1,0:T(8,128)(2,1)S(1)}, bf16[128,640]{1,0:T(8,128)(2,1)S(1)}, u32[]{:S(2)}, u32[]{:S(2)}) %collective-permute-start.23) | collective-permute-done | bytes 163872 | tf_op jit(solution)/shard_map/ppermute | solution.py:107
  72.1 1.4 %collective-permute-done.24.refs_2_.refs_6_ = bf16[128,640]{1,0:T(8,128)(2,1)S(1)} collective-permute-done((bf16[128,640]{1,0:T(8,128)(2,1)S(1)}, bf16[128,640]{1,0:T(8,128)(2,1)S(1)}, u32[]{:S(2)}, u32[]{:S(2)}) %collective-permute-start.24) | collective-permute-done | bytes 163872 | tf_op jit(solution)/shard_map/ppermute | solution.py:104
  73.5 2.5 %attn_back.1 = (bf16[256,256]{1,0:T(8,128)(2,1)S(1)}, bf16[512,512]{1,0:T(8,128)(2,1)S(1)}, f32[256,640]{1,0:T(8,128)S(1)}, bf16[256,640]{1,0:T(8,128)(2,1)S(1)}...) custom-call(s32[1,4]{1,0:T(1,128)S(1)} %copy-done.4, bf16[128,640]{1,0:T(8,128)(2,1)S(1)} %get-tuple-element.131.refs_1_.refs_5_, ...), custom_call_target="tpu_custom_call" | custom-call | flops 671088640 | bytes 5646336 | tf_op jit(solution)/shard_map/attn_back/pallas_call | solution.py:79
  76.2 1.5 %collective-permute-done.27 = bf16[320,768]{1,0:T(8,128)(2,1)S(1)} collective-permute-done((bf16[320,768]{1,0:T(8,128)(2,1)S(1)}, bf16[320,768]{1,0:T(8,128)(2,1)S(1)}, u32[]{:S(2)}, u32[]{:S(2)}) %collective-permute-start.27) | collective-permute-done | bytes 491552 | tf_op jit(solution)/shard_map/ppermute | solution.py:122
  77.8 2.4 %collective-permute-done.28 = bf16[320,768]{1,0:T(8,128)(2,1)S(1)} collective-permute-done((bf16[320,768]{1,0:T(8,128)(2,1)S(1)}, bf16[320,768]{1,0:T(8,128)(2,1)S(1)}, u32[]{:S(2)}, u32[]{:S(2)}) %collective-permute-start.28) | collective-permute-done | bytes 491552 | tf_op jit(solution)/shard_map/ppermute | solution.py:122
  82.1 1.2 collective-permute-start.31
  83.9 2.3 %collective-permute-start.35 = (bf16[128,640]{1,0:T(8,128)(2,1)S(1)}, bf16[128,640]{1,0:T(8,128)(2,1)S(1)}, u32[]{:S(2)}, u32[]{:S(2)}) collective-permute-start(bf16[128,640]{1,0:T(8,128)(2,1)S(1)} %get-tuple-element.126.refs_0_), channel_id=1, source_target_pairs={{0,2},{1,3},{2,0},{3,1},{4,6},{5,7},{6,4},{7,5},{8,10},{9,11},{10,... | collective-permute-start | bytes 491528 | tf_op jit(solution)/shard_map/ppermute | solution.py:110
  86.2 3.8 %collective-permute-done.30 = bf16[160,768]{1,0:T(8,128)(2,1)S(1)} collective-permute-done((bf16[160,768]{1,0:T(8,128)(2,1)S(1)}, bf16[160,768]{1,0:T(8,128)(2,1)S(1)}, u32[]{:S(2)}, u32[]{:S(2)}) %collective-permute-start.30) | collective-permute-done | bytes 245792 | tf_op jit(solution)/shard_map/ppermute | solution.py:122
  90.4 2.4 %collective-permute-done.26.refs_1_ = bf16[128,640]{1,0:T(8,128)(2,1)S(1)} collective-permute-done((bf16[128,640]{1,0:T(8,128)(2,1)S(1)}, bf16[128,640]{1,0:T(8,128)(2,1)S(1)}, u32[]{:S(2)}, u32[]{:S(2)}) %collective-permute-start.26) | collective-permute-done | bytes 163872 | tf_op jit(solution)/shard_map/ppermute | solution.py:107
  93.2 1.3 collective-permute-start.33
  94.5 4.8 %collective-permute-done.34 = bf16[320,512]{1,0:T(8,128)(2,1)S(1)} collective-permute-done((bf16[320,512]{1,0:T(8,128)(2,1)S(1)}, bf16[320,512]{1,0:T(8,128)(2,1)S(1)}, u32[]{:S(2)}, u32[]{:S(2)}) %collective-permute-start.34) | collective-permute-done | bytes 327712 | tf_op jit(solution)/shard_map/ppermute | solution.py:122
  99.9 2.0 %collective-permute-start.36 = (bf16[64,640]{1,0:T(8,128)(2,1)S(1)}, bf16[64,640]{1,0:T(8,128)(2,1)S(1)}, u32[]{:S(2)}, u32[]{:S(2)}) collective-permute-start(bf16[64,640]{1,0:T(8,128)(2,1)S(1)} %last_norm.1.refs_2_), channel_id=1, source_target_pairs={{0,2},{1,3},{2,0},{3,1},{4,6},{5,7},{6,4},{7,5},{8,10},{9,11},{10,... | collective-permute-start | bytes 245768 | tf_op jit(solution)/shard_map/ppermute | solution.py:110
  103.2 1.5 %collective-permute-start.39 = (bf16[160,512]{1,0:T(8,128)(2,1)S(1)}, bf16[160,512]{1,0:T(8,128)(2,1)S(1)}, u32[]{:S(2)}, u32[]{:S(2)}) collective-permute-start(bf16[160,512]{1,0:T(8,128)(2,1)S(1)} %slice.51), channel_id=1, source_target_pairs={{0,8},{8,0},{16,24},{24,16},{1,9},{9,1},{17,25},{25,17},{2,10},{10... | collective-permute-start | bytes 491528 | tf_op jit(solution)/shard_map/ppermute | solution.py:122
  106.6 2.0 %collective-permute-done.39 = bf16[160,512]{1,0:T(8,128)(2,1)S(1)} collective-permute-done((bf16[160,512]{1,0:T(8,128)(2,1)S(1)}, bf16[160,512]{1,0:T(8,128)(2,1)S(1)}, u32[]{:S(2)}, u32[]{:S(2)}) %collective-permute-start.39) | collective-permute-done | bytes 163872 | tf_op jit(solution)/shard_map/ppermute | solution.py:122
  108.7 2.0 %collective-permute-start.40 = (bf16[64,640]{1,0:T(8,128)(2,1)S(1)}, bf16[64,640]{1,0:T(8,128)(2,1)S(1)}, u32[]{:S(2)}, u32[]{:S(2)}) collective-permute-start(bf16[64,640]{1,0:T(8,128)(2,1)S(1)} %collective-permute-done.36.refs_4_), channel_id=1, source_target_pairs={{0,1},{1,0},{2,3},{3,2},{4,5},{5,4},{6,7},{7,6},{8,9},{9,8},{10,11... | collective-permute-start | bytes 245768 | tf_op jit(solution)/shard_map/ppermute | solution.py:107
  111.5 3.4 %collective-permute-done.40.refs_5_ = bf16[64,640]{1,0:T(8,128)(2,1)S(1)} collective-permute-done((bf16[64,640]{1,0:T(8,128)(2,1)S(1)}, bf16[64,640]{1,0:T(8,128)(2,1)S(1)}, u32[]{:S(2)}, u32[]{:S(2)}) %collective-permute-start.40) | collective-permute-done | bytes 81952 | tf_op jit(solution)/shard_map/ppermute | solution.py:107
  114.9 1.6 %collective-permute-done.41 = bf16[176,256]{1,0:T(8,128)(2,1)S(1)} collective-permute-done((bf16[176,256]{1,0:T(8,128)(2,1)S(1)}, bf16[176,256]{1,0:T(8,128)(2,1)S(1)}, u32[]{:S(2)}, u32[]{:S(2)}) %collective-permute-start.41) | collective-permute-done | bytes 90144 | tf_op jit(solution)/shard_map/ppermute | solution.py:107
  116.5 3.5 %collective-permute-start.48 = (bf16[176,256]{1,0:T(8,128)(2,1)S(1)}, bf16[176,256]{1,0:T(8,128)(2,1)S(1)}, u32[]{:S(2)}, u32[]{:S(2)}) collective-permute-start(bf16[176,256]{1,0:T(8,128)(2,1)S(1)} %add_convert_fusion.13), channel_id=1, source_target_pairs={{0,2},{1,3},{2,0},{3,1},{4,6},{5,7},{6,4},{7,5},{8,10},{9,11},{10,... | collective-permute-start | bytes 270344 | tf_op jit(solution)/shard_map/ppermute | solution.py:110
  120.8 4.5 %collective-permute-start.43 = (bf16[160,512]{1,0:T(8,128)(2,1)S(1)}, bf16[160,512]{1,0:T(8,128)(2,1)S(1)}, u32[]{:S(2)}, u32[]{:S(2)}) collective-permute-start(bf16[160,512]{1,0:T(8,128)(2,1)S(1)} %collective-permute-done.42.refs_6_), channel_id=1, source_target_pairs={{0,4},{4,0},{1,5},{5,1},{2,6},{6,2},{3,7},{7,3},{8,12},{12,8},{9,1... | collective-permute-start | bytes 491528 | tf_op jit(solution)/shard_map/ppermute | solution.py:104
  125.3 1.1 collective-permute-done.48
  126.6 1.3 collective-permute-done.49.refs_13_
  127.8 1.8 %finish.1 = (f32[256,640]{1,0:T(8,128)}, f32[256,640]{1,0:T(8,128)}, f32[160,256]{1,0:T(8,128)}, f32[160,256]{1,0:T(8,128)}, f32[160,256]{1,0:T(8,128)}, /*index...) custom-call(bf16[128,640]{1,0:T(8,128)(2,1)S(1)} %get-tuple-element., ...), custom_call_target="tpu_custom_call" | custom-call | bytes 5098496 | tf_op jit(solution)/shard_map/finish/pallas_call | solution.py:79
  (94 shorter events, 18.2 us)
Async XLA Ops:
  0.7 3.1 %collective-permute-start = (bf16[256,640]{1,0:T(8,128)(2,1)}, bf16[256,640]{1,0:T(8,128)(2,1)S(1)}, u32[]{:S(2)}, u32[]{:S(2)}) collective-permute-start(bf16[256,640]{1,0:T(8,128)(2,1)} %refs_2_.5), channel_id=1, source_target_pairs={{0,4},{4,0},{1,5},{5,1},{2,6},{6,2},{3,7},{7,3},{8,12},{12,8},{9,1... | collective-permute-start | bytes 983048 | tf_op jit(solution)/shard_map/ppermute | solution.py:104
  3.7 4.8 %collective-permute-start.4 = (bf16[160,512]{1,0:T(8,128)(2,1)S(1)}, bf16[160,512]{1,0:T(8,128)(2,1)S(1)}, u32[]{:S(2)}, u32[]{:S(2)}) collective-permute-start(bf16[160,512]{1,0:T(8,128)(2,1)S(1)} %get-tuple-element.105), channel_id=1, source_target_pairs={{0,0},{1,1},{2,4},{3,5},{4,2},{5,3},{6,6},{7,7},{8,8},{9,9},{10,12... | collective-permute-start | bytes 491528 | tf_op jit(solution)/shard_map/ppermute | solution.py:119
  4.4 6.0 %collective-permute-start.1 = (bf16[176,512]{1,0:T(8,128)(2,1)S(1)}, bf16[176,512]{1,0:T(8,128)(2,1)S(1)}, u32[]{:S(2)}, u32[]{:S(2)}) collective-permute-start(bf16[176,512]{1,0:T(8,128)(2,1)S(1)} %get-tuple-element.104.refs_3_), channel_id=1, source_target_pairs={{0,8},{8,0},{16,24},{24,16},{1,9},{9,1},{17,25},{25,17},{2,10},{10... | collective-permute-start | bytes 540680 | tf_op jit(solution)/shard_map/ppermute | solution.py:122
  7.0 7.5 %collective-permute-start.2 = (bf16[176,512]{1,0:T(8,128)(2,1)S(1)}, bf16[176,512]{1,0:T(8,128)(2,1)S(1)}, u32[]{:S(2)}, u32[]{:S(2)}) collective-permute-start(bf16[176,512]{1,0:T(8,128)(2,1)S(1)} %get-tuple-element.104.refs_3_), channel_id=1, source_target_pairs={{0,16},{8,24},{16,0},{24,8},{1,17},{9,25},{17,1},{25,9},{2,18},{10... | collective-permute-start | bytes 540680 | tf_op jit(solution)/shard_map/ppermute | solution.py:122
  8.5 8.0 %collective-permute-start.7 = (bf16[160,512]{1,0:T(8,128)(2,1)S(1)}, bf16[160,512]{1,0:T(8,128)(2,1)S(1)}, u32[]{:S(2)}, u32[]{:S(2)}) collective-permute-start(bf16[160,512]{1,0:T(8,128)(2,1)S(1)} %collective-permute-done.4.refs_7_), channel_id=1, source_target_pairs={{0,24},{8,16},{16,8},{24,0},{1,25},{9,17},{17,9},{25,1},{2,26},{10... | collective-permute-start | bytes 491528 | tf_op jit(solution)/shard_map/ppermute | solution.py:122
  10.5 13.6 %collective-permute-start.3 = (bf16[176,512]{1,0:T(8,128)(2,1)S(1)}, bf16[176,512]{1,0:T(8,128)(2,1)S(1)}, u32[]{:S(2)}, u32[]{:S(2)}) collective-permute-start(bf16[176,512]{1,0:T(8,128)(2,1)S(1)} %collective-permute-done.1.refs_4_), channel_id=1, source_target_pairs={{0,16},{8,24},{16,0},{24,8},{1,17},{9,25},{17,1},{25,9},{2,18},{10... | collective-permute-start | bytes 540680 | tf_op jit(solution)/shard_map/ppermute | solution.py:122
  12.5 11.6 %collective-permute-start.6 = (bf16[160,512]{1,0:T(8,128)(2,1)S(1)}, bf16[160,512]{1,0:T(8,128)(2,1)S(1)}, u32[]{:S(2)}, u32[]{:S(2)}) collective-permute-start(bf16[160,512]{1,0:T(8,128)(2,1)S(1)} %collective-permute-done.4.refs_7_), channel_id=1, source_target_pairs={{0,16},{8,24},{16,0},{24,8},{1,17},{9,25},{17,1},{25,9},{2,18},{10... | collective-permute-start | bytes 491528 | tf_op jit(solution)/shard_map/ppermute | solution.py:122
  12.6 11.5 %collective-permute-start.5 = (bf16[160,512]{1,0:T(8,128)(2,1)S(1)}, bf16[160,512]{1,0:T(8,128)(2,1)S(1)}, u32[]{:S(2)}, u32[]{:S(2)}) collective-permute-start(bf16[160,512]{1,0:T(8,128)(2,1)S(1)} %collective-permute-done.4.refs_7_), channel_id=1, source_target_pairs={{0,8},{8,0},{16,24},{24,16},{1,9},{9,1},{17,25},{25,17},{2,10},{10... | collective-permute-start | bytes 491528 | tf_op jit(solution)/shard_map/ppermute | solution.py:122
  14.5 14.6 %collective-permute-start.11 = (bf16[160,768]{1,0:T(8,128)(2,1)S(1)}, bf16[160,768]{1,0:T(8,128)(2,1)S(1)}, u32[]{:S(2)}, u32[]{:S(2)}) collective-permute-start(bf16[160,768]{1,0:T(8,128)(2,1)S(1)} %get-tuple-element.116), channel_id=1, source_target_pairs={{0,0},{1,1},{2,4},{3,5},{4,2},{5,3},{6,6},{7,7},{8,8},{9,9},{10,12... | collective-permute-start | bytes 737288 | tf_op jit(solution)/shard_map/ppermute | solution.py:119
  16.5 13.3 %collective-permute-start.15 = (bf16[160,768]{1,0:T(8,128)(2,1)S(1)}, bf16[160,768]{1,0:T(8,128)(2,1)S(1)}, u32[]{:S(2)}, u32[]{:S(2)}) collective-permute-start(bf16[160,768]{1,0:T(8,128)(2,1)S(1)} %get-tuple-element.117), channel_id=1, source_target_pairs={{0,0},{1,1},{2,4},{3,5},{4,2},{5,3},{6,6},{7,7},{8,8},{9,9},{10,12... | collective-permute-start | bytes 737288 | tf_op jit(solution)/shard_map/ppermute | solution.py:119
  27.4 3.2 %collective-permute-start.8 = (bf16[128,640]{1,0:T(8,128)(2,1)S(1)}, bf16[128,640]{1,0:T(8,128)(2,1)S(1)}, u32[]{:S(2)}, u32[]{:S(2)}) collective-permute-start(bf16[128,640]{1,0:T(8,128)(2,1)S(1)} %get-tuple-element.109), channel_id=1, source_target_pairs={{0,4},{4,0},{1,5},{5,1},{2,6},{6,2},{3,7},{7,3},{8,12},{12,8},{9,1... | collective-permute-start | bytes 491528 | tf_op jit(solution)/shard_map/ppermute | solution.py:104
  29.1 8.8 %collective-permute-start.12 = (bf16[160,768]{1,0:T(8,128)(2,1)S(1)}, bf16[160,768]{1,0:T(8,128)(2,1)S(1)}, u32[]{:S(2)}, u32[]{:S(2)}) collective-permute-start(bf16[160,768]{1,0:T(8,128)(2,1)S(1)} %collective-permute-done.11.refs_2_), channel_id=1, source_target_pairs={{0,8},{8,0},{16,24},{24,16},{1,9},{9,1},{17,25},{25,17},{2,10},{10... | collective-permute-start | bytes 737288 | tf_op jit(solution)/shard_map/ppermute | solution.py:122
  29.8 8.1 %collective-permute-start.17 = (bf16[160,768]{1,0:T(8,128)(2,1)S(1)}, bf16[160,768]{1,0:T(8,128)(2,1)S(1)}, u32[]{:S(2)}, u32[]{:S(2)}) collective-permute-start(bf16[160,768]{1,0:T(8,128)(2,1)S(1)} %collective-permute-done.15.refs_6_), channel_id=1, source_target_pairs={{0,16},{8,24},{16,0},{24,8},{1,17},{9,25},{17,1},{25,9},{2,18},{10... | collective-permute-start | bytes 737288 | tf_op jit(solution)/shard_map/ppermute | solution.py:122
  30.6 7.8 %collective-permute-start.9 = (bf16[128,640]{1,0:T(8,128)(2,1)S(1)}, bf16[128,640]{1,0:T(8,128)(2,1)S(1)}, u32[]{:S(2)}, u32[]{:S(2)}) collective-permute-start(bf16[128,640]{1,0:T(8,128)(2,1)S(1)} %add_convert_fusion.11.refs_0_), channel_id=1, source_target_pairs={{0,1},{1,0},{2,3},{3,2},{4,5},{5,4},{6,7},{7,6},{8,9},{9,8},{10,11... | collective-permute-start | bytes 491528 | tf_op jit(solution)/shard_map/ppermute | solution.py:107
  33.0 10.5 %collective-permute-start.13 = (bf16[160,768]{1,0:T(8,128)(2,1)S(1)}, bf16[160,768]{1,0:T(8,128)(2,1)S(1)}, u32[]{:S(2)}, u32[]{:S(2)}) collective-permute-start(bf16[160,768]{1,0:T(8,128)(2,1)S(1)} %collective-permute-done.11.refs_2_), channel_id=1, source_target_pairs={{0,16},{8,24},{16,0},{24,8},{1,17},{9,25},{17,1},{25,9},{2,18},{10... | collective-permute-start | bytes 737288 | tf_op jit(solution)/shard_map/ppermute | solution.py:122
  34.1 9.3 %collective-permute-start.16 = (bf16[160,768]{1,0:T(8,128)(2,1)S(1)}, bf16[160,768]{1,0:T(8,128)(2,1)S(1)}, u32[]{:S(2)}, u32[]{:S(2)}) collective-permute-start(bf16[160,768]{1,0:T(8,128)(2,1)S(1)} %collective-permute-done.15.refs_6_), channel_id=1, source_target_pairs={{0,8},{8,0},{16,24},{24,16},{1,9},{9,1},{17,25},{25,17},{2,10},{10... | collective-permute-start | bytes 737288 | tf_op jit(solution)/shard_map/ppermute | solution.py:122
  37.9 8.9 %collective-permute-start.14 = (bf16[160,768]{1,0:T(8,128)(2,1)S(1)}, bf16[160,768]{1,0:T(8,128)(2,1)S(1)}, u32[]{:S(2)}, u32[]{:S(2)}) collective-permute-start(bf16[160,768]{1,0:T(8,128)(2,1)S(1)} %collective-permute-done.12.refs_3_), channel_id=1, source_target_pairs={{0,16},{8,24},{16,0},{24,8},{1,17},{9,25},{17,1},{25,9},{2,18},{10... | collective-permute-start | bytes 737288 | tf_op jit(solution)/shard_map/ppermute | solution.py:122
  37.9 8.9 %collective-permute-start.18 = (bf16[160,768]{1,0:T(8,128)(2,1)S(1)}, bf16[160,768]{1,0:T(8,128)(2,1)S(1)}, u32[]{:S(2)}, u32[]{:S(2)}) collective-permute-start(bf16[160,768]{1,0:T(8,128)(2,1)S(1)} %collective-permute-done.17.refs_8_), channel_id=1, source_target_pairs={{0,8},{8,0},{16,24},{24,16},{1,9},{9,1},{17,25},{25,17},{2,10},{10... | collective-permute-start | bytes 737288 | tf_op jit(solution)/shard_map/ppermute | solution.py:122
  38.7 8.1 %collective-permute-start.10 = (bf16[128,640]{1,0:T(8,128)(2,1)S(1)}, bf16[128,640]{1,0:T(8,128)(2,1)S(1)}, u32[]{:S(2)}, u32[]{:S(2)}) collective-permute-start(bf16[128,640]{1,0:T(8,128)(2,1)S(1)} %get-tuple-element.115.refs_0_.refs_15_), channel_id=1, source_target_pairs={{0,4},{4,0},{1,5},{5,1},{2,6},{6,2},{3,7},{7,3},{8,12},{12,8},{9,1... | collective-permute-start | bytes 491528 | tf_op jit(solution)/shard_map/ppermute | solution.py:104
  48.0 3.8 %collective-permute-start.19 = (bf16[128,640]{1,0:T(8,128)(2,1)S(1)}, bf16[128,640]{1,0:T(8,128)(2,1)S(1)}, u32[]{:S(2)}, u32[]{:S(2)}) collective-permute-start(bf16[128,640]{1,0:T(8,128)(2,1)S(1)} %get-tuple-element.121), channel_id=1, source_target_pairs={{0,4},{4,0},{1,5},{5,1},{2,6},{6,2},{3,7},{7,3},{8,12},{12,8},{9,1... | collective-permute-start | bytes 491528 | tf_op jit(solution)/shard_map/ppermute | solution.py:104
  51.9 6.5 %collective-permute-start.20 = (bf16[128,640]{1,0:T(8,128)(2,1)S(1)}, bf16[128,640]{1,0:T(8,128)(2,1)S(1)}, u32[]{:S(2)}, u32[]{:S(2)}) collective-permute-start(bf16[128,640]{1,0:T(8,128)(2,1)S(1)} %add_convert_fusion.10.refs_0_), channel_id=1, source_target_pairs={{0,1},{1,0},{2,3},{3,2},{4,5},{5,4},{6,7},{7,6},{8,9},{9,8},{10,11... | collective-permute-start | bytes 491528 | tf_op jit(solution)/shard_map/ppermute | solution.py:107
  58.7 1.5 %collective-permute-start.21 = (bf16[128,640]{1,0:T(8,128)(2,1)S(1)}, bf16[128,640]{1,0:T(8,128)(2,1)S(1)}, u32[]{:S(2)}, u32[]{:S(2)}) collective-permute-start(bf16[128,640]{1,0:T(8,128)(2,1)S(1)} %get-tuple-element.127.refs_0_.refs_2_), channel_id=1, source_target_pairs={{0,4},{4,0},{1,5},{5,1},{2,6},{6,2},{3,7},{7,3},{8,12},{12,8},{9,1... | collective-permute-start | bytes 491528 | tf_op jit(solution)/shard_map/ppermute | solution.py:104
  64.3 13.3 %collective-permute-start.27 = (bf16[320,768]{1,0:T(8,128)(2,1)S(1)}, bf16[320,768]{1,0:T(8,128)(2,1)S(1)}, u32[]{:S(2)}, u32[]{:S(2)}) collective-permute-start(bf16[320,768]{1,0:T(8,128)(2,1)S(1)} %get-tuple-element.141), channel_id=1, source_target_pairs={{0,8},{8,0},{16,24},{24,16},{1,9},{9,1},{17,25},{25,17},{2,10},{10... | collective-permute-start | bytes 1474568 | tf_op jit(solution)/shard_map/ppermute | solution.py:122
  65.7 6.0 %collective-permute-start.23 = (bf16[128,640]{1,0:T(8,128)(2,1)S(1)}, bf16[128,640]{1,0:T(8,128)(2,1)S(1)}, u32[]{:S(2)}, u32[]{:S(2)}) collective-permute-start(bf16[128,640]{1,0:T(8,128)(2,1)S(1)} %add_convert_fusion.9.refs_0_), channel_id=1, source_target_pairs={{0,1},{1,0},{2,3},{3,2},{4,5},{5,4},{6,7},{7,6},{8,9},{9,8},{10,11... | collective-permute-start | bytes 491528 | tf_op jit(solution)/shard_map/ppermute | solution.py:107
  67.4 12.7 %collective-permute-start.28 = (bf16[320,768]{1,0:T(8,128)(2,1)S(1)}, bf16[320,768]{1,0:T(8,128)(2,1)S(1)}, u32[]{:S(2)}, u32[]{:S(2)}) collective-permute-start(bf16[320,768]{1,0:T(8,128)(2,1)S(1)} %get-tuple-element.143), channel_id=1, source_target_pairs={{0,16},{8,24},{16,0},{24,8},{1,17},{9,25},{17,1},{25,9},{2,18},{10... | collective-permute-start | bytes 1474568 | tf_op jit(solution)/shard_map/ppermute | solution.py:122
  72.1 1.5 %collective-permute-start.24 = (bf16[128,640]{1,0:T(8,128)(2,1)S(1)}, bf16[128,640]{1,0:T(8,128)(2,1)S(1)}, u32[]{:S(2)}, u32[]{:S(2)}) collective-permute-start(bf16[128,640]{1,0:T(8,128)(2,1)S(1)} %get-tuple-element.131.refs_1_.refs_5_), channel_id=1, source_target_pairs={{0,4},{4,0},{1,5},{5,1},{2,6},{6,2},{3,7},{7,3},{8,12},{12,8},{9,1... | collective-permute-start | bytes 491528 | tf_op jit(solution)/shard_map/ppermute | solution.py:104
  76.0 4.3 %collective-permute-start.25 = (bf16[256,640]{1,0:T(8,128)(2,1)S(1)}, bf16[256,640]{1,0:T(8,128)(2,1)S(1)}, u32[]{:S(2)}, u32[]{:S(2)}) collective-permute-start(bf16[256,640]{1,0:T(8,128)(2,1)S(1)} %get-tuple-element.134.refs_9_), channel_id=1, source_target_pairs={{0,4},{4,0},{1,5},{5,1},{2,6},{6,2},{3,7},{7,3},{8,12},{12,8},{9,1... | collective-permute-start | bytes 983048 | tf_op jit(solution)/shard_map/ppermute | solution.py:104
  81.5 11.3 %collective-permute-start.29 = (bf16[704,256]{1,0:T(8,128)(2,1)S(1)}, bf16[704,256]{1,0:T(8,128)(2,1)S(1)}, u32[]{:S(2)}, u32[]{:S(2)}) collective-permute-start(bf16[704,256]{1,0:T(8,128)(2,1)S(1)} %get-tuple-element.148), channel_id=1, source_target_pairs={{0,4},{4,0},{1,5},{5,1},{2,6},{6,2},{3,7},{7,3},{8,12},{12,8},{9,1... | collective-permute-start | bytes 1081352 | tf_op jit(solution)/shard_map/ppermute | solution.py:104
  81.6 8.4 %collective-permute-start.30 = (bf16[160,768]{1,0:T(8,128)(2,1)S(1)}, bf16[160,768]{1,0:T(8,128)(2,1)S(1)}, u32[]{:S(2)}, u32[]{:S(2)}) collective-permute-start(bf16[160,768]{1,0:T(8,128)(2,1)S(1)} %slice.48), channel_id=1, source_target_pairs={{0,16},{8,24},{16,0},{24,8},{1,17},{9,25},{17,1},{25,9},{2,18},{10... | collective-permute-start | bytes 737288 | tf_op jit(solution)/shard_map/ppermute | solution.py:122
  82.1 8.3 %collective-permute-start.31 = (bf16[160,768]{1,0:T(8,128)(2,1)S(1)}, bf16[160,768]{1,0:T(8,128)(2,1)S(1)}, u32[]{:S(2)}, u32[]{:S(2)}) collective-permute-start(bf16[160,768]{1,0:T(8,128)(2,1)S(1)} %slice.49), channel_id=1, source_target_pairs={{0,8},{8,0},{16,24},{24,16},{1,9},{9,1},{17,25},{25,17},{2,10},{10... | collective-permute-start | bytes 737288 | tf_op jit(solution)/shard_map/ppermute | solution.py:122
  83.3 9.5 %collective-permute-start.26 = (bf16[128,640]{1,0:T(8,128)(2,1)S(1)}, bf16[128,640]{1,0:T(8,128)(2,1)S(1)}, u32[]{:S(2)}, u32[]{:S(2)}) collective-permute-start(bf16[128,640]{1,0:T(8,128)(2,1)S(1)} %get-tuple-element.136), channel_id=1, source_target_pairs={{0,1},{1,0},{2,3},{3,2},{4,5},{5,4},{6,7},{7,6},{8,9},{9,8},{10,11... | collective-permute-start | bytes 491528 | tf_op jit(solution)/shard_map/ppermute | solution.py:107
  83.9 10.6 %collective-permute-start.35 = (bf16[128,640]{1,0:T(8,128)(2,1)S(1)}, bf16[128,640]{1,0:T(8,128)(2,1)S(1)}, u32[]{:S(2)}, u32[]{:S(2)}) collective-permute-start(bf16[128,640]{1,0:T(8,128)(2,1)S(1)} %get-tuple-element.126.refs_0_), channel_id=1, source_target_pairs={{0,2},{1,3},{2,0},{3,1},{4,6},{5,7},{6,4},{7,5},{8,10},{9,11},{10,... | collective-permute-start | bytes 491528 | tf_op jit(solution)/shard_map/ppermute | solution.py:110
  90.0 9.3 %collective-permute-start.34 = (bf16[320,512]{1,0:T(8,128)(2,1)S(1)}, bf16[320,512]{1,0:T(8,128)(2,1)S(1)}, u32[]{:S(2)}, u32[]{:S(2)}) collective-permute-start(bf16[320,512]{1,0:T(8,128)(2,1)S(1)} %get-tuple-element.153), channel_id=1, source_target_pairs={{0,16},{8,24},{16,0},{24,8},{1,17},{9,25},{17,1},{25,9},{2,18},{10... | collective-permute-start | bytes 983048 | tf_op jit(solution)/shard_map/ppermute | solution.py:122
  92.9 6.5 %collective-permute-start.32 = (bf16[64,640]{1,0:T(8,128)(2,1)S(1)}, bf16[64,640]{1,0:T(8,128)(2,1)S(1)}, u32[]{:S(2)}, u32[]{:S(2)}) collective-permute-start(bf16[64,640]{1,0:T(8,128)(2,1)S(1)} %get-tuple-element.150), channel_id=1, source_target_pairs={{0,2},{1,3},{2,0},{3,1},{4,6},{5,7},{6,4},{7,5},{8,10},{9,11},{10,... | collective-permute-start | bytes 245768 | tf_op jit(solution)/shard_map/ppermute | solution.py:110
  93.2 6.2 %collective-permute-start.33 = (bf16[352,256]{1,0:T(8,128)(2,1)S(1)}, bf16[352,256]{1,0:T(8,128)(2,1)S(1)}, u32[]{:S(2)}, u32[]{:S(2)}) collective-permute-start(bf16[352,256]{1,0:T(8,128)(2,1)S(1)} %add_convert_fusion.7), channel_id=1, source_target_pairs={{0,8},{8,0},{16,24},{24,16},{1,9},{9,1},{17,25},{25,17},{2,10},{10... | collective-permute-start | bytes 540680 | tf_op jit(solution)/shard_map/ppermute | solution.py:122
  99.6 5.9 %collective-permute-start.37 = (bf16[64,640]{1,0:T(8,128)(2,1)S(1)}, bf16[64,640]{1,0:T(8,128)(2,1)S(1)}, u32[]{:S(2)}, u32[]{:S(2)}) collective-permute-start(bf16[64,640]{1,0:T(8,128)(2,1)S(1)} %last_norm.1.refs_2_), channel_id=1, source_target_pairs={{0,1},{1,0},{2,3},{3,2},{4,5},{5,4},{6,7},{7,6},{8,9},{9,8},{10,11... | collective-permute-start | bytes 245768 | tf_op jit(solution)/shard_map/ppermute | solution.py:107
  99.9 6.2 %collective-permute-start.36 = (bf16[64,640]{1,0:T(8,128)(2,1)S(1)}, bf16[64,640]{1,0:T(8,128)(2,1)S(1)}, u32[]{:S(2)}, u32[]{:S(2)}) collective-permute-start(bf16[64,640]{1,0:T(8,128)(2,1)S(1)} %last_norm.1.refs_2_), channel_id=1, source_target_pairs={{0,2},{1,3},{2,0},{3,1},{4,6},{5,7},{6,4},{7,5},{8,10},{9,11},{10,... | collective-permute-start | bytes 245768 | tf_op jit(solution)/shard_map/ppermute | solution.py:110
  102.0 4.6 %collective-permute-start.38 = (bf16[176,256]{1,0:T(8,128)(2,1)S(1)}, bf16[176,256]{1,0:T(8,128)(2,1)S(1)}, u32[]{:S(2)}, u32[]{:S(2)}) collective-permute-start(bf16[176,256]{1,0:T(8,128)(2,1)S(1)} %slice.50), channel_id=1, source_target_pairs={{0,16},{8,24},{16,0},{24,8},{1,17},{9,25},{17,1},{25,9},{2,18},{10... | collective-permute-start | bytes 270344 | tf_op jit(solution)/shard_map/ppermute | solution.py:122
  103.2 5.4 %collective-permute-start.39 = (bf16[160,512]{1,0:T(8,128)(2,1)S(1)}, bf16[160,512]{1,0:T(8,128)(2,1)S(1)}, u32[]{:S(2)}, u32[]{:S(2)}) collective-permute-start(bf16[160,512]{1,0:T(8,128)(2,1)S(1)} %slice.51), channel_id=1, source_target_pairs={{0,8},{8,0},{16,24},{24,16},{1,9},{9,1},{17,25},{25,17},{2,10},{10... | collective-permute-start | bytes 491528 | tf_op jit(solution)/shard_map/ppermute | solution.py:122
  104.8 15.2 %collective-permute-start.44 = (bf16[160,768]{1,0:T(8,128)(2,1)S(1)}, bf16[160,768]{1,0:T(8,128)(2,1)S(1)}, u32[]{:S(2)}, u32[]{:S(2)}) collective-permute-start(bf16[160,768]{1,0:T(8,128)(2,1)S(1)} %add_convert_fusion.4), channel_id=1, source_target_pairs={{0,0},{1,1},{2,4},{3,5},{4,2},{5,3},{6,6},{7,7},{8,8},{9,9},{10,12... | collective-permute-start | bytes 737288 | tf_op jit(solution)/shard_map/ppermute | solution.py:119
  105.5 14.6 %collective-permute-start.46 = (bf16[160,768]{1,0:T(8,128)(2,1)S(1)}, bf16[160,768]{1,0:T(8,128)(2,1)S(1)}, u32[]{:S(2)}, u32[]{:S(2)}) collective-permute-start(bf16[160,768]{1,0:T(8,128)(2,1)S(1)} %add_convert_fusion.3), channel_id=1, source_target_pairs={{0,0},{1,1},{2,4},{3,5},{4,2},{5,3},{6,6},{7,7},{8,8},{9,9},{10,12... | collective-permute-start | bytes 737288 | tf_op jit(solution)/shard_map/ppermute | solution.py:119
  108.7 6.2 %collective-permute-start.40 = (bf16[64,640]{1,0:T(8,128)(2,1)S(1)}, bf16[64,640]{1,0:T(8,128)(2,1)S(1)}, u32[]{:S(2)}, u32[]{:S(2)}) collective-permute-start(bf16[64,640]{1,0:T(8,128)(2,1)S(1)} %collective-permute-done.36.refs_4_), channel_id=1, source_target_pairs={{0,1},{1,0},{2,3},{3,2},{4,5},{5,4},{6,7},{7,6},{8,9},{9,8},{10,11... | collective-permute-start | bytes 245768 | tf_op jit(solution)/shard_map/ppermute | solution.py:107
  110.7 5.8 %collective-permute-start.41 = (bf16[176,256]{1,0:T(8,128)(2,1)S(1)}, bf16[176,256]{1,0:T(8,128)(2,1)S(1)}, u32[]{:S(2)}, u32[]{:S(2)}) collective-permute-start(bf16[176,256]{1,0:T(8,128)(2,1)S(1)} %add_convert_fusion.14), channel_id=1, source_target_pairs={{0,1},{1,0},{2,3},{3,2},{4,5},{5,4},{6,7},{7,6},{8,9},{9,8},{10,11... | collective-permute-start | bytes 270344 | tf_op jit(solution)/shard_map/ppermute | solution.py:107
  110.8 10.0 %collective-permute-start.42 = (bf16[160,512]{1,0:T(8,128)(2,1)S(1)}, bf16[160,512]{1,0:T(8,128)(2,1)S(1)}, u32[]{:S(2)}, u32[]{:S(2)}) collective-permute-start(bf16[160,512]{1,0:T(8,128)(2,1)S(1)} %add_convert_fusion.8), channel_id=1, source_target_pairs={{0,0},{1,1},{2,4},{3,5},{4,2},{5,3},{6,6},{7,7},{8,8},{9,9},{10,12... | collective-permute-start | bytes 491528 | tf_op jit(solution)/shard_map/ppermute | solution.py:119
  116.5 10.0 %collective-permute-start.48 = (bf16[176,256]{1,0:T(8,128)(2,1)S(1)}, bf16[176,256]{1,0:T(8,128)(2,1)S(1)}, u32[]{:S(2)}, u32[]{:S(2)}) collective-permute-start(bf16[176,256]{1,0:T(8,128)(2,1)S(1)} %add_convert_fusion.13), channel_id=1, source_target_pairs={{0,2},{1,3},{2,0},{3,1},{4,6},{5,7},{6,4},{7,5},{8,10},{9,11},{10,... | collective-permute-start | bytes 270344 | tf_op jit(solution)/shard_map/ppermute | solution.py:110
  120.0 6.6 %collective-permute-start.45 = (bf16[160,768]{1,0:T(8,128)(2,1)S(1)}, bf16[160,768]{1,0:T(8,128)(2,1)S(1)}, u32[]{:S(2)}, u32[]{:S(2)}) collective-permute-start(bf16[160,768]{1,0:T(8,128)(2,1)S(1)} %collective-permute-done.44.refs_8_), channel_id=1, source_target_pairs={{0,4},{4,0},{1,5},{5,1},{2,6},{6,2},{3,7},{7,3},{8,12},{12,8},{9,1... | collective-permute-start | bytes 737288 | tf_op jit(solution)/shard_map/ppermute | solution.py:104
  120.0 6.6 %collective-permute-start.47 = (bf16[160,768]{1,0:T(8,128)(2,1)S(1)}, bf16[160,768]{1,0:T(8,128)(2,1)S(1)}, u32[]{:S(2)}, u32[]{:S(2)}) collective-permute-start(bf16[160,768]{1,0:T(8,128)(2,1)S(1)} %collective-permute-done.46.refs_10_), channel_id=1, source_target_pairs={{0,4},{4,0},{1,5},{5,1},{2,6},{6,2},{3,7},{7,3},{8,12},{12,8},{9,1... | collective-permute-start | bytes 737288 | tf_op jit(solution)/shard_map/ppermute | solution.py:104
  120.8 7.0 %collective-permute-start.43 = (bf16[160,512]{1,0:T(8,128)(2,1)S(1)}, bf16[160,512]{1,0:T(8,128)(2,1)S(1)}, u32[]{:S(2)}, u32[]{:S(2)}) collective-permute-start(bf16[160,512]{1,0:T(8,128)(2,1)S(1)} %collective-permute-done.42.refs_6_), channel_id=1, source_target_pairs={{0,4},{4,0},{1,5},{5,1},{2,6},{6,2},{3,7},{7,3},{8,12},{12,8},{9,1... | collective-permute-start | bytes 491528 | tf_op jit(solution)/shard_map/ppermute | solution.py:104
  (7 other events, 31.3 us)

commit v6 on v5

--- a/solution.py
+++ b/solution.py
@@ -698,7 +698,7 @@
             last_norm, "last_norm", [small_b], [row_mine, row_far, tokens, grad_hidden]
         )
         row_fars, row_nears = z_far(row_done), z_near(row_done)
-        row_fars, row_nears, kv_h2, qo_h2 = together(row_fars, row_nears, kv_h2, qo_h2)
+        row_fars, kv_h2, qo_h2 = together(row_fars, kv_h2, qo_h2)
         row_both = z_near(row_fars)
         kv_sum = last_add(kv_both, kv_h2)
         kv_n = z_near(kv_sum)

time: 130 us -> 133 us (1.023)
  waiting for transfers between devices: 54.4 us -> 58.7 us
    ppermute x7, waiting for transfers between devices: 16.1 us -> 21.6 us  [z_near(): return lax.ppermute(value, 'tensor', [(i, i ^ 1) for i in range(n_tensor)])]
    ppermute x4, starting transfers between devices: 8.03 us -> 5.15 us  [z_far(): return lax.ppermute(value, 'tensor', [(i, i ^ 2) for i in range(n_tensor)])]
    ppermute x13, starting transfers between devices: 15.7 us -> 17.7 us  [core_swap(): lax.ppermute(value, 'context', [(i, i ^ 1) for i in range(n_context)])]
where the time goes in v6:
time: 133 us
  waiting for transfers between devices  58.7 us (44%)
  starting transfers between devices  55.8 us (42%)
  Pallas kernels  14.7 us (11%)
  local copies, waits for them, and re-layouts  1.69 us (1%)
    ppermute x20, waiting for transfers between devices, fsdp_hop(): return lax.ppermute(value, 'fsdp', [(i, i ^ step) for i in range(n_fsdp)])  30.9 us
    ppermute x7, waiting for transfers between devices, z_near(): return lax.ppermute(value, 'tensor', [(i, i ^ 1) for i in range(n_tensor)])  21.6 us
    ppermute x20, starting transfers between devices, fsdp_hop(): return lax.ppermute(value, 'fsdp', [(i, i ^ step) for i in range(n_fsdp)])  20.4 us
    ppermute x13, starting transfers between devices, core_swap(): lax.ppermute(value, 'context', [(i, i ^ 1) for i in range(n_context)])  17.7 us
    pallas_call x14, Pallas kernels, call(): pl.pallas_call(wrapped, name=name, out_shape=tuple(outs), in_specs=[smem]...  14.7 us
    ppermute x7, starting transfers between devices, z_near(): return lax.ppermute(value, 'tensor', [(i, i ^ 1) for i in range(n_tensor)])  8.62 us
    ppermute x4, starting transfers between devices, z_far(): return lax.ppermute(value, 'tensor', [(i, i ^ 2) for i in range(n_tensor)])  5.15 us
    ppermute x13, waiting for transfers between devices, core_swap(): lax.ppermute(value, 'context', [(i, i ^ 1) for i in range(n_context)])  5.06 us
  transfers between devices with their start and end apart: 50, of which 22 were waited for; matrix products, arithmetic and copies ran while one was open for 1% of the time, Pallas kernels for 6%

profile of v6, /device:TPU:0, one launch (start us, length us, event | category | flops | bytes accessed | tf_op | source)
XLA Modules:
  0.0 132.8 jit_solution(8225962017564714730)
XLA Ops:
  1.8 1.9 %pack.1 = (bf16[176,512]{1,0:T(8,128)(2,1)S(1)}, bf16[160,512]{1,0:T(8,128)(2,1)S(1)}, bf16[160,768]{1,0:T(8,128)(2,1)S(1)}, bf16[160,768]{1,0:T(8,128)(2,1)S(1)...) custom-call(s32[1,4]{1,0:T(1,128)S(1)} %copy-done.3, bf16[160,256]{1,0:T(8,128)(2,1)} %refs_1_.2, ...), custom_call_target="tpu_custom_call" | custom-call | bytes 1359872 | tf_op jit(solution)/shard_map/pack/pallas_call | solution.py:79
  4.4 2.6 %collective-permute-start.1 = (bf16[176,512]{1,0:T(8,128)(2,1)S(1)}, bf16[176,512]{1,0:T(8,128)(2,1)S(1)}, u32[]{:S(2)}, u32[]{:S(2)}) collective-permute-start(bf16[176,512]{1,0:T(8,128)(2,1)S(1)} %get-tuple-element.103.refs_3_), channel_id=1, source_target_pairs={{0,8},{8,0},{16,24},{24,16},{1,9},{9,1},{17,25},{25,17},{2,10},{10... | collective-permute-start | bytes 540680 | tf_op jit(solution)/shard_map/ppermute | solution.py:122
  7.0 1.5 %collective-permute-start.2 = (bf16[176,512]{1,0:T(8,128)(2,1)S(1)}, bf16[176,512]{1,0:T(8,128)(2,1)S(1)}, u32[]{:S(2)}, u32[]{:S(2)}) collective-permute-start(bf16[176,512]{1,0:T(8,128)(2,1)S(1)} %get-tuple-element.103.refs_3_), channel_id=1, source_target_pairs={{0,16},{8,24},{16,0},{24,8},{1,17},{9,25},{17,1},{25,9},{2,18},{10... | collective-permute-start | bytes 540680 | tf_op jit(solution)/shard_map/ppermute | solution.py:122
  8.5 1.9 %collective-permute-done.1.refs_4_ = bf16[176,512]{1,0:T(8,128)(2,1)S(1)} collective-permute-done((bf16[176,512]{1,0:T(8,128)(2,1)S(1)}, bf16[176,512]{1,0:T(8,128)(2,1)S(1)}, u32[]{:S(2)}, u32[]{:S(2)}) %collective-permute-start.1) | collective-permute-done | bytes 180256 | tf_op jit(solution)/shard_map/ppermute | solution.py:122
  10.5 2.0 %collective-permute-start.3 = (bf16[176,512]{1,0:T(8,128)(2,1)S(1)}, bf16[176,512]{1,0:T(8,128)(2,1)S(1)}, u32[]{:S(2)}, u32[]{:S(2)}) collective-permute-start(bf16[176,512]{1,0:T(8,128)(2,1)S(1)} %collective-permute-done.1.refs_4_), channel_id=1, source_target_pairs={{0,16},{8,24},{16,0},{24,8},{1,17},{9,25},{17,1},{25,9},{2,18},{10... | collective-permute-start | bytes 540680 | tf_op jit(solution)/shard_map/ppermute | solution.py:122
  12.6 2.0 %collective-permute-start.5 = (bf16[160,512]{1,0:T(8,128)(2,1)S(1)}, bf16[160,512]{1,0:T(8,128)(2,1)S(1)}, u32[]{:S(2)}, u32[]{:S(2)}) collective-permute-start(bf16[160,512]{1,0:T(8,128)(2,1)S(1)} %collective-permute-done.4.refs_7_), channel_id=1, source_target_pairs={{0,8},{8,0},{16,24},{24,16},{1,9},{9,1},{17,25},{25,17},{2,10},{10... | collective-permute-start | bytes 491528 | tf_op jit(solution)/shard_map/ppermute | solution.py:122
  15.2 1.3 collective-permute-done.7.refs_10_
  17.2 6.9 %collective-permute-done.6.refs_9_ = bf16[160,512]{1,0:T(8,128)(2,1)S(1)} collective-permute-done((bf16[160,512]{1,0:T(8,128)(2,1)S(1)}, bf16[160,512]{1,0:T(8,128)(2,1)S(1)}, u32[]{:S(2)}, u32[]{:S(2)}) %collective-permute-start.6) | collective-permute-done | bytes 163872 | tf_op jit(solution)/shard_map/ppermute | solution.py:122
  25.1 2.3 %front.1 = (bf16[512,640]{1,0:T(8,128)(2,1)S(1)}, bf16[1536,256]{1,0:T(8,128)(2,1)S(1)}, f32[1032,256]{1,0:T(8,128)S(1)}, bf16[640,1024]{1,0:T(8,128)(2,1)S(1)},...) custom-call(s32[1,4]{1,0:T(1,128)S(1)} %copy-done.3, bf16[256,640]{1,0:T(8,128)(2,1)S(1)} %copy-done, ...), custom_call_target="tpu_custom_call" | custom-call | flops 469762048 | bytes 6877184 | tf_op jit(solution)/shard_map/front/pallas_call | solution.py:79
  27.4 1.7 %collective-permute-start.8 = (bf16[128,640]{1,0:T(8,128)(2,1)S(1)}, bf16[128,640]{1,0:T(8,128)(2,1)S(1)}, u32[]{:S(2)}, u32[]{:S(2)}) collective-permute-start(bf16[128,640]{1,0:T(8,128)(2,1)S(1)} %get-tuple-element.108), channel_id=1, source_target_pairs={{0,4},{4,0},{1,5},{5,1},{2,6},{6,2},{3,7},{7,3},{8,12},{12,8},{9,1... | collective-permute-start | bytes 491528 | tf_op jit(solution)/shard_map/ppermute | solution.py:104
  30.6 2.4 %collective-permute-start.9 = (bf16[128,640]{1,0:T(8,128)(2,1)S(1)}, bf16[128,640]{1,0:T(8,128)(2,1)S(1)}, u32[]{:S(2)}, u32[]{:S(2)}) collective-permute-start(bf16[128,640]{1,0:T(8,128)(2,1)S(1)} %add_convert_fusion.11.refs_0_), channel_id=1, source_target_pairs={{0,1},{1,0},{2,3},{3,2},{4,5},{5,4},{6,7},{7,6},{8,9},{9,8},{10,11... | collective-permute-start | bytes 491528 | tf_op jit(solution)/shard_map/ppermute | solution.py:107
  33.0 1.1 collective-permute-start.13
  34.1 1.4 %collective-permute-start.16 = (bf16[160,768]{1,0:T(8,128)(2,1)S(1)}, bf16[160,768]{1,0:T(8,128)(2,1)S(1)}, u32[]{:S(2)}, u32[]{:S(2)}) collective-permute-start(bf16[160,768]{1,0:T(8,128)(2,1)S(1)} %collective-permute-done.15.refs_6_), channel_id=1, source_target_pairs={{0,8},{8,0},{16,24},{24,16},{1,9},{9,1},{17,25},{25,17},{2,10},{10... | collective-permute-start | bytes 737288 | tf_op jit(solution)/shard_map/ppermute | solution.py:122
  35.5 2.4 %collective-permute-done.12.refs_3_ = bf16[160,768]{1,0:T(8,128)(2,1)S(1)} collective-permute-done((bf16[160,768]{1,0:T(8,128)(2,1)S(1)}, bf16[160,768]{1,0:T(8,128)(2,1)S(1)}, u32[]{:S(2)}, u32[]{:S(2)}) %collective-permute-start.12) | collective-permute-done | bytes 245792 | tf_op jit(solution)/shard_map/ppermute | solution.py:122
  38.7 4.7 %collective-permute-start.10 = (bf16[128,640]{1,0:T(8,128)(2,1)S(1)}, bf16[128,640]{1,0:T(8,128)(2,1)S(1)}, u32[]{:S(2)}, u32[]{:S(2)}) collective-permute-start(bf16[128,640]{1,0:T(8,128)(2,1)S(1)} %get-tuple-element.114.refs_0_.refs_15_), channel_id=1, source_target_pairs={{0,4},{4,0},{1,5},{5,1},{2,6},{6,2},{3,7},{7,3},{8,12},{12,8},{9,1... | collective-permute-start | bytes 491528 | tf_op jit(solution)/shard_map/ppermute | solution.py:104
  43.4 3.4 %collective-permute-done.14.refs_5_ = bf16[160,768]{1,0:T(8,128)(2,1)S(1)} collective-permute-done((bf16[160,768]{1,0:T(8,128)(2,1)S(1)}, bf16[160,768]{1,0:T(8,128)(2,1)S(1)}, u32[]{:S(2)}, u32[]{:S(2)}) %collective-permute-start.14) | collective-permute-done | bytes 245792 | tf_op jit(solution)/shard_map/ppermute | solution.py:122
  46.8 1.2 ffn.1
  48.0 2.8 %collective-permute-start.19 = (bf16[128,640]{1,0:T(8,128)(2,1)S(1)}, bf16[128,640]{1,0:T(8,128)(2,1)S(1)}, u32[]{:S(2)}, u32[]{:S(2)}) collective-permute-start(bf16[128,640]{1,0:T(8,128)(2,1)S(1)} %get-tuple-element.120), channel_id=1, source_target_pairs={{0,4},{4,0},{1,5},{5,1},{2,6},{6,2},{3,7},{7,3},{8,12},{12,8},{9,1... | collective-permute-start | bytes 491528 | tf_op jit(solution)/shard_map/ppermute | solution.py:104
  51.9 1.7 %collective-permute-start.20 = (bf16[128,640]{1,0:T(8,128)(2,1)S(1)}, bf16[128,640]{1,0:T(8,128)(2,1)S(1)}, u32[]{:S(2)}, u32[]{:S(2)}) collective-permute-start(bf16[128,640]{1,0:T(8,128)(2,1)S(1)} %add_convert_fusion.10.refs_0_), channel_id=1, source_target_pairs={{0,1},{1,0},{2,3},{3,2},{4,5},{5,4},{6,7},{7,6},{8,9},{9,8},{10,11... | collective-permute-start | bytes 491528 | tf_op jit(solution)/shard_map/ppermute | solution.py:107
  53.6 4.8 %collective-permute-done.20.refs_1_ = bf16[128,640]{1,0:T(8,128)(2,1)S(1)} collective-permute-done((bf16[128,640]{1,0:T(8,128)(2,1)S(1)}, bf16[128,640]{1,0:T(8,128)(2,1)S(1)}, u32[]{:S(2)}, u32[]{:S(2)}) %collective-permute-start.20) | collective-permute-done | bytes 163872 | tf_op jit(solution)/shard_map/ppermute | solution.py:107
  58.8 1.4 %collective-permute-done.21.refs_1_.refs_3_ = bf16[128,640]{1,0:T(8,128)(2,1)S(1)} collective-permute-done((bf16[128,640]{1,0:T(8,128)(2,1)S(1)}, bf16[128,640]{1,0:T(8,128)(2,1)S(1)}, u32[]{:S(2)}, u32[]{:S(2)}) %collective-permute-start.21) | collective-permute-done | bytes 163872 | tf_op jit(solution)/shard_map/ppermute | solution.py:104
  60.2 1.3 ffn_back.1
  61.7 1.2 collective-permute-done.22
  63.0 1.3 ffn_weights.1
  64.3 1.4 %collective-permute-start.27 = (bf16[320,768]{1,0:T(8,128)(2,1)S(1)}, bf16[320,768]{1,0:T(8,128)(2,1)S(1)}, u32[]{:S(2)}, u32[]{:S(2)}) collective-permute-start(bf16[320,768]{1,0:T(8,128)(2,1)S(1)} %get-tuple-element.140), channel_id=1, source_target_pairs={{0,8},{8,0},{16,24},{24,16},{1,9},{9,1},{17,25},{25,17},{2,10},{10... | collective-permute-start | bytes 1474568 | tf_op jit(solution)/shard_map/ppermute | solution.py:122
  65.7 1.7 %collective-permute-start.23 = (bf16[128,640]{1,0:T(8,128)(2,1)S(1)}, bf16[128,640]{1,0:T(8,128)(2,1)S(1)}, u32[]{:S(2)}, u32[]{:S(2)}) collective-permute-start(bf16[128,640]{1,0:T(8,128)(2,1)S(1)} %add_convert_fusion.9.refs_0_), channel_id=1, source_target_pairs={{0,1},{1,0},{2,3},{3,2},{4,5},{5,4},{6,7},{7,6},{8,9},{9,8},{10,11... | collective-permute-start | bytes 491528 | tf_op jit(solution)/shard_map/ppermute | solution.py:107
  67.8 3.8 %collective-permute-done.23.refs_1_ = bf16[128,640]{1,0:T(8,128)(2,1)S(1)} collective-permute-done((bf16[128,640]{1,0:T(8,128)(2,1)S(1)}, bf16[128,640]{1,0:T(8,128)(2,1)S(1)}, u32[]{:S(2)}, u32[]{:S(2)}) %collective-permute-start.23) | collective-permute-done | bytes 163872 | tf_op jit(solution)/shard_map/ppermute | solution.py:107
  72.1 1.4 %collective-permute-done.24.refs_2_.refs_6_ = bf16[128,640]{1,0:T(8,128)(2,1)S(1)} collective-permute-done((bf16[128,640]{1,0:T(8,128)(2,1)S(1)}, bf16[128,640]{1,0:T(8,128)(2,1)S(1)}, u32[]{:S(2)}, u32[]{:S(2)}) %collective-permute-start.24) | collective-permute-done | bytes 163872 | tf_op jit(solution)/shard_map/ppermute | solution.py:104
  73.5 2.5 %attn_back.1 = (bf16[256,256]{1,0:T(8,128)(2,1)S(1)}, bf16[512,512]{1,0:T(8,128)(2,1)S(1)}, f32[256,640]{1,0:T(8,128)S(1)}, bf16[256,640]{1,0:T(8,128)(2,1)S(1)}...) custom-call(s32[1,4]{1,0:T(1,128)S(1)} %copy-done.4, bf16[128,640]{1,0:T(8,128)(2,1)S(1)} %get-tuple-element.130.refs_1_.refs_5_, ...), custom_call_target="tpu_custom_call" | custom-call | flops 671088640 | bytes 5646336 | tf_op jit(solution)/shard_map/attn_back/pallas_call | solution.py:79
  76.2 1.5 %collective-permute-done.27 = bf16[320,768]{1,0:T(8,128)(2,1)S(1)} collective-permute-done((bf16[320,768]{1,0:T(8,128)(2,1)S(1)}, bf16[320,768]{1,0:T(8,128)(2,1)S(1)}, u32[]{:S(2)}, u32[]{:S(2)}) %collective-permute-start.27) | collective-permute-done | bytes 491552 | tf_op jit(solution)/shard_map/ppermute | solution.py:122
  77.8 2.4 %collective-permute-done.28 = bf16[320,768]{1,0:T(8,128)(2,1)S(1)} collective-permute-done((bf16[320,768]{1,0:T(8,128)(2,1)S(1)}, bf16[320,768]{1,0:T(8,128)(2,1)S(1)}, u32[]{:S(2)}, u32[]{:S(2)}) %collective-permute-start.28) | collective-permute-done | bytes 491552 | tf_op jit(solution)/shard_map/ppermute | solution.py:122
  82.1 1.2 collective-permute-start.31
  83.9 2.3 %collective-permute-start.35 = (bf16[128,640]{1,0:T(8,128)(2,1)S(1)}, bf16[128,640]{1,0:T(8,128)(2,1)S(1)}, u32[]{:S(2)}, u32[]{:S(2)}) collective-permute-start(bf16[128,640]{1,0:T(8,128)(2,1)S(1)} %get-tuple-element.125.refs_0_), channel_id=1, source_target_pairs={{0,2},{1,3},{2,0},{3,1},{4,6},{5,7},{6,4},{7,5},{8,10},{9,11},{10,... | collective-permute-start | bytes 491528 | tf_op jit(solution)/shard_map/ppermute | solution.py:110
  86.2 3.8 %collective-permute-done.30 = bf16[160,768]{1,0:T(8,128)(2,1)S(1)} collective-permute-done((bf16[160,768]{1,0:T(8,128)(2,1)S(1)}, bf16[160,768]{1,0:T(8,128)(2,1)S(1)}, u32[]{:S(2)}, u32[]{:S(2)}) %collective-permute-start.30) | collective-permute-done | bytes 245792 | tf_op jit(solution)/shard_map/ppermute | solution.py:122
  90.4 2.4 %collective-permute-done.26.refs_1_ = bf16[128,640]{1,0:T(8,128)(2,1)S(1)} collective-permute-done((bf16[128,640]{1,0:T(8,128)(2,1)S(1)}, bf16[128,640]{1,0:T(8,128)(2,1)S(1)}, u32[]{:S(2)}, u32[]{:S(2)}) %collective-permute-start.26) | collective-permute-done | bytes 163872 | tf_op jit(solution)/shard_map/ppermute | solution.py:107
  93.2 1.3 collective-permute-start.33
  94.5 4.8 %collective-permute-done.34 = bf16[320,512]{1,0:T(8,128)(2,1)S(1)} collective-permute-done((bf16[320,512]{1,0:T(8,128)(2,1)S(1)}, bf16[320,512]{1,0:T(8,128)(2,1)S(1)}, u32[]{:S(2)}, u32[]{:S(2)}) %collective-permute-start.34) | collective-permute-done | bytes 327712 | tf_op jit(solution)/shard_map/ppermute | solution.py:122
  99.7 2.2 %collective-permute-start.37 = (bf16[64,640]{1,0:T(8,128)(2,1)S(1)}, bf16[64,640]{1,0:T(8,128)(2,1)S(1)}, u32[]{:S(2)}, u32[]{:S(2)}) collective-permute-start(bf16[64,640]{1,0:T(8,128)(2,1)S(1)} %last_norm.1.refs_2_), channel_id=1, source_target_pairs={{0,2},{1,3},{2,0},{3,1},{4,6},{5,7},{6,4},{7,5},{8,10},{9,11},{10,... | collective-permute-start | bytes 245768 | tf_op jit(solution)/shard_map/ppermute | solution.py:110
  103.1 1.5 %collective-permute-start.39 = (bf16[160,512]{1,0:T(8,128)(2,1)S(1)}, bf16[160,512]{1,0:T(8,128)(2,1)S(1)}, u32[]{:S(2)}, u32[]{:S(2)}) collective-permute-start(bf16[160,512]{1,0:T(8,128)(2,1)S(1)} %slice.51), channel_id=1, source_target_pairs={{0,8},{8,0},{16,24},{24,16},{1,9},{9,1},{17,25},{25,17},{2,10},{10... | collective-permute-start | bytes 491528 | tf_op jit(solution)/shard_map/ppermute | solution.py:122
  106.4 2.1 %collective-permute-done.39 = bf16[160,512]{1,0:T(8,128)(2,1)S(1)} collective-permute-done((bf16[160,512]{1,0:T(8,128)(2,1)S(1)}, bf16[160,512]{1,0:T(8,128)(2,1)S(1)}, u32[]{:S(2)}, u32[]{:S(2)}) %collective-permute-start.39) | collective-permute-done | bytes 163872 | tf_op jit(solution)/shard_map/ppermute | solution.py:122
  108.6 2.0 %collective-permute-start.41 = (bf16[176,256]{1,0:T(8,128)(2,1)S(1)}, bf16[176,256]{1,0:T(8,128)(2,1)S(1)}, u32[]{:S(2)}, u32[]{:S(2)}) collective-permute-start(bf16[176,256]{1,0:T(8,128)(2,1)S(1)} %add_convert_fusion.14), channel_id=1, source_target_pairs={{0,1},{1,0},{2,3},{3,2},{4,5},{5,4},{6,7},{7,6},{8,9},{9,8},{10,11... | collective-permute-start | bytes 270344 | tf_op jit(solution)/shard_map/ppermute | solution.py:107
  111.3 2.6 %collective-permute-done.40.refs_5_ = bf16[64,640]{1,0:T(8,128)(2,1)S(1)} collective-permute-done((bf16[64,640]{1,0:T(8,128)(2,1)S(1)}, bf16[64,640]{1,0:T(8,128)(2,1)S(1)}, u32[]{:S(2)}, u32[]{:S(2)}) %collective-permute-start.40) | collective-permute-done | bytes 81952 | tf_op jit(solution)/shard_map/ppermute | solution.py:107
  114.0 3.2 %collective-permute-done.41 = bf16[176,256]{1,0:T(8,128)(2,1)S(1)} collective-permute-done((bf16[176,256]{1,0:T(8,128)(2,1)S(1)}, bf16[176,256]{1,0:T(8,128)(2,1)S(1)}, u32[]{:S(2)}, u32[]{:S(2)}) %collective-permute-start.41) | collective-permute-done | bytes 90144 | tf_op jit(solution)/shard_map/ppermute | solution.py:107
  117.6 5.0 %collective-permute-start.47 = (bf16[160,768]{1,0:T(8,128)(2,1)S(1)}, bf16[160,768]{1,0:T(8,128)(2,1)S(1)}, u32[]{:S(2)}, u32[]{:S(2)}) collective-permute-start(bf16[160,768]{1,0:T(8,128)(2,1)S(1)} %collective-permute-done.46.refs_10_), channel_id=1, source_target_pairs={{0,4},{4,0},{1,5},{5,1},{2,6},{6,2},{3,7},{7,3},{8,12},{12,8},{9,1... | collective-permute-start | bytes 737288 | tf_op jit(solution)/shard_map/ppermute | solution.py:104
  122.6 2.2 %collective-permute-start.43 = (bf16[160,512]{1,0:T(8,128)(2,1)S(1)}, bf16[160,512]{1,0:T(8,128)(2,1)S(1)}, u32[]{:S(2)}, u32[]{:S(2)}) collective-permute-start(bf16[160,512]{1,0:T(8,128)(2,1)S(1)} %collective-permute-done.42.refs_6_), channel_id=1, source_target_pairs={{0,4},{4,0},{1,5},{5,1},{2,6},{6,2},{3,7},{7,3},{8,12},{12,8},{9,1... | collective-permute-start | bytes 491528 | tf_op jit(solution)/shard_map/ppermute | solution.py:104
  124.9 1.1 collective-permute-done.48
  126.2 4.8 %collective-permute-done.36.refs_3_ = bf16[64,640]{1,0:T(8,128)(2,1)S(1)} collective-permute-done((bf16[64,640]{1,0:T(8,128)(2,1)S(1)}, bf16[64,640]{1,0:T(8,128)(2,1)S(1)}, u32[]{:S(2)}, u32[]{:S(2)}) %collective-permute-start.36) | collective-permute-done | bytes 81952 | tf_op jit(solution)/shard_map/ppermute | solution.py:107
  131.0 1.8 %finish.1 = (f32[256,640]{1,0:T(8,128)}, f32[256,640]{1,0:T(8,128)}, f32[160,256]{1,0:T(8,128)}, f32[160,256]{1,0:T(8,128)}, f32[160,256]{1,0:T(8,128)}, /*index...) custom-call(bf16[128,640]{1,0:T(8,128)(2,1)S(1)} %get-tuple-element., ...), custom_call_target="tpu_custom_call" | custom-call | bytes 5098496 | tf_op jit(solution)/shard_map/finish/pallas_call | solution.py:79
  (94 shorter events, 17.5 us)
Async XLA Ops:
  0.7 3.1 %collective-permute-start = (bf16[256,640]{1,0:T(8,128)(2,1)}, bf16[256,640]{1,0:T(8,128)(2,1)S(1)}, u32[]{:S(2)}, u32[]{:S(2)}) collective-permute-start(bf16[256,640]{1,0:T(8,128)(2,1)} %refs_2_.5), channel_id=1, source_target_pairs={{0,4},{4,0},{1,5},{5,1},{2,6},{6,2},{3,7},{7,3},{8,12},{12,8},{9,1... | collective-permute-start | bytes 983048 | tf_op jit(solution)/shard_map/ppermute | solution.py:104
  3.7 4.8 %collective-permute-start.4 = (bf16[160,512]{1,0:T(8,128)(2,1)S(1)}, bf16[160,512]{1,0:T(8,128)(2,1)S(1)}, u32[]{:S(2)}, u32[]{:S(2)}) collective-permute-start(bf16[160,512]{1,0:T(8,128)(2,1)S(1)} %get-tuple-element.104), channel_id=1, source_target_pairs={{0,0},{1,1},{2,4},{3,5},{4,2},{5,3},{6,6},{7,7},{8,8},{9,9},{10,12... | collective-permute-start | bytes 491528 | tf_op jit(solution)/shard_map/ppermute | solution.py:119
  4.4 6.0 %collective-permute-start.1 = (bf16[176,512]{1,0:T(8,128)(2,1)S(1)}, bf16[176,512]{1,0:T(8,128)(2,1)S(1)}, u32[]{:S(2)}, u32[]{:S(2)}) collective-permute-start(bf16[176,512]{1,0:T(8,128)(2,1)S(1)} %get-tuple-element.103.refs_3_), channel_id=1, source_target_pairs={{0,8},{8,0},{16,24},{24,16},{1,9},{9,1},{17,25},{25,17},{2,10},{10... | collective-permute-start | bytes 540680 | tf_op jit(solution)/shard_map/ppermute | solution.py:122
  7.0 7.5 %collective-permute-start.2 = (bf16[176,512]{1,0:T(8,128)(2,1)S(1)}, bf16[176,512]{1,0:T(8,128)(2,1)S(1)}, u32[]{:S(2)}, u32[]{:S(2)}) collective-permute-start(bf16[176,512]{1,0:T(8,128)(2,1)S(1)} %get-tuple-element.103.refs_3_), channel_id=1, source_target_pairs={{0,16},{8,24},{16,0},{24,8},{1,17},{9,25},{17,1},{25,9},{2,18},{10... | collective-permute-start | bytes 540680 | tf_op jit(solution)/shard_map/ppermute | solution.py:122
  8.5 8.0 %collective-permute-start.7 = (bf16[160,512]{1,0:T(8,128)(2,1)S(1)}, bf16[160,512]{1,0:T(8,128)(2,1)S(1)}, u32[]{:S(2)}, u32[]{:S(2)}) collective-permute-start(bf16[160,512]{1,0:T(8,128)(2,1)S(1)} %collective-permute-done.4.refs_7_), channel_id=1, source_target_pairs={{0,24},{8,16},{16,8},{24,0},{1,25},{9,17},{17,9},{25,1},{2,26},{10... | collective-permute-start | bytes 491528 | tf_op jit(solution)/shard_map/ppermute | solution.py:122
  10.5 13.6 %collective-permute-start.3 = (bf16[176,512]{1,0:T(8,128)(2,1)S(1)}, bf16[176,512]{1,0:T(8,128)(2,1)S(1)}, u32[]{:S(2)}, u32[]{:S(2)}) collective-permute-start(bf16[176,512]{1,0:T(8,128)(2,1)S(1)} %collective-permute-done.1.refs_4_), channel_id=1, source_target_pairs={{0,16},{8,24},{16,0},{24,8},{1,17},{9,25},{17,1},{25,9},{2,18},{10... | collective-permute-start | bytes 540680 | tf_op jit(solution)/shard_map/ppermute | solution.py:122
  12.5 11.6 %collective-permute-start.6 = (bf16[160,512]{1,0:T(8,128)(2,1)S(1)}, bf16[160,512]{1,0:T(8,128)(2,1)S(1)}, u32[]{:S(2)}, u32[]{:S(2)}) collective-permute-start(bf16[160,512]{1,0:T(8,128)(2,1)S(1)} %collective-permute-done.4.refs_7_), channel_id=1, source_target_pairs={{0,16},{8,24},{16,0},{24,8},{1,17},{9,25},{17,1},{25,9},{2,18},{10... | collective-permute-start | bytes 491528 | tf_op jit(solution)/shard_map/ppermute | solution.py:122
  12.6 11.5 %collective-permute-start.5 = (bf16[160,512]{1,0:T(8,128)(2,1)S(1)}, bf16[160,512]{1,0:T(8,128)(2,1)S(1)}, u32[]{:S(2)}, u32[]{:S(2)}) collective-permute-start(bf16[160,512]{1,0:T(8,128)(2,1)S(1)} %collective-permute-done.4.refs_7_), channel_id=1, source_target_pairs={{0,8},{8,0},{16,24},{24,16},{1,9},{9,1},{17,25},{25,17},{2,10},{10... | collective-permute-start | bytes 491528 | tf_op jit(solution)/shard_map/ppermute | solution.py:122
  14.5 14.6 %collective-permute-start.11 = (bf16[160,768]{1,0:T(8,128)(2,1)S(1)}, bf16[160,768]{1,0:T(8,128)(2,1)S(1)}, u32[]{:S(2)}, u32[]{:S(2)}) collective-permute-start(bf16[160,768]{1,0:T(8,128)(2,1)S(1)} %get-tuple-element.115), channel_id=1, source_target_pairs={{0,0},{1,1},{2,4},{3,5},{4,2},{5,3},{6,6},{7,7},{8,8},{9,9},{10,12... | collective-permute-start | bytes 737288 | tf_op jit(solution)/shard_map/ppermute | solution.py:119
  16.5 13.3 %collective-permute-start.15 = (bf16[160,768]{1,0:T(8,128)(2,1)S(1)}, bf16[160,768]{1,0:T(8,128)(2,1)S(1)}, u32[]{:S(2)}, u32[]{:S(2)}) collective-permute-start(bf16[160,768]{1,0:T(8,128)(2,1)S(1)} %get-tuple-element.116), channel_id=1, source_target_pairs={{0,0},{1,1},{2,4},{3,5},{4,2},{5,3},{6,6},{7,7},{8,8},{9,9},{10,12... | collective-permute-start | bytes 737288 | tf_op jit(solution)/shard_map/ppermute | solution.py:119
  27.4 3.2 %collective-permute-start.8 = (bf16[128,640]{1,0:T(8,128)(2,1)S(1)}, bf16[128,640]{1,0:T(8,128)(2,1)S(1)}, u32[]{:S(2)}, u32[]{:S(2)}) collective-permute-start(bf16[128,640]{1,0:T(8,128)(2,1)S(1)} %get-tuple-element.108), channel_id=1, source_target_pairs={{0,4},{4,0},{1,5},{5,1},{2,6},{6,2},{3,7},{7,3},{8,12},{12,8},{9,1... | collective-permute-start | bytes 491528 | tf_op jit(solution)/shard_map/ppermute | solution.py:104
  29.1 8.8 %collective-permute-start.12 = (bf16[160,768]{1,0:T(8,128)(2,1)S(1)}, bf16[160,768]{1,0:T(8,128)(2,1)S(1)}, u32[]{:S(2)}, u32[]{:S(2)}) collective-permute-start(bf16[160,768]{1,0:T(8,128)(2,1)S(1)} %collective-permute-done.11.refs_2_), channel_id=1, source_target_pairs={{0,8},{8,0},{16,24},{24,16},{1,9},{9,1},{17,25},{25,17},{2,10},{10... | collective-permute-start | bytes 737288 | tf_op jit(solution)/shard_map/ppermute | solution.py:122
  29.8 8.1 %collective-permute-start.17 = (bf16[160,768]{1,0:T(8,128)(2,1)S(1)}, bf16[160,768]{1,0:T(8,128)(2,1)S(1)}, u32[]{:S(2)}, u32[]{:S(2)}) collective-permute-start(bf16[160,768]{1,0:T(8,128)(2,1)S(1)} %collective-permute-done.15.refs_6_), channel_id=1, source_target_pairs={{0,16},{8,24},{16,0},{24,8},{1,17},{9,25},{17,1},{25,9},{2,18},{10... | collective-permute-start | bytes 737288 | tf_op jit(solution)/shard_map/ppermute | solution.py:122
  30.6 7.8 %collective-permute-start.9 = (bf16[128,640]{1,0:T(8,128)(2,1)S(1)}, bf16[128,640]{1,0:T(8,128)(2,1)S(1)}, u32[]{:S(2)}, u32[]{:S(2)}) collective-permute-start(bf16[128,640]{1,0:T(8,128)(2,1)S(1)} %add_convert_fusion.11.refs_0_), channel_id=1, source_target_pairs={{0,1},{1,0},{2,3},{3,2},{4,5},{5,4},{6,7},{7,6},{8,9},{9,8},{10,11... | collective-permute-start | bytes 491528 | tf_op jit(solution)/shard_map/ppermute | solution.py:107
  33.0 10.5 %collective-permute-start.13 = (bf16[160,768]{1,0:T(8,128)(2,1)S(1)}, bf16[160,768]{1,0:T(8,128)(2,1)S(1)}, u32[]{:S(2)}, u32[]{:S(2)}) collective-permute-start(bf16[160,768]{1,0:T(8,128)(2,1)S(1)} %collective-permute-done.11.refs_2_), channel_id=1, source_target_pairs={{0,16},{8,24},{16,0},{24,8},{1,17},{9,25},{17,1},{25,9},{2,18},{10... | collective-permute-start | bytes 737288 | tf_op jit(solution)/shard_map/ppermute | solution.py:122
  34.1 9.3 %collective-permute-start.16 = (bf16[160,768]{1,0:T(8,128)(2,1)S(1)}, bf16[160,768]{1,0:T(8,128)(2,1)S(1)}, u32[]{:S(2)}, u32[]{:S(2)}) collective-permute-start(bf16[160,768]{1,0:T(8,128)(2,1)S(1)} %collective-permute-done.15.refs_6_), channel_id=1, source_target_pairs={{0,8},{8,0},{16,24},{24,16},{1,9},{9,1},{17,25},{25,17},{2,10},{10... | collective-permute-start | bytes 737288 | tf_op jit(solution)/shard_map/ppermute | solution.py:122
  37.9 8.9 %collective-permute-start.14 = (bf16[160,768]{1,0:T(8,128)(2,1)S(1)}, bf16[160,768]{1,0:T(8,128)(2,1)S(1)}, u32[]{:S(2)}, u32[]{:S(2)}) collective-permute-start(bf16[160,768]{1,0:T(8,128)(2,1)S(1)} %collective-permute-done.12.refs_3_), channel_id=1, source_target_pairs={{0,16},{8,24},{16,0},{24,8},{1,17},{9,25},{17,1},{25,9},{2,18},{10... | collective-permute-start | bytes 737288 | tf_op jit(solution)/shard_map/ppermute | solution.py:122
  37.9 8.9 %collective-permute-start.18 = (bf16[160,768]{1,0:T(8,128)(2,1)S(1)}, bf16[160,768]{1,0:T(8,128)(2,1)S(1)}, u32[]{:S(2)}, u32[]{:S(2)}) collective-permute-start(bf16[160,768]{1,0:T(8,128)(2,1)S(1)} %collective-permute-done.17.refs_8_), channel_id=1, source_target_pairs={{0,8},{8,0},{16,24},{24,16},{1,9},{9,1},{17,25},{25,17},{2,10},{10... | collective-permute-start | bytes 737288 | tf_op jit(solution)/shard_map/ppermute | solution.py:122
  38.7 8.1 %collective-permute-start.10 = (bf16[128,640]{1,0:T(8,128)(2,1)S(1)}, bf16[128,640]{1,0:T(8,128)(2,1)S(1)}, u32[]{:S(2)}, u32[]{:S(2)}) collective-permute-start(bf16[128,640]{1,0:T(8,128)(2,1)S(1)} %get-tuple-element.114.refs_0_.refs_15_), channel_id=1, source_target_pairs={{0,4},{4,0},{1,5},{5,1},{2,6},{6,2},{3,7},{7,3},{8,12},{12,8},{9,1... | collective-permute-start | bytes 491528 | tf_op jit(solution)/shard_map/ppermute | solution.py:104
  48.0 3.8 %collective-permute-start.19 = (bf16[128,640]{1,0:T(8,128)(2,1)S(1)}, bf16[128,640]{1,0:T(8,128)(2,1)S(1)}, u32[]{:S(2)}, u32[]{:S(2)}) collective-permute-start(bf16[128,640]{1,0:T(8,128)(2,1)S(1)} %get-tuple-element.120), channel_id=1, source_target_pairs={{0,4},{4,0},{1,5},{5,1},{2,6},{6,2},{3,7},{7,3},{8,12},{12,8},{9,1... | collective-permute-start | bytes 491528 | tf_op jit(solution)/shard_map/ppermute | solution.py:104
  51.9 6.5 %collective-permute-start.20 = (bf16[128,640]{1,0:T(8,128)(2,1)S(1)}, bf16[128,640]{1,0:T(8,128)(2,1)S(1)}, u32[]{:S(2)}, u32[]{:S(2)}) collective-permute-start(bf16[128,640]{1,0:T(8,128)(2,1)S(1)} %add_convert_fusion.10.refs_0_), channel_id=1, source_target_pairs={{0,1},{1,0},{2,3},{3,2},{4,5},{5,4},{6,7},{7,6},{8,9},{9,8},{10,11... | collective-permute-start | bytes 491528 | tf_op jit(solution)/shard_map/ppermute | solution.py:107
  58.7 1.5 %collective-permute-start.21 = (bf16[128,640]{1,0:T(8,128)(2,1)S(1)}, bf16[128,640]{1,0:T(8,128)(2,1)S(1)}, u32[]{:S(2)}, u32[]{:S(2)}) collective-permute-start(bf16[128,640]{1,0:T(8,128)(2,1)S(1)} %get-tuple-element.126.refs_0_.refs_2_), channel_id=1, source_target_pairs={{0,4},{4,0},{1,5},{5,1},{2,6},{6,2},{3,7},{7,3},{8,12},{12,8},{9,1... | collective-permute-start | bytes 491528 | tf_op jit(solution)/shard_map/ppermute | solution.py:104
  64.3 13.3 %collective-permute-start.27 = (bf16[320,768]{1,0:T(8,128)(2,1)S(1)}, bf16[320,768]{1,0:T(8,128)(2,1)S(1)}, u32[]{:S(2)}, u32[]{:S(2)}) collective-permute-start(bf16[320,768]{1,0:T(8,128)(2,1)S(1)} %get-tuple-element.140), channel_id=1, source_target_pairs={{0,8},{8,0},{16,24},{24,16},{1,9},{9,1},{17,25},{25,17},{2,10},{10... | collective-permute-start | bytes 1474568 | tf_op jit(solution)/shard_map/ppermute | solution.py:122
  65.7 6.0 %collective-permute-start.23 = (bf16[128,640]{1,0:T(8,128)(2,1)S(1)}, bf16[128,640]{1,0:T(8,128)(2,1)S(1)}, u32[]{:S(2)}, u32[]{:S(2)}) collective-permute-start(bf16[128,640]{1,0:T(8,128)(2,1)S(1)} %add_convert_fusion.9.refs_0_), channel_id=1, source_target_pairs={{0,1},{1,0},{2,3},{3,2},{4,5},{5,4},{6,7},{7,6},{8,9},{9,8},{10,11... | collective-permute-start | bytes 491528 | tf_op jit(solution)/shard_map/ppermute | solution.py:107
  67.4 12.7 %collective-permute-start.28 = (bf16[320,768]{1,0:T(8,128)(2,1)S(1)}, bf16[320,768]{1,0:T(8,128)(2,1)S(1)}, u32[]{:S(2)}, u32[]{:S(2)}) collective-permute-start(bf16[320,768]{1,0:T(8,128)(2,1)S(1)} %get-tuple-element.142), channel_id=1, source_target_pairs={{0,16},{8,24},{16,0},{24,8},{1,17},{9,25},{17,1},{25,9},{2,18},{10... | collective-permute-start | bytes 1474568 | tf_op jit(solution)/shard_map/ppermute | solution.py:122
  76.0 4.3 %collective-permute-start.25 = (bf16[256,640]{1,0:T(8,128)(2,1)S(1)}, bf16[256,640]{1,0:T(8,128)(2,1)S(1)}, u32[]{:S(2)}, u32[]{:S(2)}) collective-permute-start(bf16[256,640]{1,0:T(8,128)(2,1)S(1)} %get-tuple-element.133.refs_9_), channel_id=1, source_target_pairs={{0,4},{4,0},{1,5},{5,1},{2,6},{6,2},{3,7},{7,3},{8,12},{12,8},{9,1... | collective-permute-start | bytes 983048 | tf_op jit(solution)/shard_map/ppermute | solution.py:104
  81.5 11.3 %collective-permute-start.29 = (bf16[704,256]{1,0:T(8,128)(2,1)S(1)}, bf16[704,256]{1,0:T(8,128)(2,1)S(1)}, u32[]{:S(2)}, u32[]{:S(2)}) collective-permute-start(bf16[704,256]{1,0:T(8,128)(2,1)S(1)} %get-tuple-element.147), channel_id=1, source_target_pairs={{0,4},{4,0},{1,5},{5,1},{2,6},{6,2},{3,7},{7,3},{8,12},{12,8},{9,1... | collective-permute-start | bytes 1081352 | tf_op jit(solution)/shard_map/ppermute | solution.py:104
  81.6 8.4 %collective-permute-start.30 = (bf16[160,768]{1,0:T(8,128)(2,1)S(1)}, bf16[160,768]{1,0:T(8,128)(2,1)S(1)}, u32[]{:S(2)}, u32[]{:S(2)}) collective-permute-start(bf16[160,768]{1,0:T(8,128)(2,1)S(1)} %slice.48), channel_id=1, source_target_pairs={{0,16},{8,24},{16,0},{24,8},{1,17},{9,25},{17,1},{25,9},{2,18},{10... | collective-permute-start | bytes 737288 | tf_op jit(solution)/shard_map/ppermute | solution.py:122
  82.1 8.3 %collective-permute-start.31 = (bf16[160,768]{1,0:T(8,128)(2,1)S(1)}, bf16[160,768]{1,0:T(8,128)(2,1)S(1)}, u32[]{:S(2)}, u32[]{:S(2)}) collective-permute-start(bf16[160,768]{1,0:T(8,128)(2,1)S(1)} %slice.49), channel_id=1, source_target_pairs={{0,8},{8,0},{16,24},{24,16},{1,9},{9,1},{17,25},{25,17},{2,10},{10... | collective-permute-start | bytes 737288 | tf_op jit(solution)/shard_map/ppermute | solution.py:122
  83.3 9.5 %collective-permute-start.26 = (bf16[128,640]{1,0:T(8,128)(2,1)S(1)}, bf16[128,640]{1,0:T(8,128)(2,1)S(1)}, u32[]{:S(2)}, u32[]{:S(2)}) collective-permute-start(bf16[128,640]{1,0:T(8,128)(2,1)S(1)} %get-tuple-element.135), channel_id=1, source_target_pairs={{0,1},{1,0},{2,3},{3,2},{4,5},{5,4},{6,7},{7,6},{8,9},{9,8},{10,11... | collective-permute-start | bytes 491528 | tf_op jit(solution)/shard_map/ppermute | solution.py:107
  83.9 10.6 %collective-permute-start.35 = (bf16[128,640]{1,0:T(8,128)(2,1)S(1)}, bf16[128,640]{1,0:T(8,128)(2,1)S(1)}, u32[]{:S(2)}, u32[]{:S(2)}) collective-permute-start(bf16[128,640]{1,0:T(8,128)(2,1)S(1)} %get-tuple-element.125.refs_0_), channel_id=1, source_target_pairs={{0,2},{1,3},{2,0},{3,1},{4,6},{5,7},{6,4},{7,5},{8,10},{9,11},{10,... | collective-permute-start | bytes 491528 | tf_op jit(solution)/shard_map/ppermute | solution.py:110
  90.0 9.3 %collective-permute-start.34 = (bf16[320,512]{1,0:T(8,128)(2,1)S(1)}, bf16[320,512]{1,0:T(8,128)(2,1)S(1)}, u32[]{:S(2)}, u32[]{:S(2)}) collective-permute-start(bf16[320,512]{1,0:T(8,128)(2,1)S(1)} %get-tuple-element.152), channel_id=1, source_target_pairs={{0,16},{8,24},{16,0},{24,8},{1,17},{9,25},{17,1},{25,9},{2,18},{10... | collective-permute-start | bytes 983048 | tf_op jit(solution)/shard_map/ppermute | solution.py:122
  92.9 6.5 %collective-permute-start.32 = (bf16[64,640]{1,0:T(8,128)(2,1)S(1)}, bf16[64,640]{1,0:T(8,128)(2,1)S(1)}, u32[]{:S(2)}, u32[]{:S(2)}) collective-permute-start(bf16[64,640]{1,0:T(8,128)(2,1)S(1)} %get-tuple-element.149), channel_id=1, source_target_pairs={{0,2},{1,3},{2,0},{3,1},{4,6},{5,7},{6,4},{7,5},{8,10},{9,11},{10,... | collective-permute-start | bytes 245768 | tf_op jit(solution)/shard_map/ppermute | solution.py:110
  93.2 6.2 %collective-permute-start.33 = (bf16[352,256]{1,0:T(8,128)(2,1)S(1)}, bf16[352,256]{1,0:T(8,128)(2,1)S(1)}, u32[]{:S(2)}, u32[]{:S(2)}) collective-permute-start(bf16[352,256]{1,0:T(8,128)(2,1)S(1)} %add_convert_fusion.7), channel_id=1, source_target_pairs={{0,8},{8,0},{16,24},{24,16},{1,9},{9,1},{17,25},{25,17},{2,10},{10... | collective-permute-start | bytes 540680 | tf_op jit(solution)/shard_map/ppermute | solution.py:122
  99.7 6.3 %collective-permute-start.37 = (bf16[64,640]{1,0:T(8,128)(2,1)S(1)}, bf16[64,640]{1,0:T(8,128)(2,1)S(1)}, u32[]{:S(2)}, u32[]{:S(2)}) collective-permute-start(bf16[64,640]{1,0:T(8,128)(2,1)S(1)} %last_norm.1.refs_2_), channel_id=1, source_target_pairs={{0,2},{1,3},{2,0},{3,1},{4,6},{5,7},{6,4},{7,5},{8,10},{9,11},{10,... | collective-permute-start | bytes 245768 | tf_op jit(solution)/shard_map/ppermute | solution.py:110
  101.9 4.5 %collective-permute-start.38 = (bf16[176,256]{1,0:T(8,128)(2,1)S(1)}, bf16[176,256]{1,0:T(8,128)(2,1)S(1)}, u32[]{:S(2)}, u32[]{:S(2)}) collective-permute-start(bf16[176,256]{1,0:T(8,128)(2,1)S(1)} %slice.50), channel_id=1, source_target_pairs={{0,16},{8,24},{16,0},{24,8},{1,17},{9,25},{17,1},{25,9},{2,18},{10... | collective-permute-start | bytes 270344 | tf_op jit(solution)/shard_map/ppermute | solution.py:122
  103.1 5.4 %collective-permute-start.39 = (bf16[160,512]{1,0:T(8,128)(2,1)S(1)}, bf16[160,512]{1,0:T(8,128)(2,1)S(1)}, u32[]{:S(2)}, u32[]{:S(2)}) collective-permute-start(bf16[160,512]{1,0:T(8,128)(2,1)S(1)} %slice.51), channel_id=1, source_target_pairs={{0,8},{8,0},{16,24},{24,16},{1,9},{9,1},{17,25},{25,17},{2,10},{10... | collective-permute-start | bytes 491528 | tf_op jit(solution)/shard_map/ppermute | solution.py:122
  104.6 13.0 %collective-permute-start.44 = (bf16[160,768]{1,0:T(8,128)(2,1)S(1)}, bf16[160,768]{1,0:T(8,128)(2,1)S(1)}, u32[]{:S(2)}, u32[]{:S(2)}) collective-permute-start(bf16[160,768]{1,0:T(8,128)(2,1)S(1)} %add_convert_fusion.4), channel_id=1, source_target_pairs={{0,0},{1,1},{2,4},{3,5},{4,2},{5,3},{6,6},{7,7},{8,8},{9,9},{10,12... | collective-permute-start | bytes 737288 | tf_op jit(solution)/shard_map/ppermute | solution.py:119
  105.3 12.3 %collective-permute-start.46 = (bf16[160,768]{1,0:T(8,128)(2,1)S(1)}, bf16[160,768]{1,0:T(8,128)(2,1)S(1)}, u32[]{:S(2)}, u32[]{:S(2)}) collective-permute-start(bf16[160,768]{1,0:T(8,128)(2,1)S(1)} %add_convert_fusion.3), channel_id=1, source_target_pairs={{0,0},{1,1},{2,4},{3,5},{4,2},{5,3},{6,6},{7,7},{8,8},{9,9},{10,12... | collective-permute-start | bytes 737288 | tf_op jit(solution)/shard_map/ppermute | solution.py:119
  108.5 5.5 %collective-permute-start.40 = (bf16[64,640]{1,0:T(8,128)(2,1)S(1)}, bf16[64,640]{1,0:T(8,128)(2,1)S(1)}, u32[]{:S(2)}, u32[]{:S(2)}) collective-permute-start(bf16[64,640]{1,0:T(8,128)(2,1)S(1)} %collective-permute-done.37.refs_4_), channel_id=1, source_target_pairs={{0,1},{1,0},{2,3},{3,2},{4,5},{5,4},{6,7},{7,6},{8,9},{9,8},{10,11... | collective-permute-start | bytes 245768 | tf_op jit(solution)/shard_map/ppermute | solution.py:107
  108.6 8.6 %collective-permute-start.41 = (bf16[176,256]{1,0:T(8,128)(2,1)S(1)}, bf16[176,256]{1,0:T(8,128)(2,1)S(1)}, u32[]{:S(2)}, u32[]{:S(2)}) collective-permute-start(bf16[176,256]{1,0:T(8,128)(2,1)S(1)} %add_convert_fusion.14), channel_id=1, source_target_pairs={{0,1},{1,0},{2,3},{3,2},{4,5},{5,4},{6,7},{7,6},{8,9},{9,8},{10,11... | collective-permute-start | bytes 270344 | tf_op jit(solution)/shard_map/ppermute | solution.py:107
  110.7 12.0 %collective-permute-start.42 = (bf16[160,512]{1,0:T(8,128)(2,1)S(1)}, bf16[160,512]{1,0:T(8,128)(2,1)S(1)}, u32[]{:S(2)}, u32[]{:S(2)}) collective-permute-start(bf16[160,512]{1,0:T(8,128)(2,1)S(1)} %add_convert_fusion.8), channel_id=1, source_target_pairs={{0,0},{1,1},{2,4},{3,5},{4,2},{5,3},{6,6},{7,7},{8,8},{9,9},{10,12... | collective-permute-start | bytes 491528 | tf_op jit(solution)/shard_map/ppermute | solution.py:119
  117.2 8.8 %collective-permute-start.48 = (bf16[176,256]{1,0:T(8,128)(2,1)S(1)}, bf16[176,256]{1,0:T(8,128)(2,1)S(1)}, u32[]{:S(2)}, u32[]{:S(2)}) collective-permute-start(bf16[176,256]{1,0:T(8,128)(2,1)S(1)} %add_convert_fusion.13), channel_id=1, source_target_pairs={{0,2},{1,3},{2,0},{3,1},{4,6},{5,7},{6,4},{7,5},{8,10},{9,11},{10,... | collective-permute-start | bytes 270344 | tf_op jit(solution)/shard_map/ppermute | solution.py:110
  117.6 13.3 %collective-permute-start.45 = (bf16[160,768]{1,0:T(8,128)(2,1)S(1)}, bf16[160,768]{1,0:T(8,128)(2,1)S(1)}, u32[]{:S(2)}, u32[]{:S(2)}) collective-permute-start(bf16[160,768]{1,0:T(8,128)(2,1)S(1)} %collective-permute-done.44.refs_8_), channel_id=1, source_target_pairs={{0,4},{4,0},{1,5},{5,1},{2,6},{6,2},{3,7},{7,3},{8,12},{12,8},{9,1... | collective-permute-start | bytes 737288 | tf_op jit(solution)/shard_map/ppermute | solution.py:104
  117.6 13.3 %collective-permute-start.47 = (bf16[160,768]{1,0:T(8,128)(2,1)S(1)}, bf16[160,768]{1,0:T(8,128)(2,1)S(1)}, u32[]{:S(2)}, u32[]{:S(2)}) collective-permute-start(bf16[160,768]{1,0:T(8,128)(2,1)S(1)} %collective-permute-done.46.refs_10_), channel_id=1, source_target_pairs={{0,4},{4,0},{1,5},{5,1},{2,6},{6,2},{3,7},{7,3},{8,12},{12,8},{9,1... | collective-permute-start | bytes 737288 | tf_op jit(solution)/shard_map/ppermute | solution.py:104
  122.6 8.4 %collective-permute-start.43 = (bf16[160,512]{1,0:T(8,128)(2,1)S(1)}, bf16[160,512]{1,0:T(8,128)(2,1)S(1)}, u32[]{:S(2)}, u32[]{:S(2)}) collective-permute-start(bf16[160,512]{1,0:T(8,128)(2,1)S(1)} %collective-permute-done.42.refs_6_), channel_id=1, source_target_pairs={{0,4},{4,0},{1,5},{5,1},{2,6},{6,2},{3,7},{7,3},{8,12},{12,8},{9,1... | collective-permute-start | bytes 491528 | tf_op jit(solution)/shard_map/ppermute | solution.py:104
  126.0 4.9 %collective-permute-start.49 = (bf16[176,256]{1,0:T(8,128)(2,1)S(1)}, bf16[176,256]{1,0:T(8,128)(2,1)S(1)}, u32[]{:S(2)}, u32[]{:S(2)}) collective-permute-start(bf16[176,256]{1,0:T(8,128)(2,1)S(1)} %add_convert_fusion.12.refs_12_), channel_id=1, source_target_pairs={{0,4},{4,0},{1,5},{5,1},{2,6},{6,2},{3,7},{7,3},{8,12},{12,8},{9,1... | collective-permute-start | bytes 270344 | tf_op jit(solution)/shard_map/ppermute | solution.py:104
  126.1 4.9 %collective-permute-start.36 = (bf16[64,640]{1,0:T(8,128)(2,1)S(1)}, bf16[64,640]{1,0:T(8,128)(2,1)S(1)}, u32[]{:S(2)}, u32[]{:S(2)}) collective-permute-start(bf16[64,640]{1,0:T(8,128)(2,1)S(1)} %last_norm.1.refs_2_), channel_id=1, source_target_pairs={{0,1},{1,0},{2,3},{3,2},{4,5},{5,4},{6,7},{7,6},{8,9},{9,8},{10,11... | collective-permute-start | bytes 245768 | tf_op jit(solution)/shard_map/ppermute | solution.py:107
  (7 other events, 31.4 us)
